TPU v7x, 32 devices: a whole 2x2x4 slice. The times are simulated.
32 devices in a mesh: seq: 16 (over z, x, core), tp: 2 (over y).
Axes of the slice: x: 2, y: 2, z: 4, core: 2. Of those that a mesh axis runs over, the one named last changes fastest.
Arguments:
- tokens: bfloat16 [2048, 5120], P('seq', 'tp'), may hold values from -4 to 4
- self_queries: bfloat16 [2048, 3072], P('seq', 'tp'), may hold values from -12 to 12
- self_keys: bfloat16 [2048, 3072], P('seq', 'tp'), may hold values from -12 to 12
- self_values: bfloat16 [2048, 3072], P('seq', 'tp'), may hold values from -6 to 6
- cross_queries: bfloat16 [2048, 3072], P('seq', 'tp'), may hold values from -12 to 12
- caption_keys: bfloat16 [512, 3072], P('seq', 'tp'), may hold values from -12 to 12
- caption_values: bfloat16 [512, 3072], P('seq', 'tp'), may hold values from -6 to 6
- out_weight: bfloat16 [3072, 5120], P('tp'), may hold values from -0.15625 to 0.15625
- gate_vector: float32 [5120], P('tp'), may hold values from -6 to 6
Outputs:
- updated: bfloat16 [2048, 5120], P('seq', 'tp')
- cross_heads: bfloat16 [2048, 3072], P('seq', 'tp')
All inputs are finite; a program needn't handle non-finite values.
Results may differ from a plain program's by a relative error of at most 0.0085.
Values may be sent and summed in bfloat16 or wider, within the bound.
No kernel may reach another device: no remote copies, remote signals or barrier semaphores. Data moves between devices by JAX's collectives and lax.ppermute only.
A program may use at most 128 MiB of HBM per device.

v0:
```python
import math

import jax
import jax.numpy as jnp
from jax import lax
from jax.sharding import PartitionSpec as P

DH = 128


def online_step(running, pieces, query_split, score_scale):
    maxima, totals, accum = running
    keys_piece, values_piece = pieces
    row_count = keys_piece.shape[0]
    heads_here = query_split.shape[1]
    keys_split = keys_piece.reshape(row_count, heads_here, DH)
    values_split = values_piece.reshape(row_count, heads_here, DH)
    scores = (
        jnp.einsum("thd,khd->thk", query_split, keys_split, preferred_element_type=jnp.float32)
        * score_scale
    )
    new_max = jnp.maximum(maxima, jnp.max(scores, axis=2))
    rescale = jnp.exp(maxima - new_max)
    exp_scores = jnp.exp(scores - new_max[:, :, None])
    totals = totals * rescale + jnp.sum(exp_scores, axis=2)
    weights = exp_scores.astype(jnp.bfloat16)
    accum = accum * rescale[:, :, None] + jnp.einsum(
        "thk,khd->thd", weights, values_split, preferred_element_type=jnp.float32
    )
    return (new_max, totals, accum)


def bounded_step(running, pieces, query_split, score_scale):
    row_count = pieces[0].shape[0]
    block_rows = math.gcd(row_count, 1024)
    if block_rows == row_count:
        return online_step(running, pieces, query_split, score_scale)

    def loop_body(position, current):
        keys_piece = lax.dynamic_slice_in_dim(pieces[0], position * block_rows, block_rows, 0)
        values_piece = lax.dynamic_slice_in_dim(pieces[1], position * block_rows, block_rows, 0)
        return online_step(current, (keys_piece, values_piece), query_split, score_scale)

    return lax.fori_loop(0, row_count // block_rows, loop_body, running)


def initial_state(row_count, heads_here):
    return (
        jnp.full((row_count, heads_here), -1e30, jnp.float32),
        jnp.zeros((row_count, heads_here), jnp.float32),
        jnp.zeros((row_count, heads_here, DH), jnp.float32),
    )


def finish(running):
    maxima, totals, accum = running
    row_count, heads_here = totals.shape
    return (accum / totals[:, :, None]).reshape(row_count, heads_here * DH).astype(jnp.bfloat16)


def shards(
    tokens,
    self_queries,
    self_keys,
    self_values,
    cross_queries,
    caption_keys,
    caption_values,
    out_weight,
    gate_vector,
):
    row_count = self_queries.shape[0]
    heads_here = self_queries.shape[1] // DH
    score_scale = 1.0 / math.sqrt(DH)
    self_split = self_queries.reshape(row_count, heads_here, DH)
    cross_split = cross_queries.reshape(row_count, heads_here, DH)
    self_state = bounded_step(
        initial_state(row_count, heads_here),
        (
            lax.all_gather(self_keys, "seq", axis=0, tiled=True),
            lax.all_gather(self_values, "seq", axis=0, tiled=True),
        ),
        self_split,
        score_scale,
    )
    self_heads = finish(self_state)
    caption_all = (
        lax.all_gather(caption_keys, "seq", axis=0, tiled=True),
        lax.all_gather(caption_values, "seq", axis=0, tiled=True),
    )
    cross_state = bounded_step(
        initial_state(row_count, heads_here), caption_all, cross_split, score_scale
    )
    cross_heads = finish(cross_state)
    partial_terms = jnp.dot(self_heads, out_weight, preferred_element_type=jnp.float32)
    projected = lax.psum_scatter(
        partial_terms.astype(jnp.bfloat16), "tp", scatter_dimension=1, tiled=True
    ).astype(jnp.float32)
    updated = (tokens.astype(jnp.float32) + gate_vector[None, :] * projected).astype(jnp.bfloat16)
    return (updated, cross_heads)


def solution(mesh):
    return jax.shard_map(
        shards,
        mesh=mesh,
        in_specs=(
            P("seq", "tp"),
            P("seq", "tp"),
            P("seq", "tp"),
            P("seq", "tp"),
            P("seq", "tp"),
            P("seq", "tp"),
            P("seq", "tp"),
            P("tp", None),
            P("tp"),
        ),
        out_specs=(P("seq", "tp"), P("seq", "tp")),
        check_vma=False,
    )
```

profile of v0, /device:TPU:0, one launch (start us, length us, event | category | flops | bytes accessed | tf_op | source)
XLA Modules:
  0.0 259.5 jit_solution(5244744670284265529)
XLA Ops:
  7.2 1.9 copy.32
  9.1 0.0 all-gather.7.cloned.1.call-start
  9.2 1.9 copy.34
  11.2 0.7 all-gather.11.cloned.1.call-update
  11.9 0.5 all-gather.9.cloned.1.call-update
  12.5 1.2 copy.33
  13.8 0.2 copy.35
  14.0 65.1 %all-gather.5.cloned.1.call-done = bf16[2048,1536]{0,1:T(8,128)(2,1)} async-done(((bf16[128,1536]{0,1:T(8,128)(2,1)}), bf16[2048,1536]{0,1:T(8,128)(2,1)}) %all-gather.5.cloned.1.call-update) | async-done | bytes 6291472 | tf_op jit(solution)/shard_map/all_gather | solution.py:80
  79.1 66.6 %all-gather.7.cloned.1.call-done = bf16[2048,1536]{0,1:T(8,128)(2,1)} async-done(((bf16[128,1536]{0,1:T(8,128)(2,1)}), bf16[2048,1536]{0,1:T(8,128)(2,1)}) %all-gather.7.cloned.1.call-update) | async-done | bytes 6291472 | tf_op jit(solution)/shard_map/all_gather | solution.py:81
  145.7 30.5 %while.18 = (s32[]{:T(128)}, f32[128,12]{0,1:T(8,128)S(1)}, f32[128,12]{0,1:T(8,128)}, f32[128,12,128]{0,2,1:T(8,128)}, bf16[2048,1536]{0,1:T(8,128)(2,1)}, /*in...) while((s32[]{:T(128)}, f32[128,12]{0,1:T(8,128)S(1)}, ...), condition=%wide.region_3.0_spmd.clone, body=%wide.region_0.0_spmd.clone.sunk | while | flops 818486784 | bytes 65028356 | solution.py:44
  145.7 3.6 %constant_dynamic-slice_fusion.3 = (bf16[1024,1536]{0,1:T(8,128)(2,1)S(1)}, bf16[1024,1536]{0,1:T(8,128)(2,1)S(1)}) fusion(bf16[2048,1536]{0,1:T(8,128)(2,1)} %get-tuple-element.280, s32[]{:T(128)S(6)} %select_n.10, bf16[2048,1536]{0,1:T(8,128)(2,1)} %get-tuple-element.278), kind=kLoop, calls=%fused_computation.15.clone.1 | loop fusion | bytes 12582916 | tf_op jit(solution)/shard_map/while/body/eval_jaxpr/dynamic_slice | solution.py:41
  149.3 3.8 %bitcast_reduce_fusion.3 = (f32[128,12]{0,1:T(8,128)S(1)}, f32[12,1024,128]{2,1,0:T(8,128)}) fusion(bf16[1024,12,128]{0,2,1:T(8,128)(2,1)S(1)} %bitcast.79, bf16[128,12,128]{2,0,1:T(8,128)(2,1)S(1)} %get-tuple-element.279), kind=kOutput, calls=%fused_computation.1.clone.1 | convolution fusion | flops 405797376 | bytes 9836544 | tf_op jit(solution)/shard_map/while/body/eval_jaxpr/thd,khd->thk/dot_general | solution.py:19
  153.1 4.0 %fusion.55 = f32[128,12]{0,1:T(8,128)S(1)} fusion(f32[12,1024,128]{2,1,0:T(8,128)} %get-tuple-element.248, f32[128,12]{0,1:T(8,128)S(1)} %select_maximum_fusion.2), kind=kLoop, calls=%fused_computation.4.clone.1 | loop fusion | flops 4717056 | bytes 6303744 | tf_op jit(solution)/shard_map/while/body/eval_jaxpr/reduce_sum | solution.py:25
  157.2 0.6 copy-done
  157.8 2.5 fusion.57
  160.4 3.6 %constant_dynamic-slice_fusion.3 = (bf16[1024,1536]{0,1:T(8,128)(2,1)S(1)}, bf16[1024,1536]{0,1:T(8,128)(2,1)S(1)}) fusion(bf16[2048,1536]{0,1:T(8,128)(2,1)} %get-tuple-element.280, s32[]{:T(128)S(6)} %select_n.10, bf16[2048,1536]{0,1:T(8,128)(2,1)} %get-tuple-element.278), kind=kLoop, calls=%fused_computation.15.clone.1 | loop fusion | bytes 12582916 | tf_op jit(solution)/shard_map/while/body/eval_jaxpr/dynamic_slice | solution.py:41
  163.9 3.8 %bitcast_reduce_fusion.3 = (f32[128,12]{0,1:T(8,128)S(1)}, f32[12,1024,128]{2,1,0:T(8,128)}) fusion(bf16[1024,12,128]{0,2,1:T(8,128)(2,1)S(1)} %bitcast.79, bf16[128,12,128]{2,0,1:T(8,128)(2,1)S(1)} %get-tuple-element.279), kind=kOutput, calls=%fused_computation.1.clone.1 | convolution fusion | flops 405797376 | bytes 9836544 | tf_op jit(solution)/shard_map/while/body/eval_jaxpr/thd,khd->thk/dot_general | solution.py:19
  167.8 4.0 %fusion.55 = f32[128,12]{0,1:T(8,128)S(1)} fusion(f32[12,1024,128]{2,1,0:T(8,128)} %get-tuple-element.248, f32[128,12]{0,1:T(8,128)S(1)} %select_maximum_fusion.2), kind=kLoop, calls=%fused_computation.4.clone.1 | loop fusion | flops 4717056 | bytes 6303744 | tf_op jit(solution)/shard_map/while/body/eval_jaxpr/reduce_sum | solution.py:25
  171.8 0.8 copy-done
  172.6 3.7 %fusion.57 = f32[128,12,128]{0,2,1:T(8,128)} fusion(bf16[1024,12,128]{0,2,1:T(8,128)(2,1)S(1)} %bitcast.78, f32[12,1024,128]{2,1,0:T(8,128)S(1)} %copy-done, f32[128,12]{0,1:T(8,128)S(1)} %select_maximum_fusion.2, f32[128,12,128]{0,2,1:T(8,128)} %get-tuple-element.266, f32[128,12]{0,1:T(8,128)S(1)} %get-tuple-element.251, pred[]{:T(512)S(6)} %compare.3), kind=kOutput, calls=%fused_computation.9.clone.1 | convolution fusion | flops 407961600 | bytes 11022337 | tf_op jit(solution)/shard_map/while/body/eval_jaxpr/thk,khd->thd/dot_general | solution.py:27
  176.2 1.2 divide_convert_fusion
  177.5 9.0 %convolution_convert_fusion = bf16[128,5120]{1,0:T(8,128)(2,1)} fusion(bf16[128,1536]{0,1:T(8,128)(2,1)S(1)} %bitcast.81, bf16[1536,5120]{1,0:T(8,128)(2,1)} %param.18), kind=kOutput, calls=%fused_computation.18 | convolution fusion | flops 2013921280 | bytes 17432576 | tf_op jit(solution)/shard_map/dot_general | solution.py:95
  186.5 0.2 copy.37
  186.8 1.7 copy.40
  188.5 38.1 %all-gather.9.cloned.1.call-done = bf16[512,1536]{1,0:T(8,128)(2,1)} async-done(((bf16[32,1536]{1,0:T(8,128)(2,1)}), bf16[512,1536]{1,0:T(8,128)(2,1)}) %all-gather.9.cloned.1.call-update) | async-done | bytes 1572880 | tf_op jit(solution)/shard_map/all_gather | solution.py:88
  226.6 1.7 copy.36
  228.4 0.7 bitcast_reduce_fusion.1
  229.1 0.5 fusion.16
  229.6 0.9 fusion.31
  230.5 0.9 copy.42
  231.4 19.4 %reduce-scatter.2.cloned.1.call-done = bf16[128,2560]{1,0:T(8,128)(2,1)} async-done(((bf16[128,5120]{1,0:T(8,128)(2,1)}), bf16[128,2560]{1,0:T(8,128)(2,1)}) %reduce-scatter.2.cloned.1.call-update) | async-done | bytes 655376 | tf_op jit(solution)/shard_map/reduce_scatter | solution.py:96
  250.9 2.1 add_convert_fusion
  (35 shorter events, 0.3 us)
Async XLA Ops:
  7.2 72.0 %all-gather.5.cloned.1.call-start = ((), (), s32[]{:S(2)}) async-start(), calls=%async_computation.1 | async-start | bytes 6684672 | tf_op jit(solution)/shard_map/all_gather | solution.py:80
  9.1 136.6 %all-gather.7.cloned.1.call-start = ((), (), s32[]{:S(2)}) async-start(), calls=%async_computation.2 | async-start | bytes 6684672 | tf_op jit(solution)/shard_map/all_gather | solution.py:81
  11.1 175.6 %all-gather.11.cloned.1.call-start = ((), (), s32[]{:S(2)}) async-start(), calls=%async_computation.5 | async-start | bytes 1671168 | tf_op jit(solution)/shard_map/all_gather | solution.py:89
  11.9 214.8 %all-gather.9.cloned.1.call-start = ((), (), s32[]{:S(2)}) async-start(), calls=%async_computation.4 | async-start | bytes 1671168 | tf_op jit(solution)/shard_map/all_gather | solution.py:88
  12.5 238.4 %reduce-scatter.2.cloned.1.call-start = ((), (), s32[]{:S(2)}) async-start(), calls=%async_computation.3 | async-start | bytes 1966080 | tf_op jit(solution)/shard_map/reduce_scatter | solution.py:96
  153.1 4.0 %copy-start.3 = (f32[128,12]{0,1:T(8,128)S(1)}, f32[128,12]{0,1:T(8,128)}, u32[]{:S(2)}) copy-start(f32[128,12]{0,1:T(8,128)} %get-tuple-element.265) | copy-start | bytes 18436 | tf_op jit(solution)/shard_map/while
  153.1 4.7 %copy-start = (f32[12,1024,128]{2,1,0:T(8,128)S(1)}, f32[12,1024,128]{2,1,0:T(8,128)}, u32[]{:S(2)}) copy-start(f32[12,1024,128]{2,1,0:T(8,128)} %get-tuple-element.248) | copy-start | bytes 18874372 | tf_op jit(solution)/shard_map/while
  157.2 3.2 %copy-start.4 = (f32[128,12]{0,1:T(8,128)}, f32[128,12]{0,1:T(8,128)S(1)}, u32[]{:S(2)}) copy-start(f32[128,12]{0,1:T(8,128)S(1)} %get-tuple-element.276) | copy-start | bytes 18436 | tf_op jit(solution)/shard_map/while
  167.8 4.0 %copy-start.3 = (f32[128,12]{0,1:T(8,128)S(1)}, f32[128,12]{0,1:T(8,128)}, u32[]{:S(2)}) copy-start(f32[128,12]{0,1:T(8,128)} %get-tuple-element.265) | copy-start | bytes 18436 | tf_op jit(solution)/shard_map/while
  167.8 4.8 %copy-start = (f32[12,1024,128]{2,1,0:T(8,128)S(1)}, f32[12,1024,128]{2,1,0:T(8,128)}, u32[]{:S(2)}) copy-start(f32[12,1024,128]{2,1,0:T(8,128)} %get-tuple-element.248) | copy-start | bytes 18874372 | tf_op jit(solution)/shard_map/while
  171.8 4.5 %copy-start.4 = (f32[128,12]{0,1:T(8,128)}, f32[128,12]{0,1:T(8,128)S(1)}, u32[]{:S(2)}) copy-start(f32[128,12]{0,1:T(8,128)S(1)} %get-tuple-element.276) | copy-start | bytes 18436 | tf_op jit(solution)/shard_map/while
  177.5 9.0 %copy-start.2 = (bf16[128,1536]{1,0:T(8,128)(2,1)S(1)}, bf16[128,1536]{1,0:T(8,128)(2,1)}, u32[]{:S(2)}) copy-start(bf16[128,1536]{1,0:T(8,128)(2,1)} %param.15) | copy-start | bytes 1179652
  229.6 21.2 %copy-start.1 = (bf16[128,2560]{1,0:T(8,128)(2,1)S(1)}, bf16[128,2560]{1,0:T(8,128)(2,1)}, u32[]{:S(2)}) copy-start(bf16[128,2560]{1,0:T(8,128)(2,1)} %param.11) | copy-start | bytes 1966084
  229.6 21.2 %copy-start.5 = (f32[2560]{0:T(1024)S(1)}, f32[2560]{0:T(1024)}, u32[]{:S(2)}) copy-start(f32[2560]{0:T(1024)} %param.19) | copy-start | bytes 30724
Sparse Core Ops, SparseCore 0:
  10.7 68.3 all-gather.4
  81.9 63.8 all-gather.6
  148.0 37.8 all-gather.10
  188.0 38.5 all-gather.8
  228.7 22.0 reduce-scatter.1
where the time goes:
time: 260 us
  waiting for transfers between devices  191 us (73%)
  matrix products  24.4 us (9%)
  local copies, waits for them, and re-layouts  18.4 us (7%)
  between operations  13.9 us (5%)
  other arithmetic  11.9 us (5%)
    all_gather x1, waiting for transfers between devices, shards(): lax.all_gather(self_values, 'seq', axis=0, tiled=True)  66.6 us
    all_gather x1, waiting for transfers between devices, shards(): lax.all_gather(self_keys, 'seq', axis=0, tiled=True)  65.1 us
    all_gather x1, waiting for transfers between devices, shards(): lax.all_gather(caption_keys, 'seq', axis=0, tiled=True)  38.1 us
    reduce_scatter x1, waiting for transfers between devices, shards(): lax.psum_scatter(partial_terms.astype(jnp.bfloat16), 'tp', scatter_dimens...  19.4 us
    dot_general x1, matrix products, shards(): jnp.dot(self_heads, out_weight, preferred_element_type=jnp.float32)  8.99 us
    reduce_sum x3, other arithmetic, online_step(): totals = totals * rescale + jnp.sum(exp_scores, axis=2)  8.54 us
    dot_general x3, matrix products, online_step(): jnp.einsum('thd,khd->thk', query_split, keys_split, preferred_element_typ...  8.36 us
    dynamic_slice x2, local copies, waits for them, and re-layouts, loop_body(): lax.dynamic_slice_in_dim(pieces[1], position * block_rows, block_rows, 0)  7.11 us
  transfers between devices with their start and end apart: 5, of which 4 were waited for; matrix products, arithmetic and copies ran while one was open for 19% of the time, Pallas kernels for 0%

commit v1 on v0

v1 whole, which is shorter than its diff:
```python
import math

import jax
import jax.numpy as jnp
from jax import lax
from jax.experimental import pallas as pl
from jax.experimental.pallas import tpu as pltpu
from jax.sharding import PartitionSpec as P

DH = 128
F32 = jnp.float32
BF16 = jnp.bfloat16
VMEM = pltpu.VMEM
LOG2E = 1.4426950408889634


def whole():
    return pl.BlockSpec(memory_space=VMEM)


def cost(flops, nbytes, transcendentals=0):
    return pl.CostEstimate(
        flops=int(flops), bytes_accessed=int(nbytes), transcendentals=int(transcendentals)
    )


def softmax_mix(query, keys, values, factor):
    scores = [
        lax.dot_general(query, block, (((1,), (1,)), ((), ())), preferred_element_type=F32)
        for block in keys
    ]
    top = jnp.max(scores[0], axis=1, keepdims=True)
    for block in scores[1:]:
        top = jnp.maximum(top, jnp.max(block, axis=1, keepdims=True))
    total = None
    mixed = None
    for block, value in zip(scores, values):
        weight = jnp.exp2((block - top) * factor)
        part = jnp.sum(weight, axis=1, keepdims=True)
        total = part if total is None else total + part
        term = jnp.dot(weight.astype(BF16), value, preferred_element_type=F32)
        mixed = term if mixed is None else mixed + term
    return mixed / total


def pack_kernel(groups, zi_ref, q_ref, k_ref, v_ref, ck_ref, cv_ref, *outs):
    width = q_ref.shape[1] // groups
    heads = width // DH
    zi = zi_ref[0]
    for r in range(groups):
        base = pl.multiple_of(lax.rem(zi + r, groups) * width, DH)
        outs[r][...] = q_ref[:, pl.ds(base, width)]
        for h in range(heads):
            out = outs[groups + r * heads + h]
            at = pl.multiple_of(base + h * DH, DH)
            out[:, :DH] = k_ref[:, pl.ds(at, DH)]
            out[:, DH:] = v_ref[:, pl.ds(at, DH)]
    cap = outs[-1]
    rows = ck_ref.shape[0]
    cap[:rows, :] = ck_ref[...]
    cap[rows:, :] = cv_ref[...]


def pack(groups, zi, q, k, v, ck, cv):
    rows, columns = q.shape
    width = columns // groups
    heads = width // DH
    shapes = [jax.ShapeDtypeStruct((rows, width), BF16)] * groups
    shapes += [jax.ShapeDtypeStruct((rows, 2 * DH), BF16)] * (groups * heads)
    shapes += [jax.ShapeDtypeStruct((2 * ck.shape[0], columns), BF16)]
    outs = pl.pallas_call(
        lambda *refs: pack_kernel(groups, *refs),
        out_shape=shapes,
        in_specs=[pl.BlockSpec(memory_space=pltpu.SMEM)] + [whole()] * 5,
        out_specs=[whole()] * len(shapes),
        cost_estimate=cost(0, 6 * rows * columns * 2),
        name="pack",
    )(zi, q, k, v, ck, cv)
    queries = outs[:groups]
    pairs = [outs[groups + r * heads : groups + (r + 1) * heads] for r in range(groups)]
    return queries, pairs, outs[-1]


def attend_kernel(parts, head, factor, *refs):
    queries, pairs, outs = refs[:parts], refs[parts:-parts], refs[-parts:]
    keys = [ref[:, :DH] for ref in pairs]
    values = [ref[:, DH:] for ref in pairs]
    for query, out in zip(queries, outs):
        out[...] = softmax_mix(
            query[:, head * DH : (head + 1) * DH], keys, values, factor
        ).astype(BF16)


def attend(queries, pairs, head, factor):
    parts = len(queries)
    rows = queries[0].shape[0]
    total_keys = sum(p.shape[0] for p in pairs)
    return pl.pallas_call(
        lambda *refs: attend_kernel(parts, head, factor, *refs),
        out_shape=[jax.ShapeDtypeStruct((rows, DH), BF16)] * parts,
        in_specs=[whole()] * (parts + len(pairs)),
        out_specs=[whole()] * parts,
        cost_estimate=cost(
            4 * parts * rows * total_keys * DH, total_keys * DH * 4, parts * rows * total_keys
        ),
        name="attend_%d" % head,
    )(*queries, *pairs)


def cross_kernel(factor, q_ref, *refs):
    pieces, out = refs[:-1], refs[-1]
    rows = pieces[0].shape[0] // 2
    for h in range(q_ref.shape[1] // DH):
        at = slice(h * DH, (h + 1) * DH)
        keys = jnp.concatenate([p[:rows, at] for p in pieces], axis=0)
        values = jnp.concatenate([p[rows:, at] for p in pieces], axis=0)
        out[:, at] = softmax_mix(q_ref[:, at], [keys], [values], factor).astype(BF16)


def cross(q, pieces, factor):
    rows, columns = q.shape
    total_keys = sum(p.shape[0] for p in pieces) // 2
    return pl.pallas_call(
        lambda *refs: cross_kernel(factor, *refs),
        out_shape=jax.ShapeDtypeStruct((rows, columns), BF16),
        in_specs=[whole()] * (1 + len(pieces)),
        out_specs=whole(),
        cost_estimate=cost(
            4 * rows * total_keys * columns,
            (2 * rows + 2 * total_keys) * columns * 2,
            rows * total_keys * columns // DH,
        ),
        name="cross",
    )(q, *pieces)


def project_kernel(groups, heads, at_ref, *refs):
    lhs, w_ref, out = refs[: groups * heads], refs[-2], refs[-1]
    width = heads * DH
    total = None
    for r in range(groups):
        base = pl.multiple_of(lax.rem(at_ref[0] + r, groups) * width, DH)
        left = jnp.concatenate([lhs[r * heads + h][...] for h in range(heads)], axis=1)
        term = jnp.dot(left, w_ref[pl.ds(base, width), :], preferred_element_type=F32)
        total = term if total is None else total + term
    out[...] = total.astype(out.dtype)


def project(groups, at, lhs, weight, columns, dtype, name):
    heads = len(lhs) // groups
    rows = lhs[0].shape[0]
    depth = weight.shape[0]
    block = math.gcd(columns, 512)
    steps = columns // block
    return pl.pallas_call(
        lambda *refs: project_kernel(groups, heads, *refs),
        out_shape=jax.ShapeDtypeStruct((rows, columns), dtype),
        grid_spec=pltpu.PrefetchScalarGridSpec(
            num_scalar_prefetch=1,
            grid=(steps,),
            in_specs=[pl.BlockSpec((rows, DH), lambda n, at: (0, 0))] * len(lhs)
            + [pl.BlockSpec((depth, block), lambda n, at: (0, at[1] * steps + n))],
            out_specs=pl.BlockSpec((rows, block), lambda n, at: (0, n)),
        ),
        cost_estimate=cost(
            2 * rows * depth * columns, depth * columns * 2 + rows * columns * 4
        ),
        name=name,
    )(at, *lhs, weight)


def shards(
    seq_size,
    tp_size,
    tokens,
    self_queries,
    self_keys,
    self_values,
    cross_queries,
    caption_keys,
    caption_values,
    out_weight,
    gate_vector,
):
    rows, columns = self_queries.shape
    heads_here = columns // DH
    factor = LOG2E / math.sqrt(DH)
    groups = math.gcd(heads_here, seq_size)
    members = seq_size // groups
    heads = heads_here // groups
    zi = (lax.axis_index("seq") // members).astype(jnp.int32)
    tpi = lax.axis_index("tp").astype(jnp.int32)

    def rotate(x, r):
        if r % groups == 0:
            return x
        step = (r % groups) * members
        return lax.ppermute(x, "seq", [(s, (s + step) % seq_size) for s in range(seq_size)])

    def swap(x, bit):
        return lax.ppermute(x, "seq", [(s, s ^ bit) for s in range(seq_size)])

    def spread(pieces):
        if members & (members - 1):
            index_groups = [
                [g * members + m for m in range(members)] for g in range(groups)
            ]
            return [
                part
                for x in pieces
                for part in lax.all_gather(x, "seq", axis=0, axis_index_groups=index_groups)
            ]
        bit = members // 2
        while bit:
            pieces = pieces + [swap(x, bit) for x in pieces]
            bit //= 2
        return pieces

    queries, pairs, caption = pack(
        groups, zi[None], self_queries, self_keys, self_values, caption_keys, caption_values
    )
    queries = [rotate(x, r) for r, x in enumerate(queries)]
    mixed = []
    for h in range(heads):
        mine = jnp.concatenate([rotate(pairs[r][h], r) for r in range(groups)], axis=0)
        outs = attend(queries, spread([mine]), h, factor)
        mixed.append([rotate(x, groups - r) for r, x in enumerate(outs)])

    captions = jnp.concatenate([rotate(caption, r) for r in range(groups)], axis=0)
    captions = spread([captions])
    cap_rows = caption.shape[0]
    pieces = [x[g * cap_rows : (g + 1) * cap_rows] for x in captions for g in range(groups)]
    cross_heads = cross(cross_queries, pieces, factor)

    lhs = [mixed[h][r] for r in range(groups) for h in range(heads)]
    out_columns = tokens.shape[1]
    if tp_size == 2:
        away = project(
            groups, jnp.stack([zi, 1 - tpi]), lhs, out_weight, out_columns, BF16, "away"
        )
        away = lax.ppermute(away, "tp", [(0, 1), (1, 0)])
        home = project(groups, jnp.stack([zi, tpi]), lhs, out_weight, out_columns, F32, "home")
        projected = home + away.astype(F32)
    else:
        both = project(
            groups,
            jnp.stack([zi, jnp.zeros_like(tpi)]),
            lhs,
            out_weight,
            out_weight.shape[1],
            BF16,
            "home",
        )
        projected = lax.psum_scatter(both, "tp", scatter_dimension=1, tiled=True).astype(F32)
    updated = (tokens.astype(F32) + gate_vector[None, :] * projected).astype(BF16)
    return (updated, cross_heads)


def solution(mesh):
    seq_size, tp_size = mesh.shape["seq"], mesh.shape["tp"]
    return jax.shard_map(
        lambda *args: shards(seq_size, tp_size, *args),
        mesh=mesh,
        in_specs=(
            P("seq", "tp"),
            P("seq", "tp"),
            P("seq", "tp"),
            P("seq", "tp"),
            P("seq", "tp"),
            P("seq", "tp"),
            P("seq", "tp"),
            P("tp", None),
            P("tp"),
        ),
        out_specs=(P("seq", "tp"), P("seq", "tp")),
        check_vma=False,
    )
```

time: 260 us -> 151 us (0.58)
  waiting for transfers between devices: 191 us -> 61 us
  starting transfers between devices: 0.2 us -> 42.7 us
  Pallas kernels: 0 us -> 35.6 us
  matrix products: 24.4 us -> 0 us
  between operations: 13.9 us -> 0.99 us
  local copies, waits for them, and re-layouts: 18.4 us -> 7.69 us
  other arithmetic: 11.9 us -> 2.35 us
    all_gather x4 -> x0, waiting for transfers between devices: 170 us -> none  [the longest x1 66.6 us: shards(): lax.all_gather(self_values, 'seq', axis=0, tiled=True)]
    ppermute x0 -> x37, waiting for transfers between devices: none -> 61 us  [the longest x24 51.6 us: rotate(): lax.ppermute(x, 'seq', [(s, (s + step) % seq_size) for s in range(seq_siz...]
    ppermute x0 -> x37, starting transfers between devices: none -> 42.7 us  [the longest x24 36.9 us: rotate(): lax.ppermute(x, 'seq', [(s, (s + step) % seq_size) for s in range(seq_siz...]
    pallas_call x0 -> x7, Pallas kernels: none -> 35.6 us  [the longest x2 14.6 us: project(): pl.pallas_call(lambda *refs: project_kernel(groups, heads, *refs), out_sh...]
    dot_general x7 -> x0, matrix products: 24.4 us -> none  [the longest x1 8.99 us: shards(): jnp.dot(self_heads, out_weight, preferred_element_type=jnp.float32)]
    reduce_scatter x1 -> x0, waiting for transfers between devices: 19.4 us -> none  [shards(): lax.psum_scatter(partial_terms.astype(jnp.bfloat16), 'tp', scatter_dimens...]
    reduce_sum x3 -> x0, other arithmetic: 8.54 us -> none  [online_step(): totals = totals * rescale + jnp.sum(exp_scores, axis=2)]
    dynamic_slice x2 -> x0, local copies, waits for them, and re-layouts: 7.11 us -> none  [loop_body(): lax.dynamic_slice_in_dim(pieces[1], position * block_rows, block_rows, 0)]
  transfers between devices with their start and end apart: 5 -> 37, of which waited for: 4 -> 20; matrix products, arithmetic and copies ran while one was open for 19% -> 5% of each run, Pallas kernels for 0% -> 18%
where the time goes in v1:
time: 151 us; the launch traced here: 150 us
  waiting for transfers between devices  61 us (40%)
  starting transfers between devices  42.7 us (28%)
  Pallas kernels  35.6 us (24%)
  local copies, waits for them, and re-layouts  7.69 us (5%)
  other arithmetic  2.35 us (2%)
    ppermute x24, waiting for transfers between devices, rotate(): lax.ppermute(x, 'seq', [(s, (s + step) % seq_size) for s in range(seq_siz...  51.6 us
    ppermute x24, starting transfers between devices, rotate(): lax.ppermute(x, 'seq', [(s, (s + step) % seq_size) for s in range(seq_siz...  36.9 us
    pallas_call x2, Pallas kernels, project(): pl.pallas_call(lambda *refs: project_kernel(groups, heads, *refs), out_sh...  14.6 us
    pallas_call x3, Pallas kernels, attend(): pl.pallas_call(lambda *refs: attend_kernel(parts, head, factor, *refs), o...  12.4 us
    pallas_call x1, Pallas kernels, cross(): pl.pallas_call(lambda *refs: cross_kernel(factor, *refs), out_shape=jax.S...  6.08 us
    ppermute x12, waiting for transfers between devices, swap(): return lax.ppermute(x, 'seq', [(s, s ^ bit) for s in range(seq_size)])  5.74 us
    unnamed x80, local copies, waits for them, and re-layouts  4.9 us
    ppermute x12, starting transfers between devices, swap(): return lax.ppermute(x, 'seq', [(s, s ^ bit) for s in range(seq_size)])  4.22 us
  transfers between devices with their start and end apart: 37, of which 20 were waited for; matrix products, arithmetic and copies ran while one was open for 5% of the time, Pallas kernels for 18%

profile of v1, /device:TPU:0, one launch (start us, length us, event | category | flops | bytes accessed | tf_op | source)
XLA Modules:
  0.0 150.4 jit_solution(10632915459795948369)
XLA Ops:
  0.6 2.6 %pack.1 = (bf16[128,384]{1,0:T(8,128)(2,1)}, bf16[128,384]{1,0:T(8,128)(2,1)}, bf16[128,384]{1,0:T(8,128)(2,1)}, bf16[128,384]{1,0:T(8,128)(2,1)}, bf16[128,256]...) custom-call(s32[1]{0:T(128)} %bitcast.refs_0_, ...), custom_call_target="tpu_custom_call" | custom-call | bytes 2359296 | tf_op jit(solution)/shard_map/pack/pallas_call | solution.py:71
  3.3 3.1 %collective-permute-start.31 = (bf16[64,1536]{1,0:T(8,128)(2,1)}, bf16[64,1536]{1,0:T(8,128)(2,1)S(1)}, u32[]{:S(2)}, u32[]{:S(2)}) collective-permute-start(bf16[64,1536]{1,0:T(8,128)(2,1)} %get-tuple-element.59.refs_1_), channel_id=1, source_target_pairs={{0,8},{2,10},{4,12},{6,14},{8,16},{10,18},{12,20},{14,22},{16,24},... | collective-permute-start | bytes 589832 | tf_op jit(solution)/shard_map/ppermute | solution.py:198
  6.3 2.6 %collective-permute-start.32 = (bf16[64,1536]{1,0:T(8,128)(2,1)}, bf16[64,1536]{1,0:T(8,128)(2,1)S(1)}, u32[]{:S(2)}, u32[]{:S(2)}) collective-permute-start(bf16[64,1536]{1,0:T(8,128)(2,1)} %get-tuple-element.59.refs_1_), channel_id=1, source_target_pairs={{0,16},{2,18},{4,20},{6,22},{8,24},{10,26},{12,28},{14,30},{16,0},... | collective-permute-start | bytes 589832 | tf_op jit(solution)/shard_map/ppermute | solution.py:198
  9.0 1.8 %collective-permute-start.1 = (bf16[128,384]{1,0:T(8,128)(2,1)}, bf16[128,384]{1,0:T(8,128)(2,1)S(1)}, u32[]{:S(2)}, u32[]{:S(2)}) collective-permute-start(bf16[128,384]{1,0:T(8,128)(2,1)} %get-tuple-element.33), channel_id=1, source_target_pairs={{0,16},{2,18},{4,20},{6,22},{8,24},{10,26},{12,28},{14,30},{16,0},... | collective-permute-start | bytes 294920 | tf_op jit(solution)/shard_map/ppermute | solution.py:198
  10.8 2.5 %collective-permute-start.3 = (bf16[128,256]{1,0:T(8,128)(2,1)}, bf16[128,256]{1,0:T(8,128)(2,1)S(1)}, u32[]{:S(2)}, u32[]{:S(2)}) collective-permute-start(bf16[128,256]{1,0:T(8,128)(2,1)} %get-tuple-element.36), channel_id=1, source_target_pairs={{0,8},{2,10},{4,12},{6,14},{8,16},{10,18},{12,20},{14,22},{16,24},... | collective-permute-start | bytes 196616 | tf_op jit(solution)/shard_map/ppermute | solution.py:198
  16.8 6.6 %collective-permute-done.3 = bf16[128,256]{1,0:T(8,128)(2,1)S(1)} collective-permute-done((bf16[128,256]{1,0:T(8,128)(2,1)}, bf16[128,256]{1,0:T(8,128)(2,1)S(1)}, u32[]{:S(2)}, u32[]{:S(2)}) %collective-permute-start.3) | collective-permute-done | bytes 65568 | tf_op jit(solution)/shard_map/ppermute | solution.py:198
  23.4 7.2 %collective-permute-start.4 = (bf16[128,256]{1,0:T(8,128)(2,1)}, bf16[128,256]{1,0:T(8,128)(2,1)S(1)}, u32[]{:S(2)}, u32[]{:S(2)}) collective-permute-start(bf16[128,256]{1,0:T(8,128)(2,1)} %get-tuple-element.37), channel_id=1, source_target_pairs={{0,16},{2,18},{4,20},{6,22},{8,24},{10,26},{12,28},{14,30},{16,0},... | collective-permute-start | bytes 196616 | tf_op jit(solution)/shard_map/ppermute | solution.py:198
  30.6 3.1 %collective-permute-done.4 = bf16[128,256]{1,0:T(8,128)(2,1)S(1)} collective-permute-done((bf16[128,256]{1,0:T(8,128)(2,1)}, bf16[128,256]{1,0:T(8,128)(2,1)S(1)}, u32[]{:S(2)}, u32[]{:S(2)}) %collective-permute-start.4) | collective-permute-done | bytes 65568 | tf_op jit(solution)/shard_map/ppermute | solution.py:198
  33.8 4.5 %collective-permute-done.5 = bf16[128,256]{1,0:T(8,128)(2,1)S(1)} collective-permute-done((bf16[128,256]{1,0:T(8,128)(2,1)}, bf16[128,256]{1,0:T(8,128)(2,1)S(1)}, u32[]{:S(2)}, u32[]{:S(2)}) %collective-permute-start.5) | collective-permute-done | bytes 65568 | tf_op jit(solution)/shard_map/ppermute | solution.py:198
  39.5 5.1 %collective-permute-done.9 = bf16[128,256]{1,0:T(8,128)(2,1)S(1)} collective-permute-done((bf16[128,256]{1,0:T(8,128)(2,1)}, bf16[128,256]{1,0:T(8,128)(2,1)S(1)}, u32[]{:S(2)}, u32[]{:S(2)}) %collective-permute-start.9) | collective-permute-done | bytes 65568 | tf_op jit(solution)/shard_map/ppermute | solution.py:198
  45.9 4.2 %collective-permute-done.10 = bf16[128,256]{1,0:T(8,128)(2,1)S(1)} collective-permute-done((bf16[128,256]{1,0:T(8,128)(2,1)}, bf16[128,256]{1,0:T(8,128)(2,1)S(1)}, u32[]{:S(2)}, u32[]{:S(2)}) %collective-permute-start.10) | collective-permute-done | bytes 65568 | tf_op jit(solution)/shard_map/ppermute | solution.py:198
  51.2 3.1 %collective-permute-done.11 = bf16[128,256]{1,0:T(8,128)(2,1)S(1)} collective-permute-done((bf16[128,256]{1,0:T(8,128)(2,1)S(1)}, bf16[128,256]{1,0:T(8,128)(2,1)S(1)}, u32[]{:S(2)}, u32[]{:S(2)}) %collective-permute-start.11) | collective-permute-done | bytes 65568 | tf_op jit(solution)/shard_map/ppermute | solution.py:198
  54.5 6.4 %collective-permute-done.15 = bf16[128,256]{1,0:T(8,128)(2,1)S(1)} collective-permute-done((bf16[128,256]{1,0:T(8,128)(2,1)S(1)}, bf16[128,256]{1,0:T(8,128)(2,1)S(1)}, u32[]{:S(2)}, u32[]{:S(2)}) %collective-permute-start.15) | collective-permute-done | bytes 65568 | tf_op jit(solution)/shard_map/ppermute | solution.py:198
  60.9 5.3 %collective-permute-done.16 = bf16[128,256]{1,0:T(8,128)(2,1)S(1)} collective-permute-done((bf16[128,256]{1,0:T(8,128)(2,1)S(1)}, bf16[128,256]{1,0:T(8,128)(2,1)S(1)}, u32[]{:S(2)}, u32[]{:S(2)}) %collective-permute-start.16) | collective-permute-done | bytes 65568 | tf_op jit(solution)/shard_map/ppermute | solution.py:198
  67.5 3.0 %collective-permute-done.17 = bf16[128,256]{1,0:T(8,128)(2,1)S(1)} collective-permute-done((bf16[128,256]{1,0:T(8,128)(2,1)S(1)}, bf16[128,256]{1,0:T(8,128)(2,1)S(1)}, u32[]{:S(2)}, u32[]{:S(2)}) %collective-permute-start.17) | collective-permute-done | bytes 65568 | tf_op jit(solution)/shard_map/ppermute | solution.py:198
  71.9 3.2 %collective-permute-start.2 = (bf16[128,384]{1,0:T(8,128)(2,1)S(1)}, bf16[128,384]{1,0:T(8,128)(2,1)S(1)}, u32[]{:S(2)}, u32[]{:S(2)}) collective-permute-start(bf16[128,384]{1,0:T(8,128)(2,1)S(1)} %copy-done.24), channel_id=1, source_target_pairs={{0,24},{2,26},{4,28},{6,30},{8,0},{10,2},{12,4},{14,6},{16,8},{18,... | collective-permute-start | bytes 294920 | tf_op jit(solution)/shard_map/ppermute | solution.py:198
  75.8 1.5 collective-permute-done.2.refs_3_
  78.1 3.3 %collective-permute-done.33.refs_4_ = bf16[64,1536]{1,0:T(8,128)(2,1)S(1)} collective-permute-done((bf16[64,1536]{1,0:T(8,128)(2,1)S(1)}, bf16[64,1536]{1,0:T(8,128)(2,1)S(1)}, u32[]{:S(2)}, u32[]{:S(2)}) %collective-permute-start.33) | collective-permute-done | bytes 196640 | tf_op jit(solution)/shard_map/ppermute | solution.py:198
  83.5 4.7 %collective-permute-done.18.refs_5_ = bf16[512,256]{1,0:T(8,128)(2,1)} collective-permute-done((bf16[512,256]{1,0:T(8,128)(2,1)S(1)}, bf16[512,256]{1,0:T(8,128)(2,1)}, u32[]{:S(2)}, u32[]{:S(2)}) %collective-permute-start.18) | collective-permute-done | bytes 262176 | tf_op jit(solution)/shard_map/ppermute | solution.py:201
  89.4 4.1 %attend_0.1 = (bf16[128,128]{1,0:T(8,128)(2,1)}, bf16[128,128]{1,0:T(8,128)(2,1)}, bf16[128,128]{1,0:T(8,128)(2,1)}, bf16[128,128]{1,0:T(8,128)(2,1)}) custom-call(bf16[128,384]{1,0:T(8,128)(2,1)} %get-tuple-element.31.refs_0_, bf16[128,384]{1,0:T(8,128)(2,1)} %copy-done.22, bf16[128,384]{1,0:T(8,128)(2,1)} %copy-done.23, bf16[128,384]{1,0:T(8,128)(2,1)} %copy-done.25, ...), custom_call_target="tpu_custom_call" | custom-call | flops 536870912 | bytes 1048576 | tf_op jit(solution)/shard_map/attend_0/pallas_call | solution.py:98
  93.6 2.7 %collective-permute-start.21 = (bf16[128,128]{1,0:T(8,128)(2,1)}, bf16[128,128]{1,0:T(8,128)(2,1)S(1)}, u32[]{:S(2)}, u32[]{:S(2)}) collective-permute-start(bf16[128,128]{1,0:T(8,128)(2,1)} %get-tuple-element.50), channel_id=1, source_target_pairs={{0,24},{2,26},{4,28},{6,30},{8,0},{10,2},{12,4},{14,6},{16,8},{18,... | collective-permute-start | bytes 98312 | tf_op jit(solution)/shard_map/ppermute | solution.py:198
  96.3 4.1 %attend_1.1 = (bf16[128,128]{1,0:T(8,128)(2,1)}, bf16[128,128]{1,0:T(8,128)(2,1)}, bf16[128,128]{1,0:T(8,128)(2,1)}, bf16[128,128]{1,0:T(8,128)(2,1)}) custom-call(bf16[128,384]{1,0:T(8,128)(2,1)} %get-tuple-element.31.refs_0_, bf16[128,384]{1,0:T(8,128)(2,1)} %copy-done.22, bf16[128,384]{1,0:T(8,128)(2,1)} %copy-done.23, bf16[128,384]{1,0:T(8,128)(2,1)} %copy-done.25, ...), custom_call_target="tpu_custom_call" | custom-call | flops 536870912 | bytes 1048576 | tf_op jit(solution)/shard_map/attend_1/pallas_call | solution.py:98
  100.5 4.1 %attend_2.1 = (bf16[128,128]{1,0:T(8,128)(2,1)}, bf16[128,128]{1,0:T(8,128)(2,1)}, bf16[128,128]{1,0:T(8,128)(2,1)}, bf16[128,128]{1,0:T(8,128)(2,1)}) custom-call(bf16[128,384]{1,0:T(8,128)(2,1)} %get-tuple-element.31.refs_0_, bf16[128,384]{1,0:T(8,128)(2,1)} %copy-done.22, bf16[128,384]{1,0:T(8,128)(2,1)} %copy-done.23, bf16[128,384]{1,0:T(8,128)(2,1)} %copy-done.25, ...), custom_call_target="tpu_custom_call" | custom-call | flops 536870912 | bytes 1048576 | tf_op jit(solution)/shard_map/attend_2/pallas_call | solution.py:98
  104.7 3.5 %collective-permute-start.24 = (bf16[128,128]{1,0:T(8,128)(2,1)S(1)}, bf16[128,128]{1,0:T(8,128)(2,1)S(1)}, u32[]{:S(2)}, u32[]{:S(2)}) collective-permute-start(bf16[128,128]{1,0:T(8,128)(2,1)S(1)} %copy-done.32), channel_id=1, source_target_pairs={{0,16},{2,18},{4,20},{6,22},{8,24},{10,26},{12,28},{14,30},{16,0},... | collective-permute-start | bytes 98312 | tf_op jit(solution)/shard_map/ppermute | solution.py:198
  108.8 2.4 %collective-permute-start.26 = (bf16[128,128]{1,0:T(8,128)(2,1)}, bf16[128,128]{1,0:T(8,128)(2,1)S(1)}, u32[]{:S(2)}, u32[]{:S(2)}) collective-permute-start(bf16[128,128]{1,0:T(8,128)(2,1)} %get-tuple-element.55), channel_id=1, source_target_pairs={{0,16},{2,18},{4,20},{6,22},{8,24},{10,26},{12,28},{14,30},{16,0},... | collective-permute-start | bytes 98312 | tf_op jit(solution)/shard_map/ppermute | solution.py:198
  112.0 1.4 collective-permute-done.25.refs_8_
  113.9 1.9 %collective-permute-start.29 = (bf16[128,128]{1,0:T(8,128)(2,1)}, bf16[128,128]{1,0:T(8,128)(2,1)S(1)}, u32[]{:S(2)}, u32[]{:S(2)}) collective-permute-start(bf16[128,128]{1,0:T(8,128)(2,1)} %get-tuple-element.58), channel_id=1, source_target_pairs={{0,8},{2,10},{4,12},{6,14},{8,16},{10,18},{12,20},{14,22},{16,24},... | collective-permute-start | bytes 98312 | tf_op jit(solution)/shard_map/ppermute | solution.py:198
  120.5 7.2 %away.1 = bf16[128,2560]{1,0:T(8,128)(2,1)} custom-call(s32[2]{0:T(128)} %pad_add_fusion.1.refs_0_, bf16[128,128]{1,0:T(8,128)(2,1)} %get-tuple-element.39.refs_1_, bf16[128,128]{1,0:T(8,128)(2,1)} %get-tuple-element.44.refs_2_, bf16[128,128]{1,0:T(8,128)(2,1)} %get-tuple-element.49.refs_3_, bf16[128,128]{1,0:T(8,128)(2,1)} %copy-done.6, ...), custom_call_target="tpu_custom_call" | custom-call | flops 1006632960 | bytes 9175040 | tf_op jit(solution)/shard_map/away/pallas_call | solution.py:155
  127.6 1.6 %collective-permute-start.30 = (bf16[128,2560]{1,0:T(8,128)(2,1)}, bf16[128,2560]{1,0:T(8,128)(2,1)S(1)}, u32[]{:S(2)}, u32[]{:S(2)}) collective-permute-start(bf16[128,2560]{1,0:T(8,128)(2,1)} %away.1), channel_id=1, source_target_pairs={{0,1},{1,0},{2,3},{3,2},{4,5},{5,4},{6,7},{7,6},{8,9},{9,8},{10,11... | collective-permute-start | bytes 1966088 | tf_op jit(solution)/shard_map/ppermute | solution.py:241
  129.3 7.5 %home.1 = f32[128,2560]{1,0:T(8,128)} custom-call(s32[2]{0:T(128)} %pad_add_fusion.refs_0_, bf16[128,128]{1,0:T(8,128)(2,1)} %get-tuple-element.39.refs_1_, bf16[128,128]{1,0:T(8,128)(2,1)} %get-tuple-element.44.refs_2_, bf16[128,128]{1,0:T(8,128)(2,1)} %get-tuple-element.49.refs_3_, bf16[128,128]{1,0:T(8,128)(2,1)} %copy-done.6, ...), custom_call_target="tpu_custom_call" | custom-call | flops 1006632960 | bytes 9175040 | tf_op jit(solution)/shard_map/home/pallas_call | solution.py:155
  138.6 3.7 %collective-permute-done.30 = bf16[128,2560]{1,0:T(8,128)(2,1)S(1)} collective-permute-done((bf16[128,2560]{1,0:T(8,128)(2,1)}, bf16[128,2560]{1,0:T(8,128)(2,1)S(1)}, u32[]{:S(2)}, u32[]{:S(2)}) %collective-permute-start.30) | collective-permute-done | bytes 655392 | tf_op jit(solution)/shard_map/ppermute | solution.py:241
  144.3 6.1 %cross.1 = bf16[128,1536]{1,0:T(8,128)(2,1)} custom-call(bf16[128,1536]{1,0:T(8,128)(2,1)} %refs_0_.1, bf16[64,1536]{1,0:T(8,128)(2,1)} %get-tuple-element.59.refs_1_, bf16[64,1536]{1,0:T(8,128)(2,1)} %copy-done.2, bf16[64,1536]{1,0:T(8,128)(2,1)} %copy-done.3, bf16[64,1536]{1,0:T(8,128)(2,1)} %copy-done.4, bf16[64,1536]{1,0:T(8,128)(2,1)} %get-tuple-element.71.refs_5_, ...), custom_call_target="tpu_custom_call" | custom-call | flops 402653184 | bytes 3932160 | tf_op jit(solution)/shard_map/cross/pallas_call | solution.py:123
  (139 shorter events, 25.4 us)
Async XLA Ops:
  3.3 71.8 %collective-permute-start.31 = (bf16[64,1536]{1,0:T(8,128)(2,1)}, bf16[64,1536]{1,0:T(8,128)(2,1)S(1)}, u32[]{:S(2)}, u32[]{:S(2)}) collective-permute-start(bf16[64,1536]{1,0:T(8,128)(2,1)} %get-tuple-element.59.refs_1_), channel_id=1, source_target_pairs={{0,8},{2,10},{4,12},{6,14},{8,16},{10,18},{12,20},{14,22},{16,24},... | collective-permute-start | bytes 589832 | tf_op jit(solution)/shard_map/ppermute | solution.py:198
  6.3 71.0 %collective-permute-start.32 = (bf16[64,1536]{1,0:T(8,128)(2,1)}, bf16[64,1536]{1,0:T(8,128)(2,1)S(1)}, u32[]{:S(2)}, u32[]{:S(2)}) collective-permute-start(bf16[64,1536]{1,0:T(8,128)(2,1)} %get-tuple-element.59.refs_1_), channel_id=1, source_target_pairs={{0,16},{2,18},{4,20},{6,22},{8,24},{10,26},{12,28},{14,30},{16,0},... | collective-permute-start | bytes 589832 | tf_op jit(solution)/shard_map/ppermute | solution.py:198
  8.9 62.9 %collective-permute-start = (bf16[128,384]{1,0:T(8,128)(2,1)}, bf16[128,384]{1,0:T(8,128)(2,1)S(1)}, u32[]{:S(2)}, u32[]{:S(2)}) collective-permute-start(bf16[128,384]{1,0:T(8,128)(2,1)} %get-tuple-element.32), channel_id=1, source_target_pairs={{0,8},{2,10},{4,12},{6,14},{8,16},{10,18},{12,20},{14,22},{16,24},... | collective-permute-start | bytes 294920 | tf_op jit(solution)/shard_map/ppermute | solution.py:198
  9.0 66.7 %collective-permute-start.1 = (bf16[128,384]{1,0:T(8,128)(2,1)}, bf16[128,384]{1,0:T(8,128)(2,1)S(1)}, u32[]{:S(2)}, u32[]{:S(2)}) collective-permute-start(bf16[128,384]{1,0:T(8,128)(2,1)} %get-tuple-element.33), channel_id=1, source_target_pairs={{0,16},{2,18},{4,20},{6,22},{8,24},{10,26},{12,28},{14,30},{16,0},... | collective-permute-start | bytes 294920 | tf_op jit(solution)/shard_map/ppermute | solution.py:198
  10.8 12.6 %collective-permute-start.3 = (bf16[128,256]{1,0:T(8,128)(2,1)}, bf16[128,256]{1,0:T(8,128)(2,1)S(1)}, u32[]{:S(2)}, u32[]{:S(2)}) collective-permute-start(bf16[128,256]{1,0:T(8,128)(2,1)} %get-tuple-element.36), channel_id=1, source_target_pairs={{0,8},{2,10},{4,12},{6,14},{8,16},{10,18},{12,20},{14,22},{16,24},... | collective-permute-start | bytes 196616 | tf_op jit(solution)/shard_map/ppermute | solution.py:198
  23.4 10.4 %collective-permute-start.4 = (bf16[128,256]{1,0:T(8,128)(2,1)}, bf16[128,256]{1,0:T(8,128)(2,1)S(1)}, u32[]{:S(2)}, u32[]{:S(2)}) collective-permute-start(bf16[128,256]{1,0:T(8,128)(2,1)} %get-tuple-element.37), channel_id=1, source_target_pairs={{0,16},{2,18},{4,20},{6,22},{8,24},{10,26},{12,28},{14,30},{16,0},... | collective-permute-start | bytes 196616 | tf_op jit(solution)/shard_map/ppermute | solution.py:198
  38.3 6.4 %collective-permute-start.9 = (bf16[128,256]{1,0:T(8,128)(2,1)}, bf16[128,256]{1,0:T(8,128)(2,1)S(1)}, u32[]{:S(2)}, u32[]{:S(2)}) collective-permute-start(bf16[128,256]{1,0:T(8,128)(2,1)} %get-tuple-element.41), channel_id=1, source_target_pairs={{0,8},{2,10},{4,12},{6,14},{8,16},{10,18},{12,20},{14,22},{16,24},... | collective-permute-start | bytes 196616 | tf_op jit(solution)/shard_map/ppermute | solution.py:198
  44.6 5.5 %collective-permute-start.10 = (bf16[128,256]{1,0:T(8,128)(2,1)}, bf16[128,256]{1,0:T(8,128)(2,1)S(1)}, u32[]{:S(2)}, u32[]{:S(2)}) collective-permute-start(bf16[128,256]{1,0:T(8,128)(2,1)} %get-tuple-element.42), channel_id=1, source_target_pairs={{0,16},{2,18},{4,20},{6,22},{8,24},{10,26},{12,28},{14,30},{16,0},... | collective-permute-start | bytes 196616 | tf_op jit(solution)/shard_map/ppermute | solution.py:198
  54.4 6.6 %collective-permute-start.15 = (bf16[128,256]{1,0:T(8,128)(2,1)S(1)}, bf16[128,256]{1,0:T(8,128)(2,1)S(1)}, u32[]{:S(2)}, u32[]{:S(2)}) collective-permute-start(bf16[128,256]{1,0:T(8,128)(2,1)S(1)} %copy-done.28), channel_id=1, source_target_pairs={{0,8},{2,10},{4,12},{6,14},{8,16},{10,18},{12,20},{14,22},{16,24},... | collective-permute-start | bytes 196616 | tf_op jit(solution)/shard_map/ppermute | solution.py:198
  60.9 5.3 %collective-permute-start.16 = (bf16[128,256]{1,0:T(8,128)(2,1)S(1)}, bf16[128,256]{1,0:T(8,128)(2,1)S(1)}, u32[]{:S(2)}, u32[]{:S(2)}) collective-permute-start(bf16[128,256]{1,0:T(8,128)(2,1)S(1)} %copy-done.27), channel_id=1, source_target_pairs={{0,16},{2,18},{4,20},{6,22},{8,24},{10,26},{12,28},{14,30},{16,0},... | collective-permute-start | bytes 196616 | tf_op jit(solution)/shard_map/ppermute | solution.py:198
  70.5 7.5 %collective-permute-start.6 = (bf16[512,256]{1,0:T(8,128)(2,1)S(1)}, bf16[512,256]{1,0:T(8,128)(2,1)S(1)}, u32[]{:S(2)}, u32[]{:S(2)}) collective-permute-start(bf16[512,256]{1,0:T(8,128)(2,1)S(1)} %constant_dynamic-update-slice_fusion.refs_4_), channel_id=1, source_target_pairs={{0,4},{2,6},{4,0},{6,2},{8,12},{10,14},{12,8},{14,10},{16,20},{18,... | collective-permute-start | bytes 786440 | tf_op jit(solution)/shard_map/ppermute | solution.py:201
  71.9 5.4 %collective-permute-start.2 = (bf16[128,384]{1,0:T(8,128)(2,1)S(1)}, bf16[128,384]{1,0:T(8,128)(2,1)S(1)}, u32[]{:S(2)}, u32[]{:S(2)}) collective-permute-start(bf16[128,384]{1,0:T(8,128)(2,1)S(1)} %copy-done.24), channel_id=1, source_target_pairs={{0,24},{2,26},{4,28},{6,30},{8,0},{10,2},{12,4},{14,6},{16,8},{18,... | collective-permute-start | bytes 294920 | tf_op jit(solution)/shard_map/ppermute | solution.py:198
  75.1 7.4 %collective-permute-start.12 = (bf16[512,256]{1,0:T(8,128)(2,1)S(1)}, bf16[512,256]{1,0:T(8,128)(2,1)S(1)}, u32[]{:S(2)}, u32[]{:S(2)}) collective-permute-start(bf16[512,256]{1,0:T(8,128)(2,1)S(1)} %constant_dynamic-update-slice_fusion.4.refs_4_), channel_id=1, source_target_pairs={{0,4},{2,6},{4,0},{6,2},{8,12},{10,14},{12,8},{14,10},{16,20},{18,... | collective-permute-start | bytes 786440 | tf_op jit(solution)/shard_map/ppermute | solution.py:201
  75.7 5.7 %collective-permute-start.33 = (bf16[64,1536]{1,0:T(8,128)(2,1)S(1)}, bf16[64,1536]{1,0:T(8,128)(2,1)S(1)}, u32[]{:S(2)}, u32[]{:S(2)}) collective-permute-start(bf16[64,1536]{1,0:T(8,128)(2,1)S(1)} %copy-done.1), channel_id=1, source_target_pairs={{0,24},{2,26},{4,28},{6,30},{8,0},{10,2},{12,4},{14,6},{16,8},{18,... | collective-permute-start | bytes 589832 | tf_op jit(solution)/shard_map/ppermute | solution.py:198
  77.3 10.9 %collective-permute-start.18 = (bf16[512,256]{1,0:T(8,128)(2,1)S(1)}, bf16[512,256]{1,0:T(8,128)(2,1)}, u32[]{:S(2)}, u32[]{:S(2)}) collective-permute-start(bf16[512,256]{1,0:T(8,128)(2,1)S(1)} %constant_dynamic-update-slice_fusion.8.refs_4_), channel_id=1, source_target_pairs={{0,4},{2,6},{4,0},{6,2},{8,12},{10,14},{12,8},{14,10},{16,20},{18,... | collective-permute-start | bytes 786440 | tf_op jit(solution)/shard_map/ppermute | solution.py:201
  77.9 10.3 %collective-permute-start.8 = (bf16[512,256]{1,0:T(8,128)(2,1)S(1)}, bf16[512,256]{1,0:T(8,128)(2,1)S(1)}, u32[]{:S(2)}, u32[]{:S(2)}) collective-permute-start(bf16[512,256]{1,0:T(8,128)(2,1)S(1)} %collective-permute-done.6.refs_5_), channel_id=1, source_target_pairs={{0,2},{2,0},{4,6},{6,4},{8,10},{10,8},{12,14},{14,12},{16,18},{18,... | collective-permute-start | bytes 786440 | tf_op jit(solution)/shard_map/ppermute | solution.py:201
  81.4 12.2 %collective-permute-start.13 = (bf16[512,256]{1,0:T(8,128)(2,1)S(1)}, bf16[512,256]{1,0:T(8,128)(2,1)}, u32[]{:S(2)}, u32[]{:S(2)}) collective-permute-start(bf16[512,256]{1,0:T(8,128)(2,1)S(1)} %constant_dynamic-update-slice_fusion.4.refs_4_), channel_id=1, source_target_pairs={{0,2},{2,0},{4,6},{6,4},{8,10},{10,8},{12,14},{14,12},{16,18},{18,... | collective-permute-start | bytes 786440 | tf_op jit(solution)/shard_map/ppermute | solution.py:201
  82.5 13.8 %collective-permute-start.14 = (bf16[512,256]{1,0:T(8,128)(2,1)S(1)}, bf16[512,256]{1,0:T(8,128)(2,1)}, u32[]{:S(2)}, u32[]{:S(2)}) collective-permute-start(bf16[512,256]{1,0:T(8,128)(2,1)S(1)} %collective-permute-done.12.refs_5_), channel_id=1, source_target_pairs={{0,2},{2,0},{4,6},{6,4},{8,10},{10,8},{12,14},{14,12},{16,18},{18,... | collective-permute-start | bytes 786440 | tf_op jit(solution)/shard_map/ppermute | solution.py:201
  82.5 54.3 %collective-permute-start.34 = (bf16[256,1536]{1,0:T(8,128)(2,1)S(1)}, bf16[256,1536]{1,0:T(8,128)(2,1)S(1)}, u32[]{:S(2)}, u32[]{:S(2)}) collective-permute-start(bf16[256,1536]{1,0:T(8,128)(2,1)S(1)} %constant_dynamic-update-slice_fusion.12), channel_id=1, source_target_pairs={{0,4},{2,6},{4,0},{6,2},{8,12},{10,14},{12,8},{14,10},{16,20},{18,... | collective-permute-start | bytes 2359304 | tf_op jit(solution)/shard_map/ppermute | solution.py:201
  88.2 12.3 %collective-permute-start.19 = (bf16[512,256]{1,0:T(8,128)(2,1)S(1)}, bf16[512,256]{1,0:T(8,128)(2,1)}, u32[]{:S(2)}, u32[]{:S(2)}) collective-permute-start(bf16[512,256]{1,0:T(8,128)(2,1)S(1)} %constant_dynamic-update-slice_fusion.8.refs_4_), channel_id=1, source_target_pairs={{0,2},{2,0},{4,6},{6,4},{8,10},{10,8},{12,14},{14,12},{16,18},{18,... | collective-permute-start | bytes 786440 | tf_op jit(solution)/shard_map/ppermute | solution.py:201
  88.9 11.6 %collective-permute-start.20 = (bf16[512,256]{1,0:T(8,128)(2,1)}, bf16[512,256]{1,0:T(8,128)(2,1)}, u32[]{:S(2)}, u32[]{:S(2)}) collective-permute-start(bf16[512,256]{1,0:T(8,128)(2,1)} %collective-permute-done.18.refs_5_), channel_id=1, source_target_pairs={{0,2},{2,0},{4,6},{6,4},{8,10},{10,8},{12,14},{14,12},{16,18},{18,... | collective-permute-start | bytes 786440 | tf_op jit(solution)/shard_map/ppermute | solution.py:201
  93.6 11.1 %collective-permute-start.21 = (bf16[128,128]{1,0:T(8,128)(2,1)}, bf16[128,128]{1,0:T(8,128)(2,1)S(1)}, u32[]{:S(2)}, u32[]{:S(2)}) collective-permute-start(bf16[128,128]{1,0:T(8,128)(2,1)} %get-tuple-element.50), channel_id=1, source_target_pairs={{0,24},{2,26},{4,28},{6,30},{8,0},{10,2},{12,4},{14,6},{16,8},{18,... | collective-permute-start | bytes 98312 | tf_op jit(solution)/shard_map/ppermute | solution.py:198
  100.4 7.8 %collective-permute-start.22 = (bf16[128,128]{1,0:T(8,128)(2,1)}, bf16[128,128]{1,0:T(8,128)(2,1)S(1)}, u32[]{:S(2)}, u32[]{:S(2)}) collective-permute-start(bf16[128,128]{1,0:T(8,128)(2,1)} %get-tuple-element.51), channel_id=1, source_target_pairs={{0,24},{2,26},{4,28},{6,30},{8,0},{10,2},{12,4},{14,6},{16,8},{18,... | collective-permute-start | bytes 98312 | tf_op jit(solution)/shard_map/ppermute | solution.py:198
  104.7 33.0 %collective-permute-start.35 = (bf16[256,1536]{1,0:T(8,128)(2,1)S(1)}, bf16[256,1536]{1,0:T(8,128)(2,1)S(1)}, u32[]{:S(2)}, u32[]{:S(2)}) collective-permute-start(bf16[256,1536]{1,0:T(8,128)(2,1)S(1)} %constant_dynamic-update-slice_fusion.12), channel_id=1, source_target_pairs={{0,2},{2,0},{4,6},{6,4},{8,10},{10,8},{12,14},{14,12},{16,18},{18,... | collective-permute-start | bytes 2359304 | tf_op jit(solution)/shard_map/ppermute | solution.py:201
  104.7 7.3 %collective-permute-start.24 = (bf16[128,128]{1,0:T(8,128)(2,1)S(1)}, bf16[128,128]{1,0:T(8,128)(2,1)S(1)}, u32[]{:S(2)}, u32[]{:S(2)}) collective-permute-start(bf16[128,128]{1,0:T(8,128)(2,1)S(1)} %copy-done.32), channel_id=1, source_target_pairs={{0,16},{2,18},{4,20},{6,22},{8,24},{10,26},{12,28},{14,30},{16,0},... | collective-permute-start | bytes 98312 | tf_op jit(solution)/shard_map/ppermute | solution.py:198
  108.2 5.2 %collective-permute-start.25 = (bf16[128,128]{1,0:T(8,128)(2,1)S(1)}, bf16[128,128]{1,0:T(8,128)(2,1)S(1)}, u32[]{:S(2)}, u32[]{:S(2)}) collective-permute-start(bf16[128,128]{1,0:T(8,128)(2,1)S(1)} %copy-done.33), channel_id=1, source_target_pairs={{0,16},{2,18},{4,20},{6,22},{8,24},{10,26},{12,28},{14,30},{16,0},... | collective-permute-start | bytes 98312 | tf_op jit(solution)/shard_map/ppermute | solution.py:198
  108.8 5.2 %collective-permute-start.26 = (bf16[128,128]{1,0:T(8,128)(2,1)}, bf16[128,128]{1,0:T(8,128)(2,1)S(1)}, u32[]{:S(2)}, u32[]{:S(2)}) collective-permute-start(bf16[128,128]{1,0:T(8,128)(2,1)} %get-tuple-element.55), channel_id=1, source_target_pairs={{0,16},{2,18},{4,20},{6,22},{8,24},{10,26},{12,28},{14,30},{16,0},... | collective-permute-start | bytes 98312 | tf_op jit(solution)/shard_map/ppermute | solution.py:198
  112.0 5.8 %collective-permute-start.27 = (bf16[128,128]{1,0:T(8,128)(2,1)S(1)}, bf16[128,128]{1,0:T(8,128)(2,1)S(1)}, u32[]{:S(2)}, u32[]{:S(2)}) collective-permute-start(bf16[128,128]{1,0:T(8,128)(2,1)S(1)} %copy-done.30), channel_id=1, source_target_pairs={{0,8},{2,10},{4,12},{6,14},{8,16},{10,18},{12,20},{14,22},{16,24},... | collective-permute-start | bytes 98312 | tf_op jit(solution)/shard_map/ppermute | solution.py:198
  113.4 5.7 %collective-permute-start.28 = (bf16[128,128]{1,0:T(8,128)(2,1)S(1)}, bf16[128,128]{1,0:T(8,128)(2,1)S(1)}, u32[]{:S(2)}, u32[]{:S(2)}) collective-permute-start(bf16[128,128]{1,0:T(8,128)(2,1)S(1)} %copy-done.31), channel_id=1, source_target_pairs={{0,8},{2,10},{4,12},{6,14},{8,16},{10,18},{12,20},{14,22},{16,24},... | collective-permute-start | bytes 98312 | tf_op jit(solution)/shard_map/ppermute | solution.py:198
  113.9 5.9 %collective-permute-start.29 = (bf16[128,128]{1,0:T(8,128)(2,1)}, bf16[128,128]{1,0:T(8,128)(2,1)S(1)}, u32[]{:S(2)}, u32[]{:S(2)}) collective-permute-start(bf16[128,128]{1,0:T(8,128)(2,1)} %get-tuple-element.58), channel_id=1, source_target_pairs={{0,8},{2,10},{4,12},{6,14},{8,16},{10,18},{12,20},{14,22},{16,24},... | collective-permute-start | bytes 98312 | tf_op jit(solution)/shard_map/ppermute | solution.py:198
  127.6 14.7 %collective-permute-start.30 = (bf16[128,2560]{1,0:T(8,128)(2,1)}, bf16[128,2560]{1,0:T(8,128)(2,1)S(1)}, u32[]{:S(2)}, u32[]{:S(2)}) collective-permute-start(bf16[128,2560]{1,0:T(8,128)(2,1)} %away.1), channel_id=1, source_target_pairs={{0,1},{1,0},{2,3},{3,2},{4,5},{5,4},{6,7},{7,6},{8,9},{9,8},{10,11... | collective-permute-start | bytes 1966088 | tf_op jit(solution)/shard_map/ppermute | solution.py:241
  137.7 5.7 %collective-permute-start.36 = (bf16[256,1536]{1,0:T(8,128)(2,1)S(1)}, bf16[256,1536]{1,0:T(8,128)(2,1)S(1)}, u32[]{:S(2)}, u32[]{:S(2)}) collective-permute-start(bf16[256,1536]{1,0:T(8,128)(2,1)S(1)} %collective-permute-done.34), channel_id=1, source_target_pairs={{0,2},{2,0},{4,6},{6,4},{8,10},{10,8},{12,14},{14,12},{16,18},{18,... | collective-permute-start | bytes 2359304 | tf_op jit(solution)/shard_map/ppermute | solution.py:201
  (39 other events, 729.6 us)

commit v2 on v1

v2 whole, which is shorter than its diff:
```python
import math

import jax
import jax.numpy as jnp
from jax import lax
from jax.experimental import pallas as pl
from jax.experimental.pallas import tpu as pltpu
from jax.sharding import PartitionSpec as P

DH = 128
F32 = jnp.float32
BF16 = jnp.bfloat16
LOG2E = 1.4426950408889634


def in_vmem():
    return pl.BlockSpec(memory_space=pltpu.VMEM)


def in_smem():
    return pl.BlockSpec(memory_space=pltpu.SMEM)


def cost(flops, nbytes, transcendentals=0):
    return pl.CostEstimate(
        flops=int(flops), bytes_accessed=int(nbytes), transcendentals=int(transcendentals)
    )


def shape(rows, columns, dtype=BF16):
    return jax.ShapeDtypeStruct((rows, columns), dtype)


def after(x, *others):
    return lax.optimization_barrier((x, others))[0]


def softmax_mix(query, keys, values, factor):
    scores = [
        lax.dot_general(query, block, (((1,), (1,)), ((), ())), preferred_element_type=F32)
        for block in keys
    ]
    top = jnp.max(scores[0], axis=1, keepdims=True)
    for block in scores[1:]:
        top = jnp.maximum(top, jnp.max(block, axis=1, keepdims=True))
    total = None
    mixed = None
    for block, value in zip(scores, values):
        weight = jnp.exp2((block - top) * factor)
        part = jnp.sum(weight, axis=1, keepdims=True)
        total = part if total is None else total + part
        term = jnp.dot(weight.astype(BF16), value, preferred_element_type=F32)
        mixed = term if mixed is None else mixed + term
    return mixed / total


def pack_kernel(groups, at_ref, q_ref, k_ref, v_ref, *outs):
    width = q_ref.shape[1] // groups
    heads = width // DH
    for r in range(groups):
        base = lax.rem(at_ref[0] + r, groups) * width
        for h in range(heads):
            at = pl.ds(pl.multiple_of(base + h * DH, DH), DH)
            out = outs[r * heads + h]
            out[:, :DH] = q_ref[:, at]
            out[:, DH : 2 * DH] = k_ref[:, at]
            out[:, 2 * DH :] = v_ref[:, at]


def pack(groups, at, q, k, v):
    rows, columns = q.shape
    heads = columns // groups // DH
    outs = pl.pallas_call(
        lambda *refs: pack_kernel(groups, *refs),
        out_shape=[shape(rows, 3 * DH)] * (groups * heads),
        in_specs=[in_smem()] + [in_vmem()] * 3,
        out_specs=[in_vmem()] * (groups * heads),
        cost_estimate=cost(0, 6 * rows * columns * 2),
        name="pack",
    )(at, q, k, v)
    return [outs[r * heads : (r + 1) * heads] for r in range(groups)]


def pack_cross_kernel(at_ref, q_ref, k_ref, v_ref, *outs):
    half = q_ref.shape[1] // 2
    rows = k_ref.shape[0]
    for i in range(2):
        side = at_ref[1] if i == 0 else 1 - at_ref[1]
        at = pl.ds(pl.multiple_of(side * half, DH), half)
        outs[i][...] = q_ref[:, at]
        outs[2 + i][:rows, :] = k_ref[:, at]
        outs[2 + i][rows:, :] = v_ref[:, at]


def pack_cross(at, q, k, v):
    rows, columns = q.shape
    return pl.pallas_call(
        pack_cross_kernel,
        out_shape=[shape(rows, columns // 2)] * 2 + [shape(2 * k.shape[0], columns // 2)] * 2,
        in_specs=[in_smem()] + [in_vmem()] * 3,
        out_specs=[in_vmem()] * 4,
        cost_estimate=cost(0, 4 * (rows + 2 * k.shape[0]) * columns),
        name="pack_cross",
    )(at, q, k, v)


def attend_kernel(parts, factor, *refs):
    queries, pairs, outs = refs[:parts], refs[parts:-parts], refs[-parts:]
    keys = [ref[:, :DH] for ref in pairs]
    values = [ref[:, DH:] for ref in pairs]
    for query, out in zip(queries, outs):
        out[...] = softmax_mix(query[:, :DH], keys, values, factor).astype(BF16)


def attend(queries, pairs, factor, name):
    parts = len(queries)
    rows = queries[0].shape[0]
    total_keys = sum(p.shape[0] for p in pairs)
    return pl.pallas_call(
        lambda *refs: attend_kernel(parts, factor, *refs),
        out_shape=[shape(rows, DH)] * parts,
        in_specs=[in_vmem()] * (parts + len(pairs)),
        out_specs=[in_vmem()] * parts,
        cost_estimate=cost(
            4 * parts * rows * total_keys * DH, total_keys * DH * 4, parts * rows * total_keys
        ),
        name=name,
    )(*queries, *pairs)


def cross_kernel(factor, block, parts, *refs):
    queries, captions, outs = refs[:parts], refs[parts:-parts], refs[-parts:]
    for h in range(queries[0].shape[1] // DH):
        at = slice(h * DH, (h + 1) * DH)
        keys, values = [
            jnp.concatenate(
                [
                    c[b * block : (b + 1) * block, at]
                    for c in captions
                    for b in range(first, c.shape[0] // block, 2)
                ],
                axis=0,
            )
            for first in (0, 1)
        ]
        for query, out in zip(queries, outs):
            out[:, at] = softmax_mix(query[:, at], [keys], [values], factor).astype(BF16)


def cross(queries, captions, block, factor):
    parts = len(queries)
    rows, columns = queries[0].shape
    total_keys = sum(c.shape[0] for c in captions) // 2
    return pl.pallas_call(
        lambda *refs: cross_kernel(factor, block, parts, *refs),
        out_shape=[shape(rows, columns)] * parts,
        in_specs=[in_vmem()] * (parts + len(captions)),
        out_specs=[in_vmem()] * parts,
        cost_estimate=cost(
            4 * parts * rows * total_keys * columns,
            (2 * parts * rows + 2 * total_keys) * columns * 2,
            parts * rows * total_keys * columns // DH,
        ),
        name="cross",
    )(*queries, *captions)


def project_kernel(groups, heads, at_ref, *refs):
    lhs, w_ref, out = refs[: groups * heads], refs[-2], refs[-1]
    width = heads * DH
    columns = out.shape[1]
    first = pl.multiple_of(at_ref[1] * columns, DH)
    block = math.gcd(columns, 512)
    lefts = [
        jnp.concatenate([lhs[r * heads + h][...] for h in range(heads)], axis=1)
        for r in range(groups)
    ]
    for n in range(columns // block):
        at = pl.ds(pl.multiple_of(first + n * block, DH), block)
        total = None
        for r in range(groups):
            base = pl.multiple_of(lax.rem(at_ref[0] + r, groups) * width, DH)
            term = jnp.dot(lefts[r], w_ref[pl.ds(base, width), at], preferred_element_type=F32)
            total = term if total is None else total + term
        out[:, n * block : (n + 1) * block] = total.astype(out.dtype)


def project(groups, at, lhs, weight, columns, dtype, name):
    heads = len(lhs) // groups
    rows = lhs[0].shape[0]
    depth = weight.shape[0]
    return pl.pallas_call(
        lambda *refs: project_kernel(groups, heads, *refs),
        out_shape=shape(rows, columns, dtype),
        in_specs=[in_smem()] + [in_vmem()] * (len(lhs) + 1),
        out_specs=in_vmem(),
        cost_estimate=cost(
            2 * rows * depth * columns, depth * columns * 2 + rows * columns * 4
        ),
        name=name,
    )(at, *lhs, weight)


def finish_kernel(at_ref, tokens, gate, home, away, stay, came, updated, cross_heads):
    projected = home[...] + away[...].astype(F32)
    updated[...] = (tokens[...].astype(F32) + gate[...] * projected).astype(BF16)
    half = stay.shape[1]
    for side, half_heads in ((at_ref[1], stay), (1 - at_ref[1], came)):
        cross_heads[:, pl.ds(pl.multiple_of(side * half, DH), half)] = half_heads[...]


def finish(at, tokens, gate, home, away, stay, came):
    return pl.pallas_call(
        finish_kernel,
        out_shape=[shape(*tokens.shape), shape(stay.shape[0], 2 * stay.shape[1])],
        in_specs=[in_smem()] + [in_vmem()] * 6,
        out_specs=[in_vmem()] * 2,
        cost_estimate=cost(0, tokens.size * 10),
        name="finish",
    )(at, tokens, gate[None, :], home, away, stay, came)


def shards(
    seq_size,
    tp_size,
    tokens,
    self_queries,
    self_keys,
    self_values,
    cross_queries,
    caption_keys,
    caption_values,
    out_weight,
    gate_vector,
):
    rows, columns = self_queries.shape
    heads_here = columns // DH
    factor = LOG2E / math.sqrt(DH)
    groups = math.gcd(heads_here, seq_size)
    members = seq_size // groups
    heads = heads_here // groups
    bit = members // 2
    split = members == 4 and heads_here % 2 == 0 and tp_size == 2
    seqi = lax.axis_index("seq").astype(jnp.int32)
    tpi = lax.axis_index("tp").astype(jnp.int32)
    zi = seqi // members
    place = jnp.stack([zi, (seqi // max(bit, 1)) % 2])

    def rotate(x, r):
        if r % groups == 0:
            return x
        step = (r % groups) * members
        return lax.ppermute(x, "seq", [(s, (s + step) % seq_size) for s in range(seq_size)])

    def swap(x, by):
        return lax.ppermute(x, "seq", [(s, s ^ by) for s in range(seq_size)])

    def spread(x):
        if members == 4:
            near = swap(x, 1)
            far = swap(x, 2)
            return [x, near, far, swap(far, 1)]
        index_groups = [[g * members + m for m in range(members)] for g in range(groups)]
        return [
            lax.all_gather(x, "seq", axis=0, tiled=True, axis_index_groups=index_groups)
        ]

    pieces = pack(groups, place, self_queries, self_keys, self_values)
    if split:
        q_stay, q_go, c_stay, c_go = pack_cross(
            place, cross_queries, caption_keys, caption_values
        )

    mixed = []
    arrived = []
    for h in range(heads):
        here = [pieces[r][h] for r in range(groups)]
        if h >= 2:
            here[1:] = [after(x, arrived[h - 2][1:]) for x in here[1:]]
        here = [rotate(x, r) for r, x in enumerate(here)]
        arrived.append(here)
        mine = jnp.concatenate([x[:, DH:] for x in here], axis=0)
        outs = attend(here, spread(mine), factor, "attend_%d" % h)
        mixed.append([rotate(x, groups - r) for r, x in enumerate(outs)])

    lhs = [mixed[h][r] for r in range(groups) for h in range(heads)]
    out_columns = tokens.shape[1]
    cap_rows = caption_keys.shape[0]
    if split:
        q_come, c_come = swap(q_go, bit), swap(c_go, bit)
        caption = jnp.concatenate([c_stay, c_come], axis=0)
        caption = after(caption, arrived[-1][1:])
        caption = jnp.concatenate([rotate(caption, r) for r in range(groups)], axis=0)
        captions = [caption, swap(caption, 1)]
        stay, go = cross([q_stay, q_come], captions, cap_rows, factor)
        came = swap(go, bit)
        away = project(
            groups, jnp.stack([zi, 1 - tpi]), lhs, out_weight, out_columns, BF16, "away"
        )
        away = lax.ppermute(away, "tp", [(0, 1), (1, 0)])
        home = project(groups, jnp.stack([zi, tpi]), lhs, out_weight, out_columns, F32, "home")
        return tuple(finish(place, tokens, gate_vector, home, away, stay, came))

    caption = jnp.concatenate([caption_keys, caption_values], axis=0)
    caption = jnp.concatenate([rotate(caption, r) for r in range(groups)], axis=0)
    (cross_heads,) = cross([cross_queries], spread(caption), cap_rows, factor)
    both = project(
        groups, jnp.stack([zi, 0 * tpi]), lhs, out_weight, out_weight.shape[1], BF16, "both"
    )
    projected = lax.psum_scatter(both, "tp", scatter_dimension=1, tiled=True).astype(F32)
    updated = (tokens.astype(F32) + gate_vector[None, :] * projected).astype(BF16)
    return (updated, cross_heads)


def solution(mesh):
    seq_size, tp_size = mesh.shape["seq"], mesh.shape["tp"]
    return jax.shard_map(
        lambda *args: shards(seq_size, tp_size, *args),
        mesh=mesh,
        in_specs=(
            P("seq", "tp"),
            P("seq", "tp"),
            P("seq", "tp"),
            P("seq", "tp"),
            P("seq", "tp"),
            P("seq", "tp"),
            P("seq", "tp"),
            P("tp", None),
            P("tp"),
        ),
        out_specs=(P("seq", "tp"), P("seq", "tp")),
        check_vma=False,
    )
```

time: 151 us -> 126 us (0.83)
  waiting for transfers between devices: 61 us -> 28.2 us
  Pallas kernels: 35.6 us -> 41.8 us
  starting transfers between devices: 42.7 us -> 44.4 us
    ppermute x24 -> x21, waiting for transfers between devices: 51.6 us -> 24.2 us  [rotate(): lax.ppermute(x, 'seq', [(s, (s + step) % seq_size) for s in range(seq_siz...]
    pallas_call x5 -> x7, Pallas kernels: 21 us -> 25.3 us  [the longest x3 12.4 us: attend(): pl.pallas_call(lambda *refs: attend_kernel(parts, factor, *refs), out_sha...]
    ppermute x12 -> x13, starting transfers between devices: 4.22 us -> 8.07 us  [swap(): return lax.ppermute(x, 'seq', [(s, s ^ by) for s in range(seq_size)])]
    ppermute x1, waiting for transfers between devices: 3.68 us -> 0.01 us  [shards(): away = lax.ppermute(away, 'tp', [(0, 1), (1, 0)])]
    ppermute x24 -> x21, starting transfers between devices: 36.9 us -> 34.8 us  [rotate(): lax.ppermute(x, 'seq', [(s, (s + step) % seq_size) for s in range(seq_siz...]
    pallas_call x2, Pallas kernels: 14.6 us -> 16.5 us  [project(): pl.pallas_call(lambda *refs: project_kernel(groups, heads, *refs), out_sh...]
    ppermute x12 -> x13, waiting for transfers between devices: 5.74 us -> 4 us  [swap(): return lax.ppermute(x, 'seq', [(s, s ^ by) for s in range(seq_size)])]
    unnamed x80 -> x65, local copies, waits for them, and re-layouts: 4.9 us -> 3.93 us
  transfers between devices with their start and end apart: 37 -> 35, of which waited for: 20 -> 10; matrix products, arithmetic and copies ran while one was open for 5% -> 4% of each run, Pallas kernels for 18% -> 29%
where the time goes in v2:
time: 126 us; the launch traced here: 125 us
  starting transfers between devices  44.4 us (35%)
  Pallas kernels  41.8 us (33%)
  waiting for transfers between devices  28.2 us (22%)
  local copies, waits for them, and re-layouts  7.13 us (6%)
  other arithmetic  2.8 us (2%)
    ppermute x21, starting transfers between devices, rotate(): lax.ppermute(x, 'seq', [(s, (s + step) % seq_size) for s in range(seq_siz...  34.8 us
    ppermute x21, waiting for transfers between devices, rotate(): lax.ppermute(x, 'seq', [(s, (s + step) % seq_size) for s in range(seq_siz...  24.2 us
    pallas_call x2, Pallas kernels, project(): pl.pallas_call(lambda *refs: project_kernel(groups, heads, *refs), out_sh...  16.5 us
    pallas_call x3, Pallas kernels, attend(): pl.pallas_call(lambda *refs: attend_kernel(parts, factor, *refs), out_sha...  12.4 us
    ppermute x13, starting transfers between devices, swap(): return lax.ppermute(x, 'seq', [(s, s ^ by) for s in range(seq_size)])  8.07 us
    pallas_call x1, Pallas kernels, cross(): pl.pallas_call(lambda *refs: cross_kernel(factor, block, parts, *refs), o...  5.57 us
    ppermute x13, waiting for transfers between devices, swap(): return lax.ppermute(x, 'seq', [(s, s ^ by) for s in range(seq_size)])  4 us
    unnamed x65, local copies, waits for them, and re-layouts  3.93 us
  transfers between devices with their start and end apart: 35, of which 10 were waited for; matrix products, arithmetic and copies ran while one was open for 4% of the time, Pallas kernels for 29%

profile of v2, /device:TPU:0, one launch (start us, length us, event | category | flops | bytes accessed | tf_op | source)
XLA Modules:
  0.0 125.3 jit_solution(9145053310294979330)
XLA Ops:
  1.3 2.4 %pack.1 = (bf16[128,384]{1,0:T(8,128)(2,1)}, bf16[128,384]{1,0:T(8,128)(2,1)}, bf16[128,384]{1,0:T(8,128)(2,1)}, bf16[128,384]{1,0:T(8,128)(2,1)}, bf16[128,384]...) custom-call(s32[2]{0:T(128)} %pad_add_fusion.refs_0_.at_ref, ...), custom_call_target="tpu_custom_call" | custom-call | bytes 2359296 | tf_op jit(solution)/shard_map/pack/pallas_call | solution.py:73
  3.7 3.0 %collective-permute-start.6 = (bf16[128,384]{1,0:T(8,128)(2,1)}, bf16[128,384]{1,0:T(8,128)(2,1)S(1)}, u32[]{:S(2)}, u32[]{:S(2)}) collective-permute-start(bf16[128,384]{1,0:T(8,128)(2,1)} %get-tuple-element.42), channel_id=1, source_target_pairs={{0,8},{2,10},{4,12},{6,14},{8,16},{10,18},{12,20},{14,22},{16,24},... | collective-permute-start | bytes 294920 | tf_op jit(solution)/shard_map/ppermute | solution.py:253
  6.7 2.6 %collective-permute-start.7 = (bf16[128,384]{1,0:T(8,128)(2,1)}, bf16[128,384]{1,0:T(8,128)(2,1)S(1)}, u32[]{:S(2)}, u32[]{:S(2)}) collective-permute-start(bf16[128,384]{1,0:T(8,128)(2,1)} %get-tuple-element.43), channel_id=1, source_target_pairs={{0,16},{2,18},{4,20},{6,22},{8,24},{10,26},{12,28},{14,30},{16,0},... | collective-permute-start | bytes 294920 | tf_op jit(solution)/shard_map/ppermute | solution.py:253
  9.3 1.3 %collective-permute-start.8 = (bf16[128,384]{1,0:T(8,128)(2,1)}, bf16[128,384]{1,0:T(8,128)(2,1)S(1)}, u32[]{:S(2)}, u32[]{:S(2)}) collective-permute-start(bf16[128,384]{1,0:T(8,128)(2,1)} %get-tuple-element.44), channel_id=1, source_target_pairs={{0,24},{2,26},{4,28},{6,30},{8,0},{10,2},{12,4},{14,6},{16,8},{18,... | collective-permute-start | bytes 294920 | tf_op jit(solution)/shard_map/ppermute | solution.py:253
  14.2 1.9 %pack_cross.1 = (bf16[128,768]{1,0:T(8,128)(2,1)}, bf16[128,768]{1,0:T(8,128)(2,1)}, bf16[64,768]{1,0:T(8,128)(2,1)}, bf16[64,768]{1,0:T(8,128)(2,1)}) custom-call(s32[2]{0:T(128)} %pad_add_fusion.refs_0_.at_ref, bf16[128,1536]{1,0:T(8,128)(2,1)} %q_ref.1, bf16[32,1536]{1,0:T(8,128)(2,1)} %k_ref.1, bf16[32,1536]{1,0:T(8,128)(2,1)} %v_ref.1), custom_call_target="tpu_custom_call" | custom-call | bytes 1179648 | tf_op jit(solution)/shard_map/pack_cross/pallas_call | solution.py:97
  16.2 2.9 %collective-permute-start.2 = (bf16[128,384]{1,0:T(8,128)(2,1)}, bf16[128,384]{1,0:T(8,128)(2,1)S(1)}, u32[]{:S(2)}, u32[]{:S(2)}) collective-permute-start(bf16[128,384]{1,0:T(8,128)(2,1)} %get-tuple-element.39), channel_id=1, source_target_pairs={{0,24},{2,26},{4,28},{6,30},{8,0},{10,2},{12,4},{14,6},{16,8},{18,... | collective-permute-start | bytes 294920 | tf_op jit(solution)/shard_map/ppermute | solution.py:253
  19.7 1.6 %collective-permute-start.29 = (bf16[64,768]{1,0:T(8,128)(2,1)}, bf16[64,768]{1,0:T(8,128)(2,1)S(1)}, u32[]{:S(2)}, u32[]{:S(2)}) collective-permute-start(bf16[64,768]{1,0:T(8,128)(2,1)} %get-tuple-element.66), channel_id=1, source_target_pairs={{0,4},{2,6},{4,0},{6,2},{8,12},{10,14},{12,8},{14,10},{16,20},{18,... | collective-permute-start | bytes 294920 | tf_op jit(solution)/shard_map/ppermute | solution.py:256
  21.9 2.7 %collective-permute-done.1.refs_2_ = bf16[128,384]{1,0:T(8,128)(2,1)S(1)} collective-permute-done((bf16[128,384]{1,0:T(8,128)(2,1)}, bf16[128,384]{1,0:T(8,128)(2,1)S(1)}, u32[]{:S(2)}, u32[]{:S(2)}) %collective-permute-start.1) | collective-permute-done | bytes 98336 | tf_op jit(solution)/shard_map/ppermute | solution.py:253
  24.6 3.7 %collective-permute-start.14 = (bf16[128,384]{1,0:T(8,128)(2,1)}, bf16[128,384]{1,0:T(8,128)(2,1)S(1)}, u32[]{:S(2)}, u32[]{:S(2)}) collective-permute-start(bf16[128,384]{1,0:T(8,128)(2,1)} %get-tuple-element.52), channel_id=1, source_target_pairs={{0,24},{2,26},{4,28},{6,30},{8,0},{10,2},{12,4},{14,6},{16,8},{18,... | collective-permute-start | bytes 294920 | tf_op jit(solution)/shard_map/ppermute | solution.py:253
  29.9 1.8 %collective-permute-done.14.refs_3_ = bf16[128,384]{1,0:T(8,128)(2,1)S(1)} collective-permute-done((bf16[128,384]{1,0:T(8,128)(2,1)}, bf16[128,384]{1,0:T(8,128)(2,1)S(1)}, u32[]{:S(2)}, u32[]{:S(2)}) %collective-permute-start.14) | collective-permute-done | bytes 98336 | tf_op jit(solution)/shard_map/ppermute | solution.py:253
  31.7 1.5 %collective-permute-start.4 = (bf16[512,256]{1,0:T(8,128)(2,1)S(1)}, bf16[512,256]{1,0:T(8,128)(2,1)}, u32[]{:S(2)}, u32[]{:S(2)}) collective-permute-start(bf16[512,256]{1,0:T(8,128)(2,1)S(1)} %pad_maximum_fusion.refs_4_), channel_id=1, source_target_pairs={{0,4},{2,6},{4,0},{6,2},{8,12},{10,14},{12,8},{14,10},{16,20},{18,... | collective-permute-start | bytes 786440 | tf_op jit(solution)/shard_map/ppermute | solution.py:256
  33.2 4.6 %collective-permute-done.13.refs_2_ = bf16[128,384]{1,0:T(8,128)(2,1)S(1)} collective-permute-done((bf16[128,384]{1,0:T(8,128)(2,1)}, bf16[128,384]{1,0:T(8,128)(2,1)S(1)}, u32[]{:S(2)}, u32[]{:S(2)}) %collective-permute-start.13) | collective-permute-done | bytes 98336 | tf_op jit(solution)/shard_map/ppermute | solution.py:253
  39.5 1.2 collective-permute-start.31
  41.4 2.9 %collective-permute-start.32 = (bf16[128,768]{1,0:T(8,128)(2,1)S(1)}, bf16[128,768]{1,0:T(8,128)(2,1)S(1)}, u32[]{:S(2)}, u32[]{:S(2)}) collective-permute-start(bf16[128,768]{1,0:T(8,128)(2,1)S(1)} %pad_maximum_fusion.3), channel_id=1, source_target_pairs={{0,24},{2,26},{4,28},{6,30},{8,0},{10,2},{12,4},{14,6},{16,8},{18,... | collective-permute-start | bytes 589832 | tf_op jit(solution)/shard_map/ppermute | solution.py:253
  44.3 3.3 %collective-permute-done.30 = bf16[128,768]{1,0:T(8,128)(2,1)S(1)} collective-permute-done((bf16[128,768]{1,0:T(8,128)(2,1)S(1)}, bf16[128,768]{1,0:T(8,128)(2,1)S(1)}, u32[]{:S(2)}, u32[]{:S(2)}) %collective-permute-start.30) | collective-permute-done | bytes 196640 | tf_op jit(solution)/shard_map/ppermute | solution.py:253
  48.2 6.0 %collective-permute-done.31 = bf16[128,768]{1,0:T(8,128)(2,1)S(1)} collective-permute-done((bf16[128,768]{1,0:T(8,128)(2,1)S(1)}, bf16[128,768]{1,0:T(8,128)(2,1)S(1)}, u32[]{:S(2)}, u32[]{:S(2)}) %collective-permute-start.31) | collective-permute-done | bytes 196640 | tf_op jit(solution)/shard_map/ppermute | solution.py:253
  56.0 4.1 %attend_1.1 = (bf16[128,128]{1,0:T(8,128)(2,1)}, bf16[128,128]{1,0:T(8,128)(2,1)}, bf16[128,128]{1,0:T(8,128)(2,1)}, bf16[128,128]{1,0:T(8,128)(2,1)}) custom-call(bf16[128,384]{1,0:T(8,128)(2,1)} %get-tuple-element.41.refs_0_, bf16[128,384]{1,0:T(8,128)(2,1)} %copy-done.19, bf16[128,384]{1,0:T(8,128)(2,1)} %copy-done.20, bf16[128,384]{1,0:T(8,128)(2,1)} %copy-done.22, ...), custom_call_target="tpu_custom_call" | custom-call | flops 536870912 | bytes 1048576 | tf_op jit(solution)/shard_map/attend_1/pallas_call | solution.py:119
  60.2 5.0 %collective-permute-start.19 = (bf16[128,128]{1,0:T(8,128)(2,1)}, bf16[128,128]{1,0:T(8,128)(2,1)S(1)}, u32[]{:S(2)}, u32[]{:S(2)}) collective-permute-start(bf16[128,128]{1,0:T(8,128)(2,1)} %get-tuple-element.55), channel_id=1, source_target_pairs={{0,24},{2,26},{4,28},{6,30},{8,0},{10,2},{12,4},{14,6},{16,8},{18,... | collective-permute-start | bytes 98312 | tf_op jit(solution)/shard_map/ppermute | solution.py:253
  65.9 4.1 %attend_0.1 = (bf16[128,128]{1,0:T(8,128)(2,1)}, bf16[128,128]{1,0:T(8,128)(2,1)}, bf16[128,128]{1,0:T(8,128)(2,1)}, bf16[128,128]{1,0:T(8,128)(2,1)}) custom-call(bf16[128,384]{1,0:T(8,128)(2,1)} %get-tuple-element.36.refs_0_, bf16[128,384]{1,0:T(8,128)(2,1)} %copy-done.17, bf16[128,384]{1,0:T(8,128)(2,1)} %copy-done.18, bf16[128,384]{1,0:T(8,128)(2,1)} %copy-done.21, ...), custom_call_target="tpu_custom_call" | custom-call | flops 536870912 | bytes 1048576 | tf_op jit(solution)/shard_map/attend_0/pallas_call | solution.py:119
  70.0 3.8 %collective-permute-start.18 = (bf16[128,128]{1,0:T(8,128)(2,1)}, bf16[128,128]{1,0:T(8,128)(2,1)S(1)}, u32[]{:S(2)}, u32[]{:S(2)}) collective-permute-start(bf16[128,128]{1,0:T(8,128)(2,1)} %get-tuple-element.54), channel_id=1, source_target_pairs={{0,24},{2,26},{4,28},{6,30},{8,0},{10,2},{12,4},{14,6},{16,8},{18,... | collective-permute-start | bytes 98312 | tf_op jit(solution)/shard_map/ppermute | solution.py:253
  74.3 4.1 %attend_2.1 = (bf16[128,128]{1,0:T(8,128)(2,1)}, bf16[128,128]{1,0:T(8,128)(2,1)}, bf16[128,128]{1,0:T(8,128)(2,1)}, bf16[128,128]{1,0:T(8,128)(2,1)}) custom-call(bf16[128,384]{1,0:T(8,128)(2,1)} %get-tuple-element.46.refs_0_, bf16[128,384]{1,0:T(8,128)(2,1)} %copy-done.25, bf16[128,384]{1,0:T(8,128)(2,1)} %copy-done.24, bf16[128,384]{1,0:T(8,128)(2,1)} %copy-done.23, ...), custom_call_target="tpu_custom_call" | custom-call | flops 536870912 | bytes 1048576 | tf_op jit(solution)/shard_map/attend_2/pallas_call | solution.py:119
  78.7 3.7 %collective-permute-start.20 = (bf16[128,128]{1,0:T(8,128)(2,1)}, bf16[128,128]{1,0:T(8,128)(2,1)S(1)}, u32[]{:S(2)}, u32[]{:S(2)}) collective-permute-start(bf16[128,128]{1,0:T(8,128)(2,1)} %get-tuple-element.56), channel_id=1, source_target_pairs={{0,24},{2,26},{4,28},{6,30},{8,0},{10,2},{12,4},{14,6},{16,8},{18,... | collective-permute-start | bytes 98312 | tf_op jit(solution)/shard_map/ppermute | solution.py:253
  84.4 2.9 %collective-permute-done.23.refs_9_ = bf16[128,128]{1,0:T(8,128)(2,1)S(1)} collective-permute-done((bf16[128,128]{1,0:T(8,128)(2,1)}, bf16[128,128]{1,0:T(8,128)(2,1)S(1)}, u32[]{:S(2)}, u32[]{:S(2)}) %collective-permute-start.23) | collective-permute-done | bytes 32800 | tf_op jit(solution)/shard_map/ppermute | solution.py:253
  87.4 1.6 %collective-permute-done.26.refs_12_ = bf16[128,128]{1,0:T(8,128)(2,1)S(1)} collective-permute-done((bf16[128,128]{1,0:T(8,128)(2,1)}, bf16[128,128]{1,0:T(8,128)(2,1)S(1)}, u32[]{:S(2)}, u32[]{:S(2)}) %collective-permute-start.26) | collective-permute-done | bytes 32800 | tf_op jit(solution)/shard_map/ppermute | solution.py:253
  89.5 8.1 %away.1 = bf16[128,2560]{1,0:T(8,128)(2,1)} custom-call(s32[2]{0:T(128)} %pad_add_fusion.2.refs_0_, bf16[128,128]{1,0:T(8,128)(2,1)} %get-tuple-element.40.refs_1_, bf16[128,128]{1,0:T(8,128)(2,1)} %get-tuple-element.45.refs_2_, bf16[128,128]{1,0:T(8,128)(2,1)} %get-tuple-element.53.refs_3_, bf16[128,128]{1,0:T(8,128)(2,1)} %copy-done.11, ...), custom_call_target="tpu_custom_call" | custom-call | flops 1006632960 | bytes 9175040 | tf_op jit(solution)/shard_map/away/pallas_call | solution.py:192
  97.7 1.5 %collective-permute-start.27 = (bf16[128,2560]{1,0:T(8,128)(2,1)}, bf16[128,2560]{1,0:T(8,128)(2,1)S(1)}, u32[]{:S(2)}, u32[]{:S(2)}) collective-permute-start(bf16[128,2560]{1,0:T(8,128)(2,1)} %away.1), channel_id=1, source_target_pairs={{0,1},{1,0},{2,3},{3,2},{4,5},{5,4},{6,7},{7,6},{8,9},{9,8},{10,11... | collective-permute-start | bytes 1966088 | tf_op jit(solution)/shard_map/ppermute | solution.py:300
  99.2 1.1 collective-permute-start.28
  100.9 4.0 %collective-permute-done.28.refs_1_ = bf16[128,768]{1,0:T(8,128)(2,1)S(1)} collective-permute-done((bf16[128,768]{1,0:T(8,128)(2,1)S(1)}, bf16[128,768]{1,0:T(8,128)(2,1)S(1)}, u32[]{:S(2)}, u32[]{:S(2)}) %collective-permute-start.28) | collective-permute-done | bytes 196640 | tf_op jit(solution)/shard_map/ppermute | solution.py:256
  105.8 5.6 %cross.1 = (bf16[128,768]{1,0:T(8,128)(2,1)}, bf16[128,768]{1,0:T(8,128)(2,1)}) custom-call(bf16[128,768]{1,0:T(8,128)(2,1)} %get-tuple-element.63.refs_0_, bf16[128,768]{1,0:T(8,128)(2,1)} %copy-done.7, bf16[512,768]{1,0:T(8,128)(2,1)} %copy-done, bf16[512,768]{1,0:T(8,128)(2,1)} %copy-done.1), custom_call_target="tpu_custom_call" | custom-call | flops 402653184 | bytes 2359296 | tf_op jit(solution)/shard_map/cross/pallas_call | solution.py:154
  111.4 1.1 collective-permute-start.34
  113.1 8.4 %home.1 = f32[128,2560]{1,0:T(8,128)} custom-call(s32[2]{0:T(128)} %pad_add_fusion.1.refs_0_, bf16[128,128]{1,0:T(8,128)(2,1)} %get-tuple-element.40.refs_1_, bf16[128,128]{1,0:T(8,128)(2,1)} %get-tuple-element.45.refs_2_, bf16[128,128]{1,0:T(8,128)(2,1)} %get-tuple-element.53.refs_3_, bf16[128,128]{1,0:T(8,128)(2,1)} %copy-done.11, ...), custom_call_target="tpu_custom_call" | custom-call | flops 1006632960 | bytes 9175040 | tf_op jit(solution)/shard_map/home/pallas_call | solution.py:192
  122.4 3.0 %finish.1 = (bf16[128,2560]{1,0:T(8,128)(2,1)}, bf16[128,1536]{1,0:T(8,128)(2,1)}) custom-call(s32[2]{0:T(128)} %pad_add_fusion.refs_0_.at_ref, bf16[128,2560]{1,0:T(8,128)(2,1)} %tokens.1, f32[1,2560]{1,0:T(1,128)} %broadcast_in_dim.3.gate, f32[128,2560]{1,0:T(8,128)} %home.1, bf16[128,2560]{1,0:T(8,128)(2,1)} %copy-done.2, ...), custom_call_target="tpu_custom_call" | custom-call | bytes 3276800 | tf_op jit(solution)/shard_map/finish/pallas_call | solution.py:213
  (133 shorter events, 18.9 us)
Async XLA Ops:
  3.7 12.4 %collective-permute-start.6 = (bf16[128,384]{1,0:T(8,128)(2,1)}, bf16[128,384]{1,0:T(8,128)(2,1)S(1)}, u32[]{:S(2)}, u32[]{:S(2)}) collective-permute-start(bf16[128,384]{1,0:T(8,128)(2,1)} %get-tuple-element.42), channel_id=1, source_target_pairs={{0,8},{2,10},{4,12},{6,14},{8,16},{10,18},{12,20},{14,22},{16,24},... | collective-permute-start | bytes 294920 | tf_op jit(solution)/shard_map/ppermute | solution.py:253
  6.7 12.9 %collective-permute-start.7 = (bf16[128,384]{1,0:T(8,128)(2,1)}, bf16[128,384]{1,0:T(8,128)(2,1)S(1)}, u32[]{:S(2)}, u32[]{:S(2)}) collective-permute-start(bf16[128,384]{1,0:T(8,128)(2,1)} %get-tuple-element.43), channel_id=1, source_target_pairs={{0,16},{2,18},{4,20},{6,22},{8,24},{10,26},{12,28},{14,30},{16,0},... | collective-permute-start | bytes 294920 | tf_op jit(solution)/shard_map/ppermute | solution.py:253
  9.3 11.9 %collective-permute-start.8 = (bf16[128,384]{1,0:T(8,128)(2,1)}, bf16[128,384]{1,0:T(8,128)(2,1)S(1)}, u32[]{:S(2)}, u32[]{:S(2)}) collective-permute-start(bf16[128,384]{1,0:T(8,128)(2,1)} %get-tuple-element.44), channel_id=1, source_target_pairs={{0,24},{2,26},{4,28},{6,30},{8,0},{10,2},{12,4},{14,6},{16,8},{18,... | collective-permute-start | bytes 294920 | tf_op jit(solution)/shard_map/ppermute | solution.py:253
  10.7 11.2 %collective-permute-start = (bf16[128,384]{1,0:T(8,128)(2,1)}, bf16[128,384]{1,0:T(8,128)(2,1)S(1)}, u32[]{:S(2)}, u32[]{:S(2)}) collective-permute-start(bf16[128,384]{1,0:T(8,128)(2,1)} %get-tuple-element.37), channel_id=1, source_target_pairs={{0,8},{2,10},{4,12},{6,14},{8,16},{10,18},{12,20},{14,22},{16,24},... | collective-permute-start | bytes 294920 | tf_op jit(solution)/shard_map/ppermute | solution.py:253
  11.4 13.2 %collective-permute-start.1 = (bf16[128,384]{1,0:T(8,128)(2,1)}, bf16[128,384]{1,0:T(8,128)(2,1)S(1)}, u32[]{:S(2)}, u32[]{:S(2)}) collective-permute-start(bf16[128,384]{1,0:T(8,128)(2,1)} %get-tuple-element.38), channel_id=1, source_target_pairs={{0,16},{2,18},{4,20},{6,22},{8,24},{10,26},{12,28},{14,30},{16,0},... | collective-permute-start | bytes 294920 | tf_op jit(solution)/shard_map/ppermute | solution.py:253
  16.2 8.4 %collective-permute-start.2 = (bf16[128,384]{1,0:T(8,128)(2,1)}, bf16[128,384]{1,0:T(8,128)(2,1)S(1)}, u32[]{:S(2)}, u32[]{:S(2)}) collective-permute-start(bf16[128,384]{1,0:T(8,128)(2,1)} %get-tuple-element.39), channel_id=1, source_target_pairs={{0,24},{2,26},{4,28},{6,30},{8,0},{10,2},{12,4},{14,6},{16,8},{18,... | collective-permute-start | bytes 294920 | tf_op jit(solution)/shard_map/ppermute | solution.py:253
  19.7 9.0 %collective-permute-start.29 = (bf16[64,768]{1,0:T(8,128)(2,1)}, bf16[64,768]{1,0:T(8,128)(2,1)S(1)}, u32[]{:S(2)}, u32[]{:S(2)}) collective-permute-start(bf16[64,768]{1,0:T(8,128)(2,1)} %get-tuple-element.66), channel_id=1, source_target_pairs={{0,4},{2,6},{4,0},{6,2},{8,12},{10,14},{12,8},{14,10},{16,20},{18,... | collective-permute-start | bytes 294920 | tf_op jit(solution)/shard_map/ppermute | solution.py:256
  21.3 18.2 %collective-permute-start.10 = (bf16[512,256]{1,0:T(8,128)(2,1)S(1)}, bf16[512,256]{1,0:T(8,128)(2,1)S(1)}, u32[]{:S(2)}, u32[]{:S(2)}) collective-permute-start(bf16[512,256]{1,0:T(8,128)(2,1)S(1)} %pad_maximum_fusion.1.refs_4_), channel_id=1, source_target_pairs={{0,4},{2,6},{4,0},{6,2},{8,12},{10,14},{12,8},{14,10},{16,20},{18,... | collective-permute-start | bytes 786440 | tf_op jit(solution)/shard_map/ppermute | solution.py:256
  21.8 18.9 %collective-permute-start.9 = (bf16[512,256]{1,0:T(8,128)(2,1)S(1)}, bf16[512,256]{1,0:T(8,128)(2,1)S(1)}, u32[]{:S(2)}, u32[]{:S(2)}) collective-permute-start(bf16[512,256]{1,0:T(8,128)(2,1)S(1)} %pad_maximum_fusion.1.refs_4_), channel_id=1, source_target_pairs={{0,2},{2,0},{4,6},{6,4},{8,10},{10,8},{12,14},{14,12},{16,18},{18,... | collective-permute-start | bytes 786440 | tf_op jit(solution)/shard_map/ppermute | solution.py:256
  24.6 7.2 %collective-permute-start.14 = (bf16[128,384]{1,0:T(8,128)(2,1)}, bf16[128,384]{1,0:T(8,128)(2,1)S(1)}, u32[]{:S(2)}, u32[]{:S(2)}) collective-permute-start(bf16[128,384]{1,0:T(8,128)(2,1)} %get-tuple-element.52), channel_id=1, source_target_pairs={{0,24},{2,26},{4,28},{6,30},{8,0},{10,2},{12,4},{14,6},{16,8},{18,... | collective-permute-start | bytes 294920 | tf_op jit(solution)/shard_map/ppermute | solution.py:253
  28.2 9.6 %collective-permute-start.13 = (bf16[128,384]{1,0:T(8,128)(2,1)}, bf16[128,384]{1,0:T(8,128)(2,1)S(1)}, u32[]{:S(2)}, u32[]{:S(2)}) collective-permute-start(bf16[128,384]{1,0:T(8,128)(2,1)} %get-tuple-element.50), channel_id=1, source_target_pairs={{0,16},{2,18},{4,20},{6,22},{8,24},{10,26},{12,28},{14,30},{16,0},... | collective-permute-start | bytes 294920 | tf_op jit(solution)/shard_map/ppermute | solution.py:253
  28.7 9.1 %collective-permute-start.12 = (bf16[128,384]{1,0:T(8,128)(2,1)}, bf16[128,384]{1,0:T(8,128)(2,1)S(1)}, u32[]{:S(2)}, u32[]{:S(2)}) collective-permute-start(bf16[128,384]{1,0:T(8,128)(2,1)} %get-tuple-element.48), channel_id=1, source_target_pairs={{0,8},{2,10},{4,12},{6,14},{8,16},{10,18},{12,20},{14,22},{16,24},... | collective-permute-start | bytes 294920 | tf_op jit(solution)/shard_map/ppermute | solution.py:253
  31.7 15.9 %collective-permute-start.4 = (bf16[512,256]{1,0:T(8,128)(2,1)S(1)}, bf16[512,256]{1,0:T(8,128)(2,1)}, u32[]{:S(2)}, u32[]{:S(2)}) collective-permute-start(bf16[512,256]{1,0:T(8,128)(2,1)S(1)} %pad_maximum_fusion.refs_4_), channel_id=1, source_target_pairs={{0,4},{2,6},{4,0},{6,2},{8,12},{10,14},{12,8},{14,10},{16,20},{18,... | collective-permute-start | bytes 786440 | tf_op jit(solution)/shard_map/ppermute | solution.py:256
  37.8 9.8 %collective-permute-start.30 = (bf16[128,768]{1,0:T(8,128)(2,1)S(1)}, bf16[128,768]{1,0:T(8,128)(2,1)S(1)}, u32[]{:S(2)}, u32[]{:S(2)}) collective-permute-start(bf16[128,768]{1,0:T(8,128)(2,1)S(1)} %pad_maximum_fusion.3), channel_id=1, source_target_pairs={{0,8},{2,10},{4,12},{6,14},{8,16},{10,18},{12,20},{14,22},{16,24},... | collective-permute-start | bytes 589832 | tf_op jit(solution)/shard_map/ppermute | solution.py:253
  38.8 15.9 %collective-permute-start.16 = (bf16[512,256]{1,0:T(8,128)(2,1)S(1)}, bf16[512,256]{1,0:T(8,128)(2,1)}, u32[]{:S(2)}, u32[]{:S(2)}) collective-permute-start(bf16[512,256]{1,0:T(8,128)(2,1)S(1)} %pad_maximum_fusion.2.refs_4_), channel_id=1, source_target_pairs={{0,4},{2,6},{4,0},{6,2},{8,12},{10,14},{12,8},{14,10},{16,20},{18,... | collective-permute-start | bytes 786440 | tf_op jit(solution)/shard_map/ppermute | solution.py:256
  39.5 14.7 %collective-permute-start.31 = (bf16[128,768]{1,0:T(8,128)(2,1)S(1)}, bf16[128,768]{1,0:T(8,128)(2,1)S(1)}, u32[]{:S(2)}, u32[]{:S(2)}) collective-permute-start(bf16[128,768]{1,0:T(8,128)(2,1)S(1)} %pad_maximum_fusion.3), channel_id=1, source_target_pairs={{0,16},{2,18},{4,20},{6,22},{8,24},{10,26},{12,28},{14,30},{16,0},... | collective-permute-start | bytes 589832 | tf_op jit(solution)/shard_map/ppermute | solution.py:253
  41.4 12.8 %collective-permute-start.32 = (bf16[128,768]{1,0:T(8,128)(2,1)S(1)}, bf16[128,768]{1,0:T(8,128)(2,1)S(1)}, u32[]{:S(2)}, u32[]{:S(2)}) collective-permute-start(bf16[128,768]{1,0:T(8,128)(2,1)S(1)} %pad_maximum_fusion.3), channel_id=1, source_target_pairs={{0,24},{2,26},{4,28},{6,30},{8,0},{10,2},{12,4},{14,6},{16,8},{18,... | collective-permute-start | bytes 589832 | tf_op jit(solution)/shard_map/ppermute | solution.py:253
  47.6 7.2 %collective-permute-start.11 = (bf16[512,256]{1,0:T(8,128)(2,1)S(1)}, bf16[512,256]{1,0:T(8,128)(2,1)S(1)}, u32[]{:S(2)}, u32[]{:S(2)}) collective-permute-start(bf16[512,256]{1,0:T(8,128)(2,1)S(1)} %collective-permute-done.10.refs_6_), channel_id=1, source_target_pairs={{0,2},{2,0},{4,6},{6,4},{8,10},{10,8},{12,14},{14,12},{16,18},{18,... | collective-permute-start | bytes 786440 | tf_op jit(solution)/shard_map/ppermute | solution.py:256
  47.6 12.5 %collective-permute-start.3 = (bf16[512,256]{1,0:T(8,128)(2,1)S(1)}, bf16[512,256]{1,0:T(8,128)(2,1)}, u32[]{:S(2)}, u32[]{:S(2)}) collective-permute-start(bf16[512,256]{1,0:T(8,128)(2,1)S(1)} %pad_maximum_fusion.refs_4_), channel_id=1, source_target_pairs={{0,2},{2,0},{4,6},{6,4},{8,10},{10,8},{12,14},{14,12},{16,18},{18,... | collective-permute-start | bytes 786440 | tf_op jit(solution)/shard_map/ppermute | solution.py:256
  54.2 15.8 %collective-permute-start.15 = (bf16[512,256]{1,0:T(8,128)(2,1)S(1)}, bf16[512,256]{1,0:T(8,128)(2,1)}, u32[]{:S(2)}, u32[]{:S(2)}) collective-permute-start(bf16[512,256]{1,0:T(8,128)(2,1)S(1)} %pad_maximum_fusion.2.refs_4_), channel_id=1, source_target_pairs={{0,2},{2,0},{4,6},{6,4},{8,10},{10,8},{12,14},{14,12},{16,18},{18,... | collective-permute-start | bytes 786440 | tf_op jit(solution)/shard_map/ppermute | solution.py:256
  54.2 11.0 %collective-permute-start.5 = (bf16[512,256]{1,0:T(8,128)(2,1)}, bf16[512,256]{1,0:T(8,128)(2,1)}, u32[]{:S(2)}, u32[]{:S(2)}) collective-permute-start(bf16[512,256]{1,0:T(8,128)(2,1)} %collective-permute-done.4.refs_6_), channel_id=1, source_target_pairs={{0,2},{2,0},{4,6},{6,4},{8,10},{10,8},{12,14},{14,12},{16,18},{18,... | collective-permute-start | bytes 786440 | tf_op jit(solution)/shard_map/ppermute | solution.py:256
  54.7 19.1 %collective-permute-start.17 = (bf16[512,256]{1,0:T(8,128)(2,1)}, bf16[512,256]{1,0:T(8,128)(2,1)}, u32[]{:S(2)}, u32[]{:S(2)}) collective-permute-start(bf16[512,256]{1,0:T(8,128)(2,1)} %collective-permute-done.16.refs_6_), channel_id=1, source_target_pairs={{0,2},{2,0},{4,6},{6,4},{8,10},{10,8},{12,14},{14,12},{16,18},{18,... | collective-permute-start | bytes 786440 | tf_op jit(solution)/shard_map/ppermute | solution.py:256
  55.6 49.3 %collective-permute-start.33 = (bf16[512,768]{1,0:T(8,128)(2,1)S(1)}, bf16[512,768]{1,0:T(8,128)(2,1)S(1)}, u32[]{:S(2)}, u32[]{:S(2)}) collective-permute-start(bf16[512,768]{1,0:T(8,128)(2,1)S(1)} %constant_dynamic-update-slice_fusion.refs_2_), channel_id=1, source_target_pairs={{0,2},{2,0},{4,6},{6,4},{8,10},{10,8},{12,14},{14,12},{16,18},{18,... | collective-permute-start | bytes 2359304 | tf_op jit(solution)/shard_map/ppermute | solution.py:256
  60.2 9.9 %collective-permute-start.19 = (bf16[128,128]{1,0:T(8,128)(2,1)}, bf16[128,128]{1,0:T(8,128)(2,1)S(1)}, u32[]{:S(2)}, u32[]{:S(2)}) collective-permute-start(bf16[128,128]{1,0:T(8,128)(2,1)} %get-tuple-element.55), channel_id=1, source_target_pairs={{0,24},{2,26},{4,28},{6,30},{8,0},{10,2},{12,4},{14,6},{16,8},{18,... | collective-permute-start | bytes 98312 | tf_op jit(solution)/shard_map/ppermute | solution.py:253
  65.2 13.2 %collective-permute-start.22 = (bf16[128,128]{1,0:T(8,128)(2,1)}, bf16[128,128]{1,0:T(8,128)(2,1)S(1)}, u32[]{:S(2)}, u32[]{:S(2)}) collective-permute-start(bf16[128,128]{1,0:T(8,128)(2,1)} %get-tuple-element.58), channel_id=1, source_target_pairs={{0,16},{2,18},{4,20},{6,22},{8,24},{10,26},{12,28},{14,30},{16,0},... | collective-permute-start | bytes 98312 | tf_op jit(solution)/shard_map/ppermute | solution.py:253
  70.0 8.7 %collective-permute-start.25 = (bf16[128,128]{1,0:T(8,128)(2,1)}, bf16[128,128]{1,0:T(8,128)(2,1)S(1)}, u32[]{:S(2)}, u32[]{:S(2)}) collective-permute-start(bf16[128,128]{1,0:T(8,128)(2,1)} %get-tuple-element.61), channel_id=1, source_target_pairs={{0,8},{2,10},{4,12},{6,14},{8,16},{10,18},{12,20},{14,22},{16,24},... | collective-permute-start | bytes 98312 | tf_op jit(solution)/shard_map/ppermute | solution.py:253
  70.0 12.3 %collective-permute-start.18 = (bf16[128,128]{1,0:T(8,128)(2,1)}, bf16[128,128]{1,0:T(8,128)(2,1)S(1)}, u32[]{:S(2)}, u32[]{:S(2)}) collective-permute-start(bf16[128,128]{1,0:T(8,128)(2,1)} %get-tuple-element.54), channel_id=1, source_target_pairs={{0,24},{2,26},{4,28},{6,30},{8,0},{10,2},{12,4},{14,6},{16,8},{18,... | collective-permute-start | bytes 98312 | tf_op jit(solution)/shard_map/ppermute | solution.py:253
  73.8 9.2 %collective-permute-start.21 = (bf16[128,128]{1,0:T(8,128)(2,1)}, bf16[128,128]{1,0:T(8,128)(2,1)S(1)}, u32[]{:S(2)}, u32[]{:S(2)}) collective-permute-start(bf16[128,128]{1,0:T(8,128)(2,1)} %get-tuple-element.57), channel_id=1, source_target_pairs={{0,16},{2,18},{4,20},{6,22},{8,24},{10,26},{12,28},{14,30},{16,0},... | collective-permute-start | bytes 98312 | tf_op jit(solution)/shard_map/ppermute | solution.py:253
  78.4 6.0 %collective-permute-start.24 = (bf16[128,128]{1,0:T(8,128)(2,1)}, bf16[128,128]{1,0:T(8,128)(2,1)S(1)}, u32[]{:S(2)}, u32[]{:S(2)}) collective-permute-start(bf16[128,128]{1,0:T(8,128)(2,1)} %get-tuple-element.60), channel_id=1, source_target_pairs={{0,8},{2,10},{4,12},{6,14},{8,16},{10,18},{12,20},{14,22},{16,24},... | collective-permute-start | bytes 98312 | tf_op jit(solution)/shard_map/ppermute | solution.py:253
  83.0 5.9 %collective-permute-start.26 = (bf16[128,128]{1,0:T(8,128)(2,1)}, bf16[128,128]{1,0:T(8,128)(2,1)S(1)}, u32[]{:S(2)}, u32[]{:S(2)}) collective-permute-start(bf16[128,128]{1,0:T(8,128)(2,1)} %get-tuple-element.62), channel_id=1, source_target_pairs={{0,8},{2,10},{4,12},{6,14},{8,16},{10,18},{12,20},{14,22},{16,24},... | collective-permute-start | bytes 98312 | tf_op jit(solution)/shard_map/ppermute | solution.py:253
  97.7 23.8 %collective-permute-start.27 = (bf16[128,2560]{1,0:T(8,128)(2,1)}, bf16[128,2560]{1,0:T(8,128)(2,1)S(1)}, u32[]{:S(2)}, u32[]{:S(2)}) collective-permute-start(bf16[128,2560]{1,0:T(8,128)(2,1)} %away.1), channel_id=1, source_target_pairs={{0,1},{1,0},{2,3},{3,2},{4,5},{5,4},{6,7},{7,6},{8,9},{9,8},{10,11... | collective-permute-start | bytes 1966088 | tf_op jit(solution)/shard_map/ppermute | solution.py:300
  111.4 10.1 %collective-permute-start.34 = (bf16[128,768]{1,0:T(8,128)(2,1)}, bf16[128,768]{1,0:T(8,128)(2,1)S(1)}, u32[]{:S(2)}, u32[]{:S(2)}) collective-permute-start(bf16[128,768]{1,0:T(8,128)(2,1)} %get-tuple-element.69), channel_id=1, source_target_pairs={{0,4},{2,6},{4,0},{6,2},{8,12},{10,14},{12,8},{14,10},{16,20},{18,... | collective-permute-start | bytes 589832 | tf_op jit(solution)/shard_map/ppermute | solution.py:256
  (34 other events, 750.6 us)

commit v3 on v0

v3 whole, which is shorter than its diff:
```python
import math

import jax
import jax.numpy as jnp
from jax import lax
from jax.experimental import pallas as pl
from jax.experimental.pallas import tpu as pltpu
from jax.sharding import PartitionSpec as P

DH = 128
F32 = jnp.float32
BF16 = jnp.bfloat16
LOG2E = 1.4426950408889634


def in_vmem():
    return pl.BlockSpec(memory_space=pltpu.VMEM)


def anywhere():
    return pl.BlockSpec(memory_space=pl.ANY)


def limit(mebibytes):
    return pltpu.CompilerParams(vmem_limit_bytes=mebibytes * 2**20)


def cost(flops, nbytes, transcendentals=0):
    return pl.CostEstimate(
        flops=int(flops), bytes_accessed=int(nbytes), transcendentals=int(transcendentals)
    )


def shape(rows, columns, dtype=BF16):
    return jax.ShapeDtypeStruct((rows, columns), dtype)


def after(x, *others):
    return lax.optimization_barrier((x, others))[0]


def softmax_mix(query, keys, values, factor):
    scores = [
        lax.dot_general(query, block, (((1,), (1,)), ((), ())), preferred_element_type=F32)
        for block in keys
    ]
    top = jnp.max(scores[0], axis=1, keepdims=True)
    for block in scores[1:]:
        top = jnp.maximum(top, jnp.max(block, axis=1, keepdims=True))
    total = None
    mixed = None
    for block, value in zip(scores, values):
        weight = jnp.exp2((block - top) * factor)
        part = jnp.sum(weight, axis=1, keepdims=True)
        total = part if total is None else total + part
        term = jnp.dot(weight.astype(BF16), value, preferred_element_type=F32)
        mixed = term if mixed is None else mixed + term
    return mixed / total


def copy_all(pairs, sems):
    copies = [
        pltpu.make_async_copy(source, target, sems.at[i])
        for i, (source, target) in enumerate(pairs)
    ]
    for copy in copies:
        copy.start()
    for copy in copies:
        copy.wait()


def pack(groups, members, chosen, q, k, v):
    rows, columns = q.shape
    width = columns // groups
    count = groups * len(chosen)

    def kernel(*refs):
        sources, outs, sems = refs[:3], refs[3:-1], refs[-1]
        zi = lax.axis_index("seq") // members
        pairs = []
        for j, h in enumerate(chosen):
            for r in range(groups):
                at = pl.ds(pl.multiple_of(lax.rem(zi + r, groups) * width + h * DH, DH), DH)
                for i, source in enumerate(sources):
                    target = outs[j * groups + r].at[:, i * DH : (i + 1) * DH]
                    pairs.append((source.at[:, at], target))
        copy_all(pairs, sems)

    outs = pl.pallas_call(
        kernel,
        out_shape=[shape(rows, 3 * DH)] * count,
        in_specs=[anywhere()] * 3,
        out_specs=[anywhere()] * count,
        scratch_shapes=[pltpu.SemaphoreType.DMA((3 * count,))],
        compiler_params=limit(1),
        cost_estimate=cost(0, 6 * count * rows * DH * 2),
        name="pack_%d" % chosen[0],
    )(q, k, v)
    return [list(outs[j * groups : (j + 1) * groups]) for j in range(len(chosen))]


def pack_cross(bit, q, k, v):
    rows, columns = q.shape
    half = columns // 2
    total = rows + 2 * k.shape[0]

    def kernel(*refs):
        sources, outs, sems = refs[:3], refs[3:5], refs[5]
        xi = lax.rem(lax.axis_index("seq") // bit, 2)
        pairs = []
        for out, side in zip(outs, (xi, 1 - xi)):
            at = pl.ds(pl.multiple_of(side * half, DH), half)
            first = 0
            for source in sources:
                last = first + source.shape[0]
                pairs.append((source.at[:, at], out.at[first:last, :]))
                first = last
        copy_all(pairs, sems)

    return pl.pallas_call(
        kernel,
        out_shape=[shape(total, half)] * 2,
        in_specs=[anywhere()] * 3,
        out_specs=[anywhere()] * 2,
        scratch_shapes=[pltpu.SemaphoreType.DMA((6,))],
        compiler_params=limit(1),
        cost_estimate=cost(0, 4 * total * columns),
        name="pack_cross",
    )(q, k, v)


def attend(queries, pairs, earlier, factor, name):
    parts = len(queries)
    rows = queries[0].shape[0]
    before = earlier[0].shape[1] if earlier else 0
    total_keys = sum(p.shape[0] for p in pairs)

    def kernel(*refs):
        query_refs, refs = refs[:parts], refs[parts:]
        pair_refs, refs = refs[: len(pairs)], refs[len(pairs) :]
        early, outs = refs[:-parts], refs[-parts:]
        keys = [ref[:, :DH] for ref in pair_refs]
        values = [ref[:, DH:] for ref in pair_refs]
        for i in range(parts):
            if before:
                outs[i][:, :before] = early[i][...]
            outs[i][:, before:] = softmax_mix(
                query_refs[i][:, :DH], keys, values, factor
            ).astype(BF16)

    return pl.pallas_call(
        kernel,
        out_shape=[shape(rows, before + DH)] * parts,
        in_specs=[in_vmem()] * (parts + len(pairs) + len(earlier)),
        out_specs=[in_vmem()] * parts,
        compiler_params=limit(14),
        cost_estimate=cost(
            4 * parts * rows * total_keys * DH, total_keys * DH * 4, parts * rows * total_keys
        ),
        name=name,
    )(*queries, *pairs, *earlier)


def cross(queries, captions, rows, block, factor):
    parts = len(queries)
    columns = queries[0].shape[1]
    total_keys = sum(c.shape[0] for c in captions) // 2

    def kernel(*refs):
        query_refs, caption_refs, outs = refs[:parts], refs[parts:-parts], refs[-parts:]
        for h in range(columns // DH):
            at = slice(h * DH, (h + 1) * DH)
            keys, values = [
                jnp.concatenate(
                    [
                        c[b * block : (b + 1) * block, at]
                        for c in caption_refs
                        for b in range(first, c.shape[0] // block, 2)
                    ],
                    axis=0,
                )
                for first in (0, 1)
            ]
            for query, out in zip(query_refs, outs):
                out[:, at] = softmax_mix(query[:rows, at], [keys], [values], factor).astype(
                    BF16
                )

    return pl.pallas_call(
        kernel,
        out_shape=[shape(rows, columns)] * parts,
        in_specs=[in_vmem()] * (parts + len(captions)),
        out_specs=[in_vmem()] * parts,
        compiler_params=limit(14),
        cost_estimate=cost(
            4 * parts * rows * total_keys * columns,
            (2 * parts * rows + 2 * total_keys) * columns * 2,
            parts * rows * total_keys * columns // DH,
        ),
        name="cross",
    )(*queries, *captions)


def project(members, tp_size, turn, lhs, weight, dtype, name):
    groups = len(lhs)
    rows, width = lhs[0].shape
    depth = weight.shape[0]
    columns = weight.shape[1] // tp_size

    def kernel(*refs):
        lhs_refs, w_ref, out = refs[:groups], refs[-2], refs[-1]
        zi = lax.axis_index("seq") // members
        side = lax.rem(lax.axis_index("tp") + turn, tp_size) if tp_size > 1 else 0
        block = math.gcd(columns, 512)
        for n in range(columns // block):
            at = pl.ds(pl.multiple_of(side * columns + n * block, DH), block)
            total = None
            for r in range(groups):
                base = pl.multiple_of(lax.rem(zi + r, groups) * width, DH)
                term = jnp.dot(
                    lhs_refs[r][...], w_ref[pl.ds(base, width), at], preferred_element_type=F32
                )
                total = term if total is None else total + term
            out[:, n * block : (n + 1) * block] = total.astype(out.dtype)

    return pl.pallas_call(
        kernel,
        out_shape=shape(rows, columns, dtype),
        in_specs=[in_vmem()] * (groups + 1),
        out_specs=in_vmem(),
        compiler_params=limit(24),
        cost_estimate=cost(
            2 * rows * depth * columns, depth * columns * 2 + rows * columns * 4
        ),
        name=name,
    )(*lhs, weight)


def finish(bit, tokens, gate, home, away, stay, came):
    def kernel(tokens, gate, home, away, stay, came, updated, cross_heads):
        projected = home[...] + away[...].astype(F32)
        updated[...] = (tokens[...].astype(F32) + gate[...] * projected).astype(BF16)
        half = stay.shape[1]
        xi = lax.rem(lax.axis_index("seq") // bit, 2)
        for side, half_heads in ((xi, stay), (1 - xi, came)):
            cross_heads[:, pl.ds(pl.multiple_of(side * half, DH), half)] = half_heads[...]

    return pl.pallas_call(
        kernel,
        out_shape=[shape(*tokens.shape), shape(stay.shape[0], 2 * stay.shape[1])],
        in_specs=[in_vmem()] * 6,
        out_specs=[in_vmem()] * 2,
        compiler_params=limit(12),
        cost_estimate=cost(0, tokens.size * 10),
        name="finish",
    )(tokens, gate[None, :], home, away, stay, came)


def shards(
    seq_size,
    tp_size,
    tokens,
    self_queries,
    self_keys,
    self_values,
    cross_queries,
    caption_keys,
    caption_values,
    out_weight,
    gate_vector,
):
    rows, columns = self_queries.shape
    heads_here = columns // DH
    factor = LOG2E / math.sqrt(DH)
    groups = math.gcd(heads_here, seq_size)
    members = seq_size // groups
    heads = heads_here // groups
    bit = members // 2
    cap_rows = caption_keys.shape[0]

    def rotate(x, r):
        if r % groups == 0:
            return x
        step = (r % groups) * members
        return lax.ppermute(x, "seq", [(s, (s + step) % seq_size) for s in range(seq_size)])

    def swap(x, by):
        return lax.ppermute(x, "seq", [(s, s ^ by) for s in range(seq_size)])

    def join(*xs):
        return xs[0] if len(xs) == 1 else jnp.concatenate(xs, axis=0)

    if members != 4 or heads_here % 2 or tp_size != 2:
        index_groups = [[g * members + m for m in range(members)] for g in range(groups)]

        def gather(x):
            return lax.all_gather(
                x, "seq", axis=0, tiled=True, axis_index_groups=index_groups
            )

        pieces = pack(groups, members, range(heads), self_queries, self_keys, self_values)
        outs = []
        for h in range(heads):
            here = [rotate(x, r) for r, x in enumerate(pieces[h])]
            pair = gather(join(*[x[:, DH:] for x in here]))
            outs = attend(here, [pair], outs, factor, "attend_%d" % h)
        lhs = [rotate(x, groups - r) for r, x in enumerate(outs)]
        caption = join(caption_keys, caption_values)
        caption = gather(join(*[rotate(caption, r) for r in range(groups)]))
        (cross_heads,) = cross([cross_queries], [caption], rows, cap_rows, factor)
        both = project(members, 1, 0, lhs, out_weight, BF16, "both")
        projected = lax.psum_scatter(both, "tp", scatter_dimension=1, tiled=True).astype(F32)
        updated = (tokens.astype(F32) + gate_vector[None, :] * projected).astype(BF16)
        return (updated, cross_heads)

    pieces = pack(groups, members, [0], self_queries, self_keys, self_values)
    pieces += pack(
        groups, members, list(range(1, heads)), self_queries, self_keys, self_values
    )
    stay, go = pack_cross(bit, cross_queries, caption_keys, caption_values)
    outs, arrived, far = [], [], []
    for h in range(heads):
        here = pieces[h]
        if h >= 2:
            here = here[:1] + [after(x, arrived[h - 2][1:]) for x in here[1:]]
        here = [rotate(x, r) for r, x in enumerate(here)]
        arrived.append(here)
        mine = join(*[x[:, DH:] for x in here])
        far.append(swap(mine, 2))
        half = join(mine, far[h])
        outs = attend(here, [half, swap(half, 1)], outs, factor, "attend_%d" % h)
    lhs = [rotate(x, groups - r) for r, x in enumerate(outs)]

    come = swap(after(go, far[0]), bit)
    caption = after(join(stay[rows:], come[rows:]), arrived[-1][1:])
    caption = join(*[rotate(caption, r) for r in range(groups)])
    captions = [caption, swap(caption, 1)]

    away = project(members, tp_size, 1, lhs, out_weight, BF16, "away")
    captions[0] = after(captions[0], away)
    own, theirs = cross([stay, come], captions, rows, cap_rows, factor)
    came = swap(theirs, bit)
    away = lax.ppermute(away, "tp", [(0, 1), (1, 0)])
    home = project(members, tp_size, 0, lhs, out_weight, F32, "home")
    return tuple(finish(bit, tokens, gate_vector, home, away, own, came))


def solution(mesh):
    seq_size, tp_size = mesh.shape["seq"], mesh.shape["tp"]
    return jax.shard_map(
        lambda *args: shards(seq_size, tp_size, *args),
        mesh=mesh,
        in_specs=(
            P("seq", "tp"),
            P("seq", "tp"),
            P("seq", "tp"),
            P("seq", "tp"),
            P("seq", "tp"),
            P("seq", "tp"),
            P("seq", "tp"),
            P("tp", None),
            P("tp"),
        ),
        out_specs=(P("seq", "tp"), P("seq", "tp")),
        check_vma=False,
    )
```

time: 260 us -> 104 us (0.40)
  waiting for transfers between devices: 191 us -> 42.7 us
  starting transfers between devices: 0.2 us -> 35.6 us
  matrix products: 24.4 us -> 0 us
  Pallas kernels: 0 us -> 14.9 us
  between operations: 13.9 us -> 1.01 us
  other arithmetic: 11.9 us -> 0.08 us
  local copies, waits for them, and re-layouts: 18.4 us -> 9.74 us
    all_gather x4 -> x0, waiting for transfers between devices: 170 us -> none  [the longest x1 66.6 us: shards(): lax.all_gather(self_values, 'seq', axis=0, tiled=True)]
    ppermute x0 -> x25, waiting for transfers between devices: none -> 42.7 us  [the longest x15 24.4 us: rotate(): lax.ppermute(x, 'seq', [(s, (s + step) % seq_size) for s in range(seq_siz...]
    ppermute x0 -> x25, starting transfers between devices: none -> 35.6 us  [the longest x15 23.2 us: rotate(): lax.ppermute(x, 'seq', [(s, (s + step) % seq_size) for s in range(seq_siz...]
    dot_general x7 -> x0, matrix products: 24.4 us -> none  [the longest x1 8.99 us: shards(): jnp.dot(self_heads, out_weight, preferred_element_type=jnp.float32)]
    reduce_scatter x1 -> x0, waiting for transfers between devices: 19.4 us -> none  [shards(): lax.psum_scatter(partial_terms.astype(jnp.bfloat16), 'tp', scatter_dimens...]
    pallas_call x0 -> x10, Pallas kernels: none -> 14.9 us  [the longest x3 6.55 us: attend(): pl.pallas_call(kernel, out_shape=[shape(rows, before + DH)] * parts, in_s...]
    reduce_sum x3 -> x0, other arithmetic: 8.54 us -> none  [online_step(): totals = totals * rescale + jnp.sum(exp_scores, axis=2)]
    dynamic_slice x2 -> x0, local copies, waits for them, and re-layouts: 7.11 us -> none  [loop_body(): lax.dynamic_slice_in_dim(pieces[1], position * block_rows, block_rows, 0)]
  transfers between devices with their start and end apart: 5 -> 25, of which waited for: 4 -> 10; matrix products, arithmetic and copies ran while one was open for 19% -> 0% of each run, Pallas kernels for 0% -> 13%
where the time goes in v3:
time: 104 us
  waiting for transfers between devices  42.7 us (41%)
  starting transfers between devices  35.6 us (34%)
  Pallas kernels  14.9 us (14%)
  local copies, waits for them, and re-layouts  9.74 us (9%)
    ppermute x15, waiting for transfers between devices, rotate(): lax.ppermute(x, 'seq', [(s, (s + step) % seq_size) for s in range(seq_siz...  24.4 us
    ppermute x15, starting transfers between devices, rotate(): lax.ppermute(x, 'seq', [(s, (s + step) % seq_size) for s in range(seq_siz...  23.2 us
    ppermute x9, starting transfers between devices, swap(): return lax.ppermute(x, 'seq', [(s, s ^ by) for s in range(seq_size)])  10.8 us
    ppermute x9, waiting for transfers between devices, swap(): return lax.ppermute(x, 'seq', [(s, s ^ by) for s in range(seq_size)])  10.1 us
    unnamed x27, local copies, waits for them, and re-layouts  9.52 us
    ppermute x1, waiting for transfers between devices, shards(): away = lax.ppermute(away, 'tp', [(0, 1), (1, 0)])  8.24 us
    pallas_call x3, Pallas kernels, attend(): pl.pallas_call(kernel, out_shape=[shape(rows, before + DH)] * parts, in_s...  6.55 us
    pallas_call x1, Pallas kernels, cross(): pl.pallas_call(kernel, out_shape=[shape(rows, columns)] * parts, in_specs...  3.26 us
  transfers between devices with their start and end apart: 25, of which 10 were waited for; matrix products, arithmetic and copies ran while one was open for 0% of the time, Pallas kernels for 13%

profile of v3, /device:TPU:0, one launch (start us, length us, event | category | flops | bytes accessed | tf_op | source)
XLA Modules:
  0.0 104.0 jit_solution(1517316961435802082)
XLA Ops:
  0.7 1.1 %copy-done.1 = bf16[128,1536]{1,0:T(8,128)(2,1)S(1)} copy-done((bf16[128,1536]{1,0:T(8,128)(2,1)S(1)}, bf16[128,1536]{1,0:T(8,128)(2,1)}, u32[]{:S(2)}) %copy-start.1) | copy-done | bytes 393240
  1.8 1.2 %copy-done.3 = bf16[128,1536]{1,0:T(8,128)(2,1)S(1)} copy-done((bf16[128,1536]{1,0:T(8,128)(2,1)S(1)}, bf16[128,1536]{1,0:T(8,128)(2,1)}, u32[]{:S(2)}) %copy-start.3) | copy-done | bytes 393240
  3.0 1.4 %copy-done.5 = bf16[128,1536]{1,0:T(8,128)(2,1)S(1)} copy-done((bf16[128,1536]{1,0:T(8,128)(2,1)S(1)}, bf16[128,1536]{1,0:T(8,128)(2,1)}, u32[]{:S(2)}) %copy-start.5) | copy-done | bytes 393240
  4.6 3.1 %collective-permute-start = (bf16[128,384]{1,0:T(8,128)(2,1)S(1)}, bf16[128,384]{1,0:T(8,128)(2,1)S(1)}, u32[]{:S(2)}, u32[]{:S(2)}) collective-permute-start(bf16[128,384]{1,0:T(8,128)(2,1)S(1)} %get-tuple-element.38), channel_id=1, source_target_pairs={{0,8},{2,10},{4,12},{6,14},{8,16},{10,18},{12,20},{14,22},{16,24},... | collective-permute-start | bytes 294920 | tf_op jit(solution)/shard_map/ppermute | solution.py:285
  7.6 2.6 %collective-permute-start.1 = (bf16[128,384]{1,0:T(8,128)(2,1)S(1)}, bf16[128,384]{1,0:T(8,128)(2,1)S(1)}, u32[]{:S(2)}, u32[]{:S(2)}) collective-permute-start(bf16[128,384]{1,0:T(8,128)(2,1)S(1)} %get-tuple-element.39), channel_id=1, source_target_pairs={{0,16},{2,18},{4,20},{6,22},{8,24},{10,26},{12,28},{14,30},{16,0},... | collective-permute-start | bytes 294920 | tf_op jit(solution)/shard_map/ppermute | solution.py:285
  10.2 1.3 %collective-permute-start.2 = (bf16[128,384]{1,0:T(8,128)(2,1)S(1)}, bf16[128,384]{1,0:T(8,128)(2,1)S(1)}, u32[]{:S(2)}, u32[]{:S(2)}) collective-permute-start(bf16[128,384]{1,0:T(8,128)(2,1)S(1)} %get-tuple-element.40), channel_id=1, source_target_pairs={{0,24},{2,26},{4,28},{6,30},{8,0},{10,2},{12,4},{14,6},{16,8},{18,... | collective-permute-start | bytes 294920 | tf_op jit(solution)/shard_map/ppermute | solution.py:285
  19.1 2.9 %collective-permute-start.10 = (bf16[128,384]{1,0:T(8,128)(2,1)S(1)}, bf16[128,384]{1,0:T(8,128)(2,1)S(1)}, u32[]{:S(2)}, u32[]{:S(2)}) collective-permute-start(bf16[128,384]{1,0:T(8,128)(2,1)S(1)} %get-tuple-element.49), channel_id=1, source_target_pairs={{0,24},{2,26},{4,28},{6,30},{8,0},{10,2},{12,4},{14,6},{16,8},{18,... | collective-permute-start | bytes 294920 | tf_op jit(solution)/shard_map/ppermute | solution.py:285
  22.1 1.6 %collective-permute-start.13 = (bf16[512,256]{1,0:T(8,128)(2,1)S(1)}, bf16[512,256]{1,0:T(8,128)(2,1)S(1)}, u32[]{:S(2)}, u32[]{:S(2)}) collective-permute-start(bf16[512,256]{1,0:T(8,128)(2,1)S(1)} %pad_maximum_fusion.2), channel_id=1, source_target_pairs={{0,4},{2,6},{4,0},{6,2},{8,12},{10,14},{12,8},{14,10},{16,20},{18,... | collective-permute-start | bytes 786440 | tf_op jit(solution)/shard_map/ppermute | solution.py:288
  23.6 1.7 %collective-permute-start.5 = (bf16[128,384]{1,0:T(8,128)(2,1)S(1)}, bf16[128,384]{1,0:T(8,128)(2,1)S(1)}, u32[]{:S(2)}, u32[]{:S(2)}) collective-permute-start(bf16[128,384]{1,0:T(8,128)(2,1)S(1)} %get-tuple-element.45), channel_id=1, source_target_pairs={{0,24},{2,26},{4,28},{6,30},{8,0},{10,2},{12,4},{14,6},{16,8},{18,... | collective-permute-start | bytes 294920 | tf_op jit(solution)/shard_map/ppermute | solution.py:285
  25.3 1.4 %collective-permute-start.4 = (bf16[128,384]{1,0:T(8,128)(2,1)S(1)}, bf16[128,384]{1,0:T(8,128)(2,1)S(1)}, u32[]{:S(2)}, u32[]{:S(2)}) collective-permute-start(bf16[128,384]{1,0:T(8,128)(2,1)S(1)} %get-tuple-element.43), channel_id=1, source_target_pairs={{0,16},{2,18},{4,20},{6,22},{8,24},{10,26},{12,28},{14,30},{16,0},... | collective-permute-start | bytes 294920 | tf_op jit(solution)/shard_map/ppermute | solution.py:285
  27.8 4.2 %collective-permute-start.11 = (bf16[512,256]{1,0:T(8,128)(2,1)S(1)}, bf16[512,256]{1,0:T(8,128)(2,1)S(1)}, u32[]{:S(2)}, u32[]{:S(2)}) collective-permute-start(bf16[512,256]{1,0:T(8,128)(2,1)S(1)} %pad_maximum_fusion.1), channel_id=1, source_target_pairs={{0,4},{2,6},{4,0},{6,2},{8,12},{10,14},{12,8},{14,10},{16,20},{18,... | collective-permute-start | bytes 786440 | tf_op jit(solution)/shard_map/ppermute | solution.py:288
  32.0 3.2 %collective-permute-done.3.refs_1_ = bf16[128,384]{1,0:T(8,128)(2,1)S(1)} collective-permute-done((bf16[128,384]{1,0:T(8,128)(2,1)S(1)}, bf16[128,384]{1,0:T(8,128)(2,1)S(1)}, u32[]{:S(2)}, u32[]{:S(2)}) %collective-permute-start.3) | collective-permute-done | bytes 98336 | tf_op jit(solution)/shard_map/ppermute | solution.py:285
  35.7 1.7 %collective-permute-start.19 = (bf16[192,768]{1,0:T(8,128)(2,1)S(1)}, bf16[192,768]{1,0:T(8,128)(2,1)S(1)}, u32[]{:S(2)}, u32[]{:S(2)}) collective-permute-start(bf16[192,768]{1,0:T(8,128)(2,1)S(1)} %get-tuple-element.65), channel_id=1, source_target_pairs={{0,4},{2,6},{4,0},{6,2},{8,12},{10,14},{12,8},{14,10},{16,20},{18,... | collective-permute-start | bytes 884744 | tf_op jit(solution)/shard_map/ppermute | solution.py:288
  38.6 7.1 %collective-permute-done.19.refs_1_ = bf16[192,768]{1,0:T(8,128)(2,1)S(1)} collective-permute-done((bf16[192,768]{1,0:T(8,128)(2,1)S(1)}, bf16[192,768]{1,0:T(8,128)(2,1)S(1)}, u32[]{:S(2)}, u32[]{:S(2)}) %collective-permute-start.19) | collective-permute-done | bytes 294944 | tf_op jit(solution)/shard_map/ppermute | solution.py:288
  45.8 2.9 %collective-permute-done.6 = bf16[512,256]{1,0:T(8,128)(2,1)S(1)} collective-permute-done((bf16[512,256]{1,0:T(8,128)(2,1)S(1)}, bf16[512,256]{1,0:T(8,128)(2,1)S(1)}, u32[]{:S(2)}, u32[]{:S(2)}) %collective-permute-start.6) | collective-permute-done | bytes 262176 | tf_op jit(solution)/shard_map/ppermute | solution.py:288
  48.9 3.0 %collective-permute-start.21 = (bf16[128,768]{1,0:T(8,128)(2,1)S(1)}, bf16[128,768]{1,0:T(8,128)(2,1)S(1)}, u32[]{:S(2)}, u32[]{:S(2)}) collective-permute-start(bf16[128,768]{1,0:T(8,128)(2,1)S(1)} %pad_maximum_fusion.3), channel_id=1, source_target_pairs={{0,16},{2,18},{4,20},{6,22},{8,24},{10,26},{12,28},{14,30},{16,0},... | collective-permute-start | bytes 589832 | tf_op jit(solution)/shard_map/ppermute | solution.py:285
  51.9 1.8 %collective-permute-done.20 = bf16[128,768]{1,0:T(8,128)(2,1)S(1)} collective-permute-done((bf16[128,768]{1,0:T(8,128)(2,1)S(1)}, bf16[128,768]{1,0:T(8,128)(2,1)S(1)}, u32[]{:S(2)}, u32[]{:S(2)}) %collective-permute-start.20) | collective-permute-done | bytes 196640 | tf_op jit(solution)/shard_map/ppermute | solution.py:285
  53.8 8.1 %collective-permute-done.21 = bf16[128,768]{1,0:T(8,128)(2,1)S(1)} collective-permute-done((bf16[128,768]{1,0:T(8,128)(2,1)S(1)}, bf16[128,768]{1,0:T(8,128)(2,1)S(1)}, u32[]{:S(2)}, u32[]{:S(2)}) %collective-permute-start.21) | collective-permute-done | bytes 196640 | tf_op jit(solution)/shard_map/ppermute | solution.py:285
  61.9 1.7 %collective-permute-done.22 = bf16[128,768]{1,0:T(8,128)(2,1)S(1)} collective-permute-done((bf16[128,768]{1,0:T(8,128)(2,1)S(1)}, bf16[128,768]{1,0:T(8,128)(2,1)S(1)}, u32[]{:S(2)}, u32[]{:S(2)}) %collective-permute-start.22) | collective-permute-done | bytes 196640 | tf_op jit(solution)/shard_map/ppermute | solution.py:285
  63.6 2.2 %attend_0.1 = (bf16[128,128]{1,0:T(8,128)(2,1)S(1)}, bf16[128,128]{1,0:T(8,128)(2,1)S(1)}, bf16[128,128]{1,0:T(8,128)(2,1)S(1)}, bf16[128,128]{1,0:T(8,128)(2,1)S(1)}) custom-call(bf16[128,384]{1,0:T(8,128)(2,1)S(1)} %get-tuple-element.50.refs_0_, bf16[128,384]{1,0:T(8,128)(2,1)S(1)} %collective-permute-done.refs_1_, ...), custom_call_target="tpu_custom_call" | custom-call | flops 536870912 | bytes 1048576 | tf_op jit(solution)/shard_map/attend_0/pallas_call | solution.py:151
  65.8 2.2 %attend_1.1 = (bf16[128,256]{1,0:T(8,128)(2,1)S(1)}, bf16[128,256]{1,0:T(8,128)(2,1)S(1)}, bf16[128,256]{1,0:T(8,128)(2,1)S(1)}, bf16[128,256]{1,0:T(8,128)(2,1)S(1)}) custom-call(bf16[128,384]{1,0:T(8,128)(2,1)S(1)} %get-tuple-element.46.refs_0_, bf16[128,384]{1,0:T(8,128)(2,1)S(1)} %collective-permute-done.8.refs_1_, ...), custom_call_target="tpu_custom_call" | custom-call | flops 536870912 | bytes 1048576 | tf_op jit(solution)/shard_map/attend_1/pallas_call | solution.py:151
  68.0 2.2 %attend_2.1 = (bf16[128,384]{1,0:T(8,128)(2,1)S(1)}, bf16[128,384]{1,0:T(8,128)(2,1)S(1)}, bf16[128,384]{1,0:T(8,128)(2,1)S(1)}, bf16[128,384]{1,0:T(8,128)(2,1)S(1)}) custom-call(bf16[128,384]{1,0:T(8,128)(2,1)S(1)} %get-tuple-element.36.refs_0_, bf16[128,384]{1,0:T(8,128)(2,1)S(1)} %collective-permute-done.3.refs_1_, ...), custom_call_target="tpu_custom_call" | custom-call | flops 536870912 | bytes 1048576 | tf_op jit(solution)/shard_map/attend_2/pallas_call | solution.py:151
  70.2 4.5 %collective-permute-start.15 = (bf16[128,384]{1,0:T(8,128)(2,1)S(1)}, bf16[128,384]{1,0:T(8,128)(2,1)S(1)}, u32[]{:S(2)}, u32[]{:S(2)}) collective-permute-start(bf16[128,384]{1,0:T(8,128)(2,1)S(1)} %get-tuple-element.60), channel_id=1, source_target_pairs={{0,24},{2,26},{4,28},{6,30},{8,0},{10,2},{12,4},{14,6},{16,8},{18,... | collective-permute-start | bytes 294920 | tf_op jit(solution)/shard_map/ppermute | solution.py:285
  75.3 2.5 %collective-permute-done.15.refs_1_ = bf16[128,384]{1,0:T(8,128)(2,1)S(1)} collective-permute-done((bf16[128,384]{1,0:T(8,128)(2,1)S(1)}, bf16[128,384]{1,0:T(8,128)(2,1)S(1)}, u32[]{:S(2)}, u32[]{:S(2)}) %collective-permute-start.15) | collective-permute-done | bytes 98336 | tf_op jit(solution)/shard_map/ppermute | solution.py:285
  77.8 6.6 %collective-permute-done.16.refs_2_ = bf16[128,384]{1,0:T(8,128)(2,1)S(1)} collective-permute-done((bf16[128,384]{1,0:T(8,128)(2,1)S(1)}, bf16[128,384]{1,0:T(8,128)(2,1)S(1)}, u32[]{:S(2)}, u32[]{:S(2)}) %collective-permute-start.16) | collective-permute-done | bytes 98336 | tf_op jit(solution)/shard_map/ppermute | solution.py:285
  84.5 1.6 %away.1 = bf16[128,2560]{1,0:T(8,128)(2,1)S(1)} custom-call(bf16[128,384]{1,0:T(8,128)(2,1)S(1)} %get-tuple-element.59.refs_0_, bf16[128,384]{1,0:T(8,128)(2,1)S(1)} %collective-permute-done.15.refs_1_, bf16[128,384]{1,0:T(8,128)(2,1)S(1)} %collective-permute-done.16.refs_2_, bf16[128,384]{1,0:T(8,128)(2,1)S(1)} %collective-permute-done.17.refs_3_, ...), custom_call_target="tpu_custom_call" | custom-call | flops 1006632960 | bytes 9175040 | tf_op jit(solution)/shard_map/away/pallas_call | solution.py:226
  86.0 1.6 %collective-permute-start.18 = (bf16[128,2560]{1,0:T(8,128)(2,1)S(1)}, bf16[128,2560]{1,0:T(8,128)(2,1)S(1)}, u32[]{:S(2)}, u32[]{:S(2)}) collective-permute-start(bf16[128,2560]{1,0:T(8,128)(2,1)S(1)} %away.1), channel_id=1, source_target_pairs={{0,1},{1,0},{2,3},{3,2},{4,5},{5,4},{6,7},{7,6},{8,9},{9,8},{10,11... | collective-permute-start | bytes 1966088 | tf_op jit(solution)/shard_map/ppermute | solution.py:343
  87.6 3.3 %cross.1 = (bf16[128,768]{1,0:T(8,128)(2,1)S(1)}, bf16[128,768]{1,0:T(8,128)(2,1)S(1)}) custom-call(bf16[192,768]{1,0:T(8,128)(2,1)S(1)} %get-tuple-element.63.refs_0_, bf16[192,768]{1,0:T(8,128)(2,1)S(1)} %collective-permute-done.19.refs_1_, bf16[512,768]{1,0:T(8,128)(2,1)S(1)} %constant_dynamic-update-slice_fusion.15.refs_2_, ...), custom_call_target="tpu_custom_call" | custom-call | flops 402653184 | bytes 2359296 | tf_op jit(solution)/shard_map/cross/pallas_call | solution.py:189
  90.9 2.1 %collective-permute-start.24 = (bf16[128,768]{1,0:T(8,128)(2,1)S(1)}, bf16[128,768]{1,0:T(8,128)(2,1)S(1)}, u32[]{:S(2)}, u32[]{:S(2)}) collective-permute-start(bf16[128,768]{1,0:T(8,128)(2,1)S(1)} %get-tuple-element.69), channel_id=1, source_target_pairs={{0,4},{2,6},{4,0},{6,2},{8,12},{10,14},{12,8},{14,10},{16,20},{18,... | collective-permute-start | bytes 589832 | tf_op jit(solution)/shard_map/ppermute | solution.py:288
  93.0 1.6 %home.1 = f32[128,2560]{1,0:T(8,128)S(1)} custom-call(bf16[128,384]{1,0:T(8,128)(2,1)S(1)} %get-tuple-element.59.refs_0_, bf16[128,384]{1,0:T(8,128)(2,1)S(1)} %collective-permute-done.15.refs_1_, bf16[128,384]{1,0:T(8,128)(2,1)S(1)} %collective-permute-done.16.refs_2_, bf16[128,384]{1,0:T(8,128)(2,1)S(1)} %collective-permute-done.17.refs_3_, ...), custom_call_target="tpu_custom_call" | custom-call | flops 1006632960 | bytes 9175040 | tf_op jit(solution)/shard_map/home/pallas_call | solution.py:226
  94.5 8.2 %collective-permute-done.18.away = bf16[128,2560]{1,0:T(8,128)(2,1)S(1)} collective-permute-done((bf16[128,2560]{1,0:T(8,128)(2,1)S(1)}, bf16[128,2560]{1,0:T(8,128)(2,1)S(1)}, u32[]{:S(2)}, u32[]{:S(2)}) %collective-permute-start.18) | collective-permute-done | bytes 655392 | tf_op jit(solution)/shard_map/ppermute | solution.py:343
  102.8 1.2 %finish.1 = (bf16[128,2560]{1,0:T(8,128)(2,1)}, bf16[128,1536]{1,0:T(8,128)(2,1)}) custom-call(bf16[128,2560]{1,0:T(8,128)(2,1)S(1)} %copy-done.7, f32[1,2560]{1,0:T(1,128)S(1)} %broadcast_in_dim.3.gate, f32[128,2560]{1,0:T(8,128)S(1)} %home.1, bf16[128,2560]{1,0:T(8,128)(2,1)S(1)} %collective-permute-done.18.away, ...), custom_call_target="tpu_custom_call" | custom-call | bytes 3276800 | tf_op jit(solution)/shard_map/finish/pallas_call | solution.py:248
  (78 shorter events, 11.3 us)
Async XLA Ops:
  0.6 83.8 %copy-start = (bf16[1536,5120]{1,0:T(8,128)(2,1)S(1)}, bf16[1536,5120]{1,0:T(8,128)(2,1)}, u32[]{:S(2)}) copy-start(bf16[1536,5120]{1,0:T(8,128)(2,1)} %refs_4_.3) | copy-start | bytes 47185924
  0.6 1.1 %copy-start.1 = (bf16[128,1536]{1,0:T(8,128)(2,1)S(1)}, bf16[128,1536]{1,0:T(8,128)(2,1)}, u32[]{:S(2)}) copy-start(bf16[128,1536]{1,0:T(8,128)(2,1)} %refs_0_.4) | copy-start | bytes 1179652
  1.8 1.2 %copy-start.3 = (bf16[128,1536]{1,0:T(8,128)(2,1)S(1)}, bf16[128,1536]{1,0:T(8,128)(2,1)}, u32[]{:S(2)}) copy-start(bf16[128,1536]{1,0:T(8,128)(2,1)} %refs_1_.4) | copy-start | bytes 1179652
  3.0 1.4 %copy-start.5 = (bf16[128,1536]{1,0:T(8,128)(2,1)S(1)}, bf16[128,1536]{1,0:T(8,128)(2,1)}, u32[]{:S(2)}) copy-start(bf16[128,1536]{1,0:T(8,128)(2,1)} %refs_2_.4) | copy-start | bytes 1179652
  4.6 14.5 %collective-permute-start = (bf16[128,384]{1,0:T(8,128)(2,1)S(1)}, bf16[128,384]{1,0:T(8,128)(2,1)S(1)}, u32[]{:S(2)}, u32[]{:S(2)}) collective-permute-start(bf16[128,384]{1,0:T(8,128)(2,1)S(1)} %get-tuple-element.38), channel_id=1, source_target_pairs={{0,8},{2,10},{4,12},{6,14},{8,16},{10,18},{12,20},{14,22},{16,24},... | collective-permute-start | bytes 294920 | tf_op jit(solution)/shard_map/ppermute | solution.py:285
  7.6 14.3 %collective-permute-start.1 = (bf16[128,384]{1,0:T(8,128)(2,1)S(1)}, bf16[128,384]{1,0:T(8,128)(2,1)S(1)}, u32[]{:S(2)}, u32[]{:S(2)}) collective-permute-start(bf16[128,384]{1,0:T(8,128)(2,1)S(1)} %get-tuple-element.39), channel_id=1, source_target_pairs={{0,16},{2,18},{4,20},{6,22},{8,24},{10,26},{12,28},{14,30},{16,0},... | collective-permute-start | bytes 294920 | tf_op jit(solution)/shard_map/ppermute | solution.py:285
  10.2 11.8 %collective-permute-start.2 = (bf16[128,384]{1,0:T(8,128)(2,1)S(1)}, bf16[128,384]{1,0:T(8,128)(2,1)S(1)}, u32[]{:S(2)}, u32[]{:S(2)}) collective-permute-start(bf16[128,384]{1,0:T(8,128)(2,1)S(1)} %get-tuple-element.40), channel_id=1, source_target_pairs={{0,24},{2,26},{4,28},{6,30},{8,0},{10,2},{12,4},{14,6},{16,8},{18,... | collective-permute-start | bytes 294920 | tf_op jit(solution)/shard_map/ppermute | solution.py:285
  15.0 10.3 %collective-permute-start.8 = (bf16[128,384]{1,0:T(8,128)(2,1)S(1)}, bf16[128,384]{1,0:T(8,128)(2,1)S(1)}, u32[]{:S(2)}, u32[]{:S(2)}) collective-permute-start(bf16[128,384]{1,0:T(8,128)(2,1)S(1)} %get-tuple-element.47), channel_id=1, source_target_pairs={{0,8},{2,10},{4,12},{6,14},{8,16},{10,18},{12,20},{14,22},{16,24},... | collective-permute-start | bytes 294920 | tf_op jit(solution)/shard_map/ppermute | solution.py:285
  15.7 11.1 %collective-permute-start.9 = (bf16[128,384]{1,0:T(8,128)(2,1)S(1)}, bf16[128,384]{1,0:T(8,128)(2,1)S(1)}, u32[]{:S(2)}, u32[]{:S(2)}) collective-permute-start(bf16[128,384]{1,0:T(8,128)(2,1)S(1)} %get-tuple-element.48), channel_id=1, source_target_pairs={{0,16},{2,18},{4,20},{6,22},{8,24},{10,26},{12,28},{14,30},{16,0},... | collective-permute-start | bytes 294920 | tf_op jit(solution)/shard_map/ppermute | solution.py:285
  16.1 1.0 copy-start.8
  19.1 8.7 %collective-permute-start.10 = (bf16[128,384]{1,0:T(8,128)(2,1)S(1)}, bf16[128,384]{1,0:T(8,128)(2,1)S(1)}, u32[]{:S(2)}, u32[]{:S(2)}) collective-permute-start(bf16[128,384]{1,0:T(8,128)(2,1)S(1)} %get-tuple-element.49), channel_id=1, source_target_pairs={{0,24},{2,26},{4,28},{6,30},{8,0},{10,2},{12,4},{14,6},{16,8},{18,... | collective-permute-start | bytes 294920 | tf_op jit(solution)/shard_map/ppermute | solution.py:285
  22.0 70.9 %copy-start.11 = (f32[2560]{0:T(1024)S(1)}, f32[2560]{0:T(1024)}, u32[]{:S(2)}) copy-start(f32[2560]{0:T(1024)} %param.17) | copy-start | bytes 30724
  22.1 13.7 %collective-permute-start.13 = (bf16[512,256]{1,0:T(8,128)(2,1)S(1)}, bf16[512,256]{1,0:T(8,128)(2,1)S(1)}, u32[]{:S(2)}, u32[]{:S(2)}) collective-permute-start(bf16[512,256]{1,0:T(8,128)(2,1)S(1)} %pad_maximum_fusion.2), channel_id=1, source_target_pairs={{0,4},{2,6},{4,0},{6,2},{8,12},{10,14},{12,8},{14,10},{16,20},{18,... | collective-permute-start | bytes 786440 | tf_op jit(solution)/shard_map/ppermute | solution.py:288
  23.6 12.1 %collective-permute-start.5 = (bf16[128,384]{1,0:T(8,128)(2,1)S(1)}, bf16[128,384]{1,0:T(8,128)(2,1)S(1)}, u32[]{:S(2)}, u32[]{:S(2)}) collective-permute-start(bf16[128,384]{1,0:T(8,128)(2,1)S(1)} %get-tuple-element.45), channel_id=1, source_target_pairs={{0,24},{2,26},{4,28},{6,30},{8,0},{10,2},{12,4},{14,6},{16,8},{18,... | collective-permute-start | bytes 294920 | tf_op jit(solution)/shard_map/ppermute | solution.py:285
  25.3 10.3 %collective-permute-start.4 = (bf16[128,384]{1,0:T(8,128)(2,1)S(1)}, bf16[128,384]{1,0:T(8,128)(2,1)S(1)}, u32[]{:S(2)}, u32[]{:S(2)}) collective-permute-start(bf16[128,384]{1,0:T(8,128)(2,1)S(1)} %get-tuple-element.43), channel_id=1, source_target_pairs={{0,16},{2,18},{4,20},{6,22},{8,24},{10,26},{12,28},{14,30},{16,0},... | collective-permute-start | bytes 294920 | tf_op jit(solution)/shard_map/ppermute | solution.py:285
  26.8 8.4 %collective-permute-start.3 = (bf16[128,384]{1,0:T(8,128)(2,1)S(1)}, bf16[128,384]{1,0:T(8,128)(2,1)S(1)}, u32[]{:S(2)}, u32[]{:S(2)}) collective-permute-start(bf16[128,384]{1,0:T(8,128)(2,1)S(1)} %get-tuple-element.41), channel_id=1, source_target_pairs={{0,8},{2,10},{4,12},{6,14},{8,16},{10,18},{12,20},{14,22},{16,24},... | collective-permute-start | bytes 294920 | tf_op jit(solution)/shard_map/ppermute | solution.py:285
  27.8 10.2 %collective-permute-start.11 = (bf16[512,256]{1,0:T(8,128)(2,1)S(1)}, bf16[512,256]{1,0:T(8,128)(2,1)S(1)}, u32[]{:S(2)}, u32[]{:S(2)}) collective-permute-start(bf16[512,256]{1,0:T(8,128)(2,1)S(1)} %pad_maximum_fusion.1), channel_id=1, source_target_pairs={{0,4},{2,6},{4,0},{6,2},{8,12},{10,14},{12,8},{14,10},{16,20},{18,... | collective-permute-start | bytes 786440 | tf_op jit(solution)/shard_map/ppermute | solution.py:288
  35.7 10.0 %collective-permute-start.19 = (bf16[192,768]{1,0:T(8,128)(2,1)S(1)}, bf16[192,768]{1,0:T(8,128)(2,1)S(1)}, u32[]{:S(2)}, u32[]{:S(2)}) collective-permute-start(bf16[192,768]{1,0:T(8,128)(2,1)S(1)} %get-tuple-element.65), channel_id=1, source_target_pairs={{0,4},{2,6},{4,0},{6,2},{8,12},{10,14},{12,8},{14,10},{16,20},{18,... | collective-permute-start | bytes 884744 | tf_op jit(solution)/shard_map/ppermute | solution.py:288
  37.5 11.3 %collective-permute-start.6 = (bf16[512,256]{1,0:T(8,128)(2,1)S(1)}, bf16[512,256]{1,0:T(8,128)(2,1)S(1)}, u32[]{:S(2)}, u32[]{:S(2)}) collective-permute-start(bf16[512,256]{1,0:T(8,128)(2,1)S(1)} %pad_maximum_fusion), channel_id=1, source_target_pairs={{0,4},{2,6},{4,0},{6,2},{8,12},{10,14},{12,8},{14,10},{16,20},{18,... | collective-permute-start | bytes 786440 | tf_op jit(solution)/shard_map/ppermute | solution.py:288
  37.9 25.7 %collective-permute-start.14 = (bf16[1024,256]{1,0:T(8,128)(2,1)S(1)}, bf16[1024,256]{1,0:T(8,128)(2,1)S(1)}, u32[]{:S(2)}, u32[]{:S(2)}) collective-permute-start(bf16[1024,256]{1,0:T(8,128)(2,1)S(1)} %constant_dynamic-update-slice_fusion.10.refs_4_), channel_id=1, source_target_pairs={{0,2},{2,0},{4,6},{6,4},{8,10},{10,8},{12,14},{14,12},{16,18},{18,... | collective-permute-start | bytes 1572872 | tf_op jit(solution)/shard_map/ppermute | solution.py:288
  38.1 27.8 %collective-permute-start.12 = (bf16[1024,256]{1,0:T(8,128)(2,1)S(1)}, bf16[1024,256]{1,0:T(8,128)(2,1)S(1)}, u32[]{:S(2)}, u32[]{:S(2)}) collective-permute-start(bf16[1024,256]{1,0:T(8,128)(2,1)S(1)} %constant_dynamic-update-slice_fusion.5.refs_4_), channel_id=1, source_target_pairs={{0,2},{2,0},{4,6},{6,4},{8,10},{10,8},{12,14},{14,12},{16,18},{18,... | collective-permute-start | bytes 1572872 | tf_op jit(solution)/shard_map/ppermute | solution.py:288
  45.8 7.9 %collective-permute-start.20 = (bf16[128,768]{1,0:T(8,128)(2,1)S(1)}, bf16[128,768]{1,0:T(8,128)(2,1)S(1)}, u32[]{:S(2)}, u32[]{:S(2)}) collective-permute-start(bf16[128,768]{1,0:T(8,128)(2,1)S(1)} %pad_maximum_fusion.3), channel_id=1, source_target_pairs={{0,8},{2,10},{4,12},{6,14},{8,16},{10,18},{12,20},{14,22},{16,24},... | collective-permute-start | bytes 589832 | tf_op jit(solution)/shard_map/ppermute | solution.py:285
  48.8 19.2 %collective-permute-start.7 = (bf16[1024,256]{1,0:T(8,128)(2,1)S(1)}, bf16[1024,256]{1,0:T(8,128)(2,1)S(1)}, u32[]{:S(2)}, u32[]{:S(2)}) collective-permute-start(bf16[1024,256]{1,0:T(8,128)(2,1)S(1)} %constant_dynamic-update-slice_fusion.refs_4_), channel_id=1, source_target_pairs={{0,2},{2,0},{4,6},{6,4},{8,10},{10,8},{12,14},{14,12},{16,18},{18,... | collective-permute-start | bytes 1572872 | tf_op jit(solution)/shard_map/ppermute | solution.py:288
  48.9 12.9 %collective-permute-start.21 = (bf16[128,768]{1,0:T(8,128)(2,1)S(1)}, bf16[128,768]{1,0:T(8,128)(2,1)S(1)}, u32[]{:S(2)}, u32[]{:S(2)}) collective-permute-start(bf16[128,768]{1,0:T(8,128)(2,1)S(1)} %pad_maximum_fusion.3), channel_id=1, source_target_pairs={{0,16},{2,18},{4,20},{6,22},{8,24},{10,26},{12,28},{14,30},{16,0},... | collective-permute-start | bytes 589832 | tf_op jit(solution)/shard_map/ppermute | solution.py:285
  53.7 9.8 %collective-permute-start.22 = (bf16[128,768]{1,0:T(8,128)(2,1)S(1)}, bf16[128,768]{1,0:T(8,128)(2,1)S(1)}, u32[]{:S(2)}, u32[]{:S(2)}) collective-permute-start(bf16[128,768]{1,0:T(8,128)(2,1)S(1)} %pad_maximum_fusion.3), channel_id=1, source_target_pairs={{0,24},{2,26},{4,28},{6,30},{8,0},{10,2},{12,4},{14,6},{16,8},{18,... | collective-permute-start | bytes 589832 | tf_op jit(solution)/shard_map/ppermute | solution.py:285
  63.5 24.1 %collective-permute-start.23 = (bf16[512,768]{1,0:T(8,128)(2,1)S(1)}, bf16[512,768]{1,0:T(8,128)(2,1)S(1)}, u32[]{:S(2)}, u32[]{:S(2)}) collective-permute-start(bf16[512,768]{1,0:T(8,128)(2,1)S(1)} %constant_dynamic-update-slice_fusion.15.refs_2_), channel_id=1, source_target_pairs={{0,2},{2,0},{4,6},{6,4},{8,10},{10,8},{12,14},{14,12},{16,18},{18,... | collective-permute-start | bytes 2359304 | tf_op jit(solution)/shard_map/ppermute | solution.py:288
  70.2 7.6 %collective-permute-start.15 = (bf16[128,384]{1,0:T(8,128)(2,1)S(1)}, bf16[128,384]{1,0:T(8,128)(2,1)S(1)}, u32[]{:S(2)}, u32[]{:S(2)}) collective-permute-start(bf16[128,384]{1,0:T(8,128)(2,1)S(1)} %get-tuple-element.60), channel_id=1, source_target_pairs={{0,24},{2,26},{4,28},{6,30},{8,0},{10,2},{12,4},{14,6},{16,8},{18,... | collective-permute-start | bytes 294920 | tf_op jit(solution)/shard_map/ppermute | solution.py:285
  74.7 9.8 %collective-permute-start.16 = (bf16[128,384]{1,0:T(8,128)(2,1)S(1)}, bf16[128,384]{1,0:T(8,128)(2,1)S(1)}, u32[]{:S(2)}, u32[]{:S(2)}) collective-permute-start(bf16[128,384]{1,0:T(8,128)(2,1)S(1)} %get-tuple-element.61), channel_id=1, source_target_pairs={{0,16},{2,18},{4,20},{6,22},{8,24},{10,26},{12,28},{14,30},{16,0},... | collective-permute-start | bytes 294920 | tf_op jit(solution)/shard_map/ppermute | solution.py:285
  74.8 9.6 %collective-permute-start.17 = (bf16[128,384]{1,0:T(8,128)(2,1)S(1)}, bf16[128,384]{1,0:T(8,128)(2,1)S(1)}, u32[]{:S(2)}, u32[]{:S(2)}) collective-permute-start(bf16[128,384]{1,0:T(8,128)(2,1)S(1)} %get-tuple-element.62), channel_id=1, source_target_pairs={{0,8},{2,10},{4,12},{6,14},{8,16},{10,18},{12,20},{14,22},{16,24},... | collective-permute-start | bytes 294920 | tf_op jit(solution)/shard_map/ppermute | solution.py:285
  84.5 18.3 %copy-start.7 = (bf16[128,2560]{1,0:T(8,128)(2,1)S(1)}, bf16[128,2560]{1,0:T(8,128)(2,1)}, u32[]{:S(2)}) copy-start(bf16[128,2560]{1,0:T(8,128)(2,1)} %tokens.1) | copy-start | bytes 1966084
  86.0 16.8 %collective-permute-start.18 = (bf16[128,2560]{1,0:T(8,128)(2,1)S(1)}, bf16[128,2560]{1,0:T(8,128)(2,1)S(1)}, u32[]{:S(2)}, u32[]{:S(2)}) collective-permute-start(bf16[128,2560]{1,0:T(8,128)(2,1)S(1)} %away.1), channel_id=1, source_target_pairs={{0,1},{1,0},{2,3},{3,2},{4,5},{5,4},{6,7},{7,6},{8,9},{9,8},{10,11... | collective-permute-start | bytes 1966088 | tf_op jit(solution)/shard_map/ppermute | solution.py:343
  90.9 11.9 %collective-permute-start.24 = (bf16[128,768]{1,0:T(8,128)(2,1)S(1)}, bf16[128,768]{1,0:T(8,128)(2,1)S(1)}, u32[]{:S(2)}, u32[]{:S(2)}) collective-permute-start(bf16[128,768]{1,0:T(8,128)(2,1)S(1)} %get-tuple-element.69), channel_id=1, source_target_pairs={{0,4},{2,6},{4,0},{6,2},{8,12},{10,14},{12,8},{14,10},{16,20},{18,... | collective-permute-start | bytes 589832 | tf_op jit(solution)/shard_map/ppermute | solution.py:288
  (5 other events, 4.8 us)

commit v4 on v3

--- a/solution.py
+++ b/solution.py
@@ -19,6 +19,10 @@
 
 def anywhere():
     return pl.BlockSpec(memory_space=pl.ANY)
+
+
+def in_hbm():
+    return pl.BlockSpec(memory_space=pltpu.HBM)
 
 
 def limit(mebibytes):
@@ -69,67 +73,91 @@
         copy.wait()
 
 
-def pack(groups, members, chosen, q, k, v):
+def pack(name, out_shapes, sources, plan):
+    count = len(plan(0))
+
+    def kernel(*refs):
+        source_refs, outs, sems = refs[: len(sources)], refs[len(sources) : -1], refs[-1]
+        pairs = []
+        for i, at, width, o, row, column in plan(lax.axis_index("seq")):
+            rows = source_refs[i].shape[0]
+            if not isinstance(at, int):
+                at = pl.multiple_of(at, DH)
+            pairs.append(
+                (
+                    source_refs[i].at[:, pl.ds(at, width)],
+                    outs[o].at[row : row + rows, column : column + width],
+                )
+            )
+        copy_all(pairs, sems)
+
+    return list(
+        pl.pallas_call(
+            kernel,
+            out_shape=out_shapes,
+            in_specs=[in_hbm()] * len(sources),
+            out_specs=[anywhere()] * len(out_shapes),
+            scratch_shapes=[pltpu.SemaphoreType.DMA((count,))],
+            compiler_params=limit(1),
+            cost_estimate=cost(0, 4 * sum(math.prod(o.shape) for o in out_shapes)),
+            name=name,
+        )(*[pltpu.with_memory_space_constraint(x, pltpu.HBM) for x in sources])
+    )
+
+
+def pack_pairs(groups, members, chosen, k, v):
+    rows, columns = k.shape
+    width = columns // groups
+
+    def plan(seq):
+        return [
+            (i, lax.rem(seq // members + r, groups) * width + h * DH, DH, j * groups + r, 0, i * DH)
+            for j, h in enumerate(chosen)
+            for r in range(groups)
+            for i in range(2)
+        ]
+
+    outs = pack(
+        "pack_pairs_%d" % chosen[0],
+        [shape(rows, 2 * DH)] * (groups * len(chosen)),
+        [k, v],
+        plan,
+    )
+    return [outs[j * groups : (j + 1) * groups] for j in range(len(chosen))]
+
+
+def pack_queries(groups, members, q):
     rows, columns = q.shape
     width = columns // groups
-    count = groups * len(chosen)
-
-    def kernel(*refs):
-        sources, outs, sems = refs[:3], refs[3:-1], refs[-1]
-        zi = lax.axis_index("seq") // members
-        pairs = []
-        for j, h in enumerate(chosen):
-            for r in range(groups):
-                at = pl.ds(pl.multiple_of(lax.rem(zi + r, groups) * width + h * DH, DH), DH)
-                for i, source in enumerate(sources):
-                    target = outs[j * groups + r].at[:, i * DH : (i + 1) * DH]
-                    pairs.append((source.at[:, at], target))
-        copy_all(pairs, sems)
-
-    outs = pl.pallas_call(
-        kernel,
-        out_shape=[shape(rows, 3 * DH)] * count,
-        in_specs=[anywhere()] * 3,
-        out_specs=[anywhere()] * count,
-        scratch_shapes=[pltpu.SemaphoreType.DMA((3 * count,))],
-        compiler_params=limit(1),
-        cost_estimate=cost(0, 6 * count * rows * DH * 2),
-        name="pack_%d" % chosen[0],
-    )(q, k, v)
-    return [list(outs[j * groups : (j + 1) * groups]) for j in range(len(chosen))]
-
-
-def pack_cross(bit, q, k, v):
+
+    def plan(seq):
+        return [
+            (0, lax.rem(seq // members + r, groups) * width, width, r, 0, 0)
+            for r in range(groups)
+        ]
+
+    return pack("pack_queries", [shape(rows, width)] * groups, [q], plan)
+
+
+def pack_cross(bit, go, q, k, v):
     rows, columns = q.shape
     half = columns // 2
-    total = rows + 2 * k.shape[0]
-
-    def kernel(*refs):
-        sources, outs, sems = refs[:3], refs[3:5], refs[5]
-        xi = lax.rem(lax.axis_index("seq") // bit, 2)
-        pairs = []
-        for out, side in zip(outs, (xi, 1 - xi)):
-            at = pl.ds(pl.multiple_of(side * half, DH), half)
-            first = 0
-            for source in sources:
-                last = first + source.shape[0]
-                pairs.append((source.at[:, at], out.at[first:last, :]))
-                first = last
-        copy_all(pairs, sems)
-
-    return pl.pallas_call(
-        kernel,
-        out_shape=[shape(total, half)] * 2,
-        in_specs=[anywhere()] * 3,
-        out_specs=[anywhere()] * 2,
-        scratch_shapes=[pltpu.SemaphoreType.DMA((6,))],
-        compiler_params=limit(1),
-        cost_estimate=cost(0, 4 * total * columns),
-        name="pack_cross",
-    )(q, k, v)
-
-
-def attend(queries, pairs, earlier, factor, name):
+    more = k.shape[0]
+
+    def plan(seq):
+        xi = lax.rem(seq // bit, 2)
+        at = ((1 - xi) if go else xi) * half
+        return [
+            (0, at, half, 0, 0, 0),
+            (1, at, half, 0, rows, 0),
+            (2, at, half, 0, rows + more, 0),
+        ]
+
+    name = "pack_go" if go else "pack_stay"
+    return pack(name, [shape(rows + 2 * more, half)], [q, k, v], plan)[0]
+
+
+def attend(queries, pairs, earlier, head, factor):
     parts = len(queries)
     rows = queries[0].shape[0]
     before = earlier[0].shape[1] if earlier else 0
@@ -145,7 +173,7 @@
             if before:
                 outs[i][:, :before] = early[i][...]
             outs[i][:, before:] = softmax_mix(
-                query_refs[i][:, :DH], keys, values, factor
+                query_refs[i][:, head * DH : (head + 1) * DH], keys, values, factor
             ).astype(BF16)
 
     return pl.pallas_call(
@@ -157,7 +185,7 @@
         cost_estimate=cost(
             4 * parts * rows * total_keys * DH, total_keys * DH * 4, parts * rows * total_keys
         ),
-        name=name,
+        name="attend_%d" % head,
     )(*queries, *pairs, *earlier)
 
 
@@ -290,7 +318,7 @@
     def join(*xs):
         return xs[0] if len(xs) == 1 else jnp.concatenate(xs, axis=0)
 
-    if members != 4 or heads_here % 2 or tp_size != 2:
+    if (groups, members, tp_size) != (4, 4, 2):
         index_groups = [[g * members + m for m in range(members)] for g in range(groups)]
 
         def gather(x):
@@ -298,12 +326,13 @@
                 x, "seq", axis=0, tiled=True, axis_index_groups=index_groups
             )
 
-        pieces = pack(groups, members, range(heads), self_queries, self_keys, self_values)
+        pairs = pack_pairs(groups, members, range(heads), self_keys, self_values)
+        queries = pack_queries(groups, members, self_queries)
+        queries = [rotate(x, r) for r, x in enumerate(queries)]
         outs = []
         for h in range(heads):
-            here = [rotate(x, r) for r, x in enumerate(pieces[h])]
-            pair = gather(join(*[x[:, DH:] for x in here]))
-            outs = attend(here, [pair], outs, factor, "attend_%d" % h)
+            pair = gather(join(*[rotate(x, r) for r, x in enumerate(pairs[h])]))
+            outs = attend(queries, [pair], outs, h, factor)
         lhs = [rotate(x, groups - r) for r, x in enumerate(outs)]
         caption = join(caption_keys, caption_values)
         caption = gather(join(*[rotate(caption, r) for r in range(groups)]))
@@ -313,31 +342,41 @@
         updated = (tokens.astype(F32) + gate_vector[None, :] * projected).astype(BF16)
         return (updated, cross_heads)
 
-    pieces = pack(groups, members, [0], self_queries, self_keys, self_values)
-    pieces += pack(
-        groups, members, list(range(1, heads)), self_queries, self_keys, self_values
-    )
-    stay, go = pack_cross(bit, cross_queries, caption_keys, caption_values)
-    outs, arrived, far = [], [], []
-    for h in range(heads):
-        here = pieces[h]
-        if h >= 2:
-            here = here[:1] + [after(x, arrived[h - 2][1:]) for x in here[1:]]
+    pairs = pack_pairs(groups, members, [0], self_keys, self_values)
+    go = pack_cross(bit, True, cross_queries, caption_keys, caption_values)
+    pairs += pack_pairs(groups, members, list(range(1, heads)), self_keys, self_values)
+    queries = pack_queries(groups, members, self_queries)
+    stay = pack_cross(bit, False, cross_queries, caption_keys, caption_values)
+
+    come = swap(go, bit)
+    arrived, gathered = [], []
+    for h in range(heads + 1):
+        last = h == heads
+        here = queries if last else pairs[h]
+        if h:
+            here = here[:1] + after(here[1:], arrived[-1][1])
         here = [rotate(x, r) for r, x in enumerate(here)]
         arrived.append(here)
-        mine = join(*[x[:, DH:] for x in here])
-        far.append(swap(mine, 2))
-        half = join(mine, far[h])
-        outs = attend(here, [half, swap(half, 1)], outs, factor, "attend_%d" % h)
+        if not last:
+            mine = join(*here)
+            half = join(mine, swap(mine, 2))
+            gathered.append([half, swap(half, 1)])
+    outs = []
+    for h in range(heads):
+        outs = attend(arrived[-1], gathered[h], outs, h, factor)
     lhs = [rotate(x, groups - r) for r, x in enumerate(outs)]
 
-    come = swap(after(go, far[0]), bit)
-    caption = after(join(stay[rows:], come[rows:]), arrived[-1][1:])
-    caption = join(*[rotate(caption, r) for r in range(groups)])
-    captions = [caption, swap(caption, 1)]
+    caption = join(stay[rows:], come[rows:])
+    pair = join(caption, swap(after(caption, arrived[0][1:]), members))
+    inner = [(m + members * g, m + members * (3 - g)) for g in (1, 2) for m in range(members)]
+    outer = [(m + members * g, m + members * e) for g, e in ((1, 0), (2, 3)) for m in range(members)]
+    middle = lax.ppermute(after(pair, arrived[-1][1:]), "seq", inner)
+    ends = lax.ppermute(after(middle, outs), "seq", outer)
+    zi = lax.axis_index("seq") // members
+    other = jnp.where((zi == 1) | (zi == 2), middle, ends)
 
     away = project(members, tp_size, 1, lhs, out_weight, BF16, "away")
-    captions[0] = after(captions[0], away)
+    captions = [after(pair, away), swap(pair, 1), other, swap(other, 1)]
     own, theirs = cross([stay, come], captions, rows, cap_rows, factor)
     came = swap(theirs, bit)
     away = lax.ppermute(away, "tp", [(0, 1), (1, 0)])

time: 104 us -> 99.7 us (0.959)
  waiting for transfers between devices: 42.7 us -> 32.2 us
  starting transfers between devices: 35.6 us -> 41.1 us
  Pallas kernels: 14.9 us -> 19.2 us
  local copies, waits for them, and re-layouts: 9.74 us -> 5.63 us
    ppermute x9 -> x11, waiting for transfers between devices: 10.1 us -> 5.1 us  [swap(): return lax.ppermute(x, 'seq', [(s, s ^ by) for s in range(seq_size)])]
    pallas_call x3 -> x5, Pallas kernels: 0.79 us -> 5.14 us  [pack(): pl.pallas_call(kernel, out_shape=out_shapes, in_specs=[in_hbm()] * len(so...]
    ppermute x15, starting transfers between devices: 23.2 us -> 27.5 us  [rotate(): lax.ppermute(x, 'seq', [(s, (s + step) % seq_size) for s in range(seq_siz...]
    unnamed x27 -> x18, local copies, waits for them, and re-layouts: 9.52 us -> 5.55 us
    ppermute x1, waiting for transfers between devices: 8.24 us -> 4.37 us  [shards(): away = lax.ppermute(away, 'tp', [(0, 1), (1, 0)])]
    ppermute x0 -> x2, starting transfers between devices: none -> 1.97 us  [the longest x1 1.29 us: shards(): ends = lax.ppermute(after(middle, outs), 'seq', outer)]
    ppermute x15, waiting for transfers between devices: 24.4 us -> 22.7 us  [rotate(): lax.ppermute(x, 'seq', [(s, (s + step) % seq_size) for s in range(seq_siz...]
    ppermute x9 -> x11, starting transfers between devices: 10.8 us -> 10.1 us  [swap(): return lax.ppermute(x, 'seq', [(s, s ^ by) for s in range(seq_size)])]
  transfers between devices with their start and end apart: 25 -> 29, of which waited for: 10 -> 11; matrix products, arithmetic and copies ran while one was open for 0% -> 0% of each run, Pallas kernels for 13% -> 17%
where the time goes in v4:
time: 99.7 us; the launch traced here: 99.3 us
  starting transfers between devices  41.1 us (41%)
  waiting for transfers between devices  32.2 us (32%)
  Pallas kernels  19.2 us (19%)
  local copies, waits for them, and re-layouts  5.63 us (6%)
    ppermute x15, starting transfers between devices, rotate(): lax.ppermute(x, 'seq', [(s, (s + step) % seq_size) for s in range(seq_siz...  27.5 us
    ppermute x15, waiting for transfers between devices, rotate(): lax.ppermute(x, 'seq', [(s, (s + step) % seq_size) for s in range(seq_siz...  22.7 us
    ppermute x11, starting transfers between devices, swap(): return lax.ppermute(x, 'seq', [(s, s ^ by) for s in range(seq_size)])  10.1 us
    pallas_call x3, Pallas kernels, attend(): pl.pallas_call(kernel, out_shape=[shape(rows, before + DH)] * parts, in_s...  6.55 us
    unnamed x18, local copies, waits for them, and re-layouts  5.55 us
    pallas_call x5, Pallas kernels, pack(): pl.pallas_call(kernel, out_shape=out_shapes, in_specs=[in_hbm()] * len(so...  5.14 us
    ppermute x11, waiting for transfers between devices, swap(): return lax.ppermute(x, 'seq', [(s, s ^ by) for s in range(seq_size)])  5.1 us
    ppermute x1, waiting for transfers between devices, shards(): away = lax.ppermute(away, 'tp', [(0, 1), (1, 0)])  4.37 us
  transfers between devices with their start and end apart: 29, of which 11 were waited for; matrix products, arithmetic and copies ran while one was open for 0% of the time, Pallas kernels for 17%

profile of v4, /device:TPU:0, one launch (start us, length us, event | category | flops | bytes accessed | tf_op | source)
XLA Modules:
  0.0 99.3 jit_solution(14203041531254808604)
XLA Ops:
  1.6 3.1 %collective-permute-start = (bf16[128,256]{1,0:T(8,128)(2,1)S(1)}, bf16[128,256]{1,0:T(8,128)(2,1)S(1)}, u32[]{:S(2)}, u32[]{:S(2)}) collective-permute-start(bf16[128,256]{1,0:T(8,128)(2,1)S(1)} %get-tuple-element.55), channel_id=1, source_target_pairs={{0,8},{2,10},{4,12},{6,14},{8,16},{10,18},{12,20},{14,22},{16,24},... | collective-permute-start | bytes 196616 | tf_op jit(solution)/shard_map/ppermute | solution.py:313
  4.7 2.6 %collective-permute-start.14 = (bf16[128,256]{1,0:T(8,128)(2,1)S(1)}, bf16[128,256]{1,0:T(8,128)(2,1)S(1)}, u32[]{:S(2)}, u32[]{:S(2)}) collective-permute-start(bf16[128,256]{1,0:T(8,128)(2,1)S(1)} %get-tuple-element.68), channel_id=1, source_target_pairs={{0,16},{2,18},{4,20},{6,22},{8,24},{10,26},{12,28},{14,30},{16,0},... | collective-permute-start | bytes 196616 | tf_op jit(solution)/shard_map/ppermute | solution.py:313
  7.3 1.3 %collective-permute-start.15 = (bf16[128,256]{1,0:T(8,128)(2,1)S(1)}, bf16[128,256]{1,0:T(8,128)(2,1)S(1)}, u32[]{:S(2)}, u32[]{:S(2)}) collective-permute-start(bf16[128,256]{1,0:T(8,128)(2,1)S(1)} %get-tuple-element.69), channel_id=1, source_target_pairs={{0,24},{2,26},{4,28},{6,30},{8,0},{10,2},{12,4},{14,6},{16,8},{18,... | collective-permute-start | bytes 196616 | tf_op jit(solution)/shard_map/ppermute | solution.py:313
  9.6 1.6 %collective-permute-start.22 = (bf16[192,768]{1,0:T(8,128)(2,1)S(1)}, bf16[192,768]{1,0:T(8,128)(2,1)S(1)}, u32[]{:S(2)}, u32[]{:S(2)}) collective-permute-start(bf16[192,768]{1,0:T(8,128)(2,1)S(1)} %pack_go.1), channel_id=1, source_target_pairs={{0,4},{2,6},{4,0},{6,2},{8,12},{10,14},{12,8},{14,10},{16,20},{18,... | collective-permute-start | bytes 884744 | tf_op jit(solution)/shard_map/ppermute | solution.py:316
  11.1 1.1 %pack_pairs_1.1 = (bf16[128,256]{1,0:T(8,128)(2,1)S(1)}, bf16[128,256]{1,0:T(8,128)(2,1)S(1)}, bf16[128,256]{1,0:T(8,128)(2,1)S(1)}, bf16[128,256]{1,0:T(8,128)(...) custom-call(bf16[128,1536]{1,0:T(8,128)(2,1)} %refs_0_.7, ...), custom_call_target="tpu_custom_call" | custom-call | bytes 1048576 | tf_op jit(solution)/shard_map/pack_pairs_1/pallas_call | solution.py:95
  13.3 1.1 %pack_queries.1 = (bf16[128,384]{1,0:T(8,128)(2,1)S(1)}, bf16[128,384]{1,0:T(8,128)(2,1)S(1)}, bf16[128,384]{1,0:T(8,128)(2,1)S(1)}, bf16[128,384]{1,0:T(8,128)(2,1)S(1)}) custom-call(bf16[128,1536]{1,0:T(8,128)(2,1)} %refs_0_.5), custom_call_target="tpu_custom_call" | custom-call | bytes 786432 | tf_op jit(solution)/shard_map/pack_queries/pallas_call | solution.py:95
  16.2 2.8 %collective-permute-start.11 = (bf16[128,256]{1,0:T(8,128)(2,1)S(1)}, bf16[128,256]{1,0:T(8,128)(2,1)S(1)}, u32[]{:S(2)}, u32[]{:S(2)}) collective-permute-start(bf16[128,256]{1,0:T(8,128)(2,1)S(1)} %get-tuple-element.66), channel_id=1, source_target_pairs={{0,24},{2,26},{4,28},{6,30},{8,0},{10,2},{12,4},{14,6},{16,8},{18,... | collective-permute-start | bytes 196616 | tf_op jit(solution)/shard_map/ppermute | solution.py:313
  19.0 1.7 %collective-permute-done.1 = bf16[128,256]{1,0:T(8,128)(2,1)S(1)} collective-permute-done((bf16[128,256]{1,0:T(8,128)(2,1)S(1)}, bf16[128,256]{1,0:T(8,128)(2,1)S(1)}, u32[]{:S(2)}, u32[]{:S(2)}) %collective-permute-start.1) | collective-permute-done | bytes 65568 | tf_op jit(solution)/shard_map/ppermute | solution.py:313
  20.7 1.8 %collective-permute-done.10 = bf16[128,256]{1,0:T(8,128)(2,1)S(1)} collective-permute-done((bf16[128,256]{1,0:T(8,128)(2,1)S(1)}, bf16[128,256]{1,0:T(8,128)(2,1)S(1)}, u32[]{:S(2)}, u32[]{:S(2)}) %collective-permute-start.10) | collective-permute-done | bytes 65568 | tf_op jit(solution)/shard_map/ppermute | solution.py:313
  22.5 3.4 %collective-permute-start.7 = (bf16[128,256]{1,0:T(8,128)(2,1)S(1)}, bf16[128,256]{1,0:T(8,128)(2,1)S(1)}, u32[]{:S(2)}, u32[]{:S(2)}) collective-permute-start(bf16[128,256]{1,0:T(8,128)(2,1)S(1)} %get-tuple-element.63), channel_id=1, source_target_pairs={{0,24},{2,26},{4,28},{6,30},{8,0},{10,2},{12,4},{14,6},{16,8},{18,... | collective-permute-start | bytes 196616 | tf_op jit(solution)/shard_map/ppermute | solution.py:313
  26.7 1.3 %collective-permute-start.12 = (bf16[512,256]{1,0:T(8,128)(2,1)S(1)}, bf16[512,256]{1,0:T(8,128)(2,1)S(1)}, u32[]{:S(2)}, u32[]{:S(2)}) collective-permute-start(bf16[512,256]{1,0:T(8,128)(2,1)S(1)} %pad_maximum_fusion.2), channel_id=1, source_target_pairs={{0,4},{2,6},{4,0},{6,2},{8,12},{10,14},{12,8},{14,10},{16,20},{18,... | collective-permute-start | bytes 786440 | tf_op jit(solution)/shard_map/ppermute | solution.py:316
  29.2 3.4 %collective-permute-start.8 = (bf16[512,256]{1,0:T(8,128)(2,1)S(1)}, bf16[512,256]{1,0:T(8,128)(2,1)S(1)}, u32[]{:S(2)}, u32[]{:S(2)}) collective-permute-start(bf16[512,256]{1,0:T(8,128)(2,1)S(1)} %pad_maximum_fusion.1), channel_id=1, source_target_pairs={{0,4},{2,6},{4,0},{6,2},{8,12},{10,14},{12,8},{14,10},{16,20},{18,... | collective-permute-start | bytes 786440 | tf_op jit(solution)/shard_map/ppermute | solution.py:316
  34.4 2.7 %collective-permute-done.8 = bf16[512,256]{1,0:T(8,128)(2,1)S(1)} collective-permute-done((bf16[512,256]{1,0:T(8,128)(2,1)S(1)}, bf16[512,256]{1,0:T(8,128)(2,1)S(1)}, u32[]{:S(2)}, u32[]{:S(2)}) %collective-permute-start.8) | collective-permute-done | bytes 262176 | tf_op jit(solution)/shard_map/ppermute | solution.py:316
  37.2 1.2 %collective-permute-start.4 = (bf16[128,384]{1,0:T(8,128)(2,1)S(1)}, bf16[128,384]{1,0:T(8,128)(2,1)S(1)}, u32[]{:S(2)}, u32[]{:S(2)}) collective-permute-start(bf16[128,384]{1,0:T(8,128)(2,1)S(1)} %get-tuple-element.59), channel_id=1, source_target_pairs={{0,16},{2,18},{4,20},{6,22},{8,24},{10,26},{12,28},{14,30},{16,0},... | collective-permute-start | bytes 294920 | tf_op jit(solution)/shard_map/ppermute | solution.py:313
  38.4 2.3 %collective-permute-start.5 = (bf16[128,384]{1,0:T(8,128)(2,1)S(1)}, bf16[128,384]{1,0:T(8,128)(2,1)S(1)}, u32[]{:S(2)}, u32[]{:S(2)}) collective-permute-start(bf16[128,384]{1,0:T(8,128)(2,1)S(1)} %get-tuple-element.60), channel_id=1, source_target_pairs={{0,24},{2,26},{4,28},{6,30},{8,0},{10,2},{12,4},{14,6},{16,8},{18,... | collective-permute-start | bytes 294920 | tf_op jit(solution)/shard_map/ppermute | solution.py:313
  40.8 5.1 %collective-permute-done.4.refs_2_ = bf16[128,384]{1,0:T(8,128)(2,1)S(1)} collective-permute-done((bf16[128,384]{1,0:T(8,128)(2,1)S(1)}, bf16[128,384]{1,0:T(8,128)(2,1)S(1)}, u32[]{:S(2)}, u32[]{:S(2)}) %collective-permute-start.4) | collective-permute-done | bytes 98336 | tf_op jit(solution)/shard_map/ppermute | solution.py:313
  46.6 2.2 %attend_0.1 = (bf16[128,128]{1,0:T(8,128)(2,1)S(1)}, bf16[128,128]{1,0:T(8,128)(2,1)S(1)}, bf16[128,128]{1,0:T(8,128)(2,1)S(1)}, bf16[128,128]{1,0:T(8,128)(2,1)S(1)}) custom-call(bf16[128,384]{1,0:T(8,128)(2,1)S(1)} %get-tuple-element.45.refs_0_, bf16[128,384]{1,0:T(8,128)(2,1)S(1)} %collective-permute-done.3.refs_1_, ...), custom_call_target="tpu_custom_call" | custom-call | flops 536870912 | bytes 1048576 | tf_op jit(solution)/shard_map/attend_0/pallas_call | solution.py:179
  48.8 2.2 %attend_1.1 = (bf16[128,256]{1,0:T(8,128)(2,1)S(1)}, bf16[128,256]{1,0:T(8,128)(2,1)S(1)}, bf16[128,256]{1,0:T(8,128)(2,1)S(1)}, bf16[128,256]{1,0:T(8,128)(2,1)S(1)}) custom-call(bf16[128,384]{1,0:T(8,128)(2,1)S(1)} %get-tuple-element.45.refs_0_, bf16[128,384]{1,0:T(8,128)(2,1)S(1)} %collective-permute-done.3.refs_1_, ...), custom_call_target="tpu_custom_call" | custom-call | flops 536870912 | bytes 1048576 | tf_op jit(solution)/shard_map/attend_1/pallas_call | solution.py:179
  51.0 2.2 %attend_2.1 = (bf16[128,384]{1,0:T(8,128)(2,1)S(1)}, bf16[128,384]{1,0:T(8,128)(2,1)S(1)}, bf16[128,384]{1,0:T(8,128)(2,1)S(1)}, bf16[128,384]{1,0:T(8,128)(2,1)S(1)}) custom-call(bf16[128,384]{1,0:T(8,128)(2,1)S(1)} %get-tuple-element.45.refs_0_, bf16[128,384]{1,0:T(8,128)(2,1)S(1)} %collective-permute-done.3.refs_1_, ...), custom_call_target="tpu_custom_call" | custom-call | flops 536870912 | bytes 1048576 | tf_op jit(solution)/shard_map/attend_2/pallas_call | solution.py:179
  53.2 1.3 %collective-permute-start.26 = (bf16[256,768]{1,0:T(8,128)(2,1)S(1)}, bf16[256,768]{1,0:T(8,128)(2,1)S(1)}, u32[]{:S(2)}, u32[]{:S(2)}) collective-permute-start(bf16[256,768]{1,0:T(8,128)(2,1)S(1)} %collective-permute-done.25), channel_id=1, source_target_pairs={{8,0},{10,2},{12,4},{14,6},{16,24},{18,26},{20,28},{22,30},{9,1},{... | collective-permute-start | bytes 1179656 | tf_op jit(solution)/shard_map/ppermute | solution.py:374
  54.5 3.6 %collective-permute-start.18 = (bf16[128,384]{1,0:T(8,128)(2,1)S(1)}, bf16[128,384]{1,0:T(8,128)(2,1)S(1)}, u32[]{:S(2)}, u32[]{:S(2)}) collective-permute-start(bf16[128,384]{1,0:T(8,128)(2,1)S(1)} %get-tuple-element.79), channel_id=1, source_target_pairs={{0,24},{2,26},{4,28},{6,30},{8,0},{10,2},{12,4},{14,6},{16,8},{18,... | collective-permute-start | bytes 294920 | tf_op jit(solution)/shard_map/ppermute | solution.py:313
  58.1 5.4 %collective-permute-start.19 = (bf16[128,384]{1,0:T(8,128)(2,1)S(1)}, bf16[128,384]{1,0:T(8,128)(2,1)S(1)}, u32[]{:S(2)}, u32[]{:S(2)}) collective-permute-start(bf16[128,384]{1,0:T(8,128)(2,1)S(1)} %get-tuple-element.80), channel_id=1, source_target_pairs={{0,16},{2,18},{4,20},{6,22},{8,24},{10,26},{12,28},{14,30},{16,0},... | collective-permute-start | bytes 294920 | tf_op jit(solution)/shard_map/ppermute | solution.py:313
  63.8 12.5 %collective-permute-done.18.refs_1_ = bf16[128,384]{1,0:T(8,128)(2,1)S(1)} collective-permute-done((bf16[128,384]{1,0:T(8,128)(2,1)S(1)}, bf16[128,384]{1,0:T(8,128)(2,1)S(1)}, u32[]{:S(2)}, u32[]{:S(2)}) %collective-permute-start.18) | collective-permute-done | bytes 98336 | tf_op jit(solution)/shard_map/ppermute | solution.py:313
  76.3 5.5 %copy-done = bf16[1536,5120]{1,0:T(8,128)(2,1)S(1)} copy-done((bf16[1536,5120]{1,0:T(8,128)(2,1)S(1)}, bf16[1536,5120]{1,0:T(8,128)(2,1)}, u32[]{:S(2)}) %copy-start) | copy-done | bytes 15728664
  81.7 1.5 %away.1 = bf16[128,2560]{1,0:T(8,128)(2,1)S(1)} custom-call(bf16[128,384]{1,0:T(8,128)(2,1)S(1)} %get-tuple-element.78.refs_0_, bf16[128,384]{1,0:T(8,128)(2,1)S(1)} %collective-permute-done.18.refs_1_, bf16[128,384]{1,0:T(8,128)(2,1)S(1)} %collective-permute-done.19.refs_2_, bf16[128,384]{1,0:T(8,128)(2,1)S(1)} %collective-permute-done.20.refs_3_, ...), custom_call_target="tpu_custom_call" | custom-call | flops 1006632960 | bytes 9175040 | tf_op jit(solution)/shard_map/away/pallas_call | solution.py:254
  83.3 1.6 %collective-permute-start.21 = (bf16[128,2560]{1,0:T(8,128)(2,1)S(1)}, bf16[128,2560]{1,0:T(8,128)(2,1)S(1)}, u32[]{:S(2)}, u32[]{:S(2)}) collective-permute-start(bf16[128,2560]{1,0:T(8,128)(2,1)S(1)} %away.1), channel_id=1, source_target_pairs={{0,1},{1,0},{2,3},{3,2},{4,5},{5,4},{6,7},{7,6},{8,9},{9,8},{10,11... | collective-permute-start | bytes 1966088 | tf_op jit(solution)/shard_map/ppermute | solution.py:382
  85.0 1.7 %collective-permute-done.27.refs_5_ = bf16[256,768]{1,0:T(8,128)(2,1)S(1)} collective-permute-done((bf16[256,768]{1,0:T(8,128)(2,1)S(1)}, bf16[256,768]{1,0:T(8,128)(2,1)S(1)}, u32[]{:S(2)}, u32[]{:S(2)}) %collective-permute-start.27) | collective-permute-done | bytes 393248 | tf_op jit(solution)/shard_map/ppermute | solution.py:316
  86.7 3.3 %cross.1 = (bf16[128,768]{1,0:T(8,128)(2,1)S(1)}, bf16[128,768]{1,0:T(8,128)(2,1)S(1)}) custom-call(bf16[192,768]{1,0:T(8,128)(2,1)S(1)} %pack_stay.1.refs_0_, bf16[192,768]{1,0:T(8,128)(2,1)S(1)} %collective-permute-done.22.refs_1_, bf16[256,768]{1,0:T(8,128)(2,1)S(1)} %pad_maximum_fusion.refs_2_, bf16[256,768]{1,0:T(8,128)(2,1)S(1)} %collective-permute-done.24.refs_3_, ...), custom_call_target="tpu_custom_call" | custom-call | flops 402653184 | bytes 2359296 | tf_op jit(solution)/shard_map/cross/pallas_call | solution.py:217
  90.0 2.2 %collective-permute-start.28 = (bf16[128,768]{1,0:T(8,128)(2,1)S(1)}, bf16[128,768]{1,0:T(8,128)(2,1)S(1)}, u32[]{:S(2)}, u32[]{:S(2)}) collective-permute-start(bf16[128,768]{1,0:T(8,128)(2,1)S(1)} %get-tuple-element.87), channel_id=1, source_target_pairs={{0,4},{2,6},{4,0},{6,2},{8,12},{10,14},{12,8},{14,10},{16,20},{18,... | collective-permute-start | bytes 589832 | tf_op jit(solution)/shard_map/ppermute | solution.py:316
  92.2 1.5 %home.1 = f32[128,2560]{1,0:T(8,128)S(1)} custom-call(bf16[128,384]{1,0:T(8,128)(2,1)S(1)} %get-tuple-element.78.refs_0_, bf16[128,384]{1,0:T(8,128)(2,1)S(1)} %collective-permute-done.18.refs_1_, bf16[128,384]{1,0:T(8,128)(2,1)S(1)} %collective-permute-done.19.refs_2_, bf16[128,384]{1,0:T(8,128)(2,1)S(1)} %collective-permute-done.20.refs_3_, ...), custom_call_target="tpu_custom_call" | custom-call | flops 1006632960 | bytes 9175040 | tf_op jit(solution)/shard_map/home/pallas_call | solution.py:254
  93.7 4.4 %collective-permute-done.21.away = bf16[128,2560]{1,0:T(8,128)(2,1)S(1)} collective-permute-done((bf16[128,2560]{1,0:T(8,128)(2,1)S(1)}, bf16[128,2560]{1,0:T(8,128)(2,1)S(1)}, u32[]{:S(2)}, u32[]{:S(2)}) %collective-permute-start.21) | collective-permute-done | bytes 655392 | tf_op jit(solution)/shard_map/ppermute | solution.py:382
  98.1 1.2 %finish.1 = (bf16[128,2560]{1,0:T(8,128)(2,1)}, bf16[128,1536]{1,0:T(8,128)(2,1)}) custom-call(bf16[128,2560]{1,0:T(8,128)(2,1)S(1)} %copy-done.1, f32[1,2560]{1,0:T(1,128)S(1)} %broadcast_in_dim.3.gate, f32[128,2560]{1,0:T(8,128)S(1)} %home.1, bf16[128,2560]{1,0:T(8,128)(2,1)S(1)} %collective-permute-done.21.away, ...), custom_call_target="tpu_custom_call" | custom-call | bytes 3276800 | tf_op jit(solution)/shard_map/finish/pallas_call | solution.py:276
  (68 shorter events, 9.7 us)
Async XLA Ops:
  1.6 12.8 %collective-permute-start = (bf16[128,256]{1,0:T(8,128)(2,1)S(1)}, bf16[128,256]{1,0:T(8,128)(2,1)S(1)}, u32[]{:S(2)}, u32[]{:S(2)}) collective-permute-start(bf16[128,256]{1,0:T(8,128)(2,1)S(1)} %get-tuple-element.55), channel_id=1, source_target_pairs={{0,8},{2,10},{4,12},{6,14},{8,16},{10,18},{12,20},{14,22},{16,24},... | collective-permute-start | bytes 196616 | tf_op jit(solution)/shard_map/ppermute | solution.py:313
  4.7 10.5 %collective-permute-start.14 = (bf16[128,256]{1,0:T(8,128)(2,1)S(1)}, bf16[128,256]{1,0:T(8,128)(2,1)S(1)}, u32[]{:S(2)}, u32[]{:S(2)}) collective-permute-start(bf16[128,256]{1,0:T(8,128)(2,1)S(1)} %get-tuple-element.68), channel_id=1, source_target_pairs={{0,16},{2,18},{4,20},{6,22},{8,24},{10,26},{12,28},{14,30},{16,0},... | collective-permute-start | bytes 196616 | tf_op jit(solution)/shard_map/ppermute | solution.py:313
  7.3 7.9 %collective-permute-start.15 = (bf16[128,256]{1,0:T(8,128)(2,1)S(1)}, bf16[128,256]{1,0:T(8,128)(2,1)S(1)}, u32[]{:S(2)}, u32[]{:S(2)}) collective-permute-start(bf16[128,256]{1,0:T(8,128)(2,1)S(1)} %get-tuple-element.69), channel_id=1, source_target_pairs={{0,24},{2,26},{4,28},{6,30},{8,0},{10,2},{12,4},{14,6},{16,8},{18,... | collective-permute-start | bytes 196616 | tf_op jit(solution)/shard_map/ppermute | solution.py:313
  9.6 23.0 %collective-permute-start.22 = (bf16[192,768]{1,0:T(8,128)(2,1)S(1)}, bf16[192,768]{1,0:T(8,128)(2,1)S(1)}, u32[]{:S(2)}, u32[]{:S(2)}) collective-permute-start(bf16[192,768]{1,0:T(8,128)(2,1)S(1)} %pack_go.1), channel_id=1, source_target_pairs={{0,4},{2,6},{4,0},{6,2},{8,12},{10,14},{12,8},{14,10},{16,20},{18,... | collective-permute-start | bytes 884744 | tf_op jit(solution)/shard_map/ppermute | solution.py:316
  14.5 6.2 %collective-permute-start.1 = (bf16[128,256]{1,0:T(8,128)(2,1)S(1)}, bf16[128,256]{1,0:T(8,128)(2,1)S(1)}, u32[]{:S(2)}, u32[]{:S(2)}) collective-permute-start(bf16[128,256]{1,0:T(8,128)(2,1)S(1)} %get-tuple-element.56), channel_id=1, source_target_pairs={{0,8},{2,10},{4,12},{6,14},{8,16},{10,18},{12,20},{14,22},{16,24},... | collective-permute-start | bytes 196616 | tf_op jit(solution)/shard_map/ppermute | solution.py:313
  15.2 76.9 %copy-start.2 = (f32[2560]{0:T(1024)S(1)}, f32[2560]{0:T(1024)}, u32[]{:S(2)}) copy-start(f32[2560]{0:T(1024)} %param.17) | copy-start | bytes 30724
  15.2 18.3 %collective-permute-start.16 = (bf16[512,256]{1,0:T(8,128)(2,1)S(1)}, bf16[512,256]{1,0:T(8,128)(2,1)S(1)}, u32[]{:S(2)}, u32[]{:S(2)}) collective-permute-start(bf16[512,256]{1,0:T(8,128)(2,1)S(1)} %pad_maximum_fusion.3), channel_id=1, source_target_pairs={{0,4},{2,6},{4,0},{6,2},{8,12},{10,14},{12,8},{14,10},{16,20},{18,... | collective-permute-start | bytes 786440 | tf_op jit(solution)/shard_map/ppermute | solution.py:316
  15.8 6.7 %collective-permute-start.10 = (bf16[128,256]{1,0:T(8,128)(2,1)S(1)}, bf16[128,256]{1,0:T(8,128)(2,1)S(1)}, u32[]{:S(2)}, u32[]{:S(2)}) collective-permute-start(bf16[128,256]{1,0:T(8,128)(2,1)S(1)} %get-tuple-element.65), channel_id=1, source_target_pairs={{0,16},{2,18},{4,20},{6,22},{8,24},{10,26},{12,28},{14,30},{16,0},... | collective-permute-start | bytes 196616 | tf_op jit(solution)/shard_map/ppermute | solution.py:313
  16.2 6.3 %collective-permute-start.11 = (bf16[128,256]{1,0:T(8,128)(2,1)S(1)}, bf16[128,256]{1,0:T(8,128)(2,1)S(1)}, u32[]{:S(2)}, u32[]{:S(2)}) collective-permute-start(bf16[128,256]{1,0:T(8,128)(2,1)S(1)} %get-tuple-element.66), channel_id=1, source_target_pairs={{0,24},{2,26},{4,28},{6,30},{8,0},{10,2},{12,4},{14,6},{16,8},{18,... | collective-permute-start | bytes 196616 | tf_op jit(solution)/shard_map/ppermute | solution.py:313
  20.7 6.1 %collective-permute-start.2 = (bf16[128,256]{1,0:T(8,128)(2,1)S(1)}, bf16[128,256]{1,0:T(8,128)(2,1)S(1)}, u32[]{:S(2)}, u32[]{:S(2)}) collective-permute-start(bf16[128,256]{1,0:T(8,128)(2,1)S(1)} %get-tuple-element.57), channel_id=1, source_target_pairs={{0,8},{2,10},{4,12},{6,14},{8,16},{10,18},{12,20},{14,22},{16,24},... | collective-permute-start | bytes 196616 | tf_op jit(solution)/shard_map/ppermute | solution.py:313
  22.5 6.0 %collective-permute-start.6 = (bf16[128,256]{1,0:T(8,128)(2,1)S(1)}, bf16[128,256]{1,0:T(8,128)(2,1)S(1)}, u32[]{:S(2)}, u32[]{:S(2)}) collective-permute-start(bf16[128,256]{1,0:T(8,128)(2,1)S(1)} %get-tuple-element.62), channel_id=1, source_target_pairs={{0,16},{2,18},{4,20},{6,22},{8,24},{10,26},{12,28},{14,30},{16,0},... | collective-permute-start | bytes 196616 | tf_op jit(solution)/shard_map/ppermute | solution.py:313
  22.5 6.7 %collective-permute-start.7 = (bf16[128,256]{1,0:T(8,128)(2,1)S(1)}, bf16[128,256]{1,0:T(8,128)(2,1)S(1)}, u32[]{:S(2)}, u32[]{:S(2)}) collective-permute-start(bf16[128,256]{1,0:T(8,128)(2,1)S(1)} %get-tuple-element.63), channel_id=1, source_target_pairs={{0,24},{2,26},{4,28},{6,30},{8,0},{10,2},{12,4},{14,6},{16,8},{18,... | collective-permute-start | bytes 196616 | tf_op jit(solution)/shard_map/ppermute | solution.py:313
  26.7 7.5 %collective-permute-start.12 = (bf16[512,256]{1,0:T(8,128)(2,1)S(1)}, bf16[512,256]{1,0:T(8,128)(2,1)S(1)}, u32[]{:S(2)}, u32[]{:S(2)}) collective-permute-start(bf16[512,256]{1,0:T(8,128)(2,1)S(1)} %pad_maximum_fusion.2), channel_id=1, source_target_pairs={{0,4},{2,6},{4,0},{6,2},{8,12},{10,14},{12,8},{14,10},{16,20},{18,... | collective-permute-start | bytes 786440 | tf_op jit(solution)/shard_map/ppermute | solution.py:316
  28.5 8.7 %collective-permute-start.3 = (bf16[128,384]{1,0:T(8,128)(2,1)S(1)}, bf16[128,384]{1,0:T(8,128)(2,1)S(1)}, u32[]{:S(2)}, u32[]{:S(2)}) collective-permute-start(bf16[128,384]{1,0:T(8,128)(2,1)S(1)} %get-tuple-element.58), channel_id=1, source_target_pairs={{0,8},{2,10},{4,12},{6,14},{8,16},{10,18},{12,20},{14,22},{16,24},... | collective-permute-start | bytes 294920 | tf_op jit(solution)/shard_map/ppermute | solution.py:313
  29.2 7.9 %collective-permute-start.8 = (bf16[512,256]{1,0:T(8,128)(2,1)S(1)}, bf16[512,256]{1,0:T(8,128)(2,1)S(1)}, u32[]{:S(2)}, u32[]{:S(2)}) collective-permute-start(bf16[512,256]{1,0:T(8,128)(2,1)S(1)} %pad_maximum_fusion.1), channel_id=1, source_target_pairs={{0,4},{2,6},{4,0},{6,2},{8,12},{10,14},{12,8},{14,10},{16,20},{18,... | collective-permute-start | bytes 786440 | tf_op jit(solution)/shard_map/ppermute | solution.py:316
  32.6 5.8 %collective-permute-start.23 = (bf16[128,768]{1,0:T(8,128)(2,1)S(1)}, bf16[128,768]{1,0:T(8,128)(2,1)S(1)}, u32[]{:S(2)}, u32[]{:S(2)}) collective-permute-start(bf16[128,768]{1,0:T(8,128)(2,1)S(1)} %pad_maximum_fusion.4), channel_id=1, source_target_pairs={{0,8},{2,10},{4,12},{6,14},{8,0},{10,2},{12,4},{14,6},{16,24},{18,... | collective-permute-start | bytes 589832 | tf_op jit(solution)/shard_map/ppermute | solution.py:316
  33.5 13.0 %collective-permute-start.17 = (bf16[1024,256]{1,0:T(8,128)(2,1)S(1)}, bf16[1024,256]{1,0:T(8,128)(2,1)S(1)}, u32[]{:S(2)}, u32[]{:S(2)}) collective-permute-start(bf16[1024,256]{1,0:T(8,128)(2,1)S(1)} %constant_dynamic-update-slice_fusion.10.refs_4_), channel_id=1, source_target_pairs={{0,2},{2,0},{4,6},{6,4},{8,10},{10,8},{12,14},{14,12},{16,18},{18,... | collective-permute-start | bytes 1572872 | tf_op jit(solution)/shard_map/ppermute | solution.py:316
  34.3 14.5 %collective-permute-start.13 = (bf16[1024,256]{1,0:T(8,128)(2,1)S(1)}, bf16[1024,256]{1,0:T(8,128)(2,1)S(1)}, u32[]{:S(2)}, u32[]{:S(2)}) collective-permute-start(bf16[1024,256]{1,0:T(8,128)(2,1)S(1)} %constant_dynamic-update-slice_fusion.5.refs_4_), channel_id=1, source_target_pairs={{0,2},{2,0},{4,6},{6,4},{8,10},{10,8},{12,14},{14,12},{16,18},{18,... | collective-permute-start | bytes 1572872 | tf_op jit(solution)/shard_map/ppermute | solution.py:316
  37.1 13.8 %collective-permute-start.9 = (bf16[1024,256]{1,0:T(8,128)(2,1)S(1)}, bf16[1024,256]{1,0:T(8,128)(2,1)S(1)}, u32[]{:S(2)}, u32[]{:S(2)}) collective-permute-start(bf16[1024,256]{1,0:T(8,128)(2,1)S(1)} %constant_dynamic-update-slice_fusion.refs_4_), channel_id=1, source_target_pairs={{0,2},{2,0},{4,6},{6,4},{8,10},{10,8},{12,14},{14,12},{16,18},{18,... | collective-permute-start | bytes 1572872 | tf_op jit(solution)/shard_map/ppermute | solution.py:316
  37.2 8.7 %collective-permute-start.4 = (bf16[128,384]{1,0:T(8,128)(2,1)S(1)}, bf16[128,384]{1,0:T(8,128)(2,1)S(1)}, u32[]{:S(2)}, u32[]{:S(2)}) collective-permute-start(bf16[128,384]{1,0:T(8,128)(2,1)S(1)} %get-tuple-element.59), channel_id=1, source_target_pairs={{0,16},{2,18},{4,20},{6,22},{8,24},{10,26},{12,28},{14,30},{16,0},... | collective-permute-start | bytes 294920 | tf_op jit(solution)/shard_map/ppermute | solution.py:313
  38.4 7.4 %collective-permute-start.5 = (bf16[128,384]{1,0:T(8,128)(2,1)S(1)}, bf16[128,384]{1,0:T(8,128)(2,1)S(1)}, u32[]{:S(2)}, u32[]{:S(2)}) collective-permute-start(bf16[128,384]{1,0:T(8,128)(2,1)S(1)} %get-tuple-element.60), channel_id=1, source_target_pairs={{0,24},{2,26},{4,28},{6,30},{8,0},{10,2},{12,4},{14,6},{16,8},{18,... | collective-permute-start | bytes 294920 | tf_op jit(solution)/shard_map/ppermute | solution.py:313
  45.9 7.3 %collective-permute-start.25 = (bf16[256,768]{1,0:T(8,128)(2,1)S(1)}, bf16[256,768]{1,0:T(8,128)(2,1)S(1)}, u32[]{:S(2)}, u32[]{:S(2)}) collective-permute-start(bf16[256,768]{1,0:T(8,128)(2,1)S(1)} %pad_maximum_fusion.refs_2_), channel_id=1, source_target_pairs={{8,16},{10,18},{12,20},{14,22},{16,8},{18,10},{20,12},{22,14},{9,1... | collective-permute-start | bytes 1179656 | tf_op jit(solution)/shard_map/ppermute | solution.py:373
  53.2 31.7 %collective-permute-start.26 = (bf16[256,768]{1,0:T(8,128)(2,1)S(1)}, bf16[256,768]{1,0:T(8,128)(2,1)S(1)}, u32[]{:S(2)}, u32[]{:S(2)}) collective-permute-start(bf16[256,768]{1,0:T(8,128)(2,1)S(1)} %collective-permute-done.25), channel_id=1, source_target_pairs={{8,0},{10,2},{12,4},{14,6},{16,24},{18,26},{20,28},{22,30},{9,1},{... | collective-permute-start | bytes 1179656 | tf_op jit(solution)/shard_map/ppermute | solution.py:374
  54.5 21.8 %collective-permute-start.18 = (bf16[128,384]{1,0:T(8,128)(2,1)S(1)}, bf16[128,384]{1,0:T(8,128)(2,1)S(1)}, u32[]{:S(2)}, u32[]{:S(2)}) collective-permute-start(bf16[128,384]{1,0:T(8,128)(2,1)S(1)} %get-tuple-element.79), channel_id=1, source_target_pairs={{0,24},{2,26},{4,28},{6,30},{8,0},{10,2},{12,4},{14,6},{16,8},{18,... | collective-permute-start | bytes 294920 | tf_op jit(solution)/shard_map/ppermute | solution.py:313
  58.1 18.1 %collective-permute-start.19 = (bf16[128,384]{1,0:T(8,128)(2,1)S(1)}, bf16[128,384]{1,0:T(8,128)(2,1)S(1)}, u32[]{:S(2)}, u32[]{:S(2)}) collective-permute-start(bf16[128,384]{1,0:T(8,128)(2,1)S(1)} %get-tuple-element.80), channel_id=1, source_target_pairs={{0,16},{2,18},{4,20},{6,22},{8,24},{10,26},{12,28},{14,30},{16,0},... | collective-permute-start | bytes 294920 | tf_op jit(solution)/shard_map/ppermute | solution.py:313
  63.5 12.8 %collective-permute-start.20 = (bf16[128,384]{1,0:T(8,128)(2,1)S(1)}, bf16[128,384]{1,0:T(8,128)(2,1)S(1)}, u32[]{:S(2)}, u32[]{:S(2)}) collective-permute-start(bf16[128,384]{1,0:T(8,128)(2,1)S(1)} %get-tuple-element.81), channel_id=1, source_target_pairs={{0,8},{2,10},{4,12},{6,14},{8,16},{10,18},{12,20},{14,22},{16,24},... | collective-permute-start | bytes 294920 | tf_op jit(solution)/shard_map/ppermute | solution.py:313
  63.8 21.2 %collective-permute-start.24 = (bf16[256,768]{1,0:T(8,128)(2,1)S(1)}, bf16[256,768]{1,0:T(8,128)(2,1)S(1)}, u32[]{:S(2)}, u32[]{:S(2)}) collective-permute-start(bf16[256,768]{1,0:T(8,128)(2,1)S(1)} %pad_maximum_fusion.refs_2_), channel_id=1, source_target_pairs={{0,2},{2,0},{4,6},{6,4},{8,10},{10,8},{12,14},{14,12},{16,18},{18,... | collective-permute-start | bytes 1179656 | tf_op jit(solution)/shard_map/ppermute | solution.py:316
  76.3 5.5 %copy-start = (bf16[1536,5120]{1,0:T(8,128)(2,1)S(1)}, bf16[1536,5120]{1,0:T(8,128)(2,1)}, u32[]{:S(2)}) copy-start(bf16[1536,5120]{1,0:T(8,128)(2,1)} %refs_4_.3) | copy-start | bytes 47185924
  81.7 16.4 %copy-start.1 = (bf16[128,2560]{1,0:T(8,128)(2,1)S(1)}, bf16[128,2560]{1,0:T(8,128)(2,1)}, u32[]{:S(2)}) copy-start(bf16[128,2560]{1,0:T(8,128)(2,1)} %tokens.1) | copy-start | bytes 1966084
  83.3 14.8 %collective-permute-start.21 = (bf16[128,2560]{1,0:T(8,128)(2,1)S(1)}, bf16[128,2560]{1,0:T(8,128)(2,1)S(1)}, u32[]{:S(2)}, u32[]{:S(2)}) collective-permute-start(bf16[128,2560]{1,0:T(8,128)(2,1)S(1)} %away.1), channel_id=1, source_target_pairs={{0,1},{1,0},{2,3},{3,2},{4,5},{5,4},{6,7},{7,6},{8,9},{9,8},{10,11... | collective-permute-start | bytes 1966088 | tf_op jit(solution)/shard_map/ppermute | solution.py:382
  84.9 1.8 %collective-permute-start.27 = (bf16[256,768]{1,0:T(8,128)(2,1)S(1)}, bf16[256,768]{1,0:T(8,128)(2,1)S(1)}, u32[]{:S(2)}, u32[]{:S(2)}) collective-permute-start(bf16[256,768]{1,0:T(8,128)(2,1)S(1)} %broadcast_select_fusion.refs_4_), channel_id=1, source_target_pairs={{0,2},{2,0},{4,6},{6,4},{8,10},{10,8},{12,14},{14,12},{16,18},{18,... | collective-permute-start | bytes 1179656 | tf_op jit(solution)/shard_map/ppermute | solution.py:316
  90.0 8.1 %collective-permute-start.28 = (bf16[128,768]{1,0:T(8,128)(2,1)S(1)}, bf16[128,768]{1,0:T(8,128)(2,1)S(1)}, u32[]{:S(2)}, u32[]{:S(2)}) collective-permute-start(bf16[128,768]{1,0:T(8,128)(2,1)S(1)} %get-tuple-element.87), channel_id=1, source_target_pairs={{0,4},{2,6},{4,0},{6,2},{8,12},{10,14},{12,8},{14,10},{16,20},{18,... | collective-permute-start | bytes 589832 | tf_op jit(solution)/shard_map/ppermute | solution.py:316

commit v5 on v4

--- a/solution.py
+++ b/solution.py
@@ -111,19 +111,25 @@
 
     def plan(seq):
         return [
-            (i, lax.rem(seq // members + r, groups) * width + h * DH, DH, j * groups + r, 0, i * DH)
+            (
+                i,
+                lax.rem(seq // members + r, groups) * width + h * DH,
+                DH,
+                r,
+                0,
+                (2 * j + i) * DH,
+            )
             for j, h in enumerate(chosen)
             for r in range(groups)
             for i in range(2)
         ]
 
-    outs = pack(
+    return pack(
         "pack_pairs_%d" % chosen[0],
-        [shape(rows, 2 * DH)] * (groups * len(chosen)),
+        [shape(rows, 2 * DH * len(chosen))] * groups,
         [k, v],
         plan,
     )
-    return [outs[j * groups : (j + 1) * groups] for j in range(len(chosen))]
 
 
 def pack_queries(groups, members, q):
@@ -157,35 +163,40 @@
     return pack(name, [shape(rows + 2 * more, half)], [q, k, v], plan)[0]
 
 
-def attend(queries, pairs, earlier, head, factor):
+def attend(queries, pairs, earlier, chosen, factor):
     parts = len(queries)
     rows = queries[0].shape[0]
     before = earlier[0].shape[1] if earlier else 0
     total_keys = sum(p.shape[0] for p in pairs)
+    heads = len(chosen)
 
     def kernel(*refs):
         query_refs, refs = refs[:parts], refs[parts:]
         pair_refs, refs = refs[: len(pairs)], refs[len(pairs) :]
         early, outs = refs[:-parts], refs[-parts:]
-        keys = [ref[:, :DH] for ref in pair_refs]
-        values = [ref[:, DH:] for ref in pair_refs]
-        for i in range(parts):
-            if before:
+        if before:
+            for i in range(parts):
                 outs[i][:, :before] = early[i][...]
-            outs[i][:, before:] = softmax_mix(
-                query_refs[i][:, head * DH : (head + 1) * DH], keys, values, factor
-            ).astype(BF16)
+        for j, h in enumerate(chosen):
+            keys = [ref[:, 2 * j * DH : (2 * j + 1) * DH] for ref in pair_refs]
+            values = [ref[:, (2 * j + 1) * DH : (2 * j + 2) * DH] for ref in pair_refs]
+            for i in range(parts):
+                outs[i][:, before + j * DH : before + (j + 1) * DH] = softmax_mix(
+                    query_refs[i][:, h * DH : (h + 1) * DH], keys, values, factor
+                ).astype(BF16)
 
     return pl.pallas_call(
         kernel,
-        out_shape=[shape(rows, before + DH)] * parts,
+        out_shape=[shape(rows, before + heads * DH)] * parts,
         in_specs=[in_vmem()] * (parts + len(pairs) + len(earlier)),
         out_specs=[in_vmem()] * parts,
         compiler_params=limit(14),
         cost_estimate=cost(
-            4 * parts * rows * total_keys * DH, total_keys * DH * 4, parts * rows * total_keys
+            4 * heads * parts * rows * total_keys * DH,
+            heads * total_keys * DH * 4,
+            heads * parts * rows * total_keys,
         ),
-        name="attend_%d" % head,
+        name="attend_%d" % chosen[0],
     )(*queries, *pairs, *earlier)
 
 
@@ -326,13 +337,13 @@
                 x, "seq", axis=0, tiled=True, axis_index_groups=index_groups
             )
 
-        pairs = pack_pairs(groups, members, range(heads), self_keys, self_values)
         queries = pack_queries(groups, members, self_queries)
         queries = [rotate(x, r) for r, x in enumerate(queries)]
         outs = []
         for h in range(heads):
-            pair = gather(join(*[rotate(x, r) for r, x in enumerate(pairs[h])]))
-            outs = attend(queries, [pair], outs, h, factor)
+            pairs = pack_pairs(groups, members, [h], self_keys, self_values)
+            pair = gather(join(*[rotate(x, r) for r, x in enumerate(pairs)]))
+            outs = attend(queries, [pair], outs, [h], factor)
         lhs = [rotate(x, groups - r) for r, x in enumerate(outs)]
         caption = join(caption_keys, caption_values)
         caption = gather(join(*[rotate(caption, r) for r in range(groups)]))
@@ -342,28 +353,27 @@
         updated = (tokens.astype(F32) + gate_vector[None, :] * projected).astype(BF16)
         return (updated, cross_heads)
 
-    pairs = pack_pairs(groups, members, [0], self_keys, self_values)
+    chunks = [list(range(heads - 1)), [heads - 1]]
+    pieces = [pack_pairs(groups, members, chunks[0], self_keys, self_values)]
     go = pack_cross(bit, True, cross_queries, caption_keys, caption_values)
-    pairs += pack_pairs(groups, members, list(range(1, heads)), self_keys, self_values)
-    queries = pack_queries(groups, members, self_queries)
+    pieces += [pack_pairs(groups, members, c, self_keys, self_values) for c in chunks[1:]]
+    pieces.append(pack_queries(groups, members, self_queries))
     stay = pack_cross(bit, False, cross_queries, caption_keys, caption_values)
 
     come = swap(go, bit)
     arrived, gathered = [], []
-    for h in range(heads + 1):
-        last = h == heads
-        here = queries if last else pairs[h]
-        if h:
+    for i, here in enumerate(pieces):
+        if i:
             here = here[:1] + after(here[1:], arrived[-1][1])
         here = [rotate(x, r) for r, x in enumerate(here)]
         arrived.append(here)
-        if not last:
+        if i < len(chunks):
             mine = join(*here)
             half = join(mine, swap(mine, 2))
             gathered.append([half, swap(half, 1)])
     outs = []
-    for h in range(heads):
-        outs = attend(arrived[-1], gathered[h], outs, h, factor)
+    for chunk, pairs in zip(chunks, gathered):
+        outs = attend(arrived[-1], pairs, outs, chunk, factor)
     lhs = [rotate(x, groups - r) for r, x in enumerate(outs)]
 
     caption = join(stay[rows:], come[rows:])
@@ -371,9 +381,8 @@
     inner = [(m + members * g, m + members * (3 - g)) for g in (1, 2) for m in range(members)]
     outer = [(m + members * g, m + members * e) for g, e in ((1, 0), (2, 3)) for m in range(members)]
     middle = lax.ppermute(after(pair, arrived[-1][1:]), "seq", inner)
-    ends = lax.ppermute(after(middle, outs), "seq", outer)
-    zi = lax.axis_index("seq") // members
-    other = jnp.where((zi == 1) | (zi == 2), middle, ends)
+    ends = lax.ppermute(middle, "seq", outer)
+    other = middle + ends
 
     away = project(members, tp_size, 1, lhs, out_weight, BF16, "away")
     captions = [after(pair, away), swap(pair, 1), other, swap(other, 1)]

time: 99.7 us -> 89.7 us (0.90)
  waiting for transfers between devices: 32.2 us -> 24.7 us
  local copies, waits for them, and re-layouts: 5.63 us -> 0.16 us
  starting transfers between devices: 41.1 us -> 44.3 us
    ppermute x15 -> x12, waiting for transfers between devices: 22.7 us -> 16 us  [rotate(): lax.ppermute(x, 'seq', [(s, (s + step) % seq_size) for s in range(seq_siz...]
    unnamed x18 -> x14, local copies, waits for them, and re-layouts: 5.55 us -> 0.08 us
    ppermute x1, waiting for transfers between devices: 4.37 us -> 0.01 us  [shards(): away = lax.ppermute(away, 'tp', [(0, 1), (1, 0)])]
    ppermute x11 -> x9, waiting for transfers between devices: 5.1 us -> 8.74 us  [swap(): return lax.ppermute(x, 'seq', [(s, s ^ by) for s in range(seq_size)])]
    ppermute x15 -> x12, starting transfers between devices: 27.5 us -> 31.1 us  [rotate(): lax.ppermute(x, 'seq', [(s, (s + step) % seq_size) for s in range(seq_siz...]
    ppermute x11 -> x9, starting transfers between devices: 10.1 us -> 9.68 us  [swap(): return lax.ppermute(x, 'seq', [(s, s ^ by) for s in range(seq_size)])]
    pallas_call x3 -> x2, Pallas kernels: 6.55 us -> 6.3 us  [attend(): pl.pallas_call(kernel, out_shape=[shape(rows, before + heads * DH)] * par...]
  transfers between devices with their start and end apart: 29 -> 24, of which waited for: 11 -> 14; matrix products, arithmetic and copies ran while one was open for 0% -> 0% of each run, Pallas kernels for 17% -> 19%
where the time goes in v5:
time: 89.7 us; the launch traced here: 89.4 us
  starting transfers between devices  44.3 us (49%)
  waiting for transfers between devices  24.7 us (28%)
  Pallas kernels  19.1 us (21%)
  between operations  0.91 us (1%)
    ppermute x12, starting transfers between devices, rotate(): lax.ppermute(x, 'seq', [(s, (s + step) % seq_size) for s in range(seq_siz...  31.1 us
    ppermute x12, waiting for transfers between devices, rotate(): lax.ppermute(x, 'seq', [(s, (s + step) % seq_size) for s in range(seq_siz...  16 us
    ppermute x9, starting transfers between devices, swap(): return lax.ppermute(x, 'seq', [(s, s ^ by) for s in range(seq_size)])  9.68 us
    ppermute x9, waiting for transfers between devices, swap(): return lax.ppermute(x, 'seq', [(s, s ^ by) for s in range(seq_size)])  8.74 us
    pallas_call x2, Pallas kernels, attend(): pl.pallas_call(kernel, out_shape=[shape(rows, before + heads * DH)] * par...  6.3 us
    pallas_call x5, Pallas kernels, pack(): pl.pallas_call(kernel, out_shape=out_shapes, in_specs=[in_hbm()] * len(so...  5.29 us
    pallas_call x1, Pallas kernels, cross(): pl.pallas_call(kernel, out_shape=[shape(rows, columns)] * parts, in_specs...  3.27 us
    pallas_call x2, Pallas kernels, project(): pl.pallas_call(kernel, out_shape=shape(rows, columns, dtype), in_specs=[i...  3.12 us
  transfers between devices with their start and end apart: 24, of which 14 were waited for; matrix products, arithmetic and copies ran while one was open for 0% of the time, Pallas kernels for 19%

profile of v5, /device:TPU:0, one launch (start us, length us, event | category | flops | bytes accessed | tf_op | source)
XLA Modules:
  0.0 89.4 jit_solution(7105608412404354190)
XLA Ops:
  0.6 1.3 %pack_pairs_0.1 = (bf16[128,512]{1,0:T(8,128)(2,1)S(1)}, bf16[128,512]{1,0:T(8,128)(2,1)S(1)}, bf16[128,512]{1,0:T(8,128)(2,1)S(1)}, bf16[128,512]{1,0:T(8,128)(2,1)S(1)}) custom-call(bf16[128,1536]{1,0:T(8,128)(2,1)} %refs_0_.7, bf16[128,1536]{1,0:T(8,128)(2,1)} %refs_1_.5), custom_call_target="tpu_custom_call" | custom-call | bytes 1048576 | tf_op jit(solution)/shard_map/pack_pairs_0/pallas_call | solution.py:95
  2.0 3.1 %collective-permute-start = (bf16[128,512]{1,0:T(8,128)(2,1)S(1)}, bf16[128,512]{1,0:T(8,128)(2,1)S(1)}, u32[]{:S(2)}, u32[]{:S(2)}) collective-permute-start(bf16[128,512]{1,0:T(8,128)(2,1)S(1)} %get-tuple-element.40), channel_id=1, source_target_pairs={{0,8},{2,10},{4,12},{6,14},{8,16},{10,18},{12,20},{14,22},{16,24},... | collective-permute-start | bytes 393224 | tf_op jit(solution)/shard_map/ppermute | solution.py:324
  5.0 2.6 %collective-permute-start.9 = (bf16[128,512]{1,0:T(8,128)(2,1)S(1)}, bf16[128,512]{1,0:T(8,128)(2,1)S(1)}, u32[]{:S(2)}, u32[]{:S(2)}) collective-permute-start(bf16[128,512]{1,0:T(8,128)(2,1)S(1)} %get-tuple-element.49), channel_id=1, source_target_pairs={{0,16},{2,18},{4,20},{6,22},{8,24},{10,26},{12,28},{14,30},{16,0},... | collective-permute-start | bytes 393224 | tf_op jit(solution)/shard_map/ppermute | solution.py:324
  7.6 1.3 %collective-permute-start.10 = (bf16[128,512]{1,0:T(8,128)(2,1)S(1)}, bf16[128,512]{1,0:T(8,128)(2,1)S(1)}, u32[]{:S(2)}, u32[]{:S(2)}) collective-permute-start(bf16[128,512]{1,0:T(8,128)(2,1)S(1)} %get-tuple-element.50), channel_id=1, source_target_pairs={{0,24},{2,26},{4,28},{6,30},{8,0},{10,2},{12,4},{14,6},{16,8},{18,... | collective-permute-start | bytes 393224 | tf_op jit(solution)/shard_map/ppermute | solution.py:324
  9.9 1.6 %collective-permute-start.17 = (bf16[192,768]{1,0:T(8,128)(2,1)S(1)}, bf16[192,768]{1,0:T(8,128)(2,1)S(1)}, u32[]{:S(2)}, u32[]{:S(2)}) collective-permute-start(bf16[192,768]{1,0:T(8,128)(2,1)S(1)} %pack_go.1), channel_id=1, source_target_pairs={{0,4},{2,6},{4,0},{6,2},{8,12},{10,14},{12,8},{14,10},{16,20},{18,... | collective-permute-start | bytes 884744 | tf_op jit(solution)/shard_map/ppermute | solution.py:327
  13.4 1.1 %pack_queries.1 = (bf16[128,384]{1,0:T(8,128)(2,1)S(1)}, bf16[128,384]{1,0:T(8,128)(2,1)S(1)}, bf16[128,384]{1,0:T(8,128)(2,1)S(1)}, bf16[128,384]{1,0:T(8,128)(2,1)S(1)}) custom-call(bf16[128,1536]{1,0:T(8,128)(2,1)} %refs_0_.5), custom_call_target="tpu_custom_call" | custom-call | bytes 786432 | tf_op jit(solution)/shard_map/pack_queries/pallas_call | solution.py:95
  14.6 1.7 %collective-permute-done.9 = bf16[128,512]{1,0:T(8,128)(2,1)S(1)} collective-permute-done((bf16[128,512]{1,0:T(8,128)(2,1)S(1)}, bf16[128,512]{1,0:T(8,128)(2,1)S(1)}, u32[]{:S(2)}, u32[]{:S(2)}) %collective-permute-start.9) | collective-permute-done | bytes 131104 | tf_op jit(solution)/shard_map/ppermute | solution.py:324
  16.3 1.6 %collective-permute-start.11 = (bf16[512,512]{1,0:T(8,128)(2,1)S(1)}, bf16[512,512]{1,0:T(8,128)(2,1)S(1)}, u32[]{:S(2)}, u32[]{:S(2)}) collective-permute-start(bf16[512,512]{1,0:T(8,128)(2,1)S(1)} %pad_maximum_fusion), channel_id=1, source_target_pairs={{0,4},{2,6},{4,0},{6,2},{8,12},{10,14},{12,8},{14,10},{16,20},{18,... | collective-permute-start | bytes 1572872 | tf_op jit(solution)/shard_map/ppermute | solution.py:327
  17.9 3.3 %collective-permute-start.1 = (bf16[128,256]{1,0:T(8,128)(2,1)S(1)}, bf16[128,256]{1,0:T(8,128)(2,1)S(1)}, u32[]{:S(2)}, u32[]{:S(2)}) collective-permute-start(bf16[128,256]{1,0:T(8,128)(2,1)S(1)} %get-tuple-element.41), channel_id=1, source_target_pairs={{0,8},{2,10},{4,12},{6,14},{8,16},{10,18},{12,20},{14,22},{16,24},... | collective-permute-start | bytes 196616 | tf_op jit(solution)/shard_map/ppermute | solution.py:324
  21.2 1.6 %collective-permute-start.5 = (bf16[128,256]{1,0:T(8,128)(2,1)S(1)}, bf16[128,256]{1,0:T(8,128)(2,1)S(1)}, u32[]{:S(2)}, u32[]{:S(2)}) collective-permute-start(bf16[128,256]{1,0:T(8,128)(2,1)S(1)} %get-tuple-element.46), channel_id=1, source_target_pairs={{0,16},{2,18},{4,20},{6,22},{8,24},{10,26},{12,28},{14,30},{16,0},... | collective-permute-start | bytes 196616 | tf_op jit(solution)/shard_map/ppermute | solution.py:324
  23.6 1.5 %collective-permute-done.1 = bf16[128,256]{1,0:T(8,128)(2,1)S(1)} collective-permute-done((bf16[128,256]{1,0:T(8,128)(2,1)S(1)}, bf16[128,256]{1,0:T(8,128)(2,1)S(1)}, u32[]{:S(2)}, u32[]{:S(2)}) %collective-permute-start.1) | collective-permute-done | bytes 65568 | tf_op jit(solution)/shard_map/ppermute | solution.py:324
  25.6 2.0 %collective-permute-done.5 = bf16[128,256]{1,0:T(8,128)(2,1)S(1)} collective-permute-done((bf16[128,256]{1,0:T(8,128)(2,1)S(1)}, bf16[128,256]{1,0:T(8,128)(2,1)S(1)}, u32[]{:S(2)}, u32[]{:S(2)}) %collective-permute-start.5) | collective-permute-done | bytes 65568 | tf_op jit(solution)/shard_map/ppermute | solution.py:324
  30.5 4.0 %collective-permute-start.18 = (bf16[128,768]{1,0:T(8,128)(2,1)S(1)}, bf16[128,768]{1,0:T(8,128)(2,1)S(1)}, u32[]{:S(2)}, u32[]{:S(2)}) collective-permute-start(bf16[128,768]{1,0:T(8,128)(2,1)S(1)} %pad_maximum_fusion.3), channel_id=1, source_target_pairs={{0,8},{2,10},{4,12},{6,14},{8,0},{10,2},{12,4},{14,6},{16,24},{18,... | collective-permute-start | bytes 589832 | tf_op jit(solution)/shard_map/ppermute | solution.py:327
  34.5 1.2 %collective-permute-done.7 = bf16[512,256]{1,0:T(8,128)(2,1)S(1)} collective-permute-done((bf16[512,256]{1,0:T(8,128)(2,1)S(1)}, bf16[512,256]{1,0:T(8,128)(2,1)S(1)}, u32[]{:S(2)}, u32[]{:S(2)}) %collective-permute-start.7) | collective-permute-done | bytes 262176 | tf_op jit(solution)/shard_map/ppermute | solution.py:327
  35.8 3.4 %collective-permute-start.4 = (bf16[128,384]{1,0:T(8,128)(2,1)S(1)}, bf16[128,384]{1,0:T(8,128)(2,1)S(1)}, u32[]{:S(2)}, u32[]{:S(2)}) collective-permute-start(bf16[128,384]{1,0:T(8,128)(2,1)S(1)} %get-tuple-element.44), channel_id=1, source_target_pairs={{0,24},{2,26},{4,28},{6,30},{8,0},{10,2},{12,4},{14,6},{16,8},{18,... | collective-permute-start | bytes 294920 | tf_op jit(solution)/shard_map/ppermute | solution.py:324
  40.1 4.2 %collective-permute-done.4.refs_3_ = bf16[128,384]{1,0:T(8,128)(2,1)S(1)} collective-permute-done((bf16[128,384]{1,0:T(8,128)(2,1)S(1)}, bf16[128,384]{1,0:T(8,128)(2,1)S(1)}, u32[]{:S(2)}, u32[]{:S(2)}) %collective-permute-start.4) | collective-permute-done | bytes 98336 | tf_op jit(solution)/shard_map/ppermute | solution.py:324
  45.0 1.3 %collective-permute-start.21 = (bf16[256,768]{1,0:T(8,128)(2,1)S(1)}, bf16[256,768]{1,0:T(8,128)(2,1)S(1)}, u32[]{:S(2)}, u32[]{:S(2)}) collective-permute-start(bf16[256,768]{1,0:T(8,128)(2,1)S(1)} %collective-permute-done.20), channel_id=1, source_target_pairs={{8,0},{10,2},{12,4},{14,6},{16,24},{18,26},{20,28},{22,30},{9,1},{... | collective-permute-start | bytes 1179656 | tf_op jit(solution)/shard_map/ppermute | solution.py:384
  46.3 4.1 %attend_0.1 = (bf16[128,256]{1,0:T(8,128)(2,1)S(1)}, bf16[128,256]{1,0:T(8,128)(2,1)S(1)}, bf16[128,256]{1,0:T(8,128)(2,1)S(1)}, bf16[128,256]{1,0:T(8,128)(2,1)S(1)}) custom-call(bf16[128,384]{1,0:T(8,128)(2,1)S(1)} %get-tuple-element.33.refs_0_, bf16[128,384]{1,0:T(8,128)(2,1)S(1)} %collective-permute-done.2.refs_1_, ...), custom_call_target="tpu_custom_call" | custom-call | flops 1073741824 | bytes 2097152 | tf_op jit(solution)/shard_map/attend_0/pallas_call | solution.py:188
  50.4 2.2 %attend_2.1 = (bf16[128,384]{1,0:T(8,128)(2,1)S(1)}, bf16[128,384]{1,0:T(8,128)(2,1)S(1)}, bf16[128,384]{1,0:T(8,128)(2,1)S(1)}, bf16[128,384]{1,0:T(8,128)(2,1)S(1)}) custom-call(bf16[128,384]{1,0:T(8,128)(2,1)S(1)} %get-tuple-element.33.refs_0_, bf16[128,384]{1,0:T(8,128)(2,1)S(1)} %collective-permute-done.2.refs_1_, ...), custom_call_target="tpu_custom_call" | custom-call | flops 536870912 | bytes 1048576 | tf_op jit(solution)/shard_map/attend_2/pallas_call | solution.py:188
  52.6 1.5 %collective-permute-start.13 = (bf16[128,384]{1,0:T(8,128)(2,1)S(1)}, bf16[128,384]{1,0:T(8,128)(2,1)S(1)}, u32[]{:S(2)}, u32[]{:S(2)}) collective-permute-start(bf16[128,384]{1,0:T(8,128)(2,1)S(1)} %get-tuple-element.56), channel_id=1, source_target_pairs={{0,24},{2,26},{4,28},{6,30},{8,0},{10,2},{12,4},{14,6},{16,8},{18,... | collective-permute-start | bytes 294920 | tf_op jit(solution)/shard_map/ppermute | solution.py:324
  54.1 12.0 %collective-permute-start.14 = (bf16[128,384]{1,0:T(8,128)(2,1)S(1)}, bf16[128,384]{1,0:T(8,128)(2,1)S(1)}, u32[]{:S(2)}, u32[]{:S(2)}) collective-permute-start(bf16[128,384]{1,0:T(8,128)(2,1)S(1)} %get-tuple-element.57), channel_id=1, source_target_pairs={{0,16},{2,18},{4,20},{6,22},{8,24},{10,26},{12,28},{14,30},{16,0},... | collective-permute-start | bytes 294920 | tf_op jit(solution)/shard_map/ppermute | solution.py:324
  66.5 2.3 %collective-permute-done.13.refs_1_ = bf16[128,384]{1,0:T(8,128)(2,1)S(1)} collective-permute-done((bf16[128,384]{1,0:T(8,128)(2,1)S(1)}, bf16[128,384]{1,0:T(8,128)(2,1)S(1)}, u32[]{:S(2)}, u32[]{:S(2)}) %collective-permute-start.13) | collective-permute-done | bytes 98336 | tf_op jit(solution)/shard_map/ppermute | solution.py:324
  68.8 2.3 %collective-permute-done.14.refs_2_ = bf16[128,384]{1,0:T(8,128)(2,1)S(1)} collective-permute-done((bf16[128,384]{1,0:T(8,128)(2,1)S(1)}, bf16[128,384]{1,0:T(8,128)(2,1)S(1)}, u32[]{:S(2)}, u32[]{:S(2)}) %collective-permute-start.14) | collective-permute-done | bytes 98336 | tf_op jit(solution)/shard_map/ppermute | solution.py:324
  71.1 1.4 %collective-permute-done.15.refs_3_ = bf16[128,384]{1,0:T(8,128)(2,1)S(1)} collective-permute-done((bf16[128,384]{1,0:T(8,128)(2,1)S(1)}, bf16[128,384]{1,0:T(8,128)(2,1)S(1)}, u32[]{:S(2)}, u32[]{:S(2)}) %collective-permute-start.15) | collective-permute-done | bytes 98336 | tf_op jit(solution)/shard_map/ppermute | solution.py:324
  72.6 1.6 %away.1 = bf16[128,2560]{1,0:T(8,128)(2,1)S(1)} custom-call(bf16[128,384]{1,0:T(8,128)(2,1)S(1)} %get-tuple-element.55.refs_0_, bf16[128,384]{1,0:T(8,128)(2,1)S(1)} %collective-permute-done.13.refs_1_, bf16[128,384]{1,0:T(8,128)(2,1)S(1)} %collective-permute-done.14.refs_2_, bf16[128,384]{1,0:T(8,128)(2,1)S(1)} %collective-permute-done.15.refs_3_, ...), custom_call_target="tpu_custom_call" | custom-call | flops 1006632960 | bytes 9175040 | tf_op jit(solution)/shard_map/away/pallas_call | solution.py:265
  74.1 1.6 %collective-permute-start.16 = (bf16[128,2560]{1,0:T(8,128)(2,1)S(1)}, bf16[128,2560]{1,0:T(8,128)(2,1)S(1)}, u32[]{:S(2)}, u32[]{:S(2)}) collective-permute-start(bf16[128,2560]{1,0:T(8,128)(2,1)S(1)} %away.1), channel_id=1, source_target_pairs={{0,1},{1,0},{2,3},{3,2},{4,5},{5,4},{6,7},{7,6},{8,9},{9,8},{10,11... | collective-permute-start | bytes 1966088 | tf_op jit(solution)/shard_map/ppermute | solution.py:391
  76.4 1.0 %collective-permute-done.19.refs_3_ = bf16[256,768]{1,0:T(8,128)(2,1)S(1)} collective-permute-done((bf16[256,768]{1,0:T(8,128)(2,1)S(1)}, bf16[256,768]{1,0:T(8,128)(2,1)S(1)}, u32[]{:S(2)}, u32[]{:S(2)}) %collective-permute-start.19) | collective-permute-done | bytes 393248 | tf_op jit(solution)/shard_map/ppermute | solution.py:327
  78.0 3.3 %cross.1 = (bf16[128,768]{1,0:T(8,128)(2,1)S(1)}, bf16[128,768]{1,0:T(8,128)(2,1)S(1)}) custom-call(bf16[192,768]{1,0:T(8,128)(2,1)S(1)} %pack_stay.1.refs_0_, bf16[192,768]{1,0:T(8,128)(2,1)S(1)} %collective-permute-done.17.refs_1_, bf16[256,768]{1,0:T(8,128)(2,1)S(1)} %pad_maximum_fusion.1.refs_2_, bf16[256,768]{1,0:T(8,128)(2,1)S(1)} %collective-permute-done.19.refs_3_, ...), custom_call_target="tpu_custom_call" | custom-call | flops 402653184 | bytes 2359296 | tf_op jit(solution)/shard_map/cross/pallas_call | solution.py:228
  81.2 1.3 %collective-permute-start.23 = (bf16[128,768]{1,0:T(8,128)(2,1)S(1)}, bf16[128,768]{1,0:T(8,128)(2,1)S(1)}, u32[]{:S(2)}, u32[]{:S(2)}) collective-permute-start(bf16[128,768]{1,0:T(8,128)(2,1)S(1)} %get-tuple-element.63), channel_id=1, source_target_pairs={{0,4},{2,6},{4,0},{6,2},{8,12},{10,14},{12,8},{14,10},{16,20},{18,... | collective-permute-start | bytes 589832 | tf_op jit(solution)/shard_map/ppermute | solution.py:327
  82.6 1.6 %home.1 = f32[128,2560]{1,0:T(8,128)S(1)} custom-call(bf16[128,384]{1,0:T(8,128)(2,1)S(1)} %get-tuple-element.55.refs_0_, bf16[128,384]{1,0:T(8,128)(2,1)S(1)} %collective-permute-done.13.refs_1_, bf16[128,384]{1,0:T(8,128)(2,1)S(1)} %collective-permute-done.14.refs_2_, bf16[128,384]{1,0:T(8,128)(2,1)S(1)} %collective-permute-done.15.refs_3_, ...), custom_call_target="tpu_custom_call" | custom-call | flops 1006632960 | bytes 9175040 | tf_op jit(solution)/shard_map/home/pallas_call | solution.py:265
  84.1 4.1 %collective-permute-done.23.came = bf16[128,768]{1,0:T(8,128)(2,1)S(1)} collective-permute-done((bf16[128,768]{1,0:T(8,128)(2,1)S(1)}, bf16[128,768]{1,0:T(8,128)(2,1)S(1)}, u32[]{:S(2)}, u32[]{:S(2)}) %collective-permute-start.23) | collective-permute-done | bytes 196640 | tf_op jit(solution)/shard_map/ppermute | solution.py:327
  88.2 1.2 %finish.1 = (bf16[128,2560]{1,0:T(8,128)(2,1)}, bf16[128,1536]{1,0:T(8,128)(2,1)}) custom-call(bf16[128,2560]{1,0:T(8,128)(2,1)S(1)} %copy-done.1, f32[1,2560]{1,0:T(1,128)S(1)} %broadcast_in_dim.3.gate, f32[128,2560]{1,0:T(8,128)S(1)} %home.1, bf16[128,2560]{1,0:T(8,128)(2,1)S(1)} %collective-permute-done.16.away, ...), custom_call_target="tpu_custom_call" | custom-call | bytes 3276800 | tf_op jit(solution)/shard_map/finish/pallas_call | solution.py:287
  (51 shorter events, 10.3 us)
Async XLA Ops:
  0.6 71.9 %copy-start = (bf16[1536,5120]{1,0:T(8,128)(2,1)S(1)}, bf16[1536,5120]{1,0:T(8,128)(2,1)}, u32[]{:S(2)}) copy-start(bf16[1536,5120]{1,0:T(8,128)(2,1)} %refs_4_.3) | copy-start | bytes 47185924
  2.0 12.6 %collective-permute-start = (bf16[128,512]{1,0:T(8,128)(2,1)S(1)}, bf16[128,512]{1,0:T(8,128)(2,1)S(1)}, u32[]{:S(2)}, u32[]{:S(2)}) collective-permute-start(bf16[128,512]{1,0:T(8,128)(2,1)S(1)} %get-tuple-element.40), channel_id=1, source_target_pairs={{0,8},{2,10},{4,12},{6,14},{8,16},{10,18},{12,20},{14,22},{16,24},... | collective-permute-start | bytes 393224 | tf_op jit(solution)/shard_map/ppermute | solution.py:324
  5.0 11.2 %collective-permute-start.9 = (bf16[128,512]{1,0:T(8,128)(2,1)S(1)}, bf16[128,512]{1,0:T(8,128)(2,1)S(1)}, u32[]{:S(2)}, u32[]{:S(2)}) collective-permute-start(bf16[128,512]{1,0:T(8,128)(2,1)S(1)} %get-tuple-element.49), channel_id=1, source_target_pairs={{0,16},{2,18},{4,20},{6,22},{8,24},{10,26},{12,28},{14,30},{16,0},... | collective-permute-start | bytes 393224 | tf_op jit(solution)/shard_map/ppermute | solution.py:324
  7.6 8.6 %collective-permute-start.10 = (bf16[128,512]{1,0:T(8,128)(2,1)S(1)}, bf16[128,512]{1,0:T(8,128)(2,1)S(1)}, u32[]{:S(2)}, u32[]{:S(2)}) collective-permute-start(bf16[128,512]{1,0:T(8,128)(2,1)S(1)} %get-tuple-element.50), channel_id=1, source_target_pairs={{0,24},{2,26},{4,28},{6,30},{8,0},{10,2},{12,4},{14,6},{16,8},{18,... | collective-permute-start | bytes 393224 | tf_op jit(solution)/shard_map/ppermute | solution.py:324
  9.9 20.5 %collective-permute-start.17 = (bf16[192,768]{1,0:T(8,128)(2,1)S(1)}, bf16[192,768]{1,0:T(8,128)(2,1)S(1)}, u32[]{:S(2)}, u32[]{:S(2)}) collective-permute-start(bf16[192,768]{1,0:T(8,128)(2,1)S(1)} %pack_go.1), channel_id=1, source_target_pairs={{0,4},{2,6},{4,0},{6,2},{8,12},{10,14},{12,8},{14,10},{16,20},{18,... | collective-permute-start | bytes 884744 | tf_op jit(solution)/shard_map/ppermute | solution.py:327
  14.6 68.0 %copy-start.2 = (f32[2560]{0:T(1024)S(1)}, f32[2560]{0:T(1024)}, u32[]{:S(2)}) copy-start(f32[2560]{0:T(1024)} %param.17) | copy-start | bytes 30724
  16.3 14.0 %collective-permute-start.11 = (bf16[512,512]{1,0:T(8,128)(2,1)S(1)}, bf16[512,512]{1,0:T(8,128)(2,1)S(1)}, u32[]{:S(2)}, u32[]{:S(2)}) collective-permute-start(bf16[512,512]{1,0:T(8,128)(2,1)S(1)} %pad_maximum_fusion), channel_id=1, source_target_pairs={{0,4},{2,6},{4,0},{6,2},{8,12},{10,14},{12,8},{14,10},{16,20},{18,... | collective-permute-start | bytes 1572872 | tf_op jit(solution)/shard_map/ppermute | solution.py:327
  17.9 7.3 %collective-permute-start.1 = (bf16[128,256]{1,0:T(8,128)(2,1)S(1)}, bf16[128,256]{1,0:T(8,128)(2,1)S(1)}, u32[]{:S(2)}, u32[]{:S(2)}) collective-permute-start(bf16[128,256]{1,0:T(8,128)(2,1)S(1)} %get-tuple-element.41), channel_id=1, source_target_pairs={{0,8},{2,10},{4,12},{6,14},{8,16},{10,18},{12,20},{14,22},{16,24},... | collective-permute-start | bytes 196616 | tf_op jit(solution)/shard_map/ppermute | solution.py:324
  21.2 6.5 %collective-permute-start.5 = (bf16[128,256]{1,0:T(8,128)(2,1)S(1)}, bf16[128,256]{1,0:T(8,128)(2,1)S(1)}, u32[]{:S(2)}, u32[]{:S(2)}) collective-permute-start(bf16[128,256]{1,0:T(8,128)(2,1)S(1)} %get-tuple-element.46), channel_id=1, source_target_pairs={{0,16},{2,18},{4,20},{6,22},{8,24},{10,26},{12,28},{14,30},{16,0},... | collective-permute-start | bytes 196616 | tf_op jit(solution)/shard_map/ppermute | solution.py:324
  22.8 6.0 %collective-permute-start.6 = (bf16[128,256]{1,0:T(8,128)(2,1)S(1)}, bf16[128,256]{1,0:T(8,128)(2,1)S(1)}, u32[]{:S(2)}, u32[]{:S(2)}) collective-permute-start(bf16[128,256]{1,0:T(8,128)(2,1)S(1)} %get-tuple-element.47), channel_id=1, source_target_pairs={{0,24},{2,26},{4,28},{6,30},{8,0},{10,2},{12,4},{14,6},{16,8},{18,... | collective-permute-start | bytes 196616 | tf_op jit(solution)/shard_map/ppermute | solution.py:324
  25.1 15.0 %collective-permute-start.2 = (bf16[128,384]{1,0:T(8,128)(2,1)S(1)}, bf16[128,384]{1,0:T(8,128)(2,1)S(1)}, u32[]{:S(2)}, u32[]{:S(2)}) collective-permute-start(bf16[128,384]{1,0:T(8,128)(2,1)S(1)} %get-tuple-element.42), channel_id=1, source_target_pairs={{0,8},{2,10},{4,12},{6,14},{8,16},{10,18},{12,20},{14,22},{16,24},... | collective-permute-start | bytes 294920 | tf_op jit(solution)/shard_map/ppermute | solution.py:324
  27.6 12.5 %collective-permute-start.3 = (bf16[128,384]{1,0:T(8,128)(2,1)S(1)}, bf16[128,384]{1,0:T(8,128)(2,1)S(1)}, u32[]{:S(2)}, u32[]{:S(2)}) collective-permute-start(bf16[128,384]{1,0:T(8,128)(2,1)S(1)} %get-tuple-element.43), channel_id=1, source_target_pairs={{0,16},{2,18},{4,20},{6,22},{8,24},{10,26},{12,28},{14,30},{16,0},... | collective-permute-start | bytes 294920 | tf_op jit(solution)/shard_map/ppermute | solution.py:324
  28.8 6.9 %collective-permute-start.7 = (bf16[512,256]{1,0:T(8,128)(2,1)S(1)}, bf16[512,256]{1,0:T(8,128)(2,1)S(1)}, u32[]{:S(2)}, u32[]{:S(2)}) collective-permute-start(bf16[512,256]{1,0:T(8,128)(2,1)S(1)} %pad_maximum_fusion.2), channel_id=1, source_target_pairs={{0,4},{2,6},{4,0},{6,2},{8,12},{10,14},{12,8},{14,10},{16,20},{18,... | collective-permute-start | bytes 786440 | tf_op jit(solution)/shard_map/ppermute | solution.py:327
  30.3 16.0 %collective-permute-start.12 = (bf16[1024,512]{1,0:T(8,128)(2,1)S(1)}, bf16[1024,512]{1,0:T(8,128)(2,1)S(1)}, u32[]{:S(2)}, u32[]{:S(2)}) collective-permute-start(bf16[1024,512]{1,0:T(8,128)(2,1)S(1)} %constant_dynamic-update-slice_fusion.5.refs_4_), channel_id=1, source_target_pairs={{0,2},{2,0},{4,6},{6,4},{8,10},{10,8},{12,14},{14,12},{16,18},{18,... | collective-permute-start | bytes 3145736 | tf_op jit(solution)/shard_map/ppermute | solution.py:327
  30.5 9.6 %collective-permute-start.18 = (bf16[128,768]{1,0:T(8,128)(2,1)S(1)}, bf16[128,768]{1,0:T(8,128)(2,1)S(1)}, u32[]{:S(2)}, u32[]{:S(2)}) collective-permute-start(bf16[128,768]{1,0:T(8,128)(2,1)S(1)} %pad_maximum_fusion.3), channel_id=1, source_target_pairs={{0,8},{2,10},{4,12},{6,14},{8,0},{10,2},{12,4},{14,6},{16,24},{18,... | collective-permute-start | bytes 589832 | tf_op jit(solution)/shard_map/ppermute | solution.py:327
  35.8 8.5 %collective-permute-start.4 = (bf16[128,384]{1,0:T(8,128)(2,1)S(1)}, bf16[128,384]{1,0:T(8,128)(2,1)S(1)}, u32[]{:S(2)}, u32[]{:S(2)}) collective-permute-start(bf16[128,384]{1,0:T(8,128)(2,1)S(1)} %get-tuple-element.44), channel_id=1, source_target_pairs={{0,24},{2,26},{4,28},{6,30},{8,0},{10,2},{12,4},{14,6},{16,8},{18,... | collective-permute-start | bytes 294920 | tf_op jit(solution)/shard_map/ppermute | solution.py:324
  40.1 10.4 %collective-permute-start.8 = (bf16[1024,256]{1,0:T(8,128)(2,1)S(1)}, bf16[1024,256]{1,0:T(8,128)(2,1)S(1)}, u32[]{:S(2)}, u32[]{:S(2)}) collective-permute-start(bf16[1024,256]{1,0:T(8,128)(2,1)S(1)} %constant_dynamic-update-slice_fusion.refs_4_), channel_id=1, source_target_pairs={{0,2},{2,0},{4,6},{6,4},{8,10},{10,8},{12,14},{14,12},{16,18},{18,... | collective-permute-start | bytes 1572872 | tf_op jit(solution)/shard_map/ppermute | solution.py:327
  44.3 0.7 collective-permute-start.20
  45.0 30.7 %collective-permute-start.21 = (bf16[256,768]{1,0:T(8,128)(2,1)S(1)}, bf16[256,768]{1,0:T(8,128)(2,1)S(1)}, u32[]{:S(2)}, u32[]{:S(2)}) collective-permute-start(bf16[256,768]{1,0:T(8,128)(2,1)S(1)} %collective-permute-done.20), channel_id=1, source_target_pairs={{8,0},{10,2},{12,4},{14,6},{16,24},{18,26},{20,28},{22,30},{9,1},{... | collective-permute-start | bytes 1179656 | tf_op jit(solution)/shard_map/ppermute | solution.py:384
  52.6 16.2 %collective-permute-start.13 = (bf16[128,384]{1,0:T(8,128)(2,1)S(1)}, bf16[128,384]{1,0:T(8,128)(2,1)S(1)}, u32[]{:S(2)}, u32[]{:S(2)}) collective-permute-start(bf16[128,384]{1,0:T(8,128)(2,1)S(1)} %get-tuple-element.56), channel_id=1, source_target_pairs={{0,24},{2,26},{4,28},{6,30},{8,0},{10,2},{12,4},{14,6},{16,8},{18,... | collective-permute-start | bytes 294920 | tf_op jit(solution)/shard_map/ppermute | solution.py:324
  54.1 17.1 %collective-permute-start.14 = (bf16[128,384]{1,0:T(8,128)(2,1)S(1)}, bf16[128,384]{1,0:T(8,128)(2,1)S(1)}, u32[]{:S(2)}, u32[]{:S(2)}) collective-permute-start(bf16[128,384]{1,0:T(8,128)(2,1)S(1)} %get-tuple-element.57), channel_id=1, source_target_pairs={{0,16},{2,18},{4,20},{6,22},{8,24},{10,26},{12,28},{14,30},{16,0},... | collective-permute-start | bytes 294920 | tf_op jit(solution)/shard_map/ppermute | solution.py:324
  66.1 6.4 %collective-permute-start.15 = (bf16[128,384]{1,0:T(8,128)(2,1)S(1)}, bf16[128,384]{1,0:T(8,128)(2,1)S(1)}, u32[]{:S(2)}, u32[]{:S(2)}) collective-permute-start(bf16[128,384]{1,0:T(8,128)(2,1)S(1)} %get-tuple-element.58), channel_id=1, source_target_pairs={{0,8},{2,10},{4,12},{6,14},{8,16},{10,18},{12,20},{14,22},{16,24},... | collective-permute-start | bytes 294920 | tf_op jit(solution)/shard_map/ppermute | solution.py:324
  72.6 15.7 %copy-start.1 = (bf16[128,2560]{1,0:T(8,128)(2,1)S(1)}, bf16[128,2560]{1,0:T(8,128)(2,1)}, u32[]{:S(2)}) copy-start(bf16[128,2560]{1,0:T(8,128)(2,1)} %tokens.1) | copy-start | bytes 1966084
  74.1 14.1 %collective-permute-start.16 = (bf16[128,2560]{1,0:T(8,128)(2,1)S(1)}, bf16[128,2560]{1,0:T(8,128)(2,1)S(1)}, u32[]{:S(2)}, u32[]{:S(2)}) collective-permute-start(bf16[128,2560]{1,0:T(8,128)(2,1)S(1)} %away.1), channel_id=1, source_target_pairs={{0,1},{1,0},{2,3},{3,2},{4,5},{5,4},{6,7},{7,6},{8,9},{9,8},{10,11... | collective-permute-start | bytes 1966088 | tf_op jit(solution)/shard_map/ppermute | solution.py:391
  75.7 1.7 %collective-permute-start.19 = (bf16[256,768]{1,0:T(8,128)(2,1)S(1)}, bf16[256,768]{1,0:T(8,128)(2,1)S(1)}, u32[]{:S(2)}, u32[]{:S(2)}) collective-permute-start(bf16[256,768]{1,0:T(8,128)(2,1)S(1)} %pad_maximum_fusion.1.refs_2_), channel_id=1, source_target_pairs={{0,2},{2,0},{4,6},{6,4},{8,10},{10,8},{12,14},{14,12},{16,18},{18,... | collective-permute-start | bytes 1179656 | tf_op jit(solution)/shard_map/ppermute | solution.py:327
  75.8 2.2 %collective-permute-start.22 = (bf16[256,768]{1,0:T(8,128)(2,1)S(1)}, bf16[256,768]{1,0:T(8,128)(2,1)S(1)}, u32[]{:S(2)}, u32[]{:S(2)}) collective-permute-start(bf16[256,768]{1,0:T(8,128)(2,1)S(1)} %add.3.refs_4_), channel_id=1, source_target_pairs={{0,2},{2,0},{4,6},{6,4},{8,10},{10,8},{12,14},{14,12},{16,18},{18,... | collective-permute-start | bytes 1179656 | tf_op jit(solution)/shard_map/ppermute | solution.py:327
  81.2 7.0 %collective-permute-start.23 = (bf16[128,768]{1,0:T(8,128)(2,1)S(1)}, bf16[128,768]{1,0:T(8,128)(2,1)S(1)}, u32[]{:S(2)}, u32[]{:S(2)}) collective-permute-start(bf16[128,768]{1,0:T(8,128)(2,1)S(1)} %get-tuple-element.63), channel_id=1, source_target_pairs={{0,4},{2,6},{4,0},{6,2},{8,12},{10,14},{12,8},{14,10},{16,20},{18,... | collective-permute-start | bytes 589832 | tf_op jit(solution)/shard_map/ppermute | solution.py:327

commit v6 on v5

--- a/solution.py
+++ b/solution.py
@@ -105,44 +105,25 @@
     )
 
 
-def pack_pairs(groups, members, chosen, k, v):
-    rows, columns = k.shape
+def pack_pieces(groups, members, lists, sources, name):
+    rows, columns = sources[0].shape
     width = columns // groups
 
     def plan(seq):
         return [
-            (
-                i,
-                lax.rem(seq // members + r, groups) * width + h * DH,
-                DH,
-                r,
-                0,
-                (2 * j + i) * DH,
-            )
-            for j, h in enumerate(chosen)
+            (i, lax.rem(seq // members + r, groups) * width + h * DH, DH, n * groups + r, 0, j * DH)
+            for n, blocks in enumerate(lists)
+            for j, (i, h) in enumerate(blocks)
             for r in range(groups)
-            for i in range(2)
         ]
 
-    return pack(
-        "pack_pairs_%d" % chosen[0],
-        [shape(rows, 2 * DH * len(chosen))] * groups,
-        [k, v],
+    outs = pack(
+        name,
+        [shape(rows, DH * len(blocks)) for blocks in lists for _ in range(groups)],
+        sources,
         plan,
     )
-
-
-def pack_queries(groups, members, q):
-    rows, columns = q.shape
-    width = columns // groups
-
-    def plan(seq):
-        return [
-            (0, lax.rem(seq // members + r, groups) * width, width, r, 0, 0)
-            for r in range(groups)
-        ]
-
-    return pack("pack_queries", [shape(rows, width)] * groups, [q], plan)
+    return [outs[n * groups : (n + 1) * groups] for n in range(len(lists))]
 
 
 def pack_cross(bit, go, q, k, v):
@@ -163,7 +144,7 @@
     return pack(name, [shape(rows + 2 * more, half)], [q, k, v], plan)[0]
 
 
-def attend(queries, pairs, earlier, chosen, factor):
+def attend(queries, first, pairs, earlier, chosen, factor):
     parts = len(queries)
     rows = queries[0].shape[0]
     before = earlier[0].shape[1] if earlier else 0
@@ -180,9 +161,10 @@
         for j, h in enumerate(chosen):
             keys = [ref[:, 2 * j * DH : (2 * j + 1) * DH] for ref in pair_refs]
             values = [ref[:, (2 * j + 1) * DH : (2 * j + 2) * DH] for ref in pair_refs]
+            at = first + h * DH
             for i in range(parts):
                 outs[i][:, before + j * DH : before + (j + 1) * DH] = softmax_mix(
-                    query_refs[i][:, h * DH : (h + 1) * DH], keys, values, factor
+                    query_refs[i][:, at : at + DH], keys, values, factor
                 ).astype(BF16)
 
     return pl.pallas_call(
@@ -329,6 +311,7 @@
     def join(*xs):
         return xs[0] if len(xs) == 1 else jnp.concatenate(xs, axis=0)
 
+    sources = [self_keys, self_values, self_queries]
     if (groups, members, tp_size) != (4, 4, 2):
         index_groups = [[g * members + m for m in range(members)] for g in range(groups)]
 
@@ -337,13 +320,13 @@
                 x, "seq", axis=0, tiled=True, axis_index_groups=index_groups
             )
 
-        queries = pack_queries(groups, members, self_queries)
-        queries = [rotate(x, r) for r, x in enumerate(queries)]
         outs = []
         for h in range(heads):
-            pairs = pack_pairs(groups, members, [h], self_keys, self_values)
-            pair = gather(join(*[rotate(x, r) for r, x in enumerate(pairs)]))
-            outs = attend(queries, [pair], outs, [h], factor)
+            blocks = [(0, h), (1, h), (2, h)]
+            (pieces,) = pack_pieces(groups, members, [blocks], sources, "pack_%d" % h)
+            pieces = [rotate(x, r) for r, x in enumerate(pieces)]
+            pair = gather(join(*[x[:, : 2 * DH] for x in pieces]))
+            outs = attend(pieces, (2 - h) * DH, [pair], outs, [h], factor)
         lhs = [rotate(x, groups - r) for r, x in enumerate(outs)]
         caption = join(caption_keys, caption_values)
         caption = gather(join(*[rotate(caption, r) for r in range(groups)]))
@@ -353,39 +336,41 @@
         updated = (tokens.astype(F32) + gate_vector[None, :] * projected).astype(BF16)
         return (updated, cross_heads)
 
-    chunks = [list(range(heads - 1)), [heads - 1]]
-    pieces = [pack_pairs(groups, members, chunks[0], self_keys, self_values)]
+    chunks = [list(range(2)), list(range(2, heads))]
+    kv = [[(i, h) for h in chunk for i in range(2)] for chunk in chunks]
+    kv[1] += [(2, h) for h in range(heads)]
+    first = pack_pieces(groups, members, kv[:1], sources, "pack_first")[0]
     go = pack_cross(bit, True, cross_queries, caption_keys, caption_values)
-    pieces += [pack_pairs(groups, members, c, self_keys, self_values) for c in chunks[1:]]
-    pieces.append(pack_queries(groups, members, self_queries))
+    (second,) = pack_pieces(groups, members, kv[1:], sources, "pack_later")
     stay = pack_cross(bit, False, cross_queries, caption_keys, caption_values)
 
+    def travel(pieces, gates):
+        return pieces[:1] + [
+            rotate(x if g is None else after(x, g), r + 1)
+            for r, (x, g) in enumerate(zip(pieces[1:], gates))
+        ]
+
     come = swap(go, bit)
-    arrived, gathered = [], []
-    for i, here in enumerate(pieces):
-        if i:
-            here = here[:1] + after(here[1:], arrived[-1][1])
-        here = [rotate(x, r) for r, x in enumerate(here)]
-        arrived.append(here)
-        if i < len(chunks):
-            mine = join(*here)
-            half = join(mine, swap(mine, 2))
-            gathered.append([half, swap(half, 1)])
-    outs = []
-    for chunk, pairs in zip(chunks, gathered):
-        outs = attend(arrived[-1], pairs, outs, chunk, factor)
+    first = travel(first, [None] * 3)
+    second = travel(second, [None, (first[1], come), (first[1], come)])
+    mine = join(*first)
+    half_first = join(mine, swap(mine, 2))
+    caption = join(stay[rows:], come[rows:])
+    pair = join(caption, swap(after(caption, first[1:]), members))
+    at = 2 * DH * len(chunks[1])
+    mine = join(*[x[:, :at] for x in second])
+    half_second = join(mine, swap(after(mine, pair), 2))
+    pairs_first = [half_first, swap(half_first, 1)]
+    outs = attend(second, at, pairs_first, [], chunks[0], factor)
+    beyond = swap(after(caption, second[1:]), 2 * members)
+    pairs_second = [half_second, swap(after(half_second, (outs, beyond)), 1)]
+    outs = attend(second, at, pairs_second, outs, chunks[1], factor)
+    last = swap(after(pair[2 * cap_rows * 2 :], beyond), 2 * members)
+    other = join(beyond, last)
     lhs = [rotate(x, groups - r) for r, x in enumerate(outs)]
 
-    caption = join(stay[rows:], come[rows:])
-    pair = join(caption, swap(after(caption, arrived[0][1:]), members))
-    inner = [(m + members * g, m + members * (3 - g)) for g in (1, 2) for m in range(members)]
-    outer = [(m + members * g, m + members * e) for g, e in ((1, 0), (2, 3)) for m in range(members)]
-    middle = lax.ppermute(after(pair, arrived[-1][1:]), "seq", inner)
-    ends = lax.ppermute(middle, "seq", outer)
-    other = middle + ends
-
     away = project(members, tp_size, 1, lhs, out_weight, BF16, "away")
-    captions = [after(pair, away), swap(pair, 1), other, swap(other, 1)]
+    captions = [after(pair, away), swap(after(pair, away), 1), other, swap(other, 1)]
     own, theirs = cross([stay, come], captions, rows, cap_rows, factor)
     came = swap(theirs, bit)
     away = lax.ppermute(away, "tp", [(0, 1), (1, 0)])

time: 89.7 us -> 88.4 us (0.986)
  starting transfers between devices: 44.3 us -> 33.5 us
  waiting for transfers between devices: 24.7 us -> 35.1 us
    ppermute x12 -> x9, starting transfers between devices: 31.1 us -> 18.8 us  [rotate(): lax.ppermute(x, 'seq', [(s, (s + step) % seq_size) for s in range(seq_siz...]
    ppermute x9 -> x11, waiting for transfers between devices: 8.74 us -> 16.5 us  [swap(): return lax.ppermute(x, 'seq', [(s, s ^ by) for s in range(seq_size)])]
    ppermute x9 -> x11, starting transfers between devices: 9.68 us -> 13.1 us  [swap(): return lax.ppermute(x, 'seq', [(s, s ^ by) for s in range(seq_size)])]
    ppermute x1, waiting for transfers between devices: 0.01 us -> 2.18 us  [shards(): away = lax.ppermute(away, 'tp', [(0, 1), (1, 0)])]
    ppermute x2 -> x0, starting transfers between devices: 1.97 us -> none  [the longest x1 1.29 us: shards(): ends = lax.ppermute(middle, 'seq', outer)]
    pallas_call x5 -> x4, Pallas kernels: 5.29 us -> 4.49 us  [pack(): pl.pallas_call(kernel, out_shape=out_shapes, in_specs=[in_hbm()] * len(so...]
    ppermute x12 -> x9, waiting for transfers between devices: 16 us -> 16.4 us  [rotate(): lax.ppermute(x, 'seq', [(s, (s + step) % seq_size) for s in range(seq_siz...]
  transfers between devices with their start and end apart: 24 -> 21, of which waited for: 14 -> 12; matrix products, arithmetic and copies ran while one was open for 0% -> 0% of each run, Pallas kernels for 19% -> 18%
where the time goes in v6:
time: 88.4 us; the launch traced here: 88.1 us
  waiting for transfers between devices  35.1 us (40%)
  starting transfers between devices  33.5 us (38%)
  Pallas kernels  18.4 us (21%)
  between operations  0.89 us (1%)
    ppermute x9, starting transfers between devices, rotate(): lax.ppermute(x, 'seq', [(s, (s + step) % seq_size) for s in range(seq_siz...  18.8 us
    ppermute x11, waiting for transfers between devices, swap(): return lax.ppermute(x, 'seq', [(s, s ^ by) for s in range(seq_size)])  16.5 us
    ppermute x9, waiting for transfers between devices, rotate(): lax.ppermute(x, 'seq', [(s, (s + step) % seq_size) for s in range(seq_siz...  16.4 us
    ppermute x11, starting transfers between devices, swap(): return lax.ppermute(x, 'seq', [(s, s ^ by) for s in range(seq_size)])  13.1 us
    pallas_call x2, Pallas kernels, attend(): pl.pallas_call(kernel, out_shape=[shape(rows, before + heads * DH)] * par...  6.29 us
    pallas_call x4, Pallas kernels, pack(): pl.pallas_call(kernel, out_shape=out_shapes, in_specs=[in_hbm()] * len(so...  4.49 us
    pallas_call x1, Pallas kernels, cross(): pl.pallas_call(kernel, out_shape=[shape(rows, columns)] * parts, in_specs...  3.27 us
    pallas_call x2, Pallas kernels, project(): pl.pallas_call(kernel, out_shape=shape(rows, columns, dtype), in_specs=[i...  3.14 us
  transfers between devices with their start and end apart: 21, of which 12 were waited for; matrix products, arithmetic and copies ran while one was open for 0% of the time, Pallas kernels for 18%

profile of v6, /device:TPU:0, one launch (start us, length us, event | category | flops | bytes accessed | tf_op | source)
XLA Modules:
  0.0 88.1 jit_solution(14672170861027466865)
XLA Ops:
  0.6 1.3 %pack_first.1 = (bf16[128,512]{1,0:T(8,128)(2,1)S(1)}, bf16[128,512]{1,0:T(8,128)(2,1)S(1)}, bf16[128,512]{1,0:T(8,128)(2,1)S(1)}, bf16[128,512]{1,0:T(8,128)(2,1)S(1)}) custom-call(bf16[128,1536]{1,0:T(8,128)(2,1)} %refs_0_.5, bf16[128,1536]{1,0:T(8,128)(2,1)} %refs_1_.5, bf16[128,1536]{1,0:T(8,128)(2,1)} %refs_2_.5), custom_call_target="tpu_custom_call" | custom-call | bytes 1048576 | tf_op jit(solution)/shard_map/pack_first/pallas_call | solution.py:95
  2.0 3.1 %collective-permute-start.1 = (bf16[128,512]{1,0:T(8,128)(2,1)S(1)}, bf16[128,512]{1,0:T(8,128)(2,1)S(1)}, u32[]{:S(2)}, u32[]{:S(2)}) collective-permute-start(bf16[128,512]{1,0:T(8,128)(2,1)S(1)} %get-tuple-element.31), channel_id=1, source_target_pairs={{0,8},{2,10},{4,12},{6,14},{8,16},{10,18},{12,20},{14,22},{16,24},... | collective-permute-start | bytes 393224 | tf_op jit(solution)/shard_map/ppermute | solution.py:306
  5.0 2.6 %collective-permute-start.5 = (bf16[128,512]{1,0:T(8,128)(2,1)S(1)}, bf16[128,512]{1,0:T(8,128)(2,1)S(1)}, u32[]{:S(2)}, u32[]{:S(2)}) collective-permute-start(bf16[128,512]{1,0:T(8,128)(2,1)S(1)} %get-tuple-element.35), channel_id=1, source_target_pairs={{0,16},{2,18},{4,20},{6,22},{8,24},{10,26},{12,28},{14,30},{16,0},... | collective-permute-start | bytes 393224 | tf_op jit(solution)/shard_map/ppermute | solution.py:306
  7.6 1.3 %collective-permute-start.6 = (bf16[128,512]{1,0:T(8,128)(2,1)S(1)}, bf16[128,512]{1,0:T(8,128)(2,1)S(1)}, u32[]{:S(2)}, u32[]{:S(2)}) collective-permute-start(bf16[128,512]{1,0:T(8,128)(2,1)S(1)} %get-tuple-element.36), channel_id=1, source_target_pairs={{0,24},{2,26},{4,28},{6,30},{8,0},{10,2},{12,4},{14,6},{16,8},{18,... | collective-permute-start | bytes 393224 | tf_op jit(solution)/shard_map/ppermute | solution.py:306
  9.9 1.6 %collective-permute-start.2 = (bf16[192,768]{1,0:T(8,128)(2,1)S(1)}, bf16[192,768]{1,0:T(8,128)(2,1)S(1)}, u32[]{:S(2)}, u32[]{:S(2)}) collective-permute-start(bf16[192,768]{1,0:T(8,128)(2,1)S(1)} %pack_go.1), channel_id=1, source_target_pairs={{0,4},{2,6},{4,0},{6,2},{8,12},{10,14},{12,8},{14,10},{16,20},{18,... | collective-permute-start | bytes 884744 | tf_op jit(solution)/shard_map/ppermute | solution.py:309
  11.5 1.2 %pack_later.1 = (bf16[128,640]{1,0:T(8,128)(2,1)S(1)}, bf16[128,640]{1,0:T(8,128)(2,1)S(1)}, bf16[128,640]{1,0:T(8,128)(2,1)S(1)}, bf16[128,640]{1,0:T(8,128)(2,1)S(1)}) custom-call(bf16[128,1536]{1,0:T(8,128)(2,1)} %refs_0_.5, bf16[128,1536]{1,0:T(8,128)(2,1)} %refs_1_.5, bf16[128,1536]{1,0:T(8,128)(2,1)} %refs_2_.5), custom_call_target="tpu_custom_call" | custom-call | bytes 1310720 | tf_op jit(solution)/shard_map/pack_later/pallas_call | solution.py:95
  13.5 1.0 %pack_stay.1.refs_0_ = bf16[192,768]{1,0:T(8,128)(2,1)S(1)} custom-call(bf16[128,1536]{1,0:T(8,128)(2,1)} %refs_0_.7, bf16[32,1536]{1,0:T(8,128)(2,1)} %refs_1_.7, bf16[32,1536]{1,0:T(8,128)(2,1)} %refs_2_.7), custom_call_target="tpu_custom_call" | custom-call | bytes 589824 | tf_op jit(solution)/shard_map/pack_stay/pallas_call | solution.py:95
  14.5 2.0 %collective-permute-done.5 = bf16[128,512]{1,0:T(8,128)(2,1)S(1)} collective-permute-done((bf16[128,512]{1,0:T(8,128)(2,1)S(1)}, bf16[128,512]{1,0:T(8,128)(2,1)S(1)}, u32[]{:S(2)}, u32[]{:S(2)}) %collective-permute-start.5) | collective-permute-done | bytes 131104 | tf_op jit(solution)/shard_map/ppermute | solution.py:306
  16.6 2.4 %collective-permute-start.9 = (bf16[512,512]{1,0:T(8,128)(2,1)S(1)}, bf16[512,512]{1,0:T(8,128)(2,1)S(1)}, u32[]{:S(2)}, u32[]{:S(2)}) collective-permute-start(bf16[512,512]{1,0:T(8,128)(2,1)S(1)} %pad_maximum_fusion), channel_id=1, source_target_pairs={{0,4},{2,6},{4,0},{6,2},{8,12},{10,14},{12,8},{14,10},{16,20},{18,... | collective-permute-start | bytes 1572872 | tf_op jit(solution)/shard_map/ppermute | solution.py:309
  20.0 3.8 %collective-permute-start.3 = (bf16[128,640]{1,0:T(8,128)(2,1)S(1)}, bf16[128,640]{1,0:T(8,128)(2,1)S(1)}, u32[]{:S(2)}, u32[]{:S(2)}) collective-permute-start(bf16[128,640]{1,0:T(8,128)(2,1)S(1)} %get-tuple-element.32), channel_id=1, source_target_pairs={{0,16},{2,18},{4,20},{6,22},{8,24},{10,26},{12,28},{14,30},{16,0},... | collective-permute-start | bytes 491528 | tf_op jit(solution)/shard_map/ppermute | solution.py:306
  23.8 3.4 %collective-permute-start.4 = (bf16[128,640]{1,0:T(8,128)(2,1)S(1)}, bf16[128,640]{1,0:T(8,128)(2,1)S(1)}, u32[]{:S(2)}, u32[]{:S(2)}) collective-permute-start(bf16[128,640]{1,0:T(8,128)(2,1)S(1)} %get-tuple-element.34), channel_id=1, source_target_pairs={{0,24},{2,26},{4,28},{6,30},{8,0},{10,2},{12,4},{14,6},{16,8},{18,... | collective-permute-start | bytes 491528 | tf_op jit(solution)/shard_map/ppermute | solution.py:306
  27.3 3.5 %collective-permute-done.9 = bf16[512,512]{1,0:T(8,128)(2,1)S(1)} collective-permute-done((bf16[512,512]{1,0:T(8,128)(2,1)S(1)}, bf16[512,512]{1,0:T(8,128)(2,1)S(1)}, u32[]{:S(2)}, u32[]{:S(2)}) %collective-permute-start.9) | collective-permute-done | bytes 524320 | tf_op jit(solution)/shard_map/ppermute | solution.py:309
  30.9 1.4 %collective-permute-done.3.refs_2_ = bf16[128,640]{1,0:T(8,128)(2,1)S(1)} collective-permute-done((bf16[128,640]{1,0:T(8,128)(2,1)S(1)}, bf16[128,640]{1,0:T(8,128)(2,1)S(1)}, u32[]{:S(2)}, u32[]{:S(2)}) %collective-permute-start.3) | collective-permute-done | bytes 163872 | tf_op jit(solution)/shard_map/ppermute | solution.py:306
  32.4 3.2 %collective-permute-done.7 = bf16[128,768]{1,0:T(8,128)(2,1)S(1)} collective-permute-done((bf16[128,768]{1,0:T(8,128)(2,1)S(1)}, bf16[128,768]{1,0:T(8,128)(2,1)S(1)}, u32[]{:S(2)}, u32[]{:S(2)}) %collective-permute-start.7) | collective-permute-done | bytes 196640 | tf_op jit(solution)/shard_map/ppermute | solution.py:309
  36.3 3.7 %collective-permute-start.11 = (bf16[128,768]{1,0:T(8,128)(2,1)S(1)}, bf16[128,768]{1,0:T(8,128)(2,1)S(1)}, u32[]{:S(2)}, u32[]{:S(2)}) collective-permute-start(bf16[128,768]{1,0:T(8,128)(2,1)S(1)} %pad_maximum_fusion.3), channel_id=1, source_target_pairs={{0,16},{2,18},{4,20},{6,22},{8,24},{10,26},{12,28},{14,30},{16,0},... | collective-permute-start | bytes 589832 | tf_op jit(solution)/shard_map/ppermute | solution.py:309
  40.0 3.9 %collective-permute-done.8 = bf16[512,256]{1,0:T(8,128)(2,1)S(1)} collective-permute-done((bf16[512,256]{1,0:T(8,128)(2,1)S(1)}, bf16[512,256]{1,0:T(8,128)(2,1)S(1)}, u32[]{:S(2)}, u32[]{:S(2)}) %collective-permute-start.8) | collective-permute-done | bytes 262176 | tf_op jit(solution)/shard_map/ppermute | solution.py:309
  43.9 4.1 %attend_0.1 = (bf16[128,256]{1,0:T(8,128)(2,1)S(1)}, bf16[128,256]{1,0:T(8,128)(2,1)S(1)}, bf16[128,256]{1,0:T(8,128)(2,1)S(1)}, bf16[128,256]{1,0:T(8,128)(2,1)S(1)}) custom-call(bf16[128,640]{1,0:T(8,128)(2,1)S(1)} %get-tuple-element.28.refs_0_, bf16[128,640]{1,0:T(8,128)(2,1)S(1)} %collective-permute-done.refs_1_, ...), custom_call_target="tpu_custom_call" | custom-call | flops 1073741824 | bytes 2097152 | tf_op jit(solution)/shard_map/attend_0/pallas_call | solution.py:170
  48.1 2.8 %collective-permute-start.18 = (bf16[128,768]{1,0:T(8,128)(2,1)S(1)}, bf16[128,768]{1,0:T(8,128)(2,1)S(1)}, u32[]{:S(2)}, u32[]{:S(2)}) collective-permute-start(bf16[128,768]{1,0:T(8,128)(2,1)S(1)} %collective-permute-done.7), channel_id=1, source_target_pairs={{0,16},{2,18},{4,20},{6,22},{8,24},{10,26},{12,28},{14,30},{16,0},... | collective-permute-start | bytes 589832 | tf_op jit(solution)/shard_map/ppermute | solution.py:309
  50.8 2.2 %attend_2.1 = (bf16[128,384]{1,0:T(8,128)(2,1)S(1)}, bf16[128,384]{1,0:T(8,128)(2,1)S(1)}, bf16[128,384]{1,0:T(8,128)(2,1)S(1)}, bf16[128,384]{1,0:T(8,128)(2,1)S(1)}) custom-call(bf16[128,640]{1,0:T(8,128)(2,1)S(1)} %get-tuple-element.28.refs_0_, bf16[128,640]{1,0:T(8,128)(2,1)S(1)} %collective-permute-done.refs_1_, ...), custom_call_target="tpu_custom_call" | custom-call | flops 536870912 | bytes 1048576 | tf_op jit(solution)/shard_map/attend_2/pallas_call | solution.py:170
  53.0 2.5 %collective-permute-start.13 = (bf16[128,384]{1,0:T(8,128)(2,1)S(1)}, bf16[128,384]{1,0:T(8,128)(2,1)S(1)}, u32[]{:S(2)}, u32[]{:S(2)}) collective-permute-start(bf16[128,384]{1,0:T(8,128)(2,1)S(1)} %get-tuple-element.47), channel_id=1, source_target_pairs={{0,24},{2,26},{4,28},{6,30},{8,0},{10,2},{12,4},{14,6},{16,8},{18,... | collective-permute-start | bytes 294920 | tf_op jit(solution)/shard_map/ppermute | solution.py:306
  55.9 1.1 %collective-permute-start.15 = (bf16[128,384]{1,0:T(8,128)(2,1)S(1)}, bf16[128,384]{1,0:T(8,128)(2,1)S(1)}, u32[]{:S(2)}, u32[]{:S(2)}) collective-permute-start(bf16[128,384]{1,0:T(8,128)(2,1)S(1)} %get-tuple-element.49), channel_id=1, source_target_pairs={{0,8},{2,10},{4,12},{6,14},{8,16},{10,18},{12,20},{14,22},{16,24},... | collective-permute-start | bytes 294920 | tf_op jit(solution)/shard_map/ppermute | solution.py:306
  57.0 1.7 %collective-permute-done.13.refs_1_ = bf16[128,384]{1,0:T(8,128)(2,1)S(1)} collective-permute-done((bf16[128,384]{1,0:T(8,128)(2,1)S(1)}, bf16[128,384]{1,0:T(8,128)(2,1)S(1)}, u32[]{:S(2)}, u32[]{:S(2)}) %collective-permute-start.13) | collective-permute-done | bytes 98336 | tf_op jit(solution)/shard_map/ppermute | solution.py:306
  58.7 10.3 %collective-permute-done.14.refs_2_ = bf16[128,384]{1,0:T(8,128)(2,1)S(1)} collective-permute-done((bf16[128,384]{1,0:T(8,128)(2,1)S(1)}, bf16[128,384]{1,0:T(8,128)(2,1)S(1)}, u32[]{:S(2)}, u32[]{:S(2)}) %collective-permute-start.14) | collective-permute-done | bytes 98336 | tf_op jit(solution)/shard_map/ppermute | solution.py:306
  69.0 1.6 %away.1 = bf16[128,2560]{1,0:T(8,128)(2,1)S(1)} custom-call(bf16[128,384]{1,0:T(8,128)(2,1)S(1)} %get-tuple-element.46.refs_0_, bf16[128,384]{1,0:T(8,128)(2,1)S(1)} %collective-permute-done.13.refs_1_, bf16[128,384]{1,0:T(8,128)(2,1)S(1)} %collective-permute-done.14.refs_2_, bf16[128,384]{1,0:T(8,128)(2,1)S(1)} %collective-permute-done.15.refs_3_, ...), custom_call_target="tpu_custom_call" | custom-call | flops 1006632960 | bytes 9175040 | tf_op jit(solution)/shard_map/away/pallas_call | solution.py:247
  70.6 1.6 %collective-permute-start.16 = (bf16[128,2560]{1,0:T(8,128)(2,1)S(1)}, bf16[128,2560]{1,0:T(8,128)(2,1)S(1)}, u32[]{:S(2)}, u32[]{:S(2)}) collective-permute-start(bf16[128,2560]{1,0:T(8,128)(2,1)S(1)} %away.1), channel_id=1, source_target_pairs={{0,1},{1,0},{2,3},{3,2},{4,5},{5,4},{6,7},{7,6},{8,9},{9,8},{10,11... | collective-permute-start | bytes 1966088 | tf_op jit(solution)/shard_map/ppermute | solution.py:376
  72.7 1.2 %collective-permute-done.19.refs_5_ = bf16[256,768]{1,0:T(8,128)(2,1)S(1)} collective-permute-done((bf16[256,768]{1,0:T(8,128)(2,1)S(1)}, bf16[256,768]{1,0:T(8,128)(2,1)S(1)}, u32[]{:S(2)}, u32[]{:S(2)}) %collective-permute-start.19) | collective-permute-done | bytes 393248 | tf_op jit(solution)/shard_map/ppermute | solution.py:309
  74.5 3.3 %cross.1 = (bf16[128,768]{1,0:T(8,128)(2,1)S(1)}, bf16[128,768]{1,0:T(8,128)(2,1)S(1)}) custom-call(bf16[192,768]{1,0:T(8,128)(2,1)S(1)} %pack_stay.1.refs_0_, bf16[192,768]{1,0:T(8,128)(2,1)S(1)} %collective-permute-done.2.refs_1_, bf16[256,768]{1,0:T(8,128)(2,1)S(1)} %pad_maximum_fusion.1.refs_2_, bf16[256,768]{1,0:T(8,128)(2,1)S(1)} %collective-permute-done.17.refs_3_, ...), custom_call_target="tpu_custom_call" | custom-call | flops 402653184 | bytes 2359296 | tf_op jit(solution)/shard_map/cross/pallas_call | solution.py:210
  77.8 1.3 %collective-permute-start.20 = (bf16[128,768]{1,0:T(8,128)(2,1)S(1)}, bf16[128,768]{1,0:T(8,128)(2,1)S(1)}, u32[]{:S(2)}, u32[]{:S(2)}) collective-permute-start(bf16[128,768]{1,0:T(8,128)(2,1)S(1)} %get-tuple-element.53), channel_id=1, source_target_pairs={{0,4},{2,6},{4,0},{6,2},{8,12},{10,14},{12,8},{14,10},{16,20},{18,... | collective-permute-start | bytes 589832 | tf_op jit(solution)/shard_map/ppermute | solution.py:309
  79.1 1.6 %home.1 = f32[128,2560]{1,0:T(8,128)S(1)} custom-call(bf16[128,384]{1,0:T(8,128)(2,1)S(1)} %get-tuple-element.46.refs_0_, bf16[128,384]{1,0:T(8,128)(2,1)S(1)} %collective-permute-done.13.refs_1_, bf16[128,384]{1,0:T(8,128)(2,1)S(1)} %collective-permute-done.14.refs_2_, bf16[128,384]{1,0:T(8,128)(2,1)S(1)} %collective-permute-done.15.refs_3_, ...), custom_call_target="tpu_custom_call" | custom-call | flops 1006632960 | bytes 9175040 | tf_op jit(solution)/shard_map/home/pallas_call | solution.py:247
  80.7 4.1 %collective-permute-done.20.came = bf16[128,768]{1,0:T(8,128)(2,1)S(1)} collective-permute-done((bf16[128,768]{1,0:T(8,128)(2,1)S(1)}, bf16[128,768]{1,0:T(8,128)(2,1)S(1)}, u32[]{:S(2)}, u32[]{:S(2)}) %collective-permute-start.20) | collective-permute-done | bytes 196640 | tf_op jit(solution)/shard_map/ppermute | solution.py:309
  84.8 2.2 %collective-permute-done.16.away = bf16[128,2560]{1,0:T(8,128)(2,1)S(1)} collective-permute-done((bf16[128,2560]{1,0:T(8,128)(2,1)S(1)}, bf16[128,2560]{1,0:T(8,128)(2,1)S(1)}, u32[]{:S(2)}, u32[]{:S(2)}) %collective-permute-start.16) | collective-permute-done | bytes 655392 | tf_op jit(solution)/shard_map/ppermute | solution.py:376
  87.0 1.2 %finish.1 = (bf16[128,2560]{1,0:T(8,128)(2,1)}, bf16[128,1536]{1,0:T(8,128)(2,1)}) custom-call(bf16[128,2560]{1,0:T(8,128)(2,1)S(1)} %copy-done.1, f32[1,2560]{1,0:T(1,128)S(1)} %broadcast_in_dim.3.gate, f32[128,2560]{1,0:T(8,128)S(1)} %home.1, bf16[128,2560]{1,0:T(8,128)(2,1)S(1)} %collective-permute-done.16.away, ...), custom_call_target="tpu_custom_call" | custom-call | bytes 3276800 | tf_op jit(solution)/shard_map/finish/pallas_call | solution.py:269
  (45 shorter events, 5.2 us)
Async XLA Ops:
  0.6 68.4 %copy-start = (bf16[1536,5120]{1,0:T(8,128)(2,1)S(1)}, bf16[1536,5120]{1,0:T(8,128)(2,1)}, u32[]{:S(2)}) copy-start(bf16[1536,5120]{1,0:T(8,128)(2,1)} %refs_4_.3) | copy-start | bytes 47185924
  2.0 12.6 %collective-permute-start.1 = (bf16[128,512]{1,0:T(8,128)(2,1)S(1)}, bf16[128,512]{1,0:T(8,128)(2,1)S(1)}, u32[]{:S(2)}, u32[]{:S(2)}) collective-permute-start(bf16[128,512]{1,0:T(8,128)(2,1)S(1)} %get-tuple-element.31), channel_id=1, source_target_pairs={{0,8},{2,10},{4,12},{6,14},{8,16},{10,18},{12,20},{14,22},{16,24},... | collective-permute-start | bytes 393224 | tf_op jit(solution)/shard_map/ppermute | solution.py:306
  5.0 11.5 %collective-permute-start.5 = (bf16[128,512]{1,0:T(8,128)(2,1)S(1)}, bf16[128,512]{1,0:T(8,128)(2,1)S(1)}, u32[]{:S(2)}, u32[]{:S(2)}) collective-permute-start(bf16[128,512]{1,0:T(8,128)(2,1)S(1)} %get-tuple-element.35), channel_id=1, source_target_pairs={{0,16},{2,18},{4,20},{6,22},{8,24},{10,26},{12,28},{14,30},{16,0},... | collective-permute-start | bytes 393224 | tf_op jit(solution)/shard_map/ppermute | solution.py:306
  7.6 8.9 %collective-permute-start.6 = (bf16[128,512]{1,0:T(8,128)(2,1)S(1)}, bf16[128,512]{1,0:T(8,128)(2,1)S(1)}, u32[]{:S(2)}, u32[]{:S(2)}) collective-permute-start(bf16[128,512]{1,0:T(8,128)(2,1)S(1)} %get-tuple-element.36), channel_id=1, source_target_pairs={{0,24},{2,26},{4,28},{6,30},{8,0},{10,2},{12,4},{14,6},{16,8},{18,... | collective-permute-start | bytes 393224 | tf_op jit(solution)/shard_map/ppermute | solution.py:306
  9.9 10.0 %collective-permute-start.2 = (bf16[192,768]{1,0:T(8,128)(2,1)S(1)}, bf16[192,768]{1,0:T(8,128)(2,1)S(1)}, u32[]{:S(2)}, u32[]{:S(2)}) collective-permute-start(bf16[192,768]{1,0:T(8,128)(2,1)S(1)} %pack_go.1), channel_id=1, source_target_pairs={{0,4},{2,6},{4,0},{6,2},{8,12},{10,14},{12,8},{14,10},{16,20},{18,... | collective-permute-start | bytes 884744 | tf_op jit(solution)/shard_map/ppermute | solution.py:309
  12.7 7.2 %collective-permute-start = (bf16[128,640]{1,0:T(8,128)(2,1)S(1)}, bf16[128,640]{1,0:T(8,128)(2,1)S(1)}, u32[]{:S(2)}, u32[]{:S(2)}) collective-permute-start(bf16[128,640]{1,0:T(8,128)(2,1)S(1)} %get-tuple-element.29), channel_id=1, source_target_pairs={{0,8},{2,10},{4,12},{6,14},{8,16},{10,18},{12,20},{14,22},{16,24},... | collective-permute-start | bytes 491528 | tf_op jit(solution)/shard_map/ppermute | solution.py:306
  14.5 64.6 %copy-start.2 = (f32[2560]{0:T(1024)S(1)}, f32[2560]{0:T(1024)}, u32[]{:S(2)}) copy-start(f32[2560]{0:T(1024)} %param.17) | copy-start | bytes 30724
  16.6 14.2 %collective-permute-start.9 = (bf16[512,512]{1,0:T(8,128)(2,1)S(1)}, bf16[512,512]{1,0:T(8,128)(2,1)S(1)}, u32[]{:S(2)}, u32[]{:S(2)}) collective-permute-start(bf16[512,512]{1,0:T(8,128)(2,1)S(1)} %pad_maximum_fusion), channel_id=1, source_target_pairs={{0,4},{2,6},{4,0},{6,2},{8,12},{10,14},{12,8},{14,10},{16,20},{18,... | collective-permute-start | bytes 1572872 | tf_op jit(solution)/shard_map/ppermute | solution.py:309
  20.0 12.4 %collective-permute-start.3 = (bf16[128,640]{1,0:T(8,128)(2,1)S(1)}, bf16[128,640]{1,0:T(8,128)(2,1)S(1)}, u32[]{:S(2)}, u32[]{:S(2)}) collective-permute-start(bf16[128,640]{1,0:T(8,128)(2,1)S(1)} %get-tuple-element.32), channel_id=1, source_target_pairs={{0,16},{2,18},{4,20},{6,22},{8,24},{10,26},{12,28},{14,30},{16,0},... | collective-permute-start | bytes 491528 | tf_op jit(solution)/shard_map/ppermute | solution.py:306
  23.8 8.6 %collective-permute-start.4 = (bf16[128,640]{1,0:T(8,128)(2,1)S(1)}, bf16[128,640]{1,0:T(8,128)(2,1)S(1)}, u32[]{:S(2)}, u32[]{:S(2)}) collective-permute-start(bf16[128,640]{1,0:T(8,128)(2,1)S(1)} %get-tuple-element.34), channel_id=1, source_target_pairs={{0,24},{2,26},{4,28},{6,30},{8,0},{10,2},{12,4},{14,6},{16,8},{18,... | collective-permute-start | bytes 491528 | tf_op jit(solution)/shard_map/ppermute | solution.py:306
  27.2 8.4 %collective-permute-start.7 = (bf16[128,768]{1,0:T(8,128)(2,1)S(1)}, bf16[128,768]{1,0:T(8,128)(2,1)S(1)}, u32[]{:S(2)}, u32[]{:S(2)}) collective-permute-start(bf16[128,768]{1,0:T(8,128)(2,1)S(1)} %pad_maximum_fusion.3), channel_id=1, source_target_pairs={{0,8},{2,10},{4,12},{6,14},{8,0},{10,2},{12,4},{14,6},{16,24},{18,... | collective-permute-start | bytes 589832 | tf_op jit(solution)/shard_map/ppermute | solution.py:309
  30.9 13.0 %collective-permute-start.10 = (bf16[1024,512]{1,0:T(8,128)(2,1)S(1)}, bf16[1024,512]{1,0:T(8,128)(2,1)S(1)}, u32[]{:S(2)}, u32[]{:S(2)}) collective-permute-start(bf16[1024,512]{1,0:T(8,128)(2,1)S(1)} %constant_dynamic-update-slice_fusion.5.refs_4_), channel_id=1, source_target_pairs={{0,2},{2,0},{4,6},{6,4},{8,10},{10,8},{12,14},{14,12},{16,18},{18,... | collective-permute-start | bytes 3145736 | tf_op jit(solution)/shard_map/ppermute | solution.py:309
  35.7 8.2 %collective-permute-start.8 = (bf16[512,256]{1,0:T(8,128)(2,1)S(1)}, bf16[512,256]{1,0:T(8,128)(2,1)S(1)}, u32[]{:S(2)}, u32[]{:S(2)}) collective-permute-start(bf16[512,256]{1,0:T(8,128)(2,1)S(1)} %pad_maximum_fusion.2), channel_id=1, source_target_pairs={{0,4},{2,6},{4,0},{6,2},{8,12},{10,14},{12,8},{14,10},{16,20},{18,... | collective-permute-start | bytes 786440 | tf_op jit(solution)/shard_map/ppermute | solution.py:309
  36.3 11.7 %collective-permute-start.11 = (bf16[128,768]{1,0:T(8,128)(2,1)S(1)}, bf16[128,768]{1,0:T(8,128)(2,1)S(1)}, u32[]{:S(2)}, u32[]{:S(2)}) collective-permute-start(bf16[128,768]{1,0:T(8,128)(2,1)S(1)} %pad_maximum_fusion.3), channel_id=1, source_target_pairs={{0,16},{2,18},{4,20},{6,22},{8,24},{10,26},{12,28},{14,30},{16,0},... | collective-permute-start | bytes 589832 | tf_op jit(solution)/shard_map/ppermute | solution.py:309
  48.0 2.8 %collective-permute-start.12 = (bf16[1024,256]{1,0:T(8,128)(2,1)S(1)}, bf16[1024,256]{1,0:T(8,128)(2,1)S(1)}, u32[]{:S(2)}, u32[]{:S(2)}) collective-permute-start(bf16[1024,256]{1,0:T(8,128)(2,1)S(1)} %constant_dynamic-update-slice_fusion.refs_4_), channel_id=1, source_target_pairs={{0,2},{2,0},{4,6},{6,4},{8,10},{10,8},{12,14},{14,12},{16,18},{18,... | collective-permute-start | bytes 1572872 | tf_op jit(solution)/shard_map/ppermute | solution.py:309
  48.1 24.0 %collective-permute-start.18 = (bf16[128,768]{1,0:T(8,128)(2,1)S(1)}, bf16[128,768]{1,0:T(8,128)(2,1)S(1)}, u32[]{:S(2)}, u32[]{:S(2)}) collective-permute-start(bf16[128,768]{1,0:T(8,128)(2,1)S(1)} %collective-permute-done.7), channel_id=1, source_target_pairs={{0,16},{2,18},{4,20},{6,22},{8,24},{10,26},{12,28},{14,30},{16,0},... | collective-permute-start | bytes 589832 | tf_op jit(solution)/shard_map/ppermute | solution.py:309
  53.0 5.7 %collective-permute-start.13 = (bf16[128,384]{1,0:T(8,128)(2,1)S(1)}, bf16[128,384]{1,0:T(8,128)(2,1)S(1)}, u32[]{:S(2)}, u32[]{:S(2)}) collective-permute-start(bf16[128,384]{1,0:T(8,128)(2,1)S(1)} %get-tuple-element.47), channel_id=1, source_target_pairs={{0,24},{2,26},{4,28},{6,30},{8,0},{10,2},{12,4},{14,6},{16,8},{18,... | collective-permute-start | bytes 294920 | tf_op jit(solution)/shard_map/ppermute | solution.py:306
  55.5 13.4 %collective-permute-start.14 = (bf16[128,384]{1,0:T(8,128)(2,1)S(1)}, bf16[128,384]{1,0:T(8,128)(2,1)S(1)}, u32[]{:S(2)}, u32[]{:S(2)}) collective-permute-start(bf16[128,384]{1,0:T(8,128)(2,1)S(1)} %get-tuple-element.48), channel_id=1, source_target_pairs={{0,16},{2,18},{4,20},{6,22},{8,24},{10,26},{12,28},{14,30},{16,0},... | collective-permute-start | bytes 294920 | tf_op jit(solution)/shard_map/ppermute | solution.py:306
  55.9 13.1 %collective-permute-start.15 = (bf16[128,384]{1,0:T(8,128)(2,1)S(1)}, bf16[128,384]{1,0:T(8,128)(2,1)S(1)}, u32[]{:S(2)}, u32[]{:S(2)}) collective-permute-start(bf16[128,384]{1,0:T(8,128)(2,1)S(1)} %get-tuple-element.49), channel_id=1, source_target_pairs={{0,8},{2,10},{4,12},{6,14},{8,16},{10,18},{12,20},{14,22},{16,24},... | collective-permute-start | bytes 294920 | tf_op jit(solution)/shard_map/ppermute | solution.py:306
  69.0 18.0 %copy-start.1 = (bf16[128,2560]{1,0:T(8,128)(2,1)S(1)}, bf16[128,2560]{1,0:T(8,128)(2,1)}, u32[]{:S(2)}) copy-start(bf16[128,2560]{1,0:T(8,128)(2,1)} %tokens.1) | copy-start | bytes 1966084
  70.6 16.4 %collective-permute-start.16 = (bf16[128,2560]{1,0:T(8,128)(2,1)S(1)}, bf16[128,2560]{1,0:T(8,128)(2,1)S(1)}, u32[]{:S(2)}, u32[]{:S(2)}) collective-permute-start(bf16[128,2560]{1,0:T(8,128)(2,1)S(1)} %away.1), channel_id=1, source_target_pairs={{0,1},{1,0},{2,3},{3,2},{4,5},{5,4},{6,7},{7,6},{8,9},{9,8},{10,11... | collective-permute-start | bytes 1966088 | tf_op jit(solution)/shard_map/ppermute | solution.py:376
  72.2 1.8 %collective-permute-start.19 = (bf16[256,768]{1,0:T(8,128)(2,1)S(1)}, bf16[256,768]{1,0:T(8,128)(2,1)S(1)}, u32[]{:S(2)}, u32[]{:S(2)}) collective-permute-start(bf16[256,768]{1,0:T(8,128)(2,1)S(1)} %constant_dynamic-update-slice_fusion.10.refs_4_), channel_id=1, source_target_pairs={{0,2},{2,0},{4,6},{6,4},{8,10},{10,8},{12,14},{14,12},{16,18},{18,... | collective-permute-start | bytes 1179656 | tf_op jit(solution)/shard_map/ppermute | solution.py:309
  72.2 2.3 %collective-permute-start.17 = (bf16[256,768]{1,0:T(8,128)(2,1)S(1)}, bf16[256,768]{1,0:T(8,128)(2,1)S(1)}, u32[]{:S(2)}, u32[]{:S(2)}) collective-permute-start(bf16[256,768]{1,0:T(8,128)(2,1)S(1)} %pad_maximum_fusion.1.refs_2_), channel_id=1, source_target_pairs={{0,2},{2,0},{4,6},{6,4},{8,10},{10,8},{12,14},{14,12},{16,18},{18,... | collective-permute-start | bytes 1179656 | tf_op jit(solution)/shard_map/ppermute | solution.py:309
  77.8 7.0 %collective-permute-start.20 = (bf16[128,768]{1,0:T(8,128)(2,1)S(1)}, bf16[128,768]{1,0:T(8,128)(2,1)S(1)}, u32[]{:S(2)}, u32[]{:S(2)}) collective-permute-start(bf16[128,768]{1,0:T(8,128)(2,1)S(1)} %get-tuple-element.53), channel_id=1, source_target_pairs={{0,4},{2,6},{4,0},{6,2},{8,12},{10,14},{12,8},{14,10},{16,20},{18,... | collective-permute-start | bytes 589832 | tf_op jit(solution)/shard_map/ppermute | solution.py:309

commit v7 on v6

--- a/solution.py
+++ b/solution.py
@@ -365,7 +365,7 @@
     beyond = swap(after(caption, second[1:]), 2 * members)
     pairs_second = [half_second, swap(after(half_second, (outs, beyond)), 1)]
     outs = attend(second, at, pairs_second, outs, chunks[1], factor)
-    last = swap(after(pair[2 * cap_rows * 2 :], beyond), 2 * members)
+    last = swap(after(beyond, outs), members)
     other = join(beyond, last)
     lhs = [rotate(x, groups - r) for r, x in enumerate(outs)]
 

time: 88.4 us -> 84.3 us (0.954)
  waiting for transfers between devices: 35.1 us -> 30.6 us
    ppermute x9, waiting for transfers between devices: 16.4 us -> 10.4 us  [rotate(): lax.ppermute(x, 'seq', [(s, (s + step) % seq_size) for s in range(seq_siz...]
    ppermute x1, waiting for transfers between devices: 2.18 us -> 5.96 us  [shards(): away = lax.ppermute(away, 'tp', [(0, 1), (1, 0)])]
    ppermute x11, waiting for transfers between devices: 16.5 us -> 14.2 us  [swap(): return lax.ppermute(x, 'seq', [(s, s ^ by) for s in range(seq_size)])]
  transfers between devices with their start and end apart: 21 -> 21, of which waited for: 12 -> 11; matrix products, arithmetic and copies ran while one was open for 0% -> 0% of each run, Pallas kernels for 18% -> 16%
where the time goes in v7:
time: 84.3 us; the launch traced here: 84 us
  starting transfers between devices  34 us (40%)
  waiting for transfers between devices  30.6 us (36%)
  Pallas kernels  18.3 us (22%)
  between operations  0.9 us (1%)
    ppermute x9, starting transfers between devices, rotate(): lax.ppermute(x, 'seq', [(s, (s + step) % seq_size) for s in range(seq_siz...  19.7 us
    ppermute x11, waiting for transfers between devices, swap(): return lax.ppermute(x, 'seq', [(s, s ^ by) for s in range(seq_size)])  14.2 us
    ppermute x11, starting transfers between devices, swap(): return lax.ppermute(x, 'seq', [(s, s ^ by) for s in range(seq_size)])  12.7 us
    ppermute x9, waiting for transfers between devices, rotate(): lax.ppermute(x, 'seq', [(s, (s + step) % seq_size) for s in range(seq_siz...  10.4 us
    pallas_call x2, Pallas kernels, attend(): pl.pallas_call(kernel, out_shape=[shape(rows, before + heads * DH)] * par...  6.29 us
    ppermute x1, waiting for transfers between devices, shards(): away = lax.ppermute(away, 'tp', [(0, 1), (1, 0)])  5.96 us
    pallas_call x4, Pallas kernels, pack(): pl.pallas_call(kernel, out_shape=out_shapes, in_specs=[in_hbm()] * len(so...  4.49 us
    pallas_call x1, Pallas kernels, cross(): pl.pallas_call(kernel, out_shape=[shape(rows, columns)] * parts, in_specs...  3.25 us
  transfers between devices with their start and end apart: 21, of which 11 were waited for; matrix products, arithmetic and copies ran while one was open for 0% of the time, Pallas kernels for 16%

profile of v7, /device:TPU:0, one launch (start us, length us, event | category | flops | bytes accessed | tf_op | source)
XLA Modules:
  0.0 84.0 jit_solution(9279566451815636359)
XLA Ops:
  0.6 1.3 %pack_first.1 = (bf16[128,512]{1,0:T(8,128)(2,1)S(1)}, bf16[128,512]{1,0:T(8,128)(2,1)S(1)}, bf16[128,512]{1,0:T(8,128)(2,1)S(1)}, bf16[128,512]{1,0:T(8,128)(2,1)S(1)}) custom-call(bf16[128,1536]{1,0:T(8,128)(2,1)} %refs_0_.5, bf16[128,1536]{1,0:T(8,128)(2,1)} %refs_1_.5, bf16[128,1536]{1,0:T(8,128)(2,1)} %refs_2_.5), custom_call_target="tpu_custom_call" | custom-call | bytes 1048576 | tf_op jit(solution)/shard_map/pack_first/pallas_call | solution.py:95
  2.0 3.1 %collective-permute-start.1 = (bf16[128,512]{1,0:T(8,128)(2,1)S(1)}, bf16[128,512]{1,0:T(8,128)(2,1)S(1)}, u32[]{:S(2)}, u32[]{:S(2)}) collective-permute-start(bf16[128,512]{1,0:T(8,128)(2,1)S(1)} %get-tuple-element.31), channel_id=1, source_target_pairs={{0,8},{2,10},{4,12},{6,14},{8,16},{10,18},{12,20},{14,22},{16,24},... | collective-permute-start | bytes 393224 | tf_op jit(solution)/shard_map/ppermute | solution.py:306
  5.0 2.6 %collective-permute-start.5 = (bf16[128,512]{1,0:T(8,128)(2,1)S(1)}, bf16[128,512]{1,0:T(8,128)(2,1)S(1)}, u32[]{:S(2)}, u32[]{:S(2)}) collective-permute-start(bf16[128,512]{1,0:T(8,128)(2,1)S(1)} %get-tuple-element.35), channel_id=1, source_target_pairs={{0,16},{2,18},{4,20},{6,22},{8,24},{10,26},{12,28},{14,30},{16,0},... | collective-permute-start | bytes 393224 | tf_op jit(solution)/shard_map/ppermute | solution.py:306
  7.6 1.3 %collective-permute-start.6 = (bf16[128,512]{1,0:T(8,128)(2,1)S(1)}, bf16[128,512]{1,0:T(8,128)(2,1)S(1)}, u32[]{:S(2)}, u32[]{:S(2)}) collective-permute-start(bf16[128,512]{1,0:T(8,128)(2,1)S(1)} %get-tuple-element.36), channel_id=1, source_target_pairs={{0,24},{2,26},{4,28},{6,30},{8,0},{10,2},{12,4},{14,6},{16,8},{18,... | collective-permute-start | bytes 393224 | tf_op jit(solution)/shard_map/ppermute | solution.py:306
  9.0 1.0 %pack_go.1 = bf16[192,768]{1,0:T(8,128)(2,1)S(1)} custom-call(bf16[128,1536]{1,0:T(8,128)(2,1)} %refs_0_.7, bf16[32,1536]{1,0:T(8,128)(2,1)} %refs_1_.7, bf16[32,1536]{1,0:T(8,128)(2,1)} %refs_2_.7), custom_call_target="tpu_custom_call" | custom-call | bytes 589824 | tf_op jit(solution)/shard_map/pack_go/pallas_call | solution.py:95
  9.9 1.6 %collective-permute-start.2 = (bf16[192,768]{1,0:T(8,128)(2,1)S(1)}, bf16[192,768]{1,0:T(8,128)(2,1)S(1)}, u32[]{:S(2)}, u32[]{:S(2)}) collective-permute-start(bf16[192,768]{1,0:T(8,128)(2,1)S(1)} %pack_go.1), channel_id=1, source_target_pairs={{0,4},{2,6},{4,0},{6,2},{8,12},{10,14},{12,8},{14,10},{16,20},{18,... | collective-permute-start | bytes 884744 | tf_op jit(solution)/shard_map/ppermute | solution.py:309
  11.5 1.2 %pack_later.1 = (bf16[128,640]{1,0:T(8,128)(2,1)S(1)}, bf16[128,640]{1,0:T(8,128)(2,1)S(1)}, bf16[128,640]{1,0:T(8,128)(2,1)S(1)}, bf16[128,640]{1,0:T(8,128)(2,1)S(1)}) custom-call(bf16[128,1536]{1,0:T(8,128)(2,1)} %refs_0_.5, bf16[128,1536]{1,0:T(8,128)(2,1)} %refs_1_.5, bf16[128,1536]{1,0:T(8,128)(2,1)} %refs_2_.5), custom_call_target="tpu_custom_call" | custom-call | bytes 1310720 | tf_op jit(solution)/shard_map/pack_later/pallas_call | solution.py:95
  13.5 1.0 %pack_stay.1.refs_0_ = bf16[192,768]{1,0:T(8,128)(2,1)S(1)} custom-call(bf16[128,1536]{1,0:T(8,128)(2,1)} %refs_0_.7, bf16[32,1536]{1,0:T(8,128)(2,1)} %refs_1_.7, bf16[32,1536]{1,0:T(8,128)(2,1)} %refs_2_.7), custom_call_target="tpu_custom_call" | custom-call | bytes 589824 | tf_op jit(solution)/shard_map/pack_stay/pallas_call | solution.py:95
  14.5 2.0 %collective-permute-done.5 = bf16[128,512]{1,0:T(8,128)(2,1)S(1)} collective-permute-done((bf16[128,512]{1,0:T(8,128)(2,1)S(1)}, bf16[128,512]{1,0:T(8,128)(2,1)S(1)}, u32[]{:S(2)}, u32[]{:S(2)}) %collective-permute-start.5) | collective-permute-done | bytes 131104 | tf_op jit(solution)/shard_map/ppermute | solution.py:306
  16.6 2.4 %collective-permute-start.9 = (bf16[512,512]{1,0:T(8,128)(2,1)S(1)}, bf16[512,512]{1,0:T(8,128)(2,1)S(1)}, u32[]{:S(2)}, u32[]{:S(2)}) collective-permute-start(bf16[512,512]{1,0:T(8,128)(2,1)S(1)} %pad_maximum_fusion), channel_id=1, source_target_pairs={{0,4},{2,6},{4,0},{6,2},{8,12},{10,14},{12,8},{14,10},{16,20},{18,... | collective-permute-start | bytes 1572872 | tf_op jit(solution)/shard_map/ppermute | solution.py:309
  20.0 3.8 %collective-permute-start.3 = (bf16[128,640]{1,0:T(8,128)(2,1)S(1)}, bf16[128,640]{1,0:T(8,128)(2,1)S(1)}, u32[]{:S(2)}, u32[]{:S(2)}) collective-permute-start(bf16[128,640]{1,0:T(8,128)(2,1)S(1)} %get-tuple-element.32), channel_id=1, source_target_pairs={{0,16},{2,18},{4,20},{6,22},{8,24},{10,26},{12,28},{14,30},{16,0},... | collective-permute-start | bytes 491528 | tf_op jit(solution)/shard_map/ppermute | solution.py:306
  23.8 3.4 %collective-permute-start.4 = (bf16[128,640]{1,0:T(8,128)(2,1)S(1)}, bf16[128,640]{1,0:T(8,128)(2,1)S(1)}, u32[]{:S(2)}, u32[]{:S(2)}) collective-permute-start(bf16[128,640]{1,0:T(8,128)(2,1)S(1)} %get-tuple-element.34), channel_id=1, source_target_pairs={{0,24},{2,26},{4,28},{6,30},{8,0},{10,2},{12,4},{14,6},{16,8},{18,... | collective-permute-start | bytes 491528 | tf_op jit(solution)/shard_map/ppermute | solution.py:306
  27.3 3.5 %collective-permute-done.9 = bf16[512,512]{1,0:T(8,128)(2,1)S(1)} collective-permute-done((bf16[512,512]{1,0:T(8,128)(2,1)S(1)}, bf16[512,512]{1,0:T(8,128)(2,1)S(1)}, u32[]{:S(2)}, u32[]{:S(2)}) %collective-permute-start.9) | collective-permute-done | bytes 524320 | tf_op jit(solution)/shard_map/ppermute | solution.py:309
  30.9 1.4 %collective-permute-done.3.refs_2_ = bf16[128,640]{1,0:T(8,128)(2,1)S(1)} collective-permute-done((bf16[128,640]{1,0:T(8,128)(2,1)S(1)}, bf16[128,640]{1,0:T(8,128)(2,1)S(1)}, u32[]{:S(2)}, u32[]{:S(2)}) %collective-permute-start.3) | collective-permute-done | bytes 163872 | tf_op jit(solution)/shard_map/ppermute | solution.py:306
  32.4 3.2 %collective-permute-done.7 = bf16[128,768]{1,0:T(8,128)(2,1)S(1)} collective-permute-done((bf16[128,768]{1,0:T(8,128)(2,1)S(1)}, bf16[128,768]{1,0:T(8,128)(2,1)S(1)}, u32[]{:S(2)}, u32[]{:S(2)}) %collective-permute-start.7) | collective-permute-done | bytes 196640 | tf_op jit(solution)/shard_map/ppermute | solution.py:309
  36.3 3.7 %collective-permute-start.11 = (bf16[128,768]{1,0:T(8,128)(2,1)S(1)}, bf16[128,768]{1,0:T(8,128)(2,1)S(1)}, u32[]{:S(2)}, u32[]{:S(2)}) collective-permute-start(bf16[128,768]{1,0:T(8,128)(2,1)S(1)} %pad_maximum_fusion.3), channel_id=1, source_target_pairs={{0,16},{2,18},{4,20},{6,22},{8,24},{10,26},{12,28},{14,30},{16,0},... | collective-permute-start | bytes 589832 | tf_op jit(solution)/shard_map/ppermute | solution.py:309
  40.0 3.9 %collective-permute-done.8 = bf16[512,256]{1,0:T(8,128)(2,1)S(1)} collective-permute-done((bf16[512,256]{1,0:T(8,128)(2,1)S(1)}, bf16[512,256]{1,0:T(8,128)(2,1)S(1)}, u32[]{:S(2)}, u32[]{:S(2)}) %collective-permute-start.8) | collective-permute-done | bytes 262176 | tf_op jit(solution)/shard_map/ppermute | solution.py:309
  43.9 4.1 %attend_0.1 = (bf16[128,256]{1,0:T(8,128)(2,1)S(1)}, bf16[128,256]{1,0:T(8,128)(2,1)S(1)}, bf16[128,256]{1,0:T(8,128)(2,1)S(1)}, bf16[128,256]{1,0:T(8,128)(2,1)S(1)}) custom-call(bf16[128,640]{1,0:T(8,128)(2,1)S(1)} %get-tuple-element.28.refs_0_, bf16[128,640]{1,0:T(8,128)(2,1)S(1)} %collective-permute-done.refs_1_, ...), custom_call_target="tpu_custom_call" | custom-call | flops 1073741824 | bytes 2097152 | tf_op jit(solution)/shard_map/attend_0/pallas_call | solution.py:170
  48.1 1.9 %collective-permute-done.12.refs_5_ = bf16[1024,256]{1,0:T(8,128)(2,1)S(1)} collective-permute-done((bf16[1024,256]{1,0:T(8,128)(2,1)S(1)}, bf16[1024,256]{1,0:T(8,128)(2,1)S(1)}, u32[]{:S(2)}, u32[]{:S(2)}) %collective-permute-start.12) | collective-permute-done | bytes 524320 | tf_op jit(solution)/shard_map/ppermute | solution.py:309
  50.0 2.2 %attend_2.1 = (bf16[128,384]{1,0:T(8,128)(2,1)S(1)}, bf16[128,384]{1,0:T(8,128)(2,1)S(1)}, bf16[128,384]{1,0:T(8,128)(2,1)S(1)}, bf16[128,384]{1,0:T(8,128)(2,1)S(1)}) custom-call(bf16[128,640]{1,0:T(8,128)(2,1)S(1)} %get-tuple-element.28.refs_0_, bf16[128,640]{1,0:T(8,128)(2,1)S(1)} %collective-permute-done.refs_1_, ...), custom_call_target="tpu_custom_call" | custom-call | flops 536870912 | bytes 1048576 | tf_op jit(solution)/shard_map/attend_2/pallas_call | solution.py:170
  52.2 3.4 %collective-permute-start.13 = (bf16[128,384]{1,0:T(8,128)(2,1)S(1)}, bf16[128,384]{1,0:T(8,128)(2,1)S(1)}, u32[]{:S(2)}, u32[]{:S(2)}) collective-permute-start(bf16[128,384]{1,0:T(8,128)(2,1)S(1)} %get-tuple-element.47), channel_id=1, source_target_pairs={{0,24},{2,26},{4,28},{6,30},{8,0},{10,2},{12,4},{14,6},{16,8},{18,... | collective-permute-start | bytes 294920 | tf_op jit(solution)/shard_map/ppermute | solution.py:306
  55.9 1.1 %collective-permute-start.15 = (bf16[128,384]{1,0:T(8,128)(2,1)S(1)}, bf16[128,384]{1,0:T(8,128)(2,1)S(1)}, u32[]{:S(2)}, u32[]{:S(2)}) collective-permute-start(bf16[128,384]{1,0:T(8,128)(2,1)S(1)} %get-tuple-element.49), channel_id=1, source_target_pairs={{0,8},{2,10},{4,12},{6,14},{8,16},{10,18},{12,20},{14,22},{16,24},... | collective-permute-start | bytes 294920 | tf_op jit(solution)/shard_map/ppermute | solution.py:306
  56.9 2.1 %collective-permute-start.18 = (bf16[128,768]{1,0:T(8,128)(2,1)S(1)}, bf16[128,768]{1,0:T(8,128)(2,1)S(1)}, u32[]{:S(2)}, u32[]{:S(2)}) collective-permute-start(bf16[128,768]{1,0:T(8,128)(2,1)S(1)} %collective-permute-done.11), channel_id=1, source_target_pairs={{0,8},{2,10},{4,12},{6,14},{8,0},{10,2},{12,4},{14,6},{16,24},{18,... | collective-permute-start | bytes 589832 | tf_op jit(solution)/shard_map/ppermute | solution.py:309
  59.1 6.0 %collective-permute-done.14.refs_2_ = bf16[128,384]{1,0:T(8,128)(2,1)S(1)} collective-permute-done((bf16[128,384]{1,0:T(8,128)(2,1)S(1)}, bf16[128,384]{1,0:T(8,128)(2,1)S(1)}, u32[]{:S(2)}, u32[]{:S(2)}) %collective-permute-start.14) | collective-permute-done | bytes 98336 | tf_op jit(solution)/shard_map/ppermute | solution.py:306
  65.1 1.5 %away.1 = bf16[128,2560]{1,0:T(8,128)(2,1)S(1)} custom-call(bf16[128,384]{1,0:T(8,128)(2,1)S(1)} %get-tuple-element.46.refs_0_, bf16[128,384]{1,0:T(8,128)(2,1)S(1)} %collective-permute-done.13.refs_1_, bf16[128,384]{1,0:T(8,128)(2,1)S(1)} %collective-permute-done.14.refs_2_, bf16[128,384]{1,0:T(8,128)(2,1)S(1)} %collective-permute-done.15.refs_3_, ...), custom_call_target="tpu_custom_call" | custom-call | flops 1006632960 | bytes 9175040 | tf_op jit(solution)/shard_map/away/pallas_call | solution.py:247
  66.6 1.6 %collective-permute-start.16 = (bf16[128,2560]{1,0:T(8,128)(2,1)S(1)}, bf16[128,2560]{1,0:T(8,128)(2,1)S(1)}, u32[]{:S(2)}, u32[]{:S(2)}) collective-permute-start(bf16[128,2560]{1,0:T(8,128)(2,1)S(1)} %away.1), channel_id=1, source_target_pairs={{0,1},{1,0},{2,3},{3,2},{4,5},{5,4},{6,7},{7,6},{8,9},{9,8},{10,11... | collective-permute-start | bytes 1966088 | tf_op jit(solution)/shard_map/ppermute | solution.py:376
  68.8 1.1 %collective-permute-done.17.refs_3_ = bf16[256,768]{1,0:T(8,128)(2,1)S(1)} collective-permute-done((bf16[256,768]{1,0:T(8,128)(2,1)S(1)}, bf16[256,768]{1,0:T(8,128)(2,1)S(1)}, u32[]{:S(2)}, u32[]{:S(2)}) %collective-permute-start.17) | collective-permute-done | bytes 393248 | tf_op jit(solution)/shard_map/ppermute | solution.py:309
  70.5 3.3 %cross.1 = (bf16[128,768]{1,0:T(8,128)(2,1)S(1)}, bf16[128,768]{1,0:T(8,128)(2,1)S(1)}) custom-call(bf16[192,768]{1,0:T(8,128)(2,1)S(1)} %pack_stay.1.refs_0_, bf16[192,768]{1,0:T(8,128)(2,1)S(1)} %collective-permute-done.2.refs_1_, bf16[256,768]{1,0:T(8,128)(2,1)S(1)} %pad_maximum_fusion.1.refs_2_, bf16[256,768]{1,0:T(8,128)(2,1)S(1)} %collective-permute-done.17.refs_3_, ...), custom_call_target="tpu_custom_call" | custom-call | flops 402653184 | bytes 2359296 | tf_op jit(solution)/shard_map/cross/pallas_call | solution.py:210
  73.8 1.6 %collective-permute-start.20 = (bf16[128,768]{1,0:T(8,128)(2,1)S(1)}, bf16[128,768]{1,0:T(8,128)(2,1)S(1)}, u32[]{:S(2)}, u32[]{:S(2)}) collective-permute-start(bf16[128,768]{1,0:T(8,128)(2,1)S(1)} %get-tuple-element.53), channel_id=1, source_target_pairs={{0,4},{2,6},{4,0},{6,2},{8,12},{10,14},{12,8},{14,10},{16,20},{18,... | collective-permute-start | bytes 589832 | tf_op jit(solution)/shard_map/ppermute | solution.py:309
  75.3 1.6 %home.1 = f32[128,2560]{1,0:T(8,128)S(1)} custom-call(bf16[128,384]{1,0:T(8,128)(2,1)S(1)} %get-tuple-element.46.refs_0_, bf16[128,384]{1,0:T(8,128)(2,1)S(1)} %collective-permute-done.13.refs_1_, bf16[128,384]{1,0:T(8,128)(2,1)S(1)} %collective-permute-done.14.refs_2_, bf16[128,384]{1,0:T(8,128)(2,1)S(1)} %collective-permute-done.15.refs_3_, ...), custom_call_target="tpu_custom_call" | custom-call | flops 1006632960 | bytes 9175040 | tf_op jit(solution)/shard_map/home/pallas_call | solution.py:247
  76.9 6.0 %collective-permute-done.16.away = bf16[128,2560]{1,0:T(8,128)(2,1)S(1)} collective-permute-done((bf16[128,2560]{1,0:T(8,128)(2,1)S(1)}, bf16[128,2560]{1,0:T(8,128)(2,1)S(1)}, u32[]{:S(2)}, u32[]{:S(2)}) %collective-permute-start.16) | collective-permute-done | bytes 655392 | tf_op jit(solution)/shard_map/ppermute | solution.py:376
  82.9 1.2 %finish.1 = (bf16[128,2560]{1,0:T(8,128)(2,1)}, bf16[128,1536]{1,0:T(8,128)(2,1)}) custom-call(bf16[128,2560]{1,0:T(8,128)(2,1)S(1)} %copy-done.1, f32[1,2560]{1,0:T(1,128)S(1)} %broadcast_in_dim.3.gate, f32[128,2560]{1,0:T(8,128)S(1)} %home.1, bf16[128,2560]{1,0:T(8,128)(2,1)S(1)} %collective-permute-done.16.away, ...), custom_call_target="tpu_custom_call" | custom-call | bytes 3276800 | tf_op jit(solution)/shard_map/finish/pallas_call | solution.py:269
  (45 shorter events, 4.3 us)
Async XLA Ops:
  0.6 64.4 %copy-start = (bf16[1536,5120]{1,0:T(8,128)(2,1)S(1)}, bf16[1536,5120]{1,0:T(8,128)(2,1)}, u32[]{:S(2)}) copy-start(bf16[1536,5120]{1,0:T(8,128)(2,1)} %refs_4_.3) | copy-start | bytes 47185924
  2.0 12.6 %collective-permute-start.1 = (bf16[128,512]{1,0:T(8,128)(2,1)S(1)}, bf16[128,512]{1,0:T(8,128)(2,1)S(1)}, u32[]{:S(2)}, u32[]{:S(2)}) collective-permute-start(bf16[128,512]{1,0:T(8,128)(2,1)S(1)} %get-tuple-element.31), channel_id=1, source_target_pairs={{0,8},{2,10},{4,12},{6,14},{8,16},{10,18},{12,20},{14,22},{16,24},... | collective-permute-start | bytes 393224 | tf_op jit(solution)/shard_map/ppermute | solution.py:306
  5.0 11.5 %collective-permute-start.5 = (bf16[128,512]{1,0:T(8,128)(2,1)S(1)}, bf16[128,512]{1,0:T(8,128)(2,1)S(1)}, u32[]{:S(2)}, u32[]{:S(2)}) collective-permute-start(bf16[128,512]{1,0:T(8,128)(2,1)S(1)} %get-tuple-element.35), channel_id=1, source_target_pairs={{0,16},{2,18},{4,20},{6,22},{8,24},{10,26},{12,28},{14,30},{16,0},... | collective-permute-start | bytes 393224 | tf_op jit(solution)/shard_map/ppermute | solution.py:306
  7.6 8.9 %collective-permute-start.6 = (bf16[128,512]{1,0:T(8,128)(2,1)S(1)}, bf16[128,512]{1,0:T(8,128)(2,1)S(1)}, u32[]{:S(2)}, u32[]{:S(2)}) collective-permute-start(bf16[128,512]{1,0:T(8,128)(2,1)S(1)} %get-tuple-element.36), channel_id=1, source_target_pairs={{0,24},{2,26},{4,28},{6,30},{8,0},{10,2},{12,4},{14,6},{16,8},{18,... | collective-permute-start | bytes 393224 | tf_op jit(solution)/shard_map/ppermute | solution.py:306
  9.9 10.0 %collective-permute-start.2 = (bf16[192,768]{1,0:T(8,128)(2,1)S(1)}, bf16[192,768]{1,0:T(8,128)(2,1)S(1)}, u32[]{:S(2)}, u32[]{:S(2)}) collective-permute-start(bf16[192,768]{1,0:T(8,128)(2,1)S(1)} %pack_go.1), channel_id=1, source_target_pairs={{0,4},{2,6},{4,0},{6,2},{8,12},{10,14},{12,8},{14,10},{16,20},{18,... | collective-permute-start | bytes 884744 | tf_op jit(solution)/shard_map/ppermute | solution.py:309
  12.7 7.2 %collective-permute-start = (bf16[128,640]{1,0:T(8,128)(2,1)S(1)}, bf16[128,640]{1,0:T(8,128)(2,1)S(1)}, u32[]{:S(2)}, u32[]{:S(2)}) collective-permute-start(bf16[128,640]{1,0:T(8,128)(2,1)S(1)} %get-tuple-element.29), channel_id=1, source_target_pairs={{0,8},{2,10},{4,12},{6,14},{8,16},{10,18},{12,20},{14,22},{16,24},... | collective-permute-start | bytes 491528 | tf_op jit(solution)/shard_map/ppermute | solution.py:306
  14.5 60.8 %copy-start.2 = (f32[2560]{0:T(1024)S(1)}, f32[2560]{0:T(1024)}, u32[]{:S(2)}) copy-start(f32[2560]{0:T(1024)} %param.17) | copy-start | bytes 30724
  16.6 14.2 %collective-permute-start.9 = (bf16[512,512]{1,0:T(8,128)(2,1)S(1)}, bf16[512,512]{1,0:T(8,128)(2,1)S(1)}, u32[]{:S(2)}, u32[]{:S(2)}) collective-permute-start(bf16[512,512]{1,0:T(8,128)(2,1)S(1)} %pad_maximum_fusion), channel_id=1, source_target_pairs={{0,4},{2,6},{4,0},{6,2},{8,12},{10,14},{12,8},{14,10},{16,20},{18,... | collective-permute-start | bytes 1572872 | tf_op jit(solution)/shard_map/ppermute | solution.py:309
  20.0 12.4 %collective-permute-start.3 = (bf16[128,640]{1,0:T(8,128)(2,1)S(1)}, bf16[128,640]{1,0:T(8,128)(2,1)S(1)}, u32[]{:S(2)}, u32[]{:S(2)}) collective-permute-start(bf16[128,640]{1,0:T(8,128)(2,1)S(1)} %get-tuple-element.32), channel_id=1, source_target_pairs={{0,16},{2,18},{4,20},{6,22},{8,24},{10,26},{12,28},{14,30},{16,0},... | collective-permute-start | bytes 491528 | tf_op jit(solution)/shard_map/ppermute | solution.py:306
  23.8 8.6 %collective-permute-start.4 = (bf16[128,640]{1,0:T(8,128)(2,1)S(1)}, bf16[128,640]{1,0:T(8,128)(2,1)S(1)}, u32[]{:S(2)}, u32[]{:S(2)}) collective-permute-start(bf16[128,640]{1,0:T(8,128)(2,1)S(1)} %get-tuple-element.34), channel_id=1, source_target_pairs={{0,24},{2,26},{4,28},{6,30},{8,0},{10,2},{12,4},{14,6},{16,8},{18,... | collective-permute-start | bytes 491528 | tf_op jit(solution)/shard_map/ppermute | solution.py:306
  27.2 8.4 %collective-permute-start.7 = (bf16[128,768]{1,0:T(8,128)(2,1)S(1)}, bf16[128,768]{1,0:T(8,128)(2,1)S(1)}, u32[]{:S(2)}, u32[]{:S(2)}) collective-permute-start(bf16[128,768]{1,0:T(8,128)(2,1)S(1)} %pad_maximum_fusion.3), channel_id=1, source_target_pairs={{0,8},{2,10},{4,12},{6,14},{8,0},{10,2},{12,4},{14,6},{16,24},{18,... | collective-permute-start | bytes 589832 | tf_op jit(solution)/shard_map/ppermute | solution.py:309
  30.9 13.0 %collective-permute-start.10 = (bf16[1024,512]{1,0:T(8,128)(2,1)S(1)}, bf16[1024,512]{1,0:T(8,128)(2,1)S(1)}, u32[]{:S(2)}, u32[]{:S(2)}) collective-permute-start(bf16[1024,512]{1,0:T(8,128)(2,1)S(1)} %constant_dynamic-update-slice_fusion.5.refs_4_), channel_id=1, source_target_pairs={{0,2},{2,0},{4,6},{6,4},{8,10},{10,8},{12,14},{14,12},{16,18},{18,... | collective-permute-start | bytes 3145736 | tf_op jit(solution)/shard_map/ppermute | solution.py:309
  35.7 8.2 %collective-permute-start.8 = (bf16[512,256]{1,0:T(8,128)(2,1)S(1)}, bf16[512,256]{1,0:T(8,128)(2,1)S(1)}, u32[]{:S(2)}, u32[]{:S(2)}) collective-permute-start(bf16[512,256]{1,0:T(8,128)(2,1)S(1)} %pad_maximum_fusion.2), channel_id=1, source_target_pairs={{0,4},{2,6},{4,0},{6,2},{8,12},{10,14},{12,8},{14,10},{16,20},{18,... | collective-permute-start | bytes 786440 | tf_op jit(solution)/shard_map/ppermute | solution.py:309
  36.3 11.7 %collective-permute-start.11 = (bf16[128,768]{1,0:T(8,128)(2,1)S(1)}, bf16[128,768]{1,0:T(8,128)(2,1)S(1)}, u32[]{:S(2)}, u32[]{:S(2)}) collective-permute-start(bf16[128,768]{1,0:T(8,128)(2,1)S(1)} %pad_maximum_fusion.3), channel_id=1, source_target_pairs={{0,16},{2,18},{4,20},{6,22},{8,24},{10,26},{12,28},{14,30},{16,0},... | collective-permute-start | bytes 589832 | tf_op jit(solution)/shard_map/ppermute | solution.py:309
  48.0 2.0 %collective-permute-start.12 = (bf16[1024,256]{1,0:T(8,128)(2,1)S(1)}, bf16[1024,256]{1,0:T(8,128)(2,1)S(1)}, u32[]{:S(2)}, u32[]{:S(2)}) collective-permute-start(bf16[1024,256]{1,0:T(8,128)(2,1)S(1)} %constant_dynamic-update-slice_fusion.refs_4_), channel_id=1, source_target_pairs={{0,2},{2,0},{4,6},{6,4},{8,10},{10,8},{12,14},{14,12},{16,18},{18,... | collective-permute-start | bytes 1572872 | tf_op jit(solution)/shard_map/ppermute | solution.py:309
  52.2 6.9 %collective-permute-start.13 = (bf16[128,384]{1,0:T(8,128)(2,1)S(1)}, bf16[128,384]{1,0:T(8,128)(2,1)S(1)}, u32[]{:S(2)}, u32[]{:S(2)}) collective-permute-start(bf16[128,384]{1,0:T(8,128)(2,1)S(1)} %get-tuple-element.47), channel_id=1, source_target_pairs={{0,24},{2,26},{4,28},{6,30},{8,0},{10,2},{12,4},{14,6},{16,8},{18,... | collective-permute-start | bytes 294920 | tf_op jit(solution)/shard_map/ppermute | solution.py:306
  55.5 9.5 %collective-permute-start.14 = (bf16[128,384]{1,0:T(8,128)(2,1)S(1)}, bf16[128,384]{1,0:T(8,128)(2,1)S(1)}, u32[]{:S(2)}, u32[]{:S(2)}) collective-permute-start(bf16[128,384]{1,0:T(8,128)(2,1)S(1)} %get-tuple-element.48), channel_id=1, source_target_pairs={{0,16},{2,18},{4,20},{6,22},{8,24},{10,26},{12,28},{14,30},{16,0},... | collective-permute-start | bytes 294920 | tf_op jit(solution)/shard_map/ppermute | solution.py:306
  55.9 9.2 %collective-permute-start.15 = (bf16[128,384]{1,0:T(8,128)(2,1)S(1)}, bf16[128,384]{1,0:T(8,128)(2,1)S(1)}, u32[]{:S(2)}, u32[]{:S(2)}) collective-permute-start(bf16[128,384]{1,0:T(8,128)(2,1)S(1)} %get-tuple-element.49), channel_id=1, source_target_pairs={{0,8},{2,10},{4,12},{6,14},{8,16},{10,18},{12,20},{14,22},{16,24},... | collective-permute-start | bytes 294920 | tf_op jit(solution)/shard_map/ppermute | solution.py:306
  56.9 11.3 %collective-permute-start.18 = (bf16[128,768]{1,0:T(8,128)(2,1)S(1)}, bf16[128,768]{1,0:T(8,128)(2,1)S(1)}, u32[]{:S(2)}, u32[]{:S(2)}) collective-permute-start(bf16[128,768]{1,0:T(8,128)(2,1)S(1)} %collective-permute-done.11), channel_id=1, source_target_pairs={{0,8},{2,10},{4,12},{6,14},{8,0},{10,2},{12,4},{14,6},{16,24},{18,... | collective-permute-start | bytes 589832 | tf_op jit(solution)/shard_map/ppermute | solution.py:309
  59.0 23.8 %copy-start.1 = (bf16[128,2560]{1,0:T(8,128)(2,1)S(1)}, bf16[128,2560]{1,0:T(8,128)(2,1)}, u32[]{:S(2)}) copy-start(bf16[128,2560]{1,0:T(8,128)(2,1)} %tokens.1) | copy-start | bytes 1966084
  66.6 16.2 %collective-permute-start.16 = (bf16[128,2560]{1,0:T(8,128)(2,1)S(1)}, bf16[128,2560]{1,0:T(8,128)(2,1)S(1)}, u32[]{:S(2)}, u32[]{:S(2)}) collective-permute-start(bf16[128,2560]{1,0:T(8,128)(2,1)S(1)} %away.1), channel_id=1, source_target_pairs={{0,1},{1,0},{2,3},{3,2},{4,5},{5,4},{6,7},{7,6},{8,9},{9,8},{10,11... | collective-permute-start | bytes 1966088 | tf_op jit(solution)/shard_map/ppermute | solution.py:376
  68.2 1.7 %collective-permute-start.17 = (bf16[256,768]{1,0:T(8,128)(2,1)S(1)}, bf16[256,768]{1,0:T(8,128)(2,1)S(1)}, u32[]{:S(2)}, u32[]{:S(2)}) collective-permute-start(bf16[256,768]{1,0:T(8,128)(2,1)S(1)} %pad_maximum_fusion.1.refs_2_), channel_id=1, source_target_pairs={{0,2},{2,0},{4,6},{6,4},{8,10},{10,8},{12,14},{14,12},{16,18},{18,... | collective-permute-start | bytes 1179656 | tf_op jit(solution)/shard_map/ppermute | solution.py:309
  68.2 2.3 %collective-permute-start.19 = (bf16[256,768]{1,0:T(8,128)(2,1)S(1)}, bf16[256,768]{1,0:T(8,128)(2,1)S(1)}, u32[]{:S(2)}, u32[]{:S(2)}) collective-permute-start(bf16[256,768]{1,0:T(8,128)(2,1)S(1)} %constant_dynamic-update-slice_fusion.10.refs_4_), channel_id=1, source_target_pairs={{0,2},{2,0},{4,6},{6,4},{8,10},{10,8},{12,14},{14,12},{16,18},{18,... | collective-permute-start | bytes 1179656 | tf_op jit(solution)/shard_map/ppermute | solution.py:309
  73.8 9.1 %collective-permute-start.20 = (bf16[128,768]{1,0:T(8,128)(2,1)S(1)}, bf16[128,768]{1,0:T(8,128)(2,1)S(1)}, u32[]{:S(2)}, u32[]{:S(2)}) collective-permute-start(bf16[128,768]{1,0:T(8,128)(2,1)S(1)} %get-tuple-element.53), channel_id=1, source_target_pairs={{0,4},{2,6},{4,0},{6,2},{8,12},{10,14},{12,8},{14,10},{16,20},{18,... | collective-permute-start | bytes 589832 | tf_op jit(solution)/shard_map/ppermute | solution.py:309

commit v8 on v7

--- a/solution.py
+++ b/solution.py
@@ -352,7 +352,7 @@
 
     come = swap(go, bit)
     first = travel(first, [None] * 3)
-    second = travel(second, [None, (first[1], come), (first[1], come)])
+    second = travel(second, [come, (first[1], come), (first[1], come)])
     mine = join(*first)
     half_first = join(mine, swap(mine, 2))
     caption = join(stay[rows:], come[rows:])
@@ -362,10 +362,10 @@
     half_second = join(mine, swap(after(mine, pair), 2))
     pairs_first = [half_first, swap(half_first, 1)]
     outs = attend(second, at, pairs_first, [], chunks[0], factor)
-    beyond = swap(after(caption, second[1:]), 2 * members)
+    beyond = swap(after(caption, pair), 2 * members)
     pairs_second = [half_second, swap(after(half_second, (outs, beyond)), 1)]
     outs = attend(second, at, pairs_second, outs, chunks[1], factor)
-    last = swap(after(beyond, outs), members)
+    last = swap(after(beyond, pair), members)
     other = join(beyond, last)
     lhs = [rotate(x, groups - r) for r, x in enumerate(outs)]
 

time: 84.3 us -> 83.6 us (level)
  starting transfers between devices: 34 us -> 26.6 us
  waiting for transfers between devices: 30.6 us -> 37.2 us
    ppermute x9, waiting for transfers between devices: 10.4 us -> 17.5 us  [rotate(): lax.ppermute(x, 'seq', [(s, (s + step) % seq_size) for s in range(seq_siz...]
    ppermute x1, waiting for transfers between devices: 5.96 us -> 1.82 us  [shards(): away = lax.ppermute(away, 'tp', [(0, 1), (1, 0)])]
    ppermute x11, waiting for transfers between devices: 14.2 us -> 17.9 us  [swap(): return lax.ppermute(x, 'seq', [(s, s ^ by) for s in range(seq_size)])]
    ppermute x11, starting transfers between devices: 12.7 us -> 8.99 us  [swap(): return lax.ppermute(x, 'seq', [(s, s ^ by) for s in range(seq_size)])]
    ppermute x9, starting transfers between devices: 19.7 us -> 16 us  [rotate(): lax.ppermute(x, 'seq', [(s, (s + step) % seq_size) for s in range(seq_siz...]
  transfers between devices with their start and end apart: 21 -> 21, of which waited for: 11 -> 14; matrix products, arithmetic and copies ran while one was open for 0% -> 0% of each run, Pallas kernels for 16% -> 19%
where the time goes in v8:
time: 83.6 us; the launch traced here: 83.3 us
  waiting for transfers between devices  37.2 us (44%)
  starting transfers between devices  26.6 us (32%)
  Pallas kernels  18.3 us (22%)
  between operations  0.87 us (1%)
    ppermute x11, waiting for transfers between devices, swap(): return lax.ppermute(x, 'seq', [(s, s ^ by) for s in range(seq_size)])  17.9 us
    ppermute x9, waiting for transfers between devices, rotate(): lax.ppermute(x, 'seq', [(s, (s + step) % seq_size) for s in range(seq_siz...  17.5 us
    ppermute x9, starting transfers between devices, rotate(): lax.ppermute(x, 'seq', [(s, (s + step) % seq_size) for s in range(seq_siz...  16 us
    ppermute x11, starting transfers between devices, swap(): return lax.ppermute(x, 'seq', [(s, s ^ by) for s in range(seq_size)])  8.99 us
    pallas_call x2, Pallas kernels, attend(): pl.pallas_call(kernel, out_shape=[shape(rows, before + heads * DH)] * par...  6.29 us
    pallas_call x4, Pallas kernels, pack(): pl.pallas_call(kernel, out_shape=out_shapes, in_specs=[in_hbm()] * len(so...  4.49 us
    pallas_call x1, Pallas kernels, cross(): pl.pallas_call(kernel, out_shape=[shape(rows, columns)] * parts, in_specs...  3.27 us
    pallas_call x2, Pallas kernels, project(): pl.pallas_call(kernel, out_shape=shape(rows, columns, dtype), in_specs=[i...  3.14 us
  transfers between devices with their start and end apart: 21, of which 14 were waited for; matrix products, arithmetic and copies ran while one was open for 0% of the time, Pallas kernels for 19%

profile of v8, /device:TPU:0, one launch (start us, length us, event | category | flops | bytes accessed | tf_op | source)
XLA Modules:
  0.0 83.3 jit_solution(1643751343845123473)
XLA Ops:
  0.6 1.3 %pack_first.1 = (bf16[128,512]{1,0:T(8,128)(2,1)S(1)}, bf16[128,512]{1,0:T(8,128)(2,1)S(1)}, bf16[128,512]{1,0:T(8,128)(2,1)S(1)}, bf16[128,512]{1,0:T(8,128)(2,1)S(1)}) custom-call(bf16[128,1536]{1,0:T(8,128)(2,1)} %refs_0_.6, bf16[128,1536]{1,0:T(8,128)(2,1)} %refs_1_.6, bf16[128,1536]{1,0:T(8,128)(2,1)} %refs_2_.6), custom_call_target="tpu_custom_call" | custom-call | bytes 1048576 | tf_op jit(solution)/shard_map/pack_first/pallas_call | solution.py:95
  2.0 3.1 %collective-permute-start.2 = (bf16[128,512]{1,0:T(8,128)(2,1)S(1)}, bf16[128,512]{1,0:T(8,128)(2,1)S(1)}, u32[]{:S(2)}, u32[]{:S(2)}) collective-permute-start(bf16[128,512]{1,0:T(8,128)(2,1)S(1)} %get-tuple-element.33), channel_id=1, source_target_pairs={{0,8},{2,10},{4,12},{6,14},{8,16},{10,18},{12,20},{14,22},{16,24},... | collective-permute-start | bytes 393224 | tf_op jit(solution)/shard_map/ppermute | solution.py:306
  5.0 2.6 %collective-permute-start.5 = (bf16[128,512]{1,0:T(8,128)(2,1)S(1)}, bf16[128,512]{1,0:T(8,128)(2,1)S(1)}, u32[]{:S(2)}, u32[]{:S(2)}) collective-permute-start(bf16[128,512]{1,0:T(8,128)(2,1)S(1)} %get-tuple-element.37), channel_id=1, source_target_pairs={{0,16},{2,18},{4,20},{6,22},{8,24},{10,26},{12,28},{14,30},{16,0},... | collective-permute-start | bytes 393224 | tf_op jit(solution)/shard_map/ppermute | solution.py:306
  7.6 1.3 %collective-permute-start.6 = (bf16[128,512]{1,0:T(8,128)(2,1)S(1)}, bf16[128,512]{1,0:T(8,128)(2,1)S(1)}, u32[]{:S(2)}, u32[]{:S(2)}) collective-permute-start(bf16[128,512]{1,0:T(8,128)(2,1)S(1)} %get-tuple-element.38), channel_id=1, source_target_pairs={{0,24},{2,26},{4,28},{6,30},{8,0},{10,2},{12,4},{14,6},{16,8},{18,... | collective-permute-start | bytes 393224 | tf_op jit(solution)/shard_map/ppermute | solution.py:306
  9.9 1.6 %collective-permute-start = (bf16[192,768]{1,0:T(8,128)(2,1)S(1)}, bf16[192,768]{1,0:T(8,128)(2,1)S(1)}, u32[]{:S(2)}, u32[]{:S(2)}) collective-permute-start(bf16[192,768]{1,0:T(8,128)(2,1)S(1)} %pack_go.1), channel_id=1, source_target_pairs={{0,4},{2,6},{4,0},{6,2},{8,12},{10,14},{12,8},{14,10},{16,20},{18,... | collective-permute-start | bytes 884744 | tf_op jit(solution)/shard_map/ppermute | solution.py:309
  11.5 1.2 %pack_later.1 = (bf16[128,640]{1,0:T(8,128)(2,1)S(1)}, bf16[128,640]{1,0:T(8,128)(2,1)S(1)}, bf16[128,640]{1,0:T(8,128)(2,1)S(1)}, bf16[128,640]{1,0:T(8,128)(2,1)S(1)}) custom-call(bf16[128,1536]{1,0:T(8,128)(2,1)} %refs_0_.6, bf16[128,1536]{1,0:T(8,128)(2,1)} %refs_1_.6, bf16[128,1536]{1,0:T(8,128)(2,1)} %refs_2_.6), custom_call_target="tpu_custom_call" | custom-call | bytes 1310720 | tf_op jit(solution)/shard_map/pack_later/pallas_call | solution.py:95
  13.8 2.5 %collective-permute-done.5 = bf16[128,512]{1,0:T(8,128)(2,1)S(1)} collective-permute-done((bf16[128,512]{1,0:T(8,128)(2,1)S(1)}, bf16[128,512]{1,0:T(8,128)(2,1)S(1)}, u32[]{:S(2)}, u32[]{:S(2)}) %collective-permute-start.5) | collective-permute-done | bytes 131104 | tf_op jit(solution)/shard_map/ppermute | solution.py:306
  16.3 1.6 %collective-permute-start.9 = (bf16[512,512]{1,0:T(8,128)(2,1)S(1)}, bf16[512,512]{1,0:T(8,128)(2,1)S(1)}, u32[]{:S(2)}, u32[]{:S(2)}) collective-permute-start(bf16[512,512]{1,0:T(8,128)(2,1)S(1)} %pad_maximum_fusion), channel_id=1, source_target_pairs={{0,4},{2,6},{4,0},{6,2},{8,12},{10,14},{12,8},{14,10},{16,20},{18,... | collective-permute-start | bytes 1572872 | tf_op jit(solution)/shard_map/ppermute | solution.py:309
  17.9 3.3 %collective-permute-start.1 = (bf16[128,640]{1,0:T(8,128)(2,1)S(1)}, bf16[128,640]{1,0:T(8,128)(2,1)S(1)}, u32[]{:S(2)}, u32[]{:S(2)}) collective-permute-start(bf16[128,640]{1,0:T(8,128)(2,1)S(1)} %get-tuple-element.31), channel_id=1, source_target_pairs={{0,8},{2,10},{4,12},{6,14},{8,16},{10,18},{12,20},{14,22},{16,24},... | collective-permute-start | bytes 491528 | tf_op jit(solution)/shard_map/ppermute | solution.py:306
  21.3 1.7 %collective-permute-start.3 = (bf16[128,640]{1,0:T(8,128)(2,1)S(1)}, bf16[128,640]{1,0:T(8,128)(2,1)S(1)}, u32[]{:S(2)}, u32[]{:S(2)}) collective-permute-start(bf16[128,640]{1,0:T(8,128)(2,1)S(1)} %get-tuple-element.34), channel_id=1, source_target_pairs={{0,16},{2,18},{4,20},{6,22},{8,24},{10,26},{12,28},{14,30},{16,0},... | collective-permute-start | bytes 491528 | tf_op jit(solution)/shard_map/ppermute | solution.py:306
  23.7 1.3 %collective-permute-start.7 = (bf16[128,768]{1,0:T(8,128)(2,1)S(1)}, bf16[128,768]{1,0:T(8,128)(2,1)S(1)}, u32[]{:S(2)}, u32[]{:S(2)}) collective-permute-start(bf16[128,768]{1,0:T(8,128)(2,1)S(1)} %pad_maximum_fusion.3), channel_id=1, source_target_pairs={{0,8},{2,10},{4,12},{6,14},{8,0},{10,2},{12,4},{14,6},{16,24},{18,... | collective-permute-start | bytes 589832 | tf_op jit(solution)/shard_map/ppermute | solution.py:309
  25.1 2.2 %collective-permute-done.1.refs_1_ = bf16[128,640]{1,0:T(8,128)(2,1)S(1)} collective-permute-done((bf16[128,640]{1,0:T(8,128)(2,1)S(1)}, bf16[128,640]{1,0:T(8,128)(2,1)S(1)}, u32[]{:S(2)}, u32[]{:S(2)}) %collective-permute-start.1) | collective-permute-done | bytes 163872 | tf_op jit(solution)/shard_map/ppermute | solution.py:306
  27.3 2.8 %collective-permute-done.9 = bf16[512,512]{1,0:T(8,128)(2,1)S(1)} collective-permute-done((bf16[512,512]{1,0:T(8,128)(2,1)S(1)}, bf16[512,512]{1,0:T(8,128)(2,1)S(1)}, u32[]{:S(2)}, u32[]{:S(2)}) %collective-permute-start.9) | collective-permute-done | bytes 524320 | tf_op jit(solution)/shard_map/ppermute | solution.py:309
  30.3 2.5 %collective-permute-done.3.refs_2_ = bf16[128,640]{1,0:T(8,128)(2,1)S(1)} collective-permute-done((bf16[128,640]{1,0:T(8,128)(2,1)S(1)}, bf16[128,640]{1,0:T(8,128)(2,1)S(1)}, u32[]{:S(2)}, u32[]{:S(2)}) %collective-permute-start.3) | collective-permute-done | bytes 163872 | tf_op jit(solution)/shard_map/ppermute | solution.py:306
  32.7 1.2 %collective-permute-done.4.refs_3_ = bf16[128,640]{1,0:T(8,128)(2,1)S(1)} collective-permute-done((bf16[128,640]{1,0:T(8,128)(2,1)S(1)}, bf16[128,640]{1,0:T(8,128)(2,1)S(1)}, u32[]{:S(2)}, u32[]{:S(2)}) %collective-permute-start.4) | collective-permute-done | bytes 163872 | tf_op jit(solution)/shard_map/ppermute | solution.py:306
  33.9 2.8 %collective-permute-done.7 = bf16[128,768]{1,0:T(8,128)(2,1)S(1)} collective-permute-done((bf16[128,768]{1,0:T(8,128)(2,1)S(1)}, bf16[128,768]{1,0:T(8,128)(2,1)S(1)}, u32[]{:S(2)}, u32[]{:S(2)}) %collective-permute-start.7) | collective-permute-done | bytes 196640 | tf_op jit(solution)/shard_map/ppermute | solution.py:309
  38.2 5.6 %collective-permute-done.8 = bf16[512,256]{1,0:T(8,128)(2,1)S(1)} collective-permute-done((bf16[512,256]{1,0:T(8,128)(2,1)S(1)}, bf16[512,256]{1,0:T(8,128)(2,1)S(1)}, u32[]{:S(2)}, u32[]{:S(2)}) %collective-permute-start.8) | collective-permute-done | bytes 262176 | tf_op jit(solution)/shard_map/ppermute | solution.py:309
  43.8 4.1 %attend_0.1 = (bf16[128,256]{1,0:T(8,128)(2,1)S(1)}, bf16[128,256]{1,0:T(8,128)(2,1)S(1)}, bf16[128,256]{1,0:T(8,128)(2,1)S(1)}, bf16[128,256]{1,0:T(8,128)(2,1)S(1)}) custom-call(bf16[128,640]{1,0:T(8,128)(2,1)S(1)} %get-tuple-element.29.refs_0_, bf16[128,640]{1,0:T(8,128)(2,1)S(1)} %collective-permute-done.1.refs_1_, ...), custom_call_target="tpu_custom_call" | custom-call | flops 1073741824 | bytes 2097152 | tf_op jit(solution)/shard_map/attend_0/pallas_call | solution.py:170
  48.0 1.8 %collective-permute-start.18 = (bf16[128,768]{1,0:T(8,128)(2,1)S(1)}, bf16[128,768]{1,0:T(8,128)(2,1)S(1)}, u32[]{:S(2)}, u32[]{:S(2)}) collective-permute-start(bf16[128,768]{1,0:T(8,128)(2,1)S(1)} %collective-permute-done.11), channel_id=1, source_target_pairs={{0,8},{2,10},{4,12},{6,14},{8,0},{10,2},{12,4},{14,6},{16,24},{18,... | collective-permute-start | bytes 589832 | tf_op jit(solution)/shard_map/ppermute | solution.py:309
  49.9 2.2 %attend_2.1 = (bf16[128,384]{1,0:T(8,128)(2,1)S(1)}, bf16[128,384]{1,0:T(8,128)(2,1)S(1)}, bf16[128,384]{1,0:T(8,128)(2,1)S(1)}, bf16[128,384]{1,0:T(8,128)(2,1)S(1)}) custom-call(bf16[128,640]{1,0:T(8,128)(2,1)S(1)} %get-tuple-element.29.refs_0_, bf16[128,640]{1,0:T(8,128)(2,1)S(1)} %collective-permute-done.1.refs_1_, ...), custom_call_target="tpu_custom_call" | custom-call | flops 536870912 | bytes 1048576 | tf_op jit(solution)/shard_map/attend_2/pallas_call | solution.py:170
  52.1 2.1 %collective-permute-start.13 = (bf16[128,384]{1,0:T(8,128)(2,1)S(1)}, bf16[128,384]{1,0:T(8,128)(2,1)S(1)}, u32[]{:S(2)}, u32[]{:S(2)}) collective-permute-start(bf16[128,384]{1,0:T(8,128)(2,1)S(1)} %get-tuple-element.49), channel_id=1, source_target_pairs={{0,24},{2,26},{4,28},{6,30},{8,0},{10,2},{12,4},{14,6},{16,8},{18,... | collective-permute-start | bytes 294920 | tf_op jit(solution)/shard_map/ppermute | solution.py:306
  54.2 1.1 %collective-permute-start.14 = (bf16[128,384]{1,0:T(8,128)(2,1)S(1)}, bf16[128,384]{1,0:T(8,128)(2,1)S(1)}, u32[]{:S(2)}, u32[]{:S(2)}) collective-permute-start(bf16[128,384]{1,0:T(8,128)(2,1)S(1)} %get-tuple-element.50), channel_id=1, source_target_pairs={{0,16},{2,18},{4,20},{6,22},{8,24},{10,26},{12,28},{14,30},{16,0},... | collective-permute-start | bytes 294920 | tf_op jit(solution)/shard_map/ppermute | solution.py:306
  55.4 2.1 %collective-permute-done.13.refs_1_ = bf16[128,384]{1,0:T(8,128)(2,1)S(1)} collective-permute-done((bf16[128,384]{1,0:T(8,128)(2,1)S(1)}, bf16[128,384]{1,0:T(8,128)(2,1)S(1)}, u32[]{:S(2)}, u32[]{:S(2)}) %collective-permute-start.13) | collective-permute-done | bytes 98336 | tf_op jit(solution)/shard_map/ppermute | solution.py:306
  57.5 7.0 %collective-permute-done.14.refs_2_ = bf16[128,384]{1,0:T(8,128)(2,1)S(1)} collective-permute-done((bf16[128,384]{1,0:T(8,128)(2,1)S(1)}, bf16[128,384]{1,0:T(8,128)(2,1)S(1)}, u32[]{:S(2)}, u32[]{:S(2)}) %collective-permute-start.14) | collective-permute-done | bytes 98336 | tf_op jit(solution)/shard_map/ppermute | solution.py:306
  64.5 1.6 %away.1 = bf16[128,2560]{1,0:T(8,128)(2,1)S(1)} custom-call(bf16[128,384]{1,0:T(8,128)(2,1)S(1)} %get-tuple-element.48.refs_0_, bf16[128,384]{1,0:T(8,128)(2,1)S(1)} %collective-permute-done.13.refs_1_, bf16[128,384]{1,0:T(8,128)(2,1)S(1)} %collective-permute-done.14.refs_2_, bf16[128,384]{1,0:T(8,128)(2,1)S(1)} %collective-permute-done.15.refs_3_, ...), custom_call_target="tpu_custom_call" | custom-call | flops 1006632960 | bytes 9175040 | tf_op jit(solution)/shard_map/away/pallas_call | solution.py:247
  66.1 1.6 %collective-permute-start.16 = (bf16[128,2560]{1,0:T(8,128)(2,1)S(1)}, bf16[128,2560]{1,0:T(8,128)(2,1)S(1)}, u32[]{:S(2)}, u32[]{:S(2)}) collective-permute-start(bf16[128,2560]{1,0:T(8,128)(2,1)S(1)} %away.1), channel_id=1, source_target_pairs={{0,1},{1,0},{2,3},{3,2},{4,5},{5,4},{6,7},{7,6},{8,9},{9,8},{10,11... | collective-permute-start | bytes 1966088 | tf_op jit(solution)/shard_map/ppermute | solution.py:376
  68.3 1.2 %collective-permute-done.19.refs_5_ = bf16[256,768]{1,0:T(8,128)(2,1)S(1)} collective-permute-done((bf16[256,768]{1,0:T(8,128)(2,1)S(1)}, bf16[256,768]{1,0:T(8,128)(2,1)S(1)}, u32[]{:S(2)}, u32[]{:S(2)}) %collective-permute-start.19) | collective-permute-done | bytes 393248 | tf_op jit(solution)/shard_map/ppermute | solution.py:309
  70.1 3.3 %cross.1 = (bf16[128,768]{1,0:T(8,128)(2,1)S(1)}, bf16[128,768]{1,0:T(8,128)(2,1)S(1)}) custom-call(bf16[192,768]{1,0:T(8,128)(2,1)S(1)} %pack_stay.1.refs_0_, bf16[192,768]{1,0:T(8,128)(2,1)S(1)} %collective-permute-done.refs_1_, bf16[256,768]{1,0:T(8,128)(2,1)S(1)} %pad_maximum_fusion.1.refs_2_, bf16[256,768]{1,0:T(8,128)(2,1)S(1)} %collective-permute-done.17.refs_3_, ...), custom_call_target="tpu_custom_call" | custom-call | flops 402653184 | bytes 2359296 | tf_op jit(solution)/shard_map/cross/pallas_call | solution.py:210
  73.9 1.6 %home.1 = f32[128,2560]{1,0:T(8,128)S(1)} custom-call(bf16[128,384]{1,0:T(8,128)(2,1)S(1)} %get-tuple-element.48.refs_0_, bf16[128,384]{1,0:T(8,128)(2,1)S(1)} %collective-permute-done.13.refs_1_, bf16[128,384]{1,0:T(8,128)(2,1)S(1)} %collective-permute-done.14.refs_2_, bf16[128,384]{1,0:T(8,128)(2,1)S(1)} %collective-permute-done.15.refs_3_, ...), custom_call_target="tpu_custom_call" | custom-call | flops 1006632960 | bytes 9175040 | tf_op jit(solution)/shard_map/home/pallas_call | solution.py:247
  75.5 4.8 %collective-permute-done.20.came = bf16[128,768]{1,0:T(8,128)(2,1)S(1)} collective-permute-done((bf16[128,768]{1,0:T(8,128)(2,1)S(1)}, bf16[128,768]{1,0:T(8,128)(2,1)S(1)}, u32[]{:S(2)}, u32[]{:S(2)}) %collective-permute-start.20) | collective-permute-done | bytes 196640 | tf_op jit(solution)/shard_map/ppermute | solution.py:309
  80.3 1.8 %collective-permute-done.16.away = bf16[128,2560]{1,0:T(8,128)(2,1)S(1)} collective-permute-done((bf16[128,2560]{1,0:T(8,128)(2,1)S(1)}, bf16[128,2560]{1,0:T(8,128)(2,1)S(1)}, u32[]{:S(2)}, u32[]{:S(2)}) %collective-permute-start.16) | collective-permute-done | bytes 655392 | tf_op jit(solution)/shard_map/ppermute | solution.py:376
  82.2 1.2 %finish.1 = (bf16[128,2560]{1,0:T(8,128)(2,1)}, bf16[128,1536]{1,0:T(8,128)(2,1)}) custom-call(bf16[128,2560]{1,0:T(8,128)(2,1)S(1)} %copy-done.1, f32[1,2560]{1,0:T(1,128)S(1)} %broadcast_in_dim.3.gate, f32[128,2560]{1,0:T(8,128)S(1)} %home.1, bf16[128,2560]{1,0:T(8,128)(2,1)S(1)} %collective-permute-done.16.away, ...), custom_call_target="tpu_custom_call" | custom-call | bytes 3276800 | tf_op jit(solution)/shard_map/finish/pallas_call | solution.py:269
  (45 shorter events, 6.4 us)
Async XLA Ops:
  0.6 63.9 %copy-start = (bf16[1536,5120]{1,0:T(8,128)(2,1)S(1)}, bf16[1536,5120]{1,0:T(8,128)(2,1)}, u32[]{:S(2)}) copy-start(bf16[1536,5120]{1,0:T(8,128)(2,1)} %refs_4_.3) | copy-start | bytes 47185924
  2.0 11.8 %collective-permute-start.2 = (bf16[128,512]{1,0:T(8,128)(2,1)S(1)}, bf16[128,512]{1,0:T(8,128)(2,1)S(1)}, u32[]{:S(2)}, u32[]{:S(2)}) collective-permute-start(bf16[128,512]{1,0:T(8,128)(2,1)S(1)} %get-tuple-element.33), channel_id=1, source_target_pairs={{0,8},{2,10},{4,12},{6,14},{8,16},{10,18},{12,20},{14,22},{16,24},... | collective-permute-start | bytes 393224 | tf_op jit(solution)/shard_map/ppermute | solution.py:306
  5.0 11.2 %collective-permute-start.5 = (bf16[128,512]{1,0:T(8,128)(2,1)S(1)}, bf16[128,512]{1,0:T(8,128)(2,1)S(1)}, u32[]{:S(2)}, u32[]{:S(2)}) collective-permute-start(bf16[128,512]{1,0:T(8,128)(2,1)S(1)} %get-tuple-element.37), channel_id=1, source_target_pairs={{0,16},{2,18},{4,20},{6,22},{8,24},{10,26},{12,28},{14,30},{16,0},... | collective-permute-start | bytes 393224 | tf_op jit(solution)/shard_map/ppermute | solution.py:306
  7.6 8.6 %collective-permute-start.6 = (bf16[128,512]{1,0:T(8,128)(2,1)S(1)}, bf16[128,512]{1,0:T(8,128)(2,1)S(1)}, u32[]{:S(2)}, u32[]{:S(2)}) collective-permute-start(bf16[128,512]{1,0:T(8,128)(2,1)S(1)} %get-tuple-element.38), channel_id=1, source_target_pairs={{0,24},{2,26},{4,28},{6,30},{8,0},{10,2},{12,4},{14,6},{16,8},{18,... | collective-permute-start | bytes 393224 | tf_op jit(solution)/shard_map/ppermute | solution.py:306
  9.9 8.0 %collective-permute-start = (bf16[192,768]{1,0:T(8,128)(2,1)S(1)}, bf16[192,768]{1,0:T(8,128)(2,1)S(1)}, u32[]{:S(2)}, u32[]{:S(2)}) collective-permute-start(bf16[192,768]{1,0:T(8,128)(2,1)S(1)} %pack_go.1), channel_id=1, source_target_pairs={{0,4},{2,6},{4,0},{6,2},{8,12},{10,14},{12,8},{14,10},{16,20},{18,... | collective-permute-start | bytes 884744 | tf_op jit(solution)/shard_map/ppermute | solution.py:309
  13.8 60.1 %copy-start.2 = (f32[2560]{0:T(1024)S(1)}, f32[2560]{0:T(1024)}, u32[]{:S(2)}) copy-start(f32[2560]{0:T(1024)} %param.17) | copy-start | bytes 30724
  16.3 13.8 %collective-permute-start.9 = (bf16[512,512]{1,0:T(8,128)(2,1)S(1)}, bf16[512,512]{1,0:T(8,128)(2,1)S(1)}, u32[]{:S(2)}, u32[]{:S(2)}) collective-permute-start(bf16[512,512]{1,0:T(8,128)(2,1)S(1)} %pad_maximum_fusion), channel_id=1, source_target_pairs={{0,4},{2,6},{4,0},{6,2},{8,12},{10,14},{12,8},{14,10},{16,20},{18,... | collective-permute-start | bytes 1572872 | tf_op jit(solution)/shard_map/ppermute | solution.py:309
  17.9 9.4 %collective-permute-start.1 = (bf16[128,640]{1,0:T(8,128)(2,1)S(1)}, bf16[128,640]{1,0:T(8,128)(2,1)S(1)}, u32[]{:S(2)}, u32[]{:S(2)}) collective-permute-start(bf16[128,640]{1,0:T(8,128)(2,1)S(1)} %get-tuple-element.31), channel_id=1, source_target_pairs={{0,8},{2,10},{4,12},{6,14},{8,16},{10,18},{12,20},{14,22},{16,24},... | collective-permute-start | bytes 491528 | tf_op jit(solution)/shard_map/ppermute | solution.py:306
  21.3 11.5 %collective-permute-start.3 = (bf16[128,640]{1,0:T(8,128)(2,1)S(1)}, bf16[128,640]{1,0:T(8,128)(2,1)S(1)}, u32[]{:S(2)}, u32[]{:S(2)}) collective-permute-start(bf16[128,640]{1,0:T(8,128)(2,1)S(1)} %get-tuple-element.34), channel_id=1, source_target_pairs={{0,16},{2,18},{4,20},{6,22},{8,24},{10,26},{12,28},{14,30},{16,0},... | collective-permute-start | bytes 491528 | tf_op jit(solution)/shard_map/ppermute | solution.py:306
  23.0 10.9 %collective-permute-start.4 = (bf16[128,640]{1,0:T(8,128)(2,1)S(1)}, bf16[128,640]{1,0:T(8,128)(2,1)S(1)}, u32[]{:S(2)}, u32[]{:S(2)}) collective-permute-start(bf16[128,640]{1,0:T(8,128)(2,1)S(1)} %get-tuple-element.36), channel_id=1, source_target_pairs={{0,24},{2,26},{4,28},{6,30},{8,0},{10,2},{12,4},{14,6},{16,8},{18,... | collective-permute-start | bytes 491528 | tf_op jit(solution)/shard_map/ppermute | solution.py:306
  23.7 13.0 %collective-permute-start.7 = (bf16[128,768]{1,0:T(8,128)(2,1)S(1)}, bf16[128,768]{1,0:T(8,128)(2,1)S(1)}, u32[]{:S(2)}, u32[]{:S(2)}) collective-permute-start(bf16[128,768]{1,0:T(8,128)(2,1)S(1)} %pad_maximum_fusion.3), channel_id=1, source_target_pairs={{0,8},{2,10},{4,12},{6,14},{8,0},{10,2},{12,4},{14,6},{16,24},{18,... | collective-permute-start | bytes 589832 | tf_op jit(solution)/shard_map/ppermute | solution.py:309
  30.2 13.7 %collective-permute-start.10 = (bf16[1024,512]{1,0:T(8,128)(2,1)S(1)}, bf16[1024,512]{1,0:T(8,128)(2,1)S(1)}, u32[]{:S(2)}, u32[]{:S(2)}) collective-permute-start(bf16[1024,512]{1,0:T(8,128)(2,1)S(1)} %constant_dynamic-update-slice_fusion.5.refs_4_), channel_id=1, source_target_pairs={{0,2},{2,0},{4,6},{6,4},{8,10},{10,8},{12,14},{14,12},{16,18},{18,... | collective-permute-start | bytes 3145736 | tf_op jit(solution)/shard_map/ppermute | solution.py:309
  36.8 7.0 %collective-permute-start.8 = (bf16[512,256]{1,0:T(8,128)(2,1)S(1)}, bf16[512,256]{1,0:T(8,128)(2,1)S(1)}, u32[]{:S(2)}, u32[]{:S(2)}) collective-permute-start(bf16[512,256]{1,0:T(8,128)(2,1)S(1)} %pad_maximum_fusion.2), channel_id=1, source_target_pairs={{0,4},{2,6},{4,0},{6,2},{8,12},{10,14},{12,8},{14,10},{16,20},{18,... | collective-permute-start | bytes 786440 | tf_op jit(solution)/shard_map/ppermute | solution.py:309
  37.4 10.6 %collective-permute-start.11 = (bf16[128,768]{1,0:T(8,128)(2,1)S(1)}, bf16[128,768]{1,0:T(8,128)(2,1)S(1)}, u32[]{:S(2)}, u32[]{:S(2)}) collective-permute-start(bf16[128,768]{1,0:T(8,128)(2,1)S(1)} %pad_maximum_fusion.3), channel_id=1, source_target_pairs={{0,16},{2,18},{4,20},{6,22},{8,24},{10,26},{12,28},{14,30},{16,0},... | collective-permute-start | bytes 589832 | tf_op jit(solution)/shard_map/ppermute | solution.py:309
  48.0 2.0 %collective-permute-start.12 = (bf16[1024,256]{1,0:T(8,128)(2,1)S(1)}, bf16[1024,256]{1,0:T(8,128)(2,1)S(1)}, u32[]{:S(2)}, u32[]{:S(2)}) collective-permute-start(bf16[1024,256]{1,0:T(8,128)(2,1)S(1)} %constant_dynamic-update-slice_fusion.refs_4_), channel_id=1, source_target_pairs={{0,2},{2,0},{4,6},{6,4},{8,10},{10,8},{12,14},{14,12},{16,18},{18,... | collective-permute-start | bytes 1572872 | tf_op jit(solution)/shard_map/ppermute | solution.py:309
  48.0 19.6 %collective-permute-start.18 = (bf16[128,768]{1,0:T(8,128)(2,1)S(1)}, bf16[128,768]{1,0:T(8,128)(2,1)S(1)}, u32[]{:S(2)}, u32[]{:S(2)}) collective-permute-start(bf16[128,768]{1,0:T(8,128)(2,1)S(1)} %collective-permute-done.11), channel_id=1, source_target_pairs={{0,8},{2,10},{4,12},{6,14},{8,0},{10,2},{12,4},{14,6},{16,24},{18,... | collective-permute-start | bytes 589832 | tf_op jit(solution)/shard_map/ppermute | solution.py:309
  52.1 5.3 %collective-permute-start.13 = (bf16[128,384]{1,0:T(8,128)(2,1)S(1)}, bf16[128,384]{1,0:T(8,128)(2,1)S(1)}, u32[]{:S(2)}, u32[]{:S(2)}) collective-permute-start(bf16[128,384]{1,0:T(8,128)(2,1)S(1)} %get-tuple-element.49), channel_id=1, source_target_pairs={{0,24},{2,26},{4,28},{6,30},{8,0},{10,2},{12,4},{14,6},{16,8},{18,... | collective-permute-start | bytes 294920 | tf_op jit(solution)/shard_map/ppermute | solution.py:306
  54.2 10.3 %collective-permute-start.14 = (bf16[128,384]{1,0:T(8,128)(2,1)S(1)}, bf16[128,384]{1,0:T(8,128)(2,1)S(1)}, u32[]{:S(2)}, u32[]{:S(2)}) collective-permute-start(bf16[128,384]{1,0:T(8,128)(2,1)S(1)} %get-tuple-element.50), channel_id=1, source_target_pairs={{0,16},{2,18},{4,20},{6,22},{8,24},{10,26},{12,28},{14,30},{16,0},... | collective-permute-start | bytes 294920 | tf_op jit(solution)/shard_map/ppermute | solution.py:306
  55.4 9.1 %collective-permute-start.15 = (bf16[128,384]{1,0:T(8,128)(2,1)S(1)}, bf16[128,384]{1,0:T(8,128)(2,1)S(1)}, u32[]{:S(2)}, u32[]{:S(2)}) collective-permute-start(bf16[128,384]{1,0:T(8,128)(2,1)S(1)} %get-tuple-element.51), channel_id=1, source_target_pairs={{0,8},{2,10},{4,12},{6,14},{8,16},{10,18},{12,20},{14,22},{16,24},... | collective-permute-start | bytes 294920 | tf_op jit(solution)/shard_map/ppermute | solution.py:306
  64.5 17.7 %copy-start.1 = (bf16[128,2560]{1,0:T(8,128)(2,1)S(1)}, bf16[128,2560]{1,0:T(8,128)(2,1)}, u32[]{:S(2)}) copy-start(bf16[128,2560]{1,0:T(8,128)(2,1)} %tokens.1) | copy-start | bytes 1966084
  66.1 16.1 %collective-permute-start.16 = (bf16[128,2560]{1,0:T(8,128)(2,1)S(1)}, bf16[128,2560]{1,0:T(8,128)(2,1)S(1)}, u32[]{:S(2)}, u32[]{:S(2)}) collective-permute-start(bf16[128,2560]{1,0:T(8,128)(2,1)S(1)} %away.1), channel_id=1, source_target_pairs={{0,1},{1,0},{2,3},{3,2},{4,5},{5,4},{6,7},{7,6},{8,9},{9,8},{10,11... | collective-permute-start | bytes 1966088 | tf_op jit(solution)/shard_map/ppermute | solution.py:376
  67.7 1.8 %collective-permute-start.19 = (bf16[256,768]{1,0:T(8,128)(2,1)S(1)}, bf16[256,768]{1,0:T(8,128)(2,1)S(1)}, u32[]{:S(2)}, u32[]{:S(2)}) collective-permute-start(bf16[256,768]{1,0:T(8,128)(2,1)S(1)} %constant_dynamic-update-slice_fusion.10.refs_4_), channel_id=1, source_target_pairs={{0,2},{2,0},{4,6},{6,4},{8,10},{10,8},{12,14},{14,12},{16,18},{18,... | collective-permute-start | bytes 1179656 | tf_op jit(solution)/shard_map/ppermute | solution.py:309
  67.8 2.3 %collective-permute-start.17 = (bf16[256,768]{1,0:T(8,128)(2,1)S(1)}, bf16[256,768]{1,0:T(8,128)(2,1)S(1)}, u32[]{:S(2)}, u32[]{:S(2)}) collective-permute-start(bf16[256,768]{1,0:T(8,128)(2,1)S(1)} %pad_maximum_fusion.1.refs_2_), channel_id=1, source_target_pairs={{0,2},{2,0},{4,6},{6,4},{8,10},{10,8},{12,14},{14,12},{16,18},{18,... | collective-permute-start | bytes 1179656 | tf_op jit(solution)/shard_map/ppermute | solution.py:309
  73.3 7.0 %collective-permute-start.20 = (bf16[128,768]{1,0:T(8,128)(2,1)S(1)}, bf16[128,768]{1,0:T(8,128)(2,1)S(1)}, u32[]{:S(2)}, u32[]{:S(2)}) collective-permute-start(bf16[128,768]{1,0:T(8,128)(2,1)S(1)} %get-tuple-element.55), channel_id=1, source_target_pairs={{0,4},{2,6},{4,0},{6,2},{8,12},{10,14},{12,8},{14,10},{16,20},{18,... | collective-permute-start | bytes 589832 | tf_op jit(solution)/shard_map/ppermute | solution.py:309

commit v9 on v8

--- a/solution.py
+++ b/solution.py
@@ -51,15 +51,13 @@
     top = jnp.max(scores[0], axis=1, keepdims=True)
     for block in scores[1:]:
         top = jnp.maximum(top, jnp.max(block, axis=1, keepdims=True))
-    total = None
     mixed = None
     for block, value in zip(scores, values):
-        weight = jnp.exp2((block - top) * factor)
-        part = jnp.sum(weight, axis=1, keepdims=True)
-        total = part if total is None else total + part
-        term = jnp.dot(weight.astype(BF16), value, preferred_element_type=F32)
+        weight = jnp.exp2((block - top) * factor).astype(BF16)
+        wide = jnp.concatenate([value, jnp.ones_like(value)], axis=1)
+        term = jnp.dot(weight, wide, preferred_element_type=F32)
         mixed = term if mixed is None else mixed + term
-    return mixed / total
+    return mixed[:, :DH] / mixed[:, DH:]
 
 
 def copy_all(pairs, sems):

time: 83.6 us -> 82.3 us (0.984)
  Pallas kernels: 18.3 us -> 14.7 us
  waiting for transfers between devices: 37.2 us -> 40.4 us
  starting transfers between devices: 26.6 us -> 25.7 us
    ppermute x1, waiting for transfers between devices: 1.82 us -> 4.13 us  [shards(): away = lax.ppermute(away, 'tp', [(0, 1), (1, 0)])]
    pallas_call x1, Pallas kernels: 3.27 us -> 1.23 us  [cross(): pl.pallas_call(kernel, out_shape=[shape(rows, columns)] * parts, in_specs...]
    pallas_call x2, Pallas kernels: 6.29 us -> 4.75 us  [attend(): pl.pallas_call(kernel, out_shape=[shape(rows, before + heads * DH)] * par...]
    ppermute x11, waiting for transfers between devices: 17.9 us -> 18.8 us  [swap(): return lax.ppermute(x, 'seq', [(s, s ^ by) for s in range(seq_size)])]
  transfers between devices with their start and end apart: 21 -> 21, of which waited for: 14 -> 15; matrix products, arithmetic and copies ran while one was open for 0% -> 0% of each run, Pallas kernels for 19% -> 15%
where the time goes in v9:
time: 82.3 us; the launch traced here: 82 us
  waiting for transfers between devices  40.4 us (49%)
  starting transfers between devices  25.7 us (31%)
  Pallas kernels  14.7 us (18%)
  between operations  0.85 us (1%)
    ppermute x11, waiting for transfers between devices, swap(): return lax.ppermute(x, 'seq', [(s, s ^ by) for s in range(seq_size)])  18.8 us
    ppermute x9, waiting for transfers between devices, rotate(): lax.ppermute(x, 'seq', [(s, (s + step) % seq_size) for s in range(seq_siz...  17.5 us
    ppermute x9, starting transfers between devices, rotate(): lax.ppermute(x, 'seq', [(s, (s + step) % seq_size) for s in range(seq_siz...  15.3 us
    ppermute x11, starting transfers between devices, swap(): return lax.ppermute(x, 'seq', [(s, s ^ by) for s in range(seq_size)])  8.78 us
    pallas_call x2, Pallas kernels, attend(): pl.pallas_call(kernel, out_shape=[shape(rows, before + heads * DH)] * par...  4.75 us
    pallas_call x4, Pallas kernels, pack(): pl.pallas_call(kernel, out_shape=out_shapes, in_specs=[in_hbm()] * len(so...  4.49 us
    ppermute x1, waiting for transfers between devices, shards(): away = lax.ppermute(away, 'tp', [(0, 1), (1, 0)])  4.13 us
    pallas_call x2, Pallas kernels, project(): pl.pallas_call(kernel, out_shape=shape(rows, columns, dtype), in_specs=[i...  3.12 us
  transfers between devices with their start and end apart: 21, of which 15 were waited for; matrix products, arithmetic and copies ran while one was open for 0% of the time, Pallas kernels for 15%

profile of v9, /device:TPU:0, one launch (start us, length us, event | category | flops | bytes accessed | tf_op | source)
XLA Modules:
  0.0 82.0 jit_solution(12804436272406408555)
XLA Ops:
  0.6 1.3 %pack_first.1 = (bf16[128,512]{1,0:T(8,128)(2,1)S(1)}, bf16[128,512]{1,0:T(8,128)(2,1)S(1)}, bf16[128,512]{1,0:T(8,128)(2,1)S(1)}, bf16[128,512]{1,0:T(8,128)(2,1)S(1)}) custom-call(bf16[128,1536]{1,0:T(8,128)(2,1)} %refs_0_.6, bf16[128,1536]{1,0:T(8,128)(2,1)} %refs_1_.6, bf16[128,1536]{1,0:T(8,128)(2,1)} %refs_2_.6), custom_call_target="tpu_custom_call" | custom-call | bytes 1048576 | tf_op jit(solution)/shard_map/pack_first/pallas_call | solution.py:93
  2.0 3.1 %collective-permute-start.2 = (bf16[128,512]{1,0:T(8,128)(2,1)S(1)}, bf16[128,512]{1,0:T(8,128)(2,1)S(1)}, u32[]{:S(2)}, u32[]{:S(2)}) collective-permute-start(bf16[128,512]{1,0:T(8,128)(2,1)S(1)} %get-tuple-element.33), channel_id=1, source_target_pairs={{0,8},{2,10},{4,12},{6,14},{8,16},{10,18},{12,20},{14,22},{16,24},... | collective-permute-start | bytes 393224 | tf_op jit(solution)/shard_map/ppermute | solution.py:304
  5.0 2.6 %collective-permute-start.5 = (bf16[128,512]{1,0:T(8,128)(2,1)S(1)}, bf16[128,512]{1,0:T(8,128)(2,1)S(1)}, u32[]{:S(2)}, u32[]{:S(2)}) collective-permute-start(bf16[128,512]{1,0:T(8,128)(2,1)S(1)} %get-tuple-element.37), channel_id=1, source_target_pairs={{0,16},{2,18},{4,20},{6,22},{8,24},{10,26},{12,28},{14,30},{16,0},... | collective-permute-start | bytes 393224 | tf_op jit(solution)/shard_map/ppermute | solution.py:304
  7.6 1.3 %collective-permute-start.6 = (bf16[128,512]{1,0:T(8,128)(2,1)S(1)}, bf16[128,512]{1,0:T(8,128)(2,1)S(1)}, u32[]{:S(2)}, u32[]{:S(2)}) collective-permute-start(bf16[128,512]{1,0:T(8,128)(2,1)S(1)} %get-tuple-element.38), channel_id=1, source_target_pairs={{0,24},{2,26},{4,28},{6,30},{8,0},{10,2},{12,4},{14,6},{16,8},{18,... | collective-permute-start | bytes 393224 | tf_op jit(solution)/shard_map/ppermute | solution.py:304
  9.9 1.6 %collective-permute-start = (bf16[192,768]{1,0:T(8,128)(2,1)S(1)}, bf16[192,768]{1,0:T(8,128)(2,1)S(1)}, u32[]{:S(2)}, u32[]{:S(2)}) collective-permute-start(bf16[192,768]{1,0:T(8,128)(2,1)S(1)} %pack_go.1), channel_id=1, source_target_pairs={{0,4},{2,6},{4,0},{6,2},{8,12},{10,14},{12,8},{14,10},{16,20},{18,... | collective-permute-start | bytes 884744 | tf_op jit(solution)/shard_map/ppermute | solution.py:307
  11.5 1.2 %pack_later.1 = (bf16[128,640]{1,0:T(8,128)(2,1)S(1)}, bf16[128,640]{1,0:T(8,128)(2,1)S(1)}, bf16[128,640]{1,0:T(8,128)(2,1)S(1)}, bf16[128,640]{1,0:T(8,128)(2,1)S(1)}) custom-call(bf16[128,1536]{1,0:T(8,128)(2,1)} %refs_0_.6, bf16[128,1536]{1,0:T(8,128)(2,1)} %refs_1_.6, bf16[128,1536]{1,0:T(8,128)(2,1)} %refs_2_.6), custom_call_target="tpu_custom_call" | custom-call | bytes 1310720 | tf_op jit(solution)/shard_map/pack_later/pallas_call | solution.py:93
  13.8 2.5 %collective-permute-done.5 = bf16[128,512]{1,0:T(8,128)(2,1)S(1)} collective-permute-done((bf16[128,512]{1,0:T(8,128)(2,1)S(1)}, bf16[128,512]{1,0:T(8,128)(2,1)S(1)}, u32[]{:S(2)}, u32[]{:S(2)}) %collective-permute-start.5) | collective-permute-done | bytes 131104 | tf_op jit(solution)/shard_map/ppermute | solution.py:304
  16.3 1.6 %collective-permute-start.9 = (bf16[512,512]{1,0:T(8,128)(2,1)S(1)}, bf16[512,512]{1,0:T(8,128)(2,1)S(1)}, u32[]{:S(2)}, u32[]{:S(2)}) collective-permute-start(bf16[512,512]{1,0:T(8,128)(2,1)S(1)} %pad_maximum_fusion), channel_id=1, source_target_pairs={{0,4},{2,6},{4,0},{6,2},{8,12},{10,14},{12,8},{14,10},{16,20},{18,... | collective-permute-start | bytes 1572872 | tf_op jit(solution)/shard_map/ppermute | solution.py:307
  17.9 3.3 %collective-permute-start.1 = (bf16[128,640]{1,0:T(8,128)(2,1)S(1)}, bf16[128,640]{1,0:T(8,128)(2,1)S(1)}, u32[]{:S(2)}, u32[]{:S(2)}) collective-permute-start(bf16[128,640]{1,0:T(8,128)(2,1)S(1)} %get-tuple-element.31), channel_id=1, source_target_pairs={{0,8},{2,10},{4,12},{6,14},{8,16},{10,18},{12,20},{14,22},{16,24},... | collective-permute-start | bytes 491528 | tf_op jit(solution)/shard_map/ppermute | solution.py:304
  21.3 1.7 %collective-permute-start.3 = (bf16[128,640]{1,0:T(8,128)(2,1)S(1)}, bf16[128,640]{1,0:T(8,128)(2,1)S(1)}, u32[]{:S(2)}, u32[]{:S(2)}) collective-permute-start(bf16[128,640]{1,0:T(8,128)(2,1)S(1)} %get-tuple-element.34), channel_id=1, source_target_pairs={{0,16},{2,18},{4,20},{6,22},{8,24},{10,26},{12,28},{14,30},{16,0},... | collective-permute-start | bytes 491528 | tf_op jit(solution)/shard_map/ppermute | solution.py:304
  23.7 1.3 %collective-permute-start.7 = (bf16[128,768]{1,0:T(8,128)(2,1)S(1)}, bf16[128,768]{1,0:T(8,128)(2,1)S(1)}, u32[]{:S(2)}, u32[]{:S(2)}) collective-permute-start(bf16[128,768]{1,0:T(8,128)(2,1)S(1)} %pad_maximum_fusion.3), channel_id=1, source_target_pairs={{0,8},{2,10},{4,12},{6,14},{8,0},{10,2},{12,4},{14,6},{16,24},{18,... | collective-permute-start | bytes 589832 | tf_op jit(solution)/shard_map/ppermute | solution.py:307
  25.1 2.2 %collective-permute-done.1.refs_1_ = bf16[128,640]{1,0:T(8,128)(2,1)S(1)} collective-permute-done((bf16[128,640]{1,0:T(8,128)(2,1)S(1)}, bf16[128,640]{1,0:T(8,128)(2,1)S(1)}, u32[]{:S(2)}, u32[]{:S(2)}) %collective-permute-start.1) | collective-permute-done | bytes 163872 | tf_op jit(solution)/shard_map/ppermute | solution.py:304
  27.3 2.8 %collective-permute-done.9 = bf16[512,512]{1,0:T(8,128)(2,1)S(1)} collective-permute-done((bf16[512,512]{1,0:T(8,128)(2,1)S(1)}, bf16[512,512]{1,0:T(8,128)(2,1)S(1)}, u32[]{:S(2)}, u32[]{:S(2)}) %collective-permute-start.9) | collective-permute-done | bytes 524320 | tf_op jit(solution)/shard_map/ppermute | solution.py:307
  30.3 2.5 %collective-permute-done.3.refs_2_ = bf16[128,640]{1,0:T(8,128)(2,1)S(1)} collective-permute-done((bf16[128,640]{1,0:T(8,128)(2,1)S(1)}, bf16[128,640]{1,0:T(8,128)(2,1)S(1)}, u32[]{:S(2)}, u32[]{:S(2)}) %collective-permute-start.3) | collective-permute-done | bytes 163872 | tf_op jit(solution)/shard_map/ppermute | solution.py:304
  32.7 1.2 %collective-permute-done.4.refs_3_ = bf16[128,640]{1,0:T(8,128)(2,1)S(1)} collective-permute-done((bf16[128,640]{1,0:T(8,128)(2,1)S(1)}, bf16[128,640]{1,0:T(8,128)(2,1)S(1)}, u32[]{:S(2)}, u32[]{:S(2)}) %collective-permute-start.4) | collective-permute-done | bytes 163872 | tf_op jit(solution)/shard_map/ppermute | solution.py:304
  33.9 2.8 %collective-permute-done.7 = bf16[128,768]{1,0:T(8,128)(2,1)S(1)} collective-permute-done((bf16[128,768]{1,0:T(8,128)(2,1)S(1)}, bf16[128,768]{1,0:T(8,128)(2,1)S(1)}, u32[]{:S(2)}, u32[]{:S(2)}) %collective-permute-start.7) | collective-permute-done | bytes 196640 | tf_op jit(solution)/shard_map/ppermute | solution.py:307
  38.2 5.6 %collective-permute-done.8 = bf16[512,256]{1,0:T(8,128)(2,1)S(1)} collective-permute-done((bf16[512,256]{1,0:T(8,128)(2,1)S(1)}, bf16[512,256]{1,0:T(8,128)(2,1)S(1)}, u32[]{:S(2)}, u32[]{:S(2)}) %collective-permute-start.8) | collective-permute-done | bytes 262176 | tf_op jit(solution)/shard_map/ppermute | solution.py:307
  43.8 3.0 %attend_0.1 = (bf16[128,256]{1,0:T(8,128)(2,1)S(1)}, bf16[128,256]{1,0:T(8,128)(2,1)S(1)}, bf16[128,256]{1,0:T(8,128)(2,1)S(1)}, bf16[128,256]{1,0:T(8,128)(2,1)S(1)}) custom-call(bf16[128,640]{1,0:T(8,128)(2,1)S(1)} %get-tuple-element.29.refs_0_, bf16[128,640]{1,0:T(8,128)(2,1)S(1)} %collective-permute-done.1.refs_1_, ...), custom_call_target="tpu_custom_call" | custom-call | flops 1073741824 | bytes 2097152 | tf_op jit(solution)/shard_map/attend_0/pallas_call | solution.py:168
  47.6 1.1 %collective-permute-start.18 = (bf16[128,768]{1,0:T(8,128)(2,1)S(1)}, bf16[128,768]{1,0:T(8,128)(2,1)S(1)}, u32[]{:S(2)}, u32[]{:S(2)}) collective-permute-start(bf16[128,768]{1,0:T(8,128)(2,1)S(1)} %collective-permute-done.11), channel_id=1, source_target_pairs={{0,8},{2,10},{4,12},{6,14},{8,0},{10,2},{12,4},{14,6},{16,24},{18,... | collective-permute-start | bytes 589832 | tf_op jit(solution)/shard_map/ppermute | solution.py:307
  49.5 1.8 %attend_2.1 = (bf16[128,384]{1,0:T(8,128)(2,1)S(1)}, bf16[128,384]{1,0:T(8,128)(2,1)S(1)}, bf16[128,384]{1,0:T(8,128)(2,1)S(1)}, bf16[128,384]{1,0:T(8,128)(2,1)S(1)}) custom-call(bf16[128,640]{1,0:T(8,128)(2,1)S(1)} %get-tuple-element.29.refs_0_, bf16[128,640]{1,0:T(8,128)(2,1)S(1)} %collective-permute-done.1.refs_1_, ...), custom_call_target="tpu_custom_call" | custom-call | flops 536870912 | bytes 1048576 | tf_op jit(solution)/shard_map/attend_2/pallas_call | solution.py:168
  51.3 1.5 %collective-permute-start.13 = (bf16[128,384]{1,0:T(8,128)(2,1)S(1)}, bf16[128,384]{1,0:T(8,128)(2,1)S(1)}, u32[]{:S(2)}, u32[]{:S(2)}) collective-permute-start(bf16[128,384]{1,0:T(8,128)(2,1)S(1)} %get-tuple-element.49), channel_id=1, source_target_pairs={{0,24},{2,26},{4,28},{6,30},{8,0},{10,2},{12,4},{14,6},{16,8},{18,... | collective-permute-start | bytes 294920 | tf_op jit(solution)/shard_map/ppermute | solution.py:304
  53.8 3.5 %collective-permute-done.13.refs_1_ = bf16[128,384]{1,0:T(8,128)(2,1)S(1)} collective-permute-done((bf16[128,384]{1,0:T(8,128)(2,1)S(1)}, bf16[128,384]{1,0:T(8,128)(2,1)S(1)}, u32[]{:S(2)}, u32[]{:S(2)}) %collective-permute-start.13) | collective-permute-done | bytes 98336 | tf_op jit(solution)/shard_map/ppermute | solution.py:304
  57.4 5.6 %collective-permute-done.14.refs_2_ = bf16[128,384]{1,0:T(8,128)(2,1)S(1)} collective-permute-done((bf16[128,384]{1,0:T(8,128)(2,1)S(1)}, bf16[128,384]{1,0:T(8,128)(2,1)S(1)}, u32[]{:S(2)}, u32[]{:S(2)}) %collective-permute-start.14) | collective-permute-done | bytes 98336 | tf_op jit(solution)/shard_map/ppermute | solution.py:304
  63.0 1.6 %away.1 = bf16[128,2560]{1,0:T(8,128)(2,1)S(1)} custom-call(bf16[128,384]{1,0:T(8,128)(2,1)S(1)} %get-tuple-element.48.refs_0_, bf16[128,384]{1,0:T(8,128)(2,1)S(1)} %collective-permute-done.13.refs_1_, bf16[128,384]{1,0:T(8,128)(2,1)S(1)} %collective-permute-done.14.refs_2_, bf16[128,384]{1,0:T(8,128)(2,1)S(1)} %collective-permute-done.15.refs_3_, ...), custom_call_target="tpu_custom_call" | custom-call | flops 1006632960 | bytes 9175040 | tf_op jit(solution)/shard_map/away/pallas_call | solution.py:245
  64.5 1.6 %collective-permute-start.16 = (bf16[128,2560]{1,0:T(8,128)(2,1)S(1)}, bf16[128,2560]{1,0:T(8,128)(2,1)S(1)}, u32[]{:S(2)}, u32[]{:S(2)}) collective-permute-start(bf16[128,2560]{1,0:T(8,128)(2,1)S(1)} %away.1), channel_id=1, source_target_pairs={{0,1},{1,0},{2,3},{3,2},{4,5},{5,4},{6,7},{7,6},{8,9},{9,8},{10,11... | collective-permute-start | bytes 1966088 | tf_op jit(solution)/shard_map/ppermute | solution.py:374
  66.7 1.2 %collective-permute-done.19.refs_5_ = bf16[256,768]{1,0:T(8,128)(2,1)S(1)} collective-permute-done((bf16[256,768]{1,0:T(8,128)(2,1)S(1)}, bf16[256,768]{1,0:T(8,128)(2,1)S(1)}, u32[]{:S(2)}, u32[]{:S(2)}) %collective-permute-start.19) | collective-permute-done | bytes 393248 | tf_op jit(solution)/shard_map/ppermute | solution.py:307
  68.5 1.2 %cross.1 = (bf16[128,768]{1,0:T(8,128)(2,1)S(1)}, bf16[128,768]{1,0:T(8,128)(2,1)S(1)}) custom-call(bf16[192,768]{1,0:T(8,128)(2,1)S(1)} %pack_stay.1.refs_0_, bf16[192,768]{1,0:T(8,128)(2,1)S(1)} %collective-permute-done.refs_1_, bf16[256,768]{1,0:T(8,128)(2,1)S(1)} %pad_maximum_fusion.1.refs_2_, bf16[256,768]{1,0:T(8,128)(2,1)S(1)} %collective-permute-done.17.refs_3_, ...), custom_call_target="tpu_custom_call" | custom-call | flops 402653184 | bytes 2359296 | tf_op jit(solution)/shard_map/cross/pallas_call | solution.py:208
  69.7 1.1 %collective-permute-start.20 = (bf16[128,768]{1,0:T(8,128)(2,1)S(1)}, bf16[128,768]{1,0:T(8,128)(2,1)S(1)}, u32[]{:S(2)}, u32[]{:S(2)}) collective-permute-start(bf16[128,768]{1,0:T(8,128)(2,1)S(1)} %get-tuple-element.55), channel_id=1, source_target_pairs={{0,4},{2,6},{4,0},{6,2},{8,12},{10,14},{12,8},{14,10},{16,20},{18,... | collective-permute-start | bytes 589832 | tf_op jit(solution)/shard_map/ppermute | solution.py:307
  70.9 1.6 %home.1 = f32[128,2560]{1,0:T(8,128)S(1)} custom-call(bf16[128,384]{1,0:T(8,128)(2,1)S(1)} %get-tuple-element.48.refs_0_, bf16[128,384]{1,0:T(8,128)(2,1)S(1)} %collective-permute-done.13.refs_1_, bf16[128,384]{1,0:T(8,128)(2,1)S(1)} %collective-permute-done.14.refs_2_, bf16[128,384]{1,0:T(8,128)(2,1)S(1)} %collective-permute-done.15.refs_3_, ...), custom_call_target="tpu_custom_call" | custom-call | flops 1006632960 | bytes 9175040 | tf_op jit(solution)/shard_map/home/pallas_call | solution.py:245
  72.4 4.3 %collective-permute-done.20.came = bf16[128,768]{1,0:T(8,128)(2,1)S(1)} collective-permute-done((bf16[128,768]{1,0:T(8,128)(2,1)S(1)}, bf16[128,768]{1,0:T(8,128)(2,1)S(1)}, u32[]{:S(2)}, u32[]{:S(2)}) %collective-permute-start.20) | collective-permute-done | bytes 196640 | tf_op jit(solution)/shard_map/ppermute | solution.py:307
  76.7 4.1 %collective-permute-done.16.away = bf16[128,2560]{1,0:T(8,128)(2,1)S(1)} collective-permute-done((bf16[128,2560]{1,0:T(8,128)(2,1)S(1)}, bf16[128,2560]{1,0:T(8,128)(2,1)S(1)}, u32[]{:S(2)}, u32[]{:S(2)}) %collective-permute-start.16) | collective-permute-done | bytes 655392 | tf_op jit(solution)/shard_map/ppermute | solution.py:374
  80.9 1.2 %finish.1 = (bf16[128,2560]{1,0:T(8,128)(2,1)}, bf16[128,1536]{1,0:T(8,128)(2,1)}) custom-call(bf16[128,2560]{1,0:T(8,128)(2,1)S(1)} %copy-done.1, f32[1,2560]{1,0:T(1,128)S(1)} %broadcast_in_dim.3.gate, f32[128,2560]{1,0:T(8,128)S(1)} %home.1, bf16[128,2560]{1,0:T(8,128)(2,1)S(1)} %collective-permute-done.16.away, ...), custom_call_target="tpu_custom_call" | custom-call | bytes 3276800 | tf_op jit(solution)/shard_map/finish/pallas_call | solution.py:267
  (45 shorter events, 8.2 us)
Async XLA Ops:
  0.6 62.3 %copy-start = (bf16[1536,5120]{1,0:T(8,128)(2,1)S(1)}, bf16[1536,5120]{1,0:T(8,128)(2,1)}, u32[]{:S(2)}) copy-start(bf16[1536,5120]{1,0:T(8,128)(2,1)} %refs_4_.3) | copy-start | bytes 47185924
  2.0 11.8 %collective-permute-start.2 = (bf16[128,512]{1,0:T(8,128)(2,1)S(1)}, bf16[128,512]{1,0:T(8,128)(2,1)S(1)}, u32[]{:S(2)}, u32[]{:S(2)}) collective-permute-start(bf16[128,512]{1,0:T(8,128)(2,1)S(1)} %get-tuple-element.33), channel_id=1, source_target_pairs={{0,8},{2,10},{4,12},{6,14},{8,16},{10,18},{12,20},{14,22},{16,24},... | collective-permute-start | bytes 393224 | tf_op jit(solution)/shard_map/ppermute | solution.py:304
  5.0 11.2 %collective-permute-start.5 = (bf16[128,512]{1,0:T(8,128)(2,1)S(1)}, bf16[128,512]{1,0:T(8,128)(2,1)S(1)}, u32[]{:S(2)}, u32[]{:S(2)}) collective-permute-start(bf16[128,512]{1,0:T(8,128)(2,1)S(1)} %get-tuple-element.37), channel_id=1, source_target_pairs={{0,16},{2,18},{4,20},{6,22},{8,24},{10,26},{12,28},{14,30},{16,0},... | collective-permute-start | bytes 393224 | tf_op jit(solution)/shard_map/ppermute | solution.py:304
  7.6 8.6 %collective-permute-start.6 = (bf16[128,512]{1,0:T(8,128)(2,1)S(1)}, bf16[128,512]{1,0:T(8,128)(2,1)S(1)}, u32[]{:S(2)}, u32[]{:S(2)}) collective-permute-start(bf16[128,512]{1,0:T(8,128)(2,1)S(1)} %get-tuple-element.38), channel_id=1, source_target_pairs={{0,24},{2,26},{4,28},{6,30},{8,0},{10,2},{12,4},{14,6},{16,8},{18,... | collective-permute-start | bytes 393224 | tf_op jit(solution)/shard_map/ppermute | solution.py:304
  9.9 8.0 %collective-permute-start = (bf16[192,768]{1,0:T(8,128)(2,1)S(1)}, bf16[192,768]{1,0:T(8,128)(2,1)S(1)}, u32[]{:S(2)}, u32[]{:S(2)}) collective-permute-start(bf16[192,768]{1,0:T(8,128)(2,1)S(1)} %pack_go.1), channel_id=1, source_target_pairs={{0,4},{2,6},{4,0},{6,2},{8,12},{10,14},{12,8},{14,10},{16,20},{18,... | collective-permute-start | bytes 884744 | tf_op jit(solution)/shard_map/ppermute | solution.py:307
  13.8 57.1 %copy-start.2 = (f32[2560]{0:T(1024)S(1)}, f32[2560]{0:T(1024)}, u32[]{:S(2)}) copy-start(f32[2560]{0:T(1024)} %param.17) | copy-start | bytes 30724
  16.3 13.8 %collective-permute-start.9 = (bf16[512,512]{1,0:T(8,128)(2,1)S(1)}, bf16[512,512]{1,0:T(8,128)(2,1)S(1)}, u32[]{:S(2)}, u32[]{:S(2)}) collective-permute-start(bf16[512,512]{1,0:T(8,128)(2,1)S(1)} %pad_maximum_fusion), channel_id=1, source_target_pairs={{0,4},{2,6},{4,0},{6,2},{8,12},{10,14},{12,8},{14,10},{16,20},{18,... | collective-permute-start | bytes 1572872 | tf_op jit(solution)/shard_map/ppermute | solution.py:307
  17.9 9.4 %collective-permute-start.1 = (bf16[128,640]{1,0:T(8,128)(2,1)S(1)}, bf16[128,640]{1,0:T(8,128)(2,1)S(1)}, u32[]{:S(2)}, u32[]{:S(2)}) collective-permute-start(bf16[128,640]{1,0:T(8,128)(2,1)S(1)} %get-tuple-element.31), channel_id=1, source_target_pairs={{0,8},{2,10},{4,12},{6,14},{8,16},{10,18},{12,20},{14,22},{16,24},... | collective-permute-start | bytes 491528 | tf_op jit(solution)/shard_map/ppermute | solution.py:304
  21.3 11.5 %collective-permute-start.3 = (bf16[128,640]{1,0:T(8,128)(2,1)S(1)}, bf16[128,640]{1,0:T(8,128)(2,1)S(1)}, u32[]{:S(2)}, u32[]{:S(2)}) collective-permute-start(bf16[128,640]{1,0:T(8,128)(2,1)S(1)} %get-tuple-element.34), channel_id=1, source_target_pairs={{0,16},{2,18},{4,20},{6,22},{8,24},{10,26},{12,28},{14,30},{16,0},... | collective-permute-start | bytes 491528 | tf_op jit(solution)/shard_map/ppermute | solution.py:304
  23.0 10.9 %collective-permute-start.4 = (bf16[128,640]{1,0:T(8,128)(2,1)S(1)}, bf16[128,640]{1,0:T(8,128)(2,1)S(1)}, u32[]{:S(2)}, u32[]{:S(2)}) collective-permute-start(bf16[128,640]{1,0:T(8,128)(2,1)S(1)} %get-tuple-element.36), channel_id=1, source_target_pairs={{0,24},{2,26},{4,28},{6,30},{8,0},{10,2},{12,4},{14,6},{16,8},{18,... | collective-permute-start | bytes 491528 | tf_op jit(solution)/shard_map/ppermute | solution.py:304
  23.7 13.0 %collective-permute-start.7 = (bf16[128,768]{1,0:T(8,128)(2,1)S(1)}, bf16[128,768]{1,0:T(8,128)(2,1)S(1)}, u32[]{:S(2)}, u32[]{:S(2)}) collective-permute-start(bf16[128,768]{1,0:T(8,128)(2,1)S(1)} %pad_maximum_fusion.3), channel_id=1, source_target_pairs={{0,8},{2,10},{4,12},{6,14},{8,0},{10,2},{12,4},{14,6},{16,24},{18,... | collective-permute-start | bytes 589832 | tf_op jit(solution)/shard_map/ppermute | solution.py:307
  30.2 13.7 %collective-permute-start.10 = (bf16[1024,512]{1,0:T(8,128)(2,1)S(1)}, bf16[1024,512]{1,0:T(8,128)(2,1)S(1)}, u32[]{:S(2)}, u32[]{:S(2)}) collective-permute-start(bf16[1024,512]{1,0:T(8,128)(2,1)S(1)} %constant_dynamic-update-slice_fusion.5.refs_4_), channel_id=1, source_target_pairs={{0,2},{2,0},{4,6},{6,4},{8,10},{10,8},{12,14},{14,12},{16,18},{18,... | collective-permute-start | bytes 3145736 | tf_op jit(solution)/shard_map/ppermute | solution.py:307
  36.8 7.0 %collective-permute-start.8 = (bf16[512,256]{1,0:T(8,128)(2,1)S(1)}, bf16[512,256]{1,0:T(8,128)(2,1)S(1)}, u32[]{:S(2)}, u32[]{:S(2)}) collective-permute-start(bf16[512,256]{1,0:T(8,128)(2,1)S(1)} %pad_maximum_fusion.2), channel_id=1, source_target_pairs={{0,4},{2,6},{4,0},{6,2},{8,12},{10,14},{12,8},{14,10},{16,20},{18,... | collective-permute-start | bytes 786440 | tf_op jit(solution)/shard_map/ppermute | solution.py:307
  37.4 10.2 %collective-permute-start.11 = (bf16[128,768]{1,0:T(8,128)(2,1)S(1)}, bf16[128,768]{1,0:T(8,128)(2,1)S(1)}, u32[]{:S(2)}, u32[]{:S(2)}) collective-permute-start(bf16[128,768]{1,0:T(8,128)(2,1)S(1)} %pad_maximum_fusion.3), channel_id=1, source_target_pairs={{0,16},{2,18},{4,20},{6,22},{8,24},{10,26},{12,28},{14,30},{16,0},... | collective-permute-start | bytes 589832 | tf_op jit(solution)/shard_map/ppermute | solution.py:307
  47.6 1.9 %collective-permute-start.12 = (bf16[1024,256]{1,0:T(8,128)(2,1)S(1)}, bf16[1024,256]{1,0:T(8,128)(2,1)S(1)}, u32[]{:S(2)}, u32[]{:S(2)}) collective-permute-start(bf16[1024,256]{1,0:T(8,128)(2,1)S(1)} %constant_dynamic-update-slice_fusion.refs_4_), channel_id=1, source_target_pairs={{0,2},{2,0},{4,6},{6,4},{8,10},{10,8},{12,14},{14,12},{16,18},{18,... | collective-permute-start | bytes 1572872 | tf_op jit(solution)/shard_map/ppermute | solution.py:307
  47.6 18.5 %collective-permute-start.18 = (bf16[128,768]{1,0:T(8,128)(2,1)S(1)}, bf16[128,768]{1,0:T(8,128)(2,1)S(1)}, u32[]{:S(2)}, u32[]{:S(2)}) collective-permute-start(bf16[128,768]{1,0:T(8,128)(2,1)S(1)} %collective-permute-done.11), channel_id=1, source_target_pairs={{0,8},{2,10},{4,12},{6,14},{8,0},{10,2},{12,4},{14,6},{16,24},{18,... | collective-permute-start | bytes 589832 | tf_op jit(solution)/shard_map/ppermute | solution.py:307
  51.3 6.1 %collective-permute-start.13 = (bf16[128,384]{1,0:T(8,128)(2,1)S(1)}, bf16[128,384]{1,0:T(8,128)(2,1)S(1)}, u32[]{:S(2)}, u32[]{:S(2)}) collective-permute-start(bf16[128,384]{1,0:T(8,128)(2,1)S(1)} %get-tuple-element.49), channel_id=1, source_target_pairs={{0,24},{2,26},{4,28},{6,30},{8,0},{10,2},{12,4},{14,6},{16,8},{18,... | collective-permute-start | bytes 294920 | tf_op jit(solution)/shard_map/ppermute | solution.py:304
  52.8 10.1 %collective-permute-start.14 = (bf16[128,384]{1,0:T(8,128)(2,1)S(1)}, bf16[128,384]{1,0:T(8,128)(2,1)S(1)}, u32[]{:S(2)}, u32[]{:S(2)}) collective-permute-start(bf16[128,384]{1,0:T(8,128)(2,1)S(1)} %get-tuple-element.50), channel_id=1, source_target_pairs={{0,16},{2,18},{4,20},{6,22},{8,24},{10,26},{12,28},{14,30},{16,0},... | collective-permute-start | bytes 294920 | tf_op jit(solution)/shard_map/ppermute | solution.py:304
  53.8 9.1 %collective-permute-start.15 = (bf16[128,384]{1,0:T(8,128)(2,1)S(1)}, bf16[128,384]{1,0:T(8,128)(2,1)S(1)}, u32[]{:S(2)}, u32[]{:S(2)}) collective-permute-start(bf16[128,384]{1,0:T(8,128)(2,1)S(1)} %get-tuple-element.51), channel_id=1, source_target_pairs={{0,8},{2,10},{4,12},{6,14},{8,16},{10,18},{12,20},{14,22},{16,24},... | collective-permute-start | bytes 294920 | tf_op jit(solution)/shard_map/ppermute | solution.py:304
  63.0 17.9 %copy-start.1 = (bf16[128,2560]{1,0:T(8,128)(2,1)S(1)}, bf16[128,2560]{1,0:T(8,128)(2,1)}, u32[]{:S(2)}) copy-start(bf16[128,2560]{1,0:T(8,128)(2,1)} %tokens.1) | copy-start | bytes 1966084
  64.5 16.3 %collective-permute-start.16 = (bf16[128,2560]{1,0:T(8,128)(2,1)S(1)}, bf16[128,2560]{1,0:T(8,128)(2,1)S(1)}, u32[]{:S(2)}, u32[]{:S(2)}) collective-permute-start(bf16[128,2560]{1,0:T(8,128)(2,1)S(1)} %away.1), channel_id=1, source_target_pairs={{0,1},{1,0},{2,3},{3,2},{4,5},{5,4},{6,7},{7,6},{8,9},{9,8},{10,11... | collective-permute-start | bytes 1966088 | tf_op jit(solution)/shard_map/ppermute | solution.py:374
  66.1 1.8 %collective-permute-start.19 = (bf16[256,768]{1,0:T(8,128)(2,1)S(1)}, bf16[256,768]{1,0:T(8,128)(2,1)S(1)}, u32[]{:S(2)}, u32[]{:S(2)}) collective-permute-start(bf16[256,768]{1,0:T(8,128)(2,1)S(1)} %constant_dynamic-update-slice_fusion.10.refs_4_), channel_id=1, source_target_pairs={{0,2},{2,0},{4,6},{6,4},{8,10},{10,8},{12,14},{14,12},{16,18},{18,... | collective-permute-start | bytes 1179656 | tf_op jit(solution)/shard_map/ppermute | solution.py:307
  66.2 2.3 %collective-permute-start.17 = (bf16[256,768]{1,0:T(8,128)(2,1)S(1)}, bf16[256,768]{1,0:T(8,128)(2,1)S(1)}, u32[]{:S(2)}, u32[]{:S(2)}) collective-permute-start(bf16[256,768]{1,0:T(8,128)(2,1)S(1)} %pad_maximum_fusion.1.refs_2_), channel_id=1, source_target_pairs={{0,2},{2,0},{4,6},{6,4},{8,10},{10,8},{12,14},{14,12},{16,18},{18,... | collective-permute-start | bytes 1179656 | tf_op jit(solution)/shard_map/ppermute | solution.py:307
  69.7 7.0 %collective-permute-start.20 = (bf16[128,768]{1,0:T(8,128)(2,1)S(1)}, bf16[128,768]{1,0:T(8,128)(2,1)S(1)}, u32[]{:S(2)}, u32[]{:S(2)}) collective-permute-start(bf16[128,768]{1,0:T(8,128)(2,1)S(1)} %get-tuple-element.55), channel_id=1, source_target_pairs={{0,4},{2,6},{4,0},{6,2},{8,12},{10,14},{12,8},{14,10},{16,20},{18,... | collective-permute-start | bytes 589832 | tf_op jit(solution)/shard_map/ppermute | solution.py:307

commit v10 on v9

--- a/solution.py
+++ b/solution.py
@@ -255,24 +255,39 @@
     )(*lhs, weight)
 
 
-def finish(bit, tokens, gate, home, away, stay, came):
-    def kernel(tokens, gate, home, away, stay, came, updated, cross_heads):
+def assemble(bit, stay, came):
+    half = stay.shape[1]
+
+    def kernel(stay_ref, came_ref, out):
+        xi = lax.rem(lax.axis_index("seq") // bit, 2)
+        for side, heads in ((xi, stay_ref), (1 - xi, came_ref)):
+            out[:, pl.ds(pl.multiple_of(side * half, DH), half)] = heads[...]
+
+    return pl.pallas_call(
+        kernel,
+        out_shape=shape(stay.shape[0], 2 * half),
+        in_specs=[in_vmem()] * 2,
+        out_specs=in_vmem(),
+        compiler_params=limit(4),
+        cost_estimate=cost(0, stay.size * 8),
+        name="assemble",
+    )(stay, came)
+
+
+def finish(tokens, gate, home, away):
+    def kernel(tokens, gate, home, away, updated):
         projected = home[...] + away[...].astype(F32)
         updated[...] = (tokens[...].astype(F32) + gate[...] * projected).astype(BF16)
-        half = stay.shape[1]
-        xi = lax.rem(lax.axis_index("seq") // bit, 2)
-        for side, half_heads in ((xi, stay), (1 - xi, came)):
-            cross_heads[:, pl.ds(pl.multiple_of(side * half, DH), half)] = half_heads[...]
 
     return pl.pallas_call(
         kernel,
-        out_shape=[shape(*tokens.shape), shape(stay.shape[0], 2 * stay.shape[1])],
-        in_specs=[in_vmem()] * 6,
-        out_specs=[in_vmem()] * 2,
+        out_shape=shape(*tokens.shape),
+        in_specs=[in_vmem()] * 4,
+        out_specs=in_vmem(),
         compiler_params=limit(12),
         cost_estimate=cost(0, tokens.size * 10),
         name="finish",
-    )(tokens, gate[None, :], home, away, stay, came)
+    )(tokens, gate[None, :], home, away)
 
 
 def shards(
@@ -373,7 +388,8 @@
     came = swap(theirs, bit)
     away = lax.ppermute(away, "tp", [(0, 1), (1, 0)])
     home = project(members, tp_size, 0, lhs, out_weight, F32, "home")
-    return tuple(finish(bit, tokens, gate_vector, home, away, own, came))
+    cross_heads = assemble(bit, own, came)
+    return (finish(tokens, gate_vector, home, away), cross_heads)
 
 
 def solution(mesh):

time: 82.3 us -> 82.2 us (level)
    pallas_call x1 -> x2, Pallas kernels: 1.16 us -> 1.86 us  [the longest x1 1.07 us: finish(): pl.pallas_call(kernel, out_shape=shape(*tokens.shape), in_specs=[in_vmem(...]
  transfers between devices with their start and end apart: 21 -> 21, of which waited for: 15 -> 15; matrix products, arithmetic and copies ran while one was open for 0% -> 0% of each run, Pallas kernels for 15% -> 16%
where the time goes in v10:
time: 82.2 us; the launch traced here: 81.9 us
  waiting for transfers between devices  39.7 us (48%)
  starting transfers between devices  25.7 us (31%)
  Pallas kernels  15.4 us (19%)
  between operations  0.86 us (1%)
    ppermute x11, waiting for transfers between devices, swap(): return lax.ppermute(x, 'seq', [(s, s ^ by) for s in range(seq_size)])  18.8 us
    ppermute x9, waiting for transfers between devices, rotate(): lax.ppermute(x, 'seq', [(s, (s + step) % seq_size) for s in range(seq_siz...  17.5 us
    ppermute x9, starting transfers between devices, rotate(): lax.ppermute(x, 'seq', [(s, (s + step) % seq_size) for s in range(seq_siz...  15.3 us
    ppermute x11, starting transfers between devices, swap(): return lax.ppermute(x, 'seq', [(s, s ^ by) for s in range(seq_size)])  8.78 us
    pallas_call x2, Pallas kernels, attend(): pl.pallas_call(kernel, out_shape=[shape(rows, before + heads * DH)] * par...  4.75 us
    pallas_call x4, Pallas kernels, pack(): pl.pallas_call(kernel, out_shape=out_shapes, in_specs=[in_hbm()] * len(so...  4.49 us
    ppermute x1, waiting for transfers between devices, shards(): away = lax.ppermute(away, 'tp', [(0, 1), (1, 0)])  3.34 us
    pallas_call x2, Pallas kernels, project(): pl.pallas_call(kernel, out_shape=shape(rows, columns, dtype), in_specs=[i...  3.12 us
  transfers between devices with their start and end apart: 21, of which 15 were waited for; matrix products, arithmetic and copies ran while one was open for 0% of the time, Pallas kernels for 16%

profile of v10, /device:TPU:0, one launch (start us, length us, event | category | flops | bytes accessed | tf_op | source)
XLA Modules:
  0.0 81.9 jit_solution(18371335622058396931)
XLA Ops:
  0.6 1.3 %pack_first.1 = (bf16[128,512]{1,0:T(8,128)(2,1)S(1)}, bf16[128,512]{1,0:T(8,128)(2,1)S(1)}, bf16[128,512]{1,0:T(8,128)(2,1)S(1)}, bf16[128,512]{1,0:T(8,128)(2,1)S(1)}) custom-call(bf16[128,1536]{1,0:T(8,128)(2,1)} %refs_0_.6, bf16[128,1536]{1,0:T(8,128)(2,1)} %refs_1_.6, bf16[128,1536]{1,0:T(8,128)(2,1)} %refs_2_.6), custom_call_target="tpu_custom_call" | custom-call | bytes 1048576 | tf_op jit(solution)/shard_map/pack_first/pallas_call | solution.py:93
  2.0 3.1 %collective-permute-start.2 = (bf16[128,512]{1,0:T(8,128)(2,1)S(1)}, bf16[128,512]{1,0:T(8,128)(2,1)S(1)}, u32[]{:S(2)}, u32[]{:S(2)}) collective-permute-start(bf16[128,512]{1,0:T(8,128)(2,1)S(1)} %get-tuple-element.33), channel_id=1, source_target_pairs={{0,8},{2,10},{4,12},{6,14},{8,16},{10,18},{12,20},{14,22},{16,24},... | collective-permute-start | bytes 393224 | tf_op jit(solution)/shard_map/ppermute | solution.py:319
  5.0 2.6 %collective-permute-start.5 = (bf16[128,512]{1,0:T(8,128)(2,1)S(1)}, bf16[128,512]{1,0:T(8,128)(2,1)S(1)}, u32[]{:S(2)}, u32[]{:S(2)}) collective-permute-start(bf16[128,512]{1,0:T(8,128)(2,1)S(1)} %get-tuple-element.37), channel_id=1, source_target_pairs={{0,16},{2,18},{4,20},{6,22},{8,24},{10,26},{12,28},{14,30},{16,0},... | collective-permute-start | bytes 393224 | tf_op jit(solution)/shard_map/ppermute | solution.py:319
  7.6 1.3 %collective-permute-start.6 = (bf16[128,512]{1,0:T(8,128)(2,1)S(1)}, bf16[128,512]{1,0:T(8,128)(2,1)S(1)}, u32[]{:S(2)}, u32[]{:S(2)}) collective-permute-start(bf16[128,512]{1,0:T(8,128)(2,1)S(1)} %get-tuple-element.38), channel_id=1, source_target_pairs={{0,24},{2,26},{4,28},{6,30},{8,0},{10,2},{12,4},{14,6},{16,8},{18,... | collective-permute-start | bytes 393224 | tf_op jit(solution)/shard_map/ppermute | solution.py:319
  9.9 1.6 %collective-permute-start = (bf16[192,768]{1,0:T(8,128)(2,1)S(1)}, bf16[192,768]{1,0:T(8,128)(2,1)S(1)}, u32[]{:S(2)}, u32[]{:S(2)}) collective-permute-start(bf16[192,768]{1,0:T(8,128)(2,1)S(1)} %pack_go.1), channel_id=1, source_target_pairs={{0,4},{2,6},{4,0},{6,2},{8,12},{10,14},{12,8},{14,10},{16,20},{18,... | collective-permute-start | bytes 884744 | tf_op jit(solution)/shard_map/ppermute | solution.py:322
  11.5 1.2 %pack_later.1 = (bf16[128,640]{1,0:T(8,128)(2,1)S(1)}, bf16[128,640]{1,0:T(8,128)(2,1)S(1)}, bf16[128,640]{1,0:T(8,128)(2,1)S(1)}, bf16[128,640]{1,0:T(8,128)(2,1)S(1)}) custom-call(bf16[128,1536]{1,0:T(8,128)(2,1)} %refs_0_.6, bf16[128,1536]{1,0:T(8,128)(2,1)} %refs_1_.6, bf16[128,1536]{1,0:T(8,128)(2,1)} %refs_2_.6), custom_call_target="tpu_custom_call" | custom-call | bytes 1310720 | tf_op jit(solution)/shard_map/pack_later/pallas_call | solution.py:93
  13.8 2.5 %collective-permute-done.5 = bf16[128,512]{1,0:T(8,128)(2,1)S(1)} collective-permute-done((bf16[128,512]{1,0:T(8,128)(2,1)S(1)}, bf16[128,512]{1,0:T(8,128)(2,1)S(1)}, u32[]{:S(2)}, u32[]{:S(2)}) %collective-permute-start.5) | collective-permute-done | bytes 131104 | tf_op jit(solution)/shard_map/ppermute | solution.py:319
  16.3 1.6 %collective-permute-start.9 = (bf16[512,512]{1,0:T(8,128)(2,1)S(1)}, bf16[512,512]{1,0:T(8,128)(2,1)S(1)}, u32[]{:S(2)}, u32[]{:S(2)}) collective-permute-start(bf16[512,512]{1,0:T(8,128)(2,1)S(1)} %pad_maximum_fusion), channel_id=1, source_target_pairs={{0,4},{2,6},{4,0},{6,2},{8,12},{10,14},{12,8},{14,10},{16,20},{18,... | collective-permute-start | bytes 1572872 | tf_op jit(solution)/shard_map/ppermute | solution.py:322
  17.9 3.3 %collective-permute-start.1 = (bf16[128,640]{1,0:T(8,128)(2,1)S(1)}, bf16[128,640]{1,0:T(8,128)(2,1)S(1)}, u32[]{:S(2)}, u32[]{:S(2)}) collective-permute-start(bf16[128,640]{1,0:T(8,128)(2,1)S(1)} %get-tuple-element.31), channel_id=1, source_target_pairs={{0,8},{2,10},{4,12},{6,14},{8,16},{10,18},{12,20},{14,22},{16,24},... | collective-permute-start | bytes 491528 | tf_op jit(solution)/shard_map/ppermute | solution.py:319
  21.3 1.7 %collective-permute-start.3 = (bf16[128,640]{1,0:T(8,128)(2,1)S(1)}, bf16[128,640]{1,0:T(8,128)(2,1)S(1)}, u32[]{:S(2)}, u32[]{:S(2)}) collective-permute-start(bf16[128,640]{1,0:T(8,128)(2,1)S(1)} %get-tuple-element.34), channel_id=1, source_target_pairs={{0,16},{2,18},{4,20},{6,22},{8,24},{10,26},{12,28},{14,30},{16,0},... | collective-permute-start | bytes 491528 | tf_op jit(solution)/shard_map/ppermute | solution.py:319
  23.7 1.3 %collective-permute-start.7 = (bf16[128,768]{1,0:T(8,128)(2,1)S(1)}, bf16[128,768]{1,0:T(8,128)(2,1)S(1)}, u32[]{:S(2)}, u32[]{:S(2)}) collective-permute-start(bf16[128,768]{1,0:T(8,128)(2,1)S(1)} %pad_maximum_fusion.3), channel_id=1, source_target_pairs={{0,8},{2,10},{4,12},{6,14},{8,0},{10,2},{12,4},{14,6},{16,24},{18,... | collective-permute-start | bytes 589832 | tf_op jit(solution)/shard_map/ppermute | solution.py:322
  25.1 2.2 %collective-permute-done.1.refs_1_ = bf16[128,640]{1,0:T(8,128)(2,1)S(1)} collective-permute-done((bf16[128,640]{1,0:T(8,128)(2,1)S(1)}, bf16[128,640]{1,0:T(8,128)(2,1)S(1)}, u32[]{:S(2)}, u32[]{:S(2)}) %collective-permute-start.1) | collective-permute-done | bytes 163872 | tf_op jit(solution)/shard_map/ppermute | solution.py:319
  27.3 2.8 %collective-permute-done.9 = bf16[512,512]{1,0:T(8,128)(2,1)S(1)} collective-permute-done((bf16[512,512]{1,0:T(8,128)(2,1)S(1)}, bf16[512,512]{1,0:T(8,128)(2,1)S(1)}, u32[]{:S(2)}, u32[]{:S(2)}) %collective-permute-start.9) | collective-permute-done | bytes 524320 | tf_op jit(solution)/shard_map/ppermute | solution.py:322
  30.3 2.5 %collective-permute-done.3.refs_2_ = bf16[128,640]{1,0:T(8,128)(2,1)S(1)} collective-permute-done((bf16[128,640]{1,0:T(8,128)(2,1)S(1)}, bf16[128,640]{1,0:T(8,128)(2,1)S(1)}, u32[]{:S(2)}, u32[]{:S(2)}) %collective-permute-start.3) | collective-permute-done | bytes 163872 | tf_op jit(solution)/shard_map/ppermute | solution.py:319
  32.7 1.2 %collective-permute-done.4.refs_3_ = bf16[128,640]{1,0:T(8,128)(2,1)S(1)} collective-permute-done((bf16[128,640]{1,0:T(8,128)(2,1)S(1)}, bf16[128,640]{1,0:T(8,128)(2,1)S(1)}, u32[]{:S(2)}, u32[]{:S(2)}) %collective-permute-start.4) | collective-permute-done | bytes 163872 | tf_op jit(solution)/shard_map/ppermute | solution.py:319
  33.9 2.8 %collective-permute-done.7 = bf16[128,768]{1,0:T(8,128)(2,1)S(1)} collective-permute-done((bf16[128,768]{1,0:T(8,128)(2,1)S(1)}, bf16[128,768]{1,0:T(8,128)(2,1)S(1)}, u32[]{:S(2)}, u32[]{:S(2)}) %collective-permute-start.7) | collective-permute-done | bytes 196640 | tf_op jit(solution)/shard_map/ppermute | solution.py:322
  38.2 5.6 %collective-permute-done.8 = bf16[512,256]{1,0:T(8,128)(2,1)S(1)} collective-permute-done((bf16[512,256]{1,0:T(8,128)(2,1)S(1)}, bf16[512,256]{1,0:T(8,128)(2,1)S(1)}, u32[]{:S(2)}, u32[]{:S(2)}) %collective-permute-start.8) | collective-permute-done | bytes 262176 | tf_op jit(solution)/shard_map/ppermute | solution.py:322
  43.8 3.0 %attend_0.1 = (bf16[128,256]{1,0:T(8,128)(2,1)S(1)}, bf16[128,256]{1,0:T(8,128)(2,1)S(1)}, bf16[128,256]{1,0:T(8,128)(2,1)S(1)}, bf16[128,256]{1,0:T(8,128)(2,1)S(1)}) custom-call(bf16[128,640]{1,0:T(8,128)(2,1)S(1)} %get-tuple-element.29.refs_0_, bf16[128,640]{1,0:T(8,128)(2,1)S(1)} %collective-permute-done.1.refs_1_, ...), custom_call_target="tpu_custom_call" | custom-call | flops 1073741824 | bytes 2097152 | tf_op jit(solution)/shard_map/attend_0/pallas_call | solution.py:168
  47.6 1.1 %collective-permute-start.18 = (bf16[128,768]{1,0:T(8,128)(2,1)S(1)}, bf16[128,768]{1,0:T(8,128)(2,1)S(1)}, u32[]{:S(2)}, u32[]{:S(2)}) collective-permute-start(bf16[128,768]{1,0:T(8,128)(2,1)S(1)} %collective-permute-done.11), channel_id=1, source_target_pairs={{0,8},{2,10},{4,12},{6,14},{8,0},{10,2},{12,4},{14,6},{16,24},{18,... | collective-permute-start | bytes 589832 | tf_op jit(solution)/shard_map/ppermute | solution.py:322
  49.5 1.8 %attend_2.1 = (bf16[128,384]{1,0:T(8,128)(2,1)S(1)}, bf16[128,384]{1,0:T(8,128)(2,1)S(1)}, bf16[128,384]{1,0:T(8,128)(2,1)S(1)}, bf16[128,384]{1,0:T(8,128)(2,1)S(1)}) custom-call(bf16[128,640]{1,0:T(8,128)(2,1)S(1)} %get-tuple-element.29.refs_0_, bf16[128,640]{1,0:T(8,128)(2,1)S(1)} %collective-permute-done.1.refs_1_, ...), custom_call_target="tpu_custom_call" | custom-call | flops 536870912 | bytes 1048576 | tf_op jit(solution)/shard_map/attend_2/pallas_call | solution.py:168
  51.3 1.5 %collective-permute-start.13 = (bf16[128,384]{1,0:T(8,128)(2,1)S(1)}, bf16[128,384]{1,0:T(8,128)(2,1)S(1)}, u32[]{:S(2)}, u32[]{:S(2)}) collective-permute-start(bf16[128,384]{1,0:T(8,128)(2,1)S(1)} %get-tuple-element.49), channel_id=1, source_target_pairs={{0,24},{2,26},{4,28},{6,30},{8,0},{10,2},{12,4},{14,6},{16,8},{18,... | collective-permute-start | bytes 294920 | tf_op jit(solution)/shard_map/ppermute | solution.py:319
  53.8 3.5 %collective-permute-done.13.refs_1_ = bf16[128,384]{1,0:T(8,128)(2,1)S(1)} collective-permute-done((bf16[128,384]{1,0:T(8,128)(2,1)S(1)}, bf16[128,384]{1,0:T(8,128)(2,1)S(1)}, u32[]{:S(2)}, u32[]{:S(2)}) %collective-permute-start.13) | collective-permute-done | bytes 98336 | tf_op jit(solution)/shard_map/ppermute | solution.py:319
  57.4 5.6 %collective-permute-done.14.refs_2_ = bf16[128,384]{1,0:T(8,128)(2,1)S(1)} collective-permute-done((bf16[128,384]{1,0:T(8,128)(2,1)S(1)}, bf16[128,384]{1,0:T(8,128)(2,1)S(1)}, u32[]{:S(2)}, u32[]{:S(2)}) %collective-permute-start.14) | collective-permute-done | bytes 98336 | tf_op jit(solution)/shard_map/ppermute | solution.py:319
  63.0 1.6 %away.1 = bf16[128,2560]{1,0:T(8,128)(2,1)S(1)} custom-call(bf16[128,384]{1,0:T(8,128)(2,1)S(1)} %get-tuple-element.48.refs_0_, bf16[128,384]{1,0:T(8,128)(2,1)S(1)} %collective-permute-done.13.refs_1_, bf16[128,384]{1,0:T(8,128)(2,1)S(1)} %collective-permute-done.14.refs_2_, bf16[128,384]{1,0:T(8,128)(2,1)S(1)} %collective-permute-done.15.refs_3_, ...), custom_call_target="tpu_custom_call" | custom-call | flops 1006632960 | bytes 9175040 | tf_op jit(solution)/shard_map/away/pallas_call | solution.py:245
  64.5 1.6 %collective-permute-start.16 = (bf16[128,2560]{1,0:T(8,128)(2,1)S(1)}, bf16[128,2560]{1,0:T(8,128)(2,1)S(1)}, u32[]{:S(2)}, u32[]{:S(2)}) collective-permute-start(bf16[128,2560]{1,0:T(8,128)(2,1)S(1)} %away.1), channel_id=1, source_target_pairs={{0,1},{1,0},{2,3},{3,2},{4,5},{5,4},{6,7},{7,6},{8,9},{9,8},{10,11... | collective-permute-start | bytes 1966088 | tf_op jit(solution)/shard_map/ppermute | solution.py:389
  66.7 1.2 %collective-permute-done.19.refs_5_ = bf16[256,768]{1,0:T(8,128)(2,1)S(1)} collective-permute-done((bf16[256,768]{1,0:T(8,128)(2,1)S(1)}, bf16[256,768]{1,0:T(8,128)(2,1)S(1)}, u32[]{:S(2)}, u32[]{:S(2)}) %collective-permute-start.19) | collective-permute-done | bytes 393248 | tf_op jit(solution)/shard_map/ppermute | solution.py:322
  68.5 1.2 %cross.1 = (bf16[128,768]{1,0:T(8,128)(2,1)S(1)}, bf16[128,768]{1,0:T(8,128)(2,1)S(1)}) custom-call(bf16[192,768]{1,0:T(8,128)(2,1)S(1)} %pack_stay.1.refs_0_, bf16[192,768]{1,0:T(8,128)(2,1)S(1)} %collective-permute-done.refs_1_, bf16[256,768]{1,0:T(8,128)(2,1)S(1)} %pad_maximum_fusion.1.refs_2_, bf16[256,768]{1,0:T(8,128)(2,1)S(1)} %collective-permute-done.17.refs_3_, ...), custom_call_target="tpu_custom_call" | custom-call | flops 402653184 | bytes 2359296 | tf_op jit(solution)/shard_map/cross/pallas_call | solution.py:208
  69.7 1.1 %collective-permute-start.20 = (bf16[128,768]{1,0:T(8,128)(2,1)S(1)}, bf16[128,768]{1,0:T(8,128)(2,1)S(1)}, u32[]{:S(2)}, u32[]{:S(2)}) collective-permute-start(bf16[128,768]{1,0:T(8,128)(2,1)S(1)} %get-tuple-element.55), channel_id=1, source_target_pairs={{0,4},{2,6},{4,0},{6,2},{8,12},{10,14},{12,8},{14,10},{16,20},{18,... | collective-permute-start | bytes 589832 | tf_op jit(solution)/shard_map/ppermute | solution.py:322
  70.9 1.6 %home.1 = f32[128,2560]{1,0:T(8,128)S(1)} custom-call(bf16[128,384]{1,0:T(8,128)(2,1)S(1)} %get-tuple-element.48.refs_0_, bf16[128,384]{1,0:T(8,128)(2,1)S(1)} %collective-permute-done.13.refs_1_, bf16[128,384]{1,0:T(8,128)(2,1)S(1)} %collective-permute-done.14.refs_2_, bf16[128,384]{1,0:T(8,128)(2,1)S(1)} %collective-permute-done.15.refs_3_, ...), custom_call_target="tpu_custom_call" | custom-call | flops 1006632960 | bytes 9175040 | tf_op jit(solution)/shard_map/home/pallas_call | solution.py:245
  72.4 4.3 %collective-permute-done.20.came_ref = bf16[128,768]{1,0:T(8,128)(2,1)S(1)} collective-permute-done((bf16[128,768]{1,0:T(8,128)(2,1)S(1)}, bf16[128,768]{1,0:T(8,128)(2,1)S(1)}, u32[]{:S(2)}, u32[]{:S(2)}) %collective-permute-start.20) | collective-permute-done | bytes 196640 | tf_op jit(solution)/shard_map/ppermute | solution.py:322
  77.5 3.3 %collective-permute-done.16.away = bf16[128,2560]{1,0:T(8,128)(2,1)S(1)} collective-permute-done((bf16[128,2560]{1,0:T(8,128)(2,1)S(1)}, bf16[128,2560]{1,0:T(8,128)(2,1)S(1)}, u32[]{:S(2)}, u32[]{:S(2)}) %collective-permute-start.16) | collective-permute-done | bytes 655392 | tf_op jit(solution)/shard_map/ppermute | solution.py:389
  80.9 1.1 %finish.1 = bf16[128,2560]{1,0:T(8,128)(2,1)} custom-call(bf16[128,2560]{1,0:T(8,128)(2,1)S(1)} %copy-done.1, f32[1,2560]{1,0:T(1,128)S(1)} %broadcast_in_dim.3.gate, f32[128,2560]{1,0:T(8,128)S(1)} %home.1, bf16[128,2560]{1,0:T(8,128)(2,1)S(1)} %collective-permute-done.16.away), custom_call_target="tpu_custom_call" | custom-call | bytes 3276800 | tf_op jit(solution)/shard_map/finish/pallas_call | solution.py:282
  (46 shorter events, 9.0 us)
Async XLA Ops:
  0.6 62.3 %copy-start = (bf16[1536,5120]{1,0:T(8,128)(2,1)S(1)}, bf16[1536,5120]{1,0:T(8,128)(2,1)}, u32[]{:S(2)}) copy-start(bf16[1536,5120]{1,0:T(8,128)(2,1)} %refs_4_.3) | copy-start | bytes 47185924
  2.0 11.8 %collective-permute-start.2 = (bf16[128,512]{1,0:T(8,128)(2,1)S(1)}, bf16[128,512]{1,0:T(8,128)(2,1)S(1)}, u32[]{:S(2)}, u32[]{:S(2)}) collective-permute-start(bf16[128,512]{1,0:T(8,128)(2,1)S(1)} %get-tuple-element.33), channel_id=1, source_target_pairs={{0,8},{2,10},{4,12},{6,14},{8,16},{10,18},{12,20},{14,22},{16,24},... | collective-permute-start | bytes 393224 | tf_op jit(solution)/shard_map/ppermute | solution.py:319
  5.0 11.2 %collective-permute-start.5 = (bf16[128,512]{1,0:T(8,128)(2,1)S(1)}, bf16[128,512]{1,0:T(8,128)(2,1)S(1)}, u32[]{:S(2)}, u32[]{:S(2)}) collective-permute-start(bf16[128,512]{1,0:T(8,128)(2,1)S(1)} %get-tuple-element.37), channel_id=1, source_target_pairs={{0,16},{2,18},{4,20},{6,22},{8,24},{10,26},{12,28},{14,30},{16,0},... | collective-permute-start | bytes 393224 | tf_op jit(solution)/shard_map/ppermute | solution.py:319
  7.6 8.6 %collective-permute-start.6 = (bf16[128,512]{1,0:T(8,128)(2,1)S(1)}, bf16[128,512]{1,0:T(8,128)(2,1)S(1)}, u32[]{:S(2)}, u32[]{:S(2)}) collective-permute-start(bf16[128,512]{1,0:T(8,128)(2,1)S(1)} %get-tuple-element.38), channel_id=1, source_target_pairs={{0,24},{2,26},{4,28},{6,30},{8,0},{10,2},{12,4},{14,6},{16,8},{18,... | collective-permute-start | bytes 393224 | tf_op jit(solution)/shard_map/ppermute | solution.py:319
  9.9 8.0 %collective-permute-start = (bf16[192,768]{1,0:T(8,128)(2,1)S(1)}, bf16[192,768]{1,0:T(8,128)(2,1)S(1)}, u32[]{:S(2)}, u32[]{:S(2)}) collective-permute-start(bf16[192,768]{1,0:T(8,128)(2,1)S(1)} %pack_go.1), channel_id=1, source_target_pairs={{0,4},{2,6},{4,0},{6,2},{8,12},{10,14},{12,8},{14,10},{16,20},{18,... | collective-permute-start | bytes 884744 | tf_op jit(solution)/shard_map/ppermute | solution.py:322
  13.8 57.1 %copy-start.2 = (f32[2560]{0:T(1024)S(1)}, f32[2560]{0:T(1024)}, u32[]{:S(2)}) copy-start(f32[2560]{0:T(1024)} %param.17) | copy-start | bytes 30724
  16.3 13.8 %collective-permute-start.9 = (bf16[512,512]{1,0:T(8,128)(2,1)S(1)}, bf16[512,512]{1,0:T(8,128)(2,1)S(1)}, u32[]{:S(2)}, u32[]{:S(2)}) collective-permute-start(bf16[512,512]{1,0:T(8,128)(2,1)S(1)} %pad_maximum_fusion), channel_id=1, source_target_pairs={{0,4},{2,6},{4,0},{6,2},{8,12},{10,14},{12,8},{14,10},{16,20},{18,... | collective-permute-start | bytes 1572872 | tf_op jit(solution)/shard_map/ppermute | solution.py:322
  17.9 9.4 %collective-permute-start.1 = (bf16[128,640]{1,0:T(8,128)(2,1)S(1)}, bf16[128,640]{1,0:T(8,128)(2,1)S(1)}, u32[]{:S(2)}, u32[]{:S(2)}) collective-permute-start(bf16[128,640]{1,0:T(8,128)(2,1)S(1)} %get-tuple-element.31), channel_id=1, source_target_pairs={{0,8},{2,10},{4,12},{6,14},{8,16},{10,18},{12,20},{14,22},{16,24},... | collective-permute-start | bytes 491528 | tf_op jit(solution)/shard_map/ppermute | solution.py:319
  21.3 11.5 %collective-permute-start.3 = (bf16[128,640]{1,0:T(8,128)(2,1)S(1)}, bf16[128,640]{1,0:T(8,128)(2,1)S(1)}, u32[]{:S(2)}, u32[]{:S(2)}) collective-permute-start(bf16[128,640]{1,0:T(8,128)(2,1)S(1)} %get-tuple-element.34), channel_id=1, source_target_pairs={{0,16},{2,18},{4,20},{6,22},{8,24},{10,26},{12,28},{14,30},{16,0},... | collective-permute-start | bytes 491528 | tf_op jit(solution)/shard_map/ppermute | solution.py:319
  23.0 10.9 %collective-permute-start.4 = (bf16[128,640]{1,0:T(8,128)(2,1)S(1)}, bf16[128,640]{1,0:T(8,128)(2,1)S(1)}, u32[]{:S(2)}, u32[]{:S(2)}) collective-permute-start(bf16[128,640]{1,0:T(8,128)(2,1)S(1)} %get-tuple-element.36), channel_id=1, source_target_pairs={{0,24},{2,26},{4,28},{6,30},{8,0},{10,2},{12,4},{14,6},{16,8},{18,... | collective-permute-start | bytes 491528 | tf_op jit(solution)/shard_map/ppermute | solution.py:319
  23.7 13.0 %collective-permute-start.7 = (bf16[128,768]{1,0:T(8,128)(2,1)S(1)}, bf16[128,768]{1,0:T(8,128)(2,1)S(1)}, u32[]{:S(2)}, u32[]{:S(2)}) collective-permute-start(bf16[128,768]{1,0:T(8,128)(2,1)S(1)} %pad_maximum_fusion.3), channel_id=1, source_target_pairs={{0,8},{2,10},{4,12},{6,14},{8,0},{10,2},{12,4},{14,6},{16,24},{18,... | collective-permute-start | bytes 589832 | tf_op jit(solution)/shard_map/ppermute | solution.py:322
  30.2 13.7 %collective-permute-start.10 = (bf16[1024,512]{1,0:T(8,128)(2,1)S(1)}, bf16[1024,512]{1,0:T(8,128)(2,1)S(1)}, u32[]{:S(2)}, u32[]{:S(2)}) collective-permute-start(bf16[1024,512]{1,0:T(8,128)(2,1)S(1)} %constant_dynamic-update-slice_fusion.5.refs_4_), channel_id=1, source_target_pairs={{0,2},{2,0},{4,6},{6,4},{8,10},{10,8},{12,14},{14,12},{16,18},{18,... | collective-permute-start | bytes 3145736 | tf_op jit(solution)/shard_map/ppermute | solution.py:322
  36.8 7.0 %collective-permute-start.8 = (bf16[512,256]{1,0:T(8,128)(2,1)S(1)}, bf16[512,256]{1,0:T(8,128)(2,1)S(1)}, u32[]{:S(2)}, u32[]{:S(2)}) collective-permute-start(bf16[512,256]{1,0:T(8,128)(2,1)S(1)} %pad_maximum_fusion.2), channel_id=1, source_target_pairs={{0,4},{2,6},{4,0},{6,2},{8,12},{10,14},{12,8},{14,10},{16,20},{18,... | collective-permute-start | bytes 786440 | tf_op jit(solution)/shard_map/ppermute | solution.py:322
  37.4 10.2 %collective-permute-start.11 = (bf16[128,768]{1,0:T(8,128)(2,1)S(1)}, bf16[128,768]{1,0:T(8,128)(2,1)S(1)}, u32[]{:S(2)}, u32[]{:S(2)}) collective-permute-start(bf16[128,768]{1,0:T(8,128)(2,1)S(1)} %pad_maximum_fusion.3), channel_id=1, source_target_pairs={{0,16},{2,18},{4,20},{6,22},{8,24},{10,26},{12,28},{14,30},{16,0},... | collective-permute-start | bytes 589832 | tf_op jit(solution)/shard_map/ppermute | solution.py:322
  47.6 1.9 %collective-permute-start.12 = (bf16[1024,256]{1,0:T(8,128)(2,1)S(1)}, bf16[1024,256]{1,0:T(8,128)(2,1)S(1)}, u32[]{:S(2)}, u32[]{:S(2)}) collective-permute-start(bf16[1024,256]{1,0:T(8,128)(2,1)S(1)} %constant_dynamic-update-slice_fusion.refs_4_), channel_id=1, source_target_pairs={{0,2},{2,0},{4,6},{6,4},{8,10},{10,8},{12,14},{14,12},{16,18},{18,... | collective-permute-start | bytes 1572872 | tf_op jit(solution)/shard_map/ppermute | solution.py:322
  47.6 18.5 %collective-permute-start.18 = (bf16[128,768]{1,0:T(8,128)(2,1)S(1)}, bf16[128,768]{1,0:T(8,128)(2,1)S(1)}, u32[]{:S(2)}, u32[]{:S(2)}) collective-permute-start(bf16[128,768]{1,0:T(8,128)(2,1)S(1)} %collective-permute-done.11), channel_id=1, source_target_pairs={{0,8},{2,10},{4,12},{6,14},{8,0},{10,2},{12,4},{14,6},{16,24},{18,... | collective-permute-start | bytes 589832 | tf_op jit(solution)/shard_map/ppermute | solution.py:322
  51.3 6.1 %collective-permute-start.13 = (bf16[128,384]{1,0:T(8,128)(2,1)S(1)}, bf16[128,384]{1,0:T(8,128)(2,1)S(1)}, u32[]{:S(2)}, u32[]{:S(2)}) collective-permute-start(bf16[128,384]{1,0:T(8,128)(2,1)S(1)} %get-tuple-element.49), channel_id=1, source_target_pairs={{0,24},{2,26},{4,28},{6,30},{8,0},{10,2},{12,4},{14,6},{16,8},{18,... | collective-permute-start | bytes 294920 | tf_op jit(solution)/shard_map/ppermute | solution.py:319
  52.8 10.1 %collective-permute-start.14 = (bf16[128,384]{1,0:T(8,128)(2,1)S(1)}, bf16[128,384]{1,0:T(8,128)(2,1)S(1)}, u32[]{:S(2)}, u32[]{:S(2)}) collective-permute-start(bf16[128,384]{1,0:T(8,128)(2,1)S(1)} %get-tuple-element.50), channel_id=1, source_target_pairs={{0,16},{2,18},{4,20},{6,22},{8,24},{10,26},{12,28},{14,30},{16,0},... | collective-permute-start | bytes 294920 | tf_op jit(solution)/shard_map/ppermute | solution.py:319
  53.8 9.1 %collective-permute-start.15 = (bf16[128,384]{1,0:T(8,128)(2,1)S(1)}, bf16[128,384]{1,0:T(8,128)(2,1)S(1)}, u32[]{:S(2)}, u32[]{:S(2)}) collective-permute-start(bf16[128,384]{1,0:T(8,128)(2,1)S(1)} %get-tuple-element.51), channel_id=1, source_target_pairs={{0,8},{2,10},{4,12},{6,14},{8,16},{10,18},{12,20},{14,22},{16,24},... | collective-permute-start | bytes 294920 | tf_op jit(solution)/shard_map/ppermute | solution.py:319
  63.0 17.9 %copy-start.1 = (bf16[128,2560]{1,0:T(8,128)(2,1)S(1)}, bf16[128,2560]{1,0:T(8,128)(2,1)}, u32[]{:S(2)}) copy-start(bf16[128,2560]{1,0:T(8,128)(2,1)} %tokens.1) | copy-start | bytes 1966084
  64.5 16.3 %collective-permute-start.16 = (bf16[128,2560]{1,0:T(8,128)(2,1)S(1)}, bf16[128,2560]{1,0:T(8,128)(2,1)S(1)}, u32[]{:S(2)}, u32[]{:S(2)}) collective-permute-start(bf16[128,2560]{1,0:T(8,128)(2,1)S(1)} %away.1), channel_id=1, source_target_pairs={{0,1},{1,0},{2,3},{3,2},{4,5},{5,4},{6,7},{7,6},{8,9},{9,8},{10,11... | collective-permute-start | bytes 1966088 | tf_op jit(solution)/shard_map/ppermute | solution.py:389
  66.1 1.8 %collective-permute-start.19 = (bf16[256,768]{1,0:T(8,128)(2,1)S(1)}, bf16[256,768]{1,0:T(8,128)(2,1)S(1)}, u32[]{:S(2)}, u32[]{:S(2)}) collective-permute-start(bf16[256,768]{1,0:T(8,128)(2,1)S(1)} %constant_dynamic-update-slice_fusion.10.refs_4_), channel_id=1, source_target_pairs={{0,2},{2,0},{4,6},{6,4},{8,10},{10,8},{12,14},{14,12},{16,18},{18,... | collective-permute-start | bytes 1179656 | tf_op jit(solution)/shard_map/ppermute | solution.py:322
  66.2 2.3 %collective-permute-start.17 = (bf16[256,768]{1,0:T(8,128)(2,1)S(1)}, bf16[256,768]{1,0:T(8,128)(2,1)S(1)}, u32[]{:S(2)}, u32[]{:S(2)}) collective-permute-start(bf16[256,768]{1,0:T(8,128)(2,1)S(1)} %pad_maximum_fusion.1.refs_2_), channel_id=1, source_target_pairs={{0,2},{2,0},{4,6},{6,4},{8,10},{10,8},{12,14},{14,12},{16,18},{18,... | collective-permute-start | bytes 1179656 | tf_op jit(solution)/shard_map/ppermute | solution.py:322
  69.7 7.0 %collective-permute-start.20 = (bf16[128,768]{1,0:T(8,128)(2,1)S(1)}, bf16[128,768]{1,0:T(8,128)(2,1)S(1)}, u32[]{:S(2)}, u32[]{:S(2)}) collective-permute-start(bf16[128,768]{1,0:T(8,128)(2,1)S(1)} %get-tuple-element.55), channel_id=1, source_target_pairs={{0,4},{2,6},{4,0},{6,2},{8,12},{10,14},{12,8},{14,10},{16,20},{18,... | collective-permute-start | bytes 589832 | tf_op jit(solution)/shard_map/ppermute | solution.py:322
